TPU v7x, 32 devices: a whole 2x2x4 slice. The times are simulated.
32 devices in a mesh: dp: 2 (over core), blk: 4 (over y, x), head: 4 (over z).
Axes of the slice: x: 2, y: 2, z: 4, core: 2. Of those that a mesh axis runs over, the one named last changes fastest.
Arguments:
- activations: bfloat16 [2, 2, 2048, 1536], P(None, 'dp', ('blk', 'head')), may hold values from -6 to 6
- segments: int32 [2, 2, 2048], P(None, 'dp', 'blk'), may hold values from 0 to 15, never falling along the last dimension, each value on 1 to 1024 neighbouring positions
- cotangent: bfloat16 [2, 2, 2048, 1536], P(None, 'dp', ('blk', 'head')), may hold values from -6 to 6
- norm_gain_one: bfloat16 [1536], P(('dp', 'blk')), may hold values from 0.5 to 1.5
- query_weight: bfloat16 [1536, 1536], P(('dp', 'blk')), may hold values from -0.15625 to 0.15625
- key_weight: bfloat16 [1536, 768], P(('dp', 'blk')), may hold values from -0.15625 to 0.15625
- value_weight: bfloat16 [1536, 768], P(('dp', 'blk')), may hold values from -0.15625 to 0.15625
- output_weight: bfloat16 [1536, 1536], P(('dp', 'blk')), may hold values from -1.25 to 1.25
- norm_gain_two: bfloat16 [1536], P(('dp', 'blk')), may hold values from 0.5 to 1.5
- gate_weight: bfloat16 [1536, 4096], P(('dp', 'blk')), may hold values from -0.15625 to 0.15625
- up_weight: bfloat16 [1536, 4096], P(('dp', 'blk')), may hold values from -0.15625 to 0.15625
- down_weight: bfloat16 [4096, 1536], P(('dp', 'blk')), may hold values from -0.09375 to 0.09375
Outputs:
- block_out: bfloat16 [2, 2, 2048, 1536], P(None, 'dp', ('blk', 'head'))
- grad_input: bfloat16 [2, 2, 2048, 1536], P(None, 'dp', ('blk', 'head'))
- grad_gain_one: float32 [1536], P(('dp', 'blk'))
- grad_query: float32 [1536, 1536], P(('dp', 'blk'))
- grad_key: float32 [1536, 768], P(('dp', 'blk'))
- grad_value: float32 [1536, 768], P(('dp', 'blk'))
- grad_output: float32 [1536, 1536], P(('dp', 'blk'))
- grad_gain_two: float32 [1536], P(('dp', 'blk'))
- grad_gate: float32 [1536, 4096], P(('dp', 'blk'))
- grad_up: float32 [1536, 4096], P(('dp', 'blk'))
- grad_down: float32 [4096, 1536], P(('dp', 'blk'))
Inputs may be any that keep to these rules, and one draw needn't show every extreme that they name: `segments`: along each sequence the segment numbers never fall and every number is used; a document has at most 1024 tokens, and in every sequence one has exactly that many.
All inputs are finite; a program needn't handle non-finite values.
Results may differ from a plain program's by a relative error of at most 0.023.
Values may be sent and summed in bfloat16 or wider, within the bound.
No kernel may reach another device: no remote copies, remote signals or barrier semaphores. Data moves between devices by JAX's collectives and lax.ppermute only.
A program may use at most 320 MiB of HBM per device.

v0:
```python
import math

import jax
import jax.numpy as jnp
from jax import lax
from jax.sharding import PartitionSpec as P

D = 1536
QH = 16
KVH = 8
HD = 96
FF = 4096


EPS = 1e-05
NEG = -1e30


def shortened(value):
    return jax.tree.map(lambda a: a.astype(jnp.bfloat16) if a.dtype == jnp.float32 else a, value)


def plain_dot(left, right):
    return jnp.dot(left, right, preferred_element_type=jnp.float32)


def first_dot(left, right):
    return lax.dot_general(
        left, right, (((0,), (0,)), ((), ())), preferred_element_type=jnp.float32
    )


def last_dot(left, right):
    return lax.dot_general(
        left, right, (((1,), (1,)), ((), ())), preferred_element_type=jnp.float32
    )


def normalize(values):
    factor = lax.rsqrt(jnp.mean(values * values, -1, keepdims=True) + EPS)
    return (values * factor, factor)


def norm_back(grad_norm, gain, normed, factor):
    scaled = grad_norm * gain
    return factor * (scaled - normed * jnp.mean(scaled * normed, -1, keepdims=True))


def per_device(
    activations,
    segments,
    cotangent,
    norm_gain_one,
    query_weight,
    key_weight,
    value_weight,
    output_weight,
    norm_gain_two,
    gate_weight,
    up_weight,
    down_weight,
):
    shards = (
        norm_gain_one,
        query_weight,
        key_weight,
        value_weight,
        output_weight,
        norm_gain_two,
        gate_weight,
        up_weight,
        down_weight,
    )
    head_count = lax.axis_size("head")
    cycle_count = lax.axis_size("blk")
    tok_rows = activations.shape[2]
    span_len = tok_rows * head_count
    seq_len = span_len * cycle_count
    heads_here = QH // head_count
    kv_repeat = max(1, head_count // KVH)
    kv_here = KVH * kv_repeat // head_count
    group_size = heads_here // kv_here
    block_rows = span_len if span_len <= 1024 else 1024
    block_count = span_len // block_rows
    scale = 1.0 / math.sqrt(HD)
    first_pos = lax.axis_index("blk") * span_len
    full_shapes = (
        (D,),
        (D, QH * HD),
        (D, KVH * HD),
        (D, KVH * HD),
        (QH * HD, D),
        (D,),
        (D, FF),
        (D, FF),
        (FF, D),
    )
    totals = tuple((jnp.zeros(shape_full, jnp.float32) for shape_full in full_shapes))
    results = []
    grads_x = []
    for batch_index in range(activations.shape[0]):
        seg_rows = segments[batch_index, 0]
        cot_rows = cotangent[batch_index, 0]
        gain_one = lax.all_gather(shards[0], ("dp", "blk"), axis=0, tiled=True)
        query_w = lax.all_gather(shards[1], ("dp", "blk"), axis=0, tiled=True)
        key_w = lax.all_gather(shards[2], ("dp", "blk"), axis=0, tiled=True)
        value_w = lax.all_gather(shards[3], ("dp", "blk"), axis=0, tiled=True)
        out_w = lax.all_gather(shards[4], ("dp", "blk"), axis=0, tiled=True)
        gain_two = lax.all_gather(shards[5], ("dp", "blk"), axis=0, tiled=True)
        gate_w = lax.all_gather(shards[6], ("dp", "blk"), axis=0, tiled=True)
        up_w = lax.all_gather(shards[7], ("dp", "blk"), axis=0, tiled=True)
        down_w = lax.all_gather(shards[8], ("dp", "blk"), axis=0, tiled=True)
        gain_one_f = gain_one.astype(jnp.float32)
        gain_two_f = gain_two.astype(jnp.float32)
        x_float = activations[batch_index, 0].astype(jnp.float32)
        normed_one, factor_one = normalize(x_float)
        input_one = (normed_one * gain_one_f).astype(jnp.bfloat16)
        queries = plain_dot(input_one, query_w).astype(jnp.bfloat16).reshape(tok_rows, QH, HD)
        keys = plain_dot(input_one, key_w).astype(jnp.bfloat16).reshape(tok_rows, KVH, HD)
        values = plain_dot(input_one, value_w).astype(jnp.bfloat16).reshape(tok_rows, KVH, HD)
        if kv_repeat > 1:
            keys = jnp.repeat(keys, kv_repeat, axis=1)
            values = jnp.repeat(values, kv_repeat, axis=1)
        head_q = lax.all_to_all(queries, "head", split_axis=1, concat_axis=0, tiled=True)
        head_k = lax.all_to_all(keys, "head", split_axis=1, concat_axis=0, tiled=True)
        head_v = lax.all_to_all(values, "head", split_axis=1, concat_axis=0, tiled=True)
        query_blocks = head_q.reshape(block_count, block_rows, kv_here, group_size, HD)
        pos_blocks = (first_pos + jnp.arange(span_len, dtype=jnp.int32)).reshape(
            block_count, block_rows
        )
        seg_blocks = seg_rows.reshape(block_count, block_rows)
        key_piece = lax.all_gather(head_k, "blk", axis=0, tiled=True)
        value_piece = lax.all_gather(head_v, "blk", axis=0, tiled=True)
        seg_piece = lax.all_gather(seg_rows, "blk", axis=0, tiled=True)
        key_pos = jnp.arange(key_piece.shape[0], dtype=jnp.int32)

        def one_block(inputs):
            query_blk, query_pos, query_seg, run_max, run_sum, run_acc = inputs
            scores = (
                jnp.einsum(
                    "qhrd,khd->hrqk", query_blk, key_piece, preferred_element_type=jnp.float32
                )
                * scale
            )
            allowed = (key_pos[None, :] <= query_pos[:, None]) & (
                seg_piece[None, :] == query_seg[:, None]
            )
            new_max = jnp.maximum(run_max, jnp.max(jnp.where(allowed, scores, NEG), axis=-1))
            expo = jnp.where(allowed, jnp.exp(scores - new_max[..., None]), 0.0)
            decay = jnp.exp(run_max - new_max)
            new_sum = run_sum * decay + jnp.sum(expo, -1)
            new_acc = run_acc * decay[..., None] + jnp.einsum(
                "hrqk,khd->hrqd",
                expo.astype(jnp.bfloat16),
                value_piece,
                preferred_element_type=jnp.float32,
            )
            return (new_max, new_sum, new_acc)

        run_max, run_sum, run_acc = lax.map(
            one_block,
            (
                query_blocks,
                pos_blocks,
                seg_blocks,
                jnp.full((block_count, kv_here, group_size, block_rows), NEG, jnp.float32),
                jnp.zeros((block_count, kv_here, group_size, block_rows), jnp.float32),
                jnp.zeros((block_count, kv_here, group_size, block_rows, HD), jnp.float32),
            ),
        )
        attn_heads = run_acc / run_sum[..., None]
        log_total = run_max + jnp.log(run_sum)
        attn_low = (
            attn_heads.transpose(0, 3, 1, 2, 4)
            .reshape(span_len, heads_here, HD)
            .astype(jnp.bfloat16)
        )
        attn_tok = lax.all_to_all(
            attn_low, "head", split_axis=0, concat_axis=1, tiled=True
        ).reshape(tok_rows, QH * HD)
        x_mid = x_float + plain_dot(attn_tok, out_w)
        normed_two, factor_two = normalize(x_mid)
        input_two = (normed_two * gain_two_f).astype(jnp.bfloat16)
        gate_val = plain_dot(input_two, gate_w)
        up_val = plain_dot(input_two, up_w)
        sigma = jax.nn.sigmoid(gate_val)
        silu_val = gate_val * sigma
        hidden = (silu_val * up_val).astype(jnp.bfloat16)
        result = (x_mid + plain_dot(hidden, down_w)).astype(jnp.bfloat16)
        grad_down = first_dot(hidden, cot_rows)
        grad_hidden = last_dot(cot_rows, down_w)
        grad_gate_val = (grad_hidden * up_val * sigma * (1.0 + gate_val * (1.0 - sigma))).astype(
            jnp.bfloat16
        )
        grad_up_val = (grad_hidden * silu_val).astype(jnp.bfloat16)
        grad_gate_w = first_dot(input_two, grad_gate_val)
        grad_up_w = first_dot(input_two, grad_up_val)
        grad_input_two = last_dot(grad_gate_val, gate_w) + last_dot(grad_up_val, up_w)
        grad_gain_two = jnp.sum(grad_input_two * normed_two, 0)
        grad_mid = cot_rows.astype(jnp.float32) + norm_back(
            grad_input_two, gain_two_f, normed_two, factor_two
        )
        grad_branch = grad_mid.astype(jnp.bfloat16)
        grad_out_w = first_dot(attn_tok, grad_branch)
        grad_attn = last_dot(grad_branch, out_w).astype(jnp.bfloat16).reshape(tok_rows, QH, HD)
        grad_heads = lax.all_to_all(grad_attn, "head", split_axis=1, concat_axis=0, tiled=True)
        grad_blocks = grad_heads.reshape(block_count, block_rows, kv_here, group_size, HD)
        delta = jnp.sum(grad_blocks.astype(jnp.float32).transpose(0, 2, 3, 1, 4) * attn_heads, -1)
        full_k = lax.all_gather(head_k, "blk", axis=0, tiled=True)
        full_v = lax.all_gather(head_v, "blk", axis=0, tiled=True)
        full_seg = lax.all_gather(seg_rows, "blk", axis=0, tiled=True)
        key_k = full_k.reshape(cycle_count, span_len, kv_here, HD)
        key_v = full_v.reshape(cycle_count, span_len, kv_here, HD)
        key_seg = full_seg.reshape(cycle_count, span_len)
        key_pos = jnp.arange(seq_len, dtype=jnp.int32).reshape(cycle_count, span_len)

        def key_step(grad_total, key_inputs):
            blk_k, blk_v, blk_seg, blk_pos = key_inputs

            def query_step(carry, inputs):
                sum_k, sum_v = carry
                query_blk, query_pos, query_seg, lse_blk, delta_blk, grad_blk = inputs
                scores = (
                    jnp.einsum(
                        "qhrd,khd->hrqk", query_blk, blk_k, preferred_element_type=jnp.float32
                    )
                    * scale
                )
                allowed = (blk_pos[None, :] <= query_pos[:, None]) & (
                    blk_seg[None, :] == query_seg[:, None]
                )
                probs = jnp.where(allowed, jnp.exp(scores - lse_blk[..., None]), 0.0)
                grad_probs = jnp.einsum(
                    "qhrd,khd->hrqk", grad_blk, blk_v, preferred_element_type=jnp.float32
                )
                grad_scores = (probs * (grad_probs - delta_blk[..., None])).astype(jnp.bfloat16)
                grad_query = (
                    jnp.einsum(
                        "hrqk,khd->qhrd", grad_scores, blk_k, preferred_element_type=jnp.float32
                    )
                    * scale
                )
                sum_k = (
                    sum_k
                    + jnp.einsum(
                        "hrqk,qhrd->khd", grad_scores, query_blk, preferred_element_type=jnp.float32
                    )
                    * scale
                )
                sum_v = sum_v + jnp.einsum(
                    "hrqk,qhrd->khd",
                    probs.astype(jnp.bfloat16),
                    grad_blk,
                    preferred_element_type=jnp.float32,
                )
                return ((sum_k, sum_v), grad_query)

            empty_kv = jnp.zeros((span_len, kv_here, HD), jnp.float32)
            (sum_k, sum_v), grad_part = lax.scan(
                query_step,
                (empty_kv, empty_kv),
                (query_blocks, pos_blocks, seg_blocks, log_total, delta, grad_blocks),
            )
            return (grad_total + grad_part, (sum_k, sum_v))

        grad_start = jnp.zeros((block_count, block_rows, kv_here, group_size, HD), jnp.float32)
        grad_query, (sums_k, sums_v) = lax.scan(
            key_step, grad_start, (key_k, key_v, key_seg, key_pos)
        )
        sum_k = sums_k.reshape(seq_len, kv_here, HD)
        sum_v = sums_v.reshape(seq_len, kv_here, HD)
        owned_k = lax.psum_scatter(
            sum_k.astype(jnp.bfloat16), "blk", scatter_dimension=0, tiled=True
        ).astype(jnp.float32)
        owned_v = lax.psum_scatter(
            sum_v.astype(jnp.bfloat16), "blk", scatter_dimension=0, tiled=True
        ).astype(jnp.float32)
        grad_query = grad_query.reshape(span_len, heads_here, HD)
        tok_q = lax.all_to_all(
            grad_query.astype(jnp.bfloat16), "head", split_axis=0, concat_axis=1, tiled=True
        ).astype(grad_query.dtype)
        tok_k = lax.all_to_all(
            owned_k.astype(jnp.bfloat16), "head", split_axis=0, concat_axis=1, tiled=True
        ).astype(owned_k.dtype)
        tok_v = lax.all_to_all(
            owned_v.astype(jnp.bfloat16), "head", split_axis=0, concat_axis=1, tiled=True
        ).astype(owned_v.dtype)
        tok_q = tok_q.reshape(tok_rows, QH * HD).astype(jnp.bfloat16)
        tok_k = (
            jnp.sum(tok_k.reshape(tok_rows, KVH, kv_repeat, HD), 2)
            .reshape(tok_rows, KVH * HD)
            .astype(jnp.bfloat16)
        )
        tok_v = (
            jnp.sum(tok_v.reshape(tok_rows, KVH, kv_repeat, HD), 2)
            .reshape(tok_rows, KVH * HD)
            .astype(jnp.bfloat16)
        )
        grad_query_w = first_dot(input_one, tok_q)
        grad_key_w = first_dot(input_one, tok_k)
        grad_value_w = first_dot(input_one, tok_v)
        grad_input_one = (
            last_dot(tok_q, query_w) + last_dot(tok_k, key_w) + last_dot(tok_v, value_w)
        )
        grad_gain_one = jnp.sum(grad_input_one * normed_one, 0)
        grad_x = (grad_mid + norm_back(grad_input_one, gain_one_f, normed_one, factor_one)).astype(
            jnp.bfloat16
        )
        result, grad_x, terms = (
            result,
            grad_x,
            (
                grad_gain_one,
                grad_query_w,
                grad_key_w,
                grad_value_w,
                grad_out_w,
                grad_gain_two,
                grad_gate_w,
                grad_up_w,
                grad_down,
            ),
        )
        results.append(result)
        grads_x.append(grad_x)
        totals = tuple((left + right for left, right in zip(totals, terms)))
    owned = jax.tree.map(
        lambda part: part.astype(jnp.float32),
        lax.psum_scatter(shortened(totals), ("dp", "blk"), scatter_dimension=0, tiled=True),
    )
    owned = jax.tree.map(lambda part: part.astype(jnp.float32), lax.psum(shortened(owned), "head"))
    block_out = jnp.stack(results)[:, None]
    grad_input = jnp.stack(grads_x)[:, None]
    return (
        block_out,
        grad_input,
        owned[0],
        owned[1],
        owned[2],
        owned[3],
        owned[4],
        owned[5],
        owned[6],
        owned[7],
        owned[8],
    )


def solution(mesh):
    placed = (
        P(None, "dp", ("blk", "head"), None),
        P(None, "dp", "blk"),
        P(None, "dp", ("blk", "head"), None),
        P(("dp", "blk")),
        P(("dp", "blk"), None),
        P(("dp", "blk"), None),
        P(("dp", "blk"), None),
        P(("dp", "blk"), None),
        P(("dp", "blk")),
        P(("dp", "blk"), None),
        P(("dp", "blk"), None),
        P(("dp", "blk"), None),
    )
    return jax.shard_map(
        per_device,
        mesh=mesh,
        in_specs=placed,
        out_specs=(
            P(None, "dp", ("blk", "head"), None),
            P(None, "dp", ("blk", "head"), None),
            P(("dp", "blk")),
            P(("dp", "blk"), None),
            P(("dp", "blk"), None),
            P(("dp", "blk"), None),
            P(("dp", "blk"), None),
            P(("dp", "blk")),
            P(("dp", "blk"), None),
            P(("dp", "blk"), None),
            P(("dp", "blk"), None),
        ),
        check_vma=False,
    )
```

profile of v0, /device:TPU:8, one launch (start us, length us, event | category | flops | bytes accessed | tf_op | source)
XLA Modules:
  0.0 1425.9 jit_solution(12849763053035598999)
XLA Ops:
  13.7 14.9 %all-reduce.5 = (bf16[1536]{0:T(1024)(128)(2,1)S(1)}, bf16[1536]{0:T(1024)(128)(2,1)S(1)}) all-reduce(bf16[1536]{0:T(1024)(128)(2,1)S(1)} %dynamic-update-slice, bf16[1536]{0:T(1024)(128)(2,1)S(1)} %dynamic-update-slice.1), channel_id=1, replica_groups=mesh['dp'=2,'blk'=4,'head'=4] {'dp','blk'}, use_global_device_ids=true, to_apply=%add | all-reduce | flops 3072 | bytes 12288
  29.3 8.7 all-gather
  38.0 7.0 all-gather.1
  51.4 5.4 all-to-all-start.4
  56.7 14.8 %all-gather.14.cloned.1.call-done = bf16[1536,768]{1,0:T(8,128)(2,1)} async-done(((bf16[192,768]{1,0:T(8,128)(2,1)}), bf16[1536,768]{1,0:T(8,128)(2,1)}) %all-gather.14.cloned.1.call-update) | async-done | bytes 2359312 | tf_op jit(solution)/shard_map/all_gather | solution.py:107
  76.3 5.1 all-to-all-start.6
  87.9 5.5 all-to-all-start
  104.3 14.0 all_gather.73
  118.3 16.0 %all_gather.74 = bf16[2048,2,96]{0,2,1:T(8,128)(2,1)} all-gather(bf16[512,2,96]{0,2,1:T(8,128)(2,1)S(1)} %all_to_all.220), channel_id=1, replica_groups=mesh['dp'=2,'blk'=4,'head'=4] {'blk'}, dimensions={0}, use_global_device_ids=true | all-gather | bytes 983040 | tf_op jit(solution)/shard_map/all_gather | solution.py:133
  138.4 5.0 all-to-all-start.5
  143.4 19.7 %all_gather.63 = bf16[2048,2,96]{0,2,1:T(8,128)(2,1)} all-gather(bf16[512,2,96]{0,2,1:T(8,128)(2,1)S(1)} %all_to_all.199), channel_id=1, replica_groups=mesh['dp'=2,'blk'=4,'head'=4] {'blk'}, dimensions={0}, use_global_device_ids=true | all-gather | bytes 983040 | tf_op jit(solution)/shard_map/all_gather | solution.py:132
  163.3 11.7 all_gather.66
  175.0 4.6 convolution_convert_fusion.3
  181.5 5.3 all-to-all-start.1
  189.1 4.3 fusion.74
  197.1 4.4 fusion.208
  203.7 5.1 all-to-all-start.7
  211.0 4.6 fusion.77
  219.3 4.4 fusion.209
  225.8 5.3 all-to-all-start.3
  249.2 8.4 fusion.210
  257.5 54.8 %all-gather.20.cloned.1.call-done = bf16[1536,4096]{1,0:T(8,128)(2,1)} async-done(((bf16[192,4096]{1,0:T(8,128)(2,1)}), bf16[1536,4096]{1,0:T(8,128)(2,1)}) %all-gather.20.cloned.1.call-update) | async-done | bytes 12582928 | tf_op jit(solution)/shard_map/all_gather | solution.py:111
  312.4 7.7 fusion.211
  320.1 66.3 %all-gather.22.cloned.1.call-done = bf16[4096,1536]{1,0:T(8,128)(2,1)} async-done(((bf16[512,1536]{1,0:T(8,128)(2,1)}), bf16[4096,1536]{1,0:T(8,128)(2,1)}) %all-gather.22.cloned.1.call-update) | async-done | bytes 12582928 | tf_op jit(solution)/shard_map/all_gather | solution.py:112
  386.4 11.4 multiply_convert_fusion.2
  397.8 10.5 fusion.214
  408.4 11.6 multiply_reduce_fusion.1
  424.2 6.5 fusion.213
  430.7 9.9 multiply_convert_fusion
  440.6 9.8 fusion.216
  450.5 9.7 multiply_reduce_fusion
  463.3 5.1 all-to-all-start.12
  473.4 4.5 all-to-all-done.12
  477.9 6.7 all-to-all-start.8
  488.2 50.1 %while.25 = (s32[]{:T(128)}, f32[1,512,2,2,96]{1,4,3,2,0:T(8,128)}, bf16[4,512,2,96]{1,3,2,0:T(8,128)(2,1)}, bf16[4,512,2,96]{1,3,2,0:T(8,128)(2,1)}, bf16[4,512...) while((s32[]{:T(128)}, f32[1,512,2,2,96]{1,4,3,2,0:T(8,128)}, ...), condition=%wide.region_18.19_spmd.clone, body=%wide.region_17.18_spmd.clone.sunk | while | flops 1018593792 | bytes 67217776 | solution.py:267
  544.1 46.2 %while.24 = (s32[]{:T(128)}, f32[1,512,2,2,96]{1,4,3,2,0:T(8,128)S(1)}, bf16[4,512,2,96]{1,3,2,0:T(8,128)(2,1)}, bf16[4,512,2,96]{1,3,2,0:T(8,128)(2,1)}, bf16[4...) while((s32[]{:T(128)}, ...), condition=%wide.region_11.12_spmd.clone, body=%wide.region_10.11_spmd.clone.sunk | while | flops 1018593792 | bytes 69314976 | solution.py:267
  597.8 5.2 all-to-all-start.14
  603.0 15.8 %reduce-scatter.12.cloned.1.call-done = bf16[512,2,96]{0,2,1:T(8,128)(2,1)} async-done(((bf16[2048,2,96]{0,2,1:T(8,128)(2,1)}), bf16[512,2,96]{0,2,1:T(8,128)(2,1)}) %reduce-scatter.12.cloned.1.call-update) | async-done | bytes 196624 | tf_op jit(solution)/shard_map/reduce_scatter | solution.py:272
  620.6 5.1 all-to-all-start.10
  626.0 6.8 all-to-all-done.10
  636.3 12.0 reduce-scatter.18.cloned.1.call-done
  650.1 5.1 all-to-all-start.15
  655.2 22.1 %reduce-scatter.14.cloned.1.call-done = bf16[512,2,96]{0,2,1:T(8,128)(2,1)} async-done(((bf16[2048,2,96]{0,2,1:T(8,128)(2,1)}), bf16[512,2,96]{0,2,1:T(8,128)(2,1)}) %reduce-scatter.14.cloned.1.call-update) | async-done | bytes 196624 | tf_op jit(solution)/shard_map/reduce_scatter | solution.py:275
  679.1 5.1 all-to-all-start.11
  684.5 6.8 all-to-all-done.11
  702.5 5.5 all-to-all-start.13
  709.1 8.9 all-to-all-done.13
  718.1 6.3 all-to-all-start.9
  724.7 10.0 all-to-all-done.9
  741.2 11.8 fusion.218
  753.0 15.0 %add_convert_fusion.2 = bf16[1536,4096]{1,0:T(8,128)(2,1)} fusion(f32[1536,4096]{1,0:T(8,128)} %fusion.218, bf16[128,1536]{1,0:T(8,128)(2,1)S(1)} %copy-done.16, bf16[128,4096]{1,0:T(8,128)(2,1)S(1)} %copy-done.37), kind=kOutput, calls=%fused_computation.80 | convolution fusion | flops 1623195648 | bytes 39190528 | tf_op jit(solution)/shard_map/dot_general | solution.py:28
  768.3 11.9 fusion.219
  780.1 16.9 %add_convert_fusion.1 = bf16[1536,4096]{1,0:T(8,128)(2,1)} fusion(f32[1536,4096]{1,0:T(8,128)} %fusion.219, bf16[128,1536]{1,0:T(8,128)(2,1)S(1)} %copy-done.16, bf16[128,4096]{1,0:T(8,128)(2,1)S(1)} %copy-done.35), kind=kOutput, calls=%fused_computation.79 | convolution fusion | flops 1623195648 | bytes 39190528 | tf_op jit(solution)/shard_map/dot_general | solution.py:28
  798.3 11.9 fusion.165
  810.2 14.7 %add_convert_fusion = bf16[4096,1536]{1,0:T(8,128)(2,1)} fusion(f32[4096,1536]{1,0:T(8,128)} %fusion.165, bf16[128,4096]{1,0:T(8,128)(2,1)S(1)} %copy-done.25, bf16[2,1,128,1536]{3,2,1,0:T(8,128)(2,1)S(1)} %copy-done.45), kind=kOutput, calls=%fused_computation.78 | convolution fusion | flops 1623195648 | bytes 39190528 | tf_op jit(solution)/shard_map/dot_general | solution.py:28
  827.6 57.6 %reduce-scatter.20.cloned.1.call-done = bf16[192,1536]{1,0:T(8,128)(2,1)} async-done(((bf16[1536,1536]{1,0:T(8,128)(2,1)}), bf16[192,1536]{1,0:T(8,128)(2,1)}) %reduce-scatter.20.cloned.1.call-update) | async-done | bytes 589840 | tf_op jit(solution)/shard_map/reduce_scatter | solution.py:329
  885.2 95.8 %reduce-scatter.28.cloned.1.call-done = bf16[192,4096]{1,0:T(8,128)(2,1)} async-done(((bf16[1536,4096]{1,0:T(8,128)(2,1)}), bf16[192,4096]{1,0:T(8,128)(2,1)}) %reduce-scatter.28.cloned.1.call-update) | async-done | bytes 1572880 | tf_op jit(solution)/shard_map/reduce_scatter | solution.py:329
  981.0 95.8 %reduce-scatter.30.cloned.1.call-done = bf16[192,4096]{1,0:T(8,128)(2,1)} async-done(((bf16[1536,4096]{1,0:T(8,128)(2,1)}), bf16[192,4096]{1,0:T(8,128)(2,1)}) %reduce-scatter.30.cloned.1.call-update) | async-done | bytes 1572880 | tf_op jit(solution)/shard_map/reduce_scatter | solution.py:329
  1076.8 95.8 %reduce-scatter.32.cloned.1.call-done = bf16[512,1536]{1,0:T(8,128)(2,1)} async-done(((bf16[4096,1536]{1,0:T(8,128)(2,1)}), bf16[512,1536]{1,0:T(8,128)(2,1)}) %reduce-scatter.32.cloned.1.call-update) | async-done | bytes 1572880 | tf_op jit(solution)/shard_map/reduce_scatter | solution.py:329
  1173.3 6.5 fusion.96
  1179.9 7.6 fusion.97
  1196.7 14.5 %all-reduce.4 = (bf16[1536]{0:T(1024)(128)(2,1)S(1)}, bf16[1536]{0:T(1024)(128)(2,1)S(1)}) all-reduce(bf16[1536]{0:T(1024)(128)(2,1)S(1)} %add_convert_fusion.6, bf16[1536]{0:T(1024)(128)(2,1)S(1)} %add_convert_fusion.5), channel_id=8, replica_groups=mesh['dp'=2,'blk'=4,'head'=4] {'dp','blk'}, use_global_device_ids=true, to_apply=%region_24.25.clone | all-reduce | flops 3072 | bytes 12288
  1211.5 11.7 all-reduce.6
  1226.9 177.9 %all-reduce.10.cloned.1.call-done = (bf16[192,1536]{1,0:T(8,128)(2,1)}, bf16[192,768]{1,0:T(8,128)(2,1)}, bf16[192,768]{1,0:T(8,128)(2,1)}, bf16[192,1536]{1,0:T...) async-done(((bf16[192,1536]{1,0:T(8,128)(2,1)}, bf16[192,768]{1,0:T(8,128)(2,1)}, bf16[192,768]{1,0:T(8,128)(2,1)}, ...) | async-done | bytes 6488080 | tf_op jit(solution)/shard_map/psum | solution.py:331
  (535 shorter events, 258.9 us)
Async XLA Ops:
  7.2 21.4 %copy-start.83 = (s32[2,1,512]{2,1,0:T(1,128)S(1)}, s32[2,1,512]{2,1,0:T(1,128)}, u32[]{:S(2)}) copy-start(s32[2,1,512]{2,1,0:T(1,128)} %param.17) | copy-start | bytes 12292
  7.2 37.8 %copy-start.6 = (bf16[2,1,128,1536]{3,2,1,0:T(8,128)(2,1)S(1)}, bf16[2,1,128,1536]{3,2,1,0:T(8,128)(2,1)}, u32[]{:S(2)}) copy-start(bf16[2,1,128,1536]{3,2,1,0:T(8,128)(2,1)} %param.16) | copy-start | bytes 2359300
  7.2 41.1 %all-gather.10.cloned.1.call-start = ((), (), s32[]{:S(2)}) async-start(), calls=%async_computation.27 | async-start | bytes 2654208 | tf_op jit(solution)/shard_map/all_gather | solution.py:106
  8.0 63.6 %all-gather.14.cloned.1.call-start = ((), (), s32[]{:S(2)}) async-start(), calls=%async_computation.29 | async-start | bytes 2654208 | tf_op jit(solution)/shard_map/all_gather | solution.py:107
  8.7 125.6 %all-gather.12.cloned.1.call-start = ((), (), s32[]{:S(2)}) async-start(), calls=%async_computation.28 | async-start | bytes 5308416 | tf_op jit(solution)/shard_map/all_gather | solution.py:105
  9.5 233.8 %all-gather.16.cloned.1.call-start = ((), (), s32[]{:S(2)}) async-start(), calls=%async_computation.30 | async-start | bytes 5308416 | tf_op jit(solution)/shard_map/all_gather | solution.py:108
  10.0 239.1 %all-gather.18.cloned.1.call-start = ((), (), s32[]{:S(2)}) async-start(), calls=%async_computation.31 | async-start | bytes 14155776 | tf_op jit(solution)/shard_map/all_gather | solution.py:110
  10.6 301.8 %all-gather.20.cloned.1.call-start = ((), (), s32[]{:S(2)}) async-start(), calls=%async_computation.32 | async-start | bytes 14155776 | tf_op jit(solution)/shard_map/all_gather | solution.py:111
  11.2 375.2 %all-gather.22.cloned.1.call-start = ((), (), s32[]{:S(2)}) async-start(), calls=%async_computation.33 | async-start | bytes 14155776 | tf_op jit(solution)/shard_map/all_gather | solution.py:112
  28.6 146.3 %copy-start.73 = (f32[1536]{0:T(1024)}, f32[1536]{0:T(1024)S(1)}, u32[]{:S(2)}) copy-start(f32[1536]{0:T(1024)S(1)} %convert_element_type.334) | copy-start | bytes 18436
  45.3 89.0 %copy-start.81 = (f32[128]{0:T(128)}, f32[128]{0:T(128)S(1)}, u32[]{:S(2)}) copy-start(f32[128]{0:T(128)S(1)} %get-tuple-element.729) | copy-start | bytes 1540
  45.3 129.7 %copy-start.77 = (f32[128]{0:T(128)}, f32[128]{0:T(128)S(1)}, u32[]{:S(2)}) copy-start(f32[128]{0:T(128)S(1)} %get-tuple-element.730) | copy-start | bytes 1540
  51.4 24.9 %all-to-all-start.4 = ((bf16[128,8,96]{0,2,1:T(8,128)(2,1)}), bf16[128,8,96]{0,2,1:T(8,128)(2,1)S(1)}, u32[]{:S(2)}, u32[]{:S(2)}) async-start(bf16[128,8,96]{0,2,1:T(8,128)(2,1)} %bitcast.29), calls=%async_computation.4 | async-start | bytes 393216 | tf_op jit(solution)/shard_map/all_to_all | solution.py:125
  71.5 21.9 %copy-start.26 = (bf16[1536,768]{1,0:T(8,128)(2,1)S(1)}, bf16[1536,768]{1,0:T(8,128)(2,1)}, u32[]{:S(2)}) copy-start(bf16[1536,768]{1,0:T(8,128)(2,1)} %all-gather.14.cloned.1.call-done) | copy-start | bytes 7077892
  76.3 11.6 all-to-all-start.6
  87.9 11.3 all-to-all-start
  99.2 39.2 %all-to-all-start.2 = ((bf16[128,8,96]{0,2,1:T(8,128)(2,1)}), bf16[128,8,96]{0,2,1:T(8,128)(2,1)S(1)}, u32[]{:S(2)}, u32[]{:S(2)}) async-start(bf16[128,8,96]{0,2,1:T(8,128)(2,1)} %bitcast.13), calls=%async_computation.2 | async-start | bytes 393216 | tf_op jit(solution)/shard_map/all_to_all | solution.py:126
  118.3 70.8 %copy-start.52 = (bf16[2048,2,96]{0,2,1:T(8,128)(2,1)}, bf16[2048,2,96]{0,2,1:T(8,128)(2,1)S(1)}, u32[]{:S(2)}) copy-start(bf16[2048,2,96]{0,2,1:T(8,128)(2,1)S(1)} %all_gather.73) | copy-start | bytes 2359300
  138.4 43.2 %all-to-all-start.5 = ((bf16[128,16,96]{0,2,1:T(8,128)(2,1)}), bf16[128,16,96]{0,2,1:T(8,128)(2,1)S(1)}, u32[]{:S(2)}, u32[]{:S(2)}) async-start(bf16[128,16,96]{0,2,1:T(8,128)(2,1)} %bitcast.34), calls=%async_computation.5 | async-start | bytes 786432 | tf_op jit(solution)/shard_map/all_to_all | solution.py:124
  175.0 14.1 copy-start.40
  181.5 22.2 %all-to-all-start.1 = ((bf16[128,16,96]{0,2,1:T(8,128)(2,1)}), bf16[128,16,96]{0,2,1:T(8,128)(2,1)}, u32[]{:S(2)}, u32[]{:S(2)}) async-start(bf16[128,16,96]{0,2,1:T(8,128)(2,1)} %bitcast.9), calls=%async_computation.1 | async-start | bytes 786432 | tf_op jit(solution)/shard_map/all_to_all | solution.py:124
  197.1 13.9 copy-start.39
  203.7 22.1 %all-to-all-start.7 = ((bf16[512,4,96]{2,1,0:T(4,128)(2,1)}), bf16[512,4,96]{2,1,0:T(4,128)(2,1)S(1)}, u32[]{:S(2)}, u32[]{:S(2)}) async-start(bf16[512,4,96]{2,1,0:T(4,128)(2,1)} %copy.196), calls=%async_computation.7 | async-start | bytes 1048576 | tf_op jit(solution)/shard_map/all_to_all | solution.py:178
  223.7 13.6 copy-start.54
  225.8 15.9 %all-to-all-start.3 = ((bf16[512,4,96]{2,1,0:T(4,128)(2,1)}), bf16[512,4,96]{2,1,0:T(4,128)(2,1)}, u32[]{:S(2)}, u32[]{:S(2)}) async-start(bf16[512,4,96]{2,1,0:T(4,128)(2,1)} %copy.186), calls=%async_computation.3 | async-start | bytes 1048576 | tf_op jit(solution)/shard_map/all_to_all | solution.py:178
  249.1 63.3 %copy-start.17 = (bf16[128,1536]{1,0:T(8,128)(2,1)}, bf16[128,1536]{1,0:T(8,128)(2,1)S(1)}, u32[]{:S(2)}) copy-start(bf16[128,1536]{1,0:T(8,128)(2,1)S(1)} %multiply_convert_fusion.7) | copy-start | bytes 1179652
  257.5 128.9 %copy-start.43 = (bf16[2,1,128,1536]{3,2,1,0:T(8,128)(2,1)S(1)}, bf16[2,1,128,1536]{3,2,1,0:T(8,128)(2,1)}, u32[]{:S(2)}) copy-start(bf16[2,1,128,1536]{3,2,1,0:T(8,128)(2,1)} %param.18) | copy-start | bytes 2359300
  397.8 22.1 %slice-start = ((s8[12582912]{0:T(1024)(128)(4,1)}), s8[4194304]{0:T(1024)(128)(4,1)S(1)}, s32[]{:S(2)}) async-start(s8[12582912]{0:T(1024)(128)(4,1)} %bitcast.692), calls=%async_computation.46 | async-start | bytes 8388608
  397.8 22.1 %slice-start.1 = ((s8[12582912]{0:T(1024)(128)(4,1)}), s8[4194304]{0:T(1024)(128)(4,1)S(1)}, s32[]{:S(2)}) async-start(s8[12582912]{0:T(1024)(128)(4,1)} %bitcast.692), calls=%async_computation.47 | async-start | bytes 8388608
  463.3 14.7 %all-to-all-start.12 = ((bf16[128,16,96]{0,2,1:T(8,128)(2,1)}), bf16[128,16,96]{0,2,1:T(8,128)(2,1)S(1)}, u32[]{:S(2)}, u32[]{:S(2)}) async-start(bf16[128,16,96]{0,2,1:T(8,128)(2,1)} %bitcast.78), calls=%async_computation.14 | async-start | bytes 786432 | tf_op jit(solution)/shard_map/all_to_all | solution.py:206
  472.5 15.8 %copy-start.5 = (bf16[1,512,2,2,96]{1,4,3,2,0:T(8,128)(2,1)S(1)}, bf16[1,512,2,2,96]{1,4,3,2,0:T(8,128)(2,1)}, u32[]{:S(2)}) copy-start(bf16[1,512,2,2,96]{1,4,3,2,0:T(8,128)(2,1)} %reshape.476) | copy-start | bytes 1179652
  477.9 62.7 %all-to-all-start.8 = ((bf16[128,16,96]{0,2,1:T(8,128)(2,1)}), bf16[128,16,96]{0,2,1:T(8,128)(2,1)}, u32[]{:S(2)}, u32[]{:S(2)}) async-start(bf16[128,16,96]{0,2,1:T(8,128)(2,1)} %bitcast.57), calls=%async_computation.8 | async-start | bytes 786432 | tf_op jit(solution)/shard_map/all_to_all | solution.py:206
  484.6 111.4 %reduce-scatter.16.cloned.1.call-start = ((), (), s32[]{:S(2)}) async-start(), calls=%async_computation.36 | async-start | bytes 983040 | tf_op jit(solution)/shard_map/reduce_scatter | solution.py:272
  540.6 78.3 %reduce-scatter.12.cloned.1.call-start = ((), (), s32[]{:S(2)}) async-start(), calls=%async_computation.34 | async-start | bytes 983040 | tf_op jit(solution)/shard_map/reduce_scatter | solution.py:272
  592.6 55.7 %reduce-scatter.18.cloned.1.call-start = ((), (), s32[]{:S(2)}) async-start(), calls=%async_computation.37 | async-start | bytes 983040 | tf_op jit(solution)/shard_map/reduce_scatter | solution.py:275
  592.7 40.4 %copy-start.7 = (bf16[2,1,128,1536]{3,2,1,0:T(8,128)(2,1)S(1)}, bf16[2,1,128,1536]{3,2,1,0:T(8,128)(2,1)}, u32[]{:S(2)}) copy-start(bf16[2,1,128,1536]{3,2,1,0:T(8,128)(2,1)} %param.16) | copy-start | bytes 2359300
  592.7 40.4 %copy-start.74 = (f32[1536]{0:T(1024)S(1)}, f32[1536]{0:T(1024)}, u32[]{:S(2)}) copy-start(f32[1536]{0:T(1024)} %copy-done.73) | copy-start | bytes 18436
  592.7 40.4 %copy-start.78 = (f32[128]{0:T(128)S(1)}, f32[128]{0:T(128)}, u32[]{:S(2)}) copy-start(f32[128]{0:T(128)} %copy-done.77) | copy-start | bytes 1540
  594.9 82.4 %reduce-scatter.14.cloned.1.call-start = ((), (), s32[]{:S(2)}) async-start(), calls=%async_computation.35 | async-start | bytes 983040 | tf_op jit(solution)/shard_map/reduce_scatter | solution.py:275
  597.8 36.2 %copy-start.82 = (f32[128]{0:T(128)S(1)}, f32[128]{0:T(128)}, u32[]{:S(2)}) copy-start(f32[128]{0:T(128)} %copy-done.81) | copy-start | bytes 1540
  597.8 22.8 %all-to-all-start.14 = ((bf16[512,2,96]{2,1,0:T(2,128)(2,1)}), bf16[512,2,96]{2,1,0:T(2,128)(2,1)S(1)}, u32[]{:S(2)}, u32[]{:S(2)}) async-start(bf16[512,2,96]{2,1,0:T(2,128)(2,1)} %copy.222), calls=%async_computation.17 | async-start | bytes 524288 | tf_op jit(solution)/shard_map/all_to_all | solution.py:282
  620.6 12.2 all-to-all-start.10
  625.8 199.5 %reduce-scatter.22.cloned.1.call-start = ((), (), s32[]{:S(2)}) async-start(), calls=%async_computation.39 | async-start | bytes 2654208 | tf_op jit(solution)/shard_map/reduce_scatter | solution.py:329
  650.1 29.0 %all-to-all-start.15 = ((bf16[512,2,96]{2,1,0:T(2,128)(2,1)}), bf16[512,2,96]{2,1,0:T(2,128)(2,1)S(1)}, u32[]{:S(2)}, u32[]{:S(2)}) async-start(bf16[512,2,96]{2,1,0:T(2,128)(2,1)} %copy.226), calls=%async_computation.19 | async-start | bytes 524288 | tf_op jit(solution)/shard_map/all_to_all | solution.py:285
  679.1 12.2 all-to-all-start.11
  684.3 141.0 %reduce-scatter.24.cloned.1.call-start = ((), (), s32[]{:S(2)}) async-start(), calls=%async_computation.40 | async-start | bytes 2654208 | tf_op jit(solution)/shard_map/reduce_scatter | solution.py:329
  694.8 132.9 %reduce-scatter.26.cloned.1.call-start = ((), (), s32[]{:S(2)}) async-start(), calls=%async_computation.41 | async-start | bytes 5308416 | tf_op jit(solution)/shard_map/reduce_scatter | solution.py:329
  702.5 15.6 %all-to-all-start.13 = ((bf16[512,4,96]{2,1,0:T(4,128)(2,1)}), bf16[512,4,96]{2,1,0:T(4,128)(2,1)S(1)}, u32[]{:S(2)}, u32[]{:S(2)}) async-start(bf16[512,4,96]{2,1,0:T(4,128)(2,1)} %bitcast.83), calls=%async_computation.15 | async-start | bytes 1048576 | tf_op jit(solution)/shard_map/all_to_all | solution.py:279
  718.1 16.6 %all-to-all-start.9 = ((bf16[512,4,96]{2,1,0:T(4,128)(2,1)}), bf16[512,4,96]{2,1,0:T(4,128)(2,1)S(1)}, u32[]{:S(2)}, u32[]{:S(2)}) async-start(bf16[512,4,96]{2,1,0:T(4,128)(2,1)} %bitcast.62), calls=%async_computation.9 | async-start | bytes 1048576 | tf_op jit(solution)/shard_map/all_to_all | solution.py:279
  724.4 160.9 %reduce-scatter.20.cloned.1.call-start = ((), (), s32[]{:S(2)}) async-start(), calls=%async_computation.38 | async-start | bytes 5308416 | tf_op jit(solution)/shard_map/reduce_scatter | solution.py:329
  740.2 12.8 copy-start.16
  740.2 12.8 copy-start.37
  740.2 240.8 %reduce-scatter.28.cloned.1.call-start = ((), (), s32[]{:S(2)}) async-start(), calls=%async_computation.42 | async-start | bytes 14155776 | tf_op jit(solution)/shard_map/reduce_scatter | solution.py:329
  768.0 12.1 copy-start.35
  768.0 308.8 %reduce-scatter.30.cloned.1.call-start = ((), (), s32[]{:S(2)}) async-start(), calls=%async_computation.43 | async-start | bytes 14155776 | tf_op jit(solution)/shard_map/reduce_scatter | solution.py:329
  797.1 375.5 %reduce-scatter.32.cloned.1.call-start = ((), (), s32[]{:S(2)}) async-start(), calls=%async_computation.44 | async-start | bytes 14155776 | tf_op jit(solution)/shard_map/reduce_scatter | solution.py:329
  798.3 11.9 copy-start.25
  825.0 348.3 %copy-start.79 = (f32[1536]{0:T(1024)S(1)}, f32[1536]{0:T(1024)}, u32[]{:S(2)}) copy-start(f32[1536]{0:T(1024)} %get-tuple-element.608) | copy-start | bytes 18436
  825.0 348.3 %copy-start.80 = (f32[1536]{0:T(1024)S(1)}, f32[1536]{0:T(1024)}, u32[]{:S(2)}) copy-start(f32[1536]{0:T(1024)} %get-tuple-element.606) | copy-start | bytes 18436
  825.0 348.3 %copy-start.11 = (f32[128,1536]{1,0:T(8,128)S(1)}, f32[128,1536]{1,0:T(8,128)}, u32[]{:S(2)}) copy-start(f32[128,1536]{1,0:T(8,128)} %get-tuple-element.725) | copy-start | bytes 2359300
  825.0 579.8 %all-reduce.10.cloned.1.call-start = ((), (), s32[]{:S(2)}) async-start(), calls=%async_computation.45 | async-start | bytes 12976128 | tf_op jit(solution)/shard_map/psum | solution.py:331
  1173.3 15.2 %slice-start.3 = ((s8[4718592]{0:T(1024)(128)(4,1)}), s8[4194304]{0:T(1024)(128)(4,1)S(1)}, s32[]{:S(2)}) async-start(s8[4718592]{0:T(1024)(128)(4,1)} %bitcast.694), calls=%async_computation.49 | async-start | bytes 8388608
  1193.8 30.5 %copy-start.21 = (f32[128,1536]{1,0:T(8,128)S(1)}, f32[128,1536]{1,0:T(8,128)}, u32[]{:S(2)}) copy-start(f32[128,1536]{1,0:T(8,128)} %copy-done.19) | copy-start | bytes 2359300
  1193.8 30.5 %copy-start.24 = (f32[128,1536]{1,0:T(8,128)S(1)}, f32[128,1536]{1,0:T(8,128)}, u32[]{:S(2)}) copy-start(f32[128,1536]{1,0:T(8,128)} %copy-done.22) | copy-start | bytes 2359300
  (107 other events, 461.6 us)
Sparse Core Ops, SparseCore 0:
  9.9 30.6 all-gather.9
  42.5 28.9 all-gather.13
  73.4 41.9 all-gather.11
  117.1 46.6 all-gather.15
  165.5 72.8 all-gather.17
  240.2 72.1 all-gather.19
  314.3 72.1 all-gather.21
  540.7 26.0 reduce-scatter.15
  592.7 26.0 reduce-scatter.11
  622.2 26.0 reduce-scatter.17
  651.2 26.0 reduce-scatter.13
  681.1 42.4 reduce-scatter.21
  727.9 42.4 reduce-scatter.23
  773.7 53.8 reduce-scatter.25
  831.3 53.8 reduce-scatter.19
  888.6 92.3 reduce-scatter.27
  984.4 92.3 reduce-scatter.29
  1080.1 92.3 reduce-scatter.31
  1175.5 229.2 all-reduce.9
where the time goes:
time: 1440 us; the launch traced here: 1430 us
  waiting for transfers between devices  756 us (52%)
  matrix products  342 us (24%)
  blocking collectives  118 us (8%)
  starting transfers between devices  86.2 us (6%)
  local copies, waits for them, and re-layouts  70.2 us (5%)
  other arithmetic  35.4 us (2%)
  between operations  16.9 us (1%)
    reduce_scatter x7, waiting for transfers between devices, per_device(): lax.psum_scatter(shortened(totals), ('dp', 'blk'), scatter_dimension=0, t...  347 us
    psum x1, waiting for transfers between devices, per_device(): lax.psum(shortened(owned), 'head')  178 us
    dot_general x14, matrix products, first_dot(): lax.dot_general(left, right, (((0,), (0,)), ((), ())), preferred_element_...  98.7 us
    dot_general x14, matrix products, last_dot(): lax.dot_general(left, right, (((1,), (1,)), ((), ())), preferred_element_...  76.6 us
    all_gather x1, waiting for transfers between devices, per_device(): down_w = lax.all_gather(shards[8], ('dp', 'blk'), axis=0, tiled=True)  66.3 us
    dot_general x14, matrix products, plain_dot(): return jnp.dot(left, right, preferred_element_type=jnp.float32)  63.3 us
    all_gather x1, waiting for transfers between devices, per_device(): up_w = lax.all_gather(shards[7], ('dp', 'blk'), axis=0, tiled=True)  54.8 us
    reduce_scatter x2, waiting for transfers between devices, per_device(): lax.psum_scatter(sum_v.astype(jnp.bfloat16), 'blk', scatter_dimension=0,...  34.1 us
  transfers between devices with their start and end apart: 35, of which 19 were waited for; matrix products, arithmetic and copies ran while one was open for 24% of the time, Pallas kernels for 0%

commit v1 on v0

v1 whole, which is shorter than its diff:
```python
import functools
import math

import jax
import jax.numpy as jnp
from jax import lax
from jax.experimental import pallas as pl
from jax.experimental.pallas import tpu as pltpu
from jax.sharding import PartitionSpec as P

D = 1536
QH = 16
KVH = 8
HD = 96
HP = 128
FF = 4096
EPS = 1e-05
NEG = -1e30
BLK = 256
BF = jnp.bfloat16
F32 = jnp.float32


def dot(left, right, dims=((1,), (0,))):
    return lax.dot_general(left, right, (dims, ((), ())), preferred_element_type=F32)


def normalize(values):
    factor = lax.rsqrt(jnp.mean(values * values, -1, keepdims=True) + EPS)
    return values * factor, factor


def norm_back(grad_norm, gain, normed, factor):
    scaled = grad_norm * gain
    return factor * (scaled - normed * jnp.mean(scaled * normed, -1, keepdims=True))


def rows_of(index):
    return pl.ds(pl.multiple_of(index * BLK, BLK), BLK)


def allowed_pairs(qpos, qseg, kpos, kseg):
    return (kpos <= qpos) & (kseg == qseg)


def attn_fwd_kernel(need, q_ref, kv_ref, qp_ref, qs_ref, kp_ref, ks_ref, o_ref, lse_ref, m_sc, l_sc, acc_sc):
    scale = 1.0 / math.sqrt(HD)
    n_q, n_k = q_ref.shape[0] // BLK, kv_ref.shape[0] // BLK

    def one_query(i, _):
        qr = rows_of(i)
        m_sc[...] = jnp.full_like(m_sc, NEG)
        l_sc[...] = jnp.zeros_like(l_sc)
        acc_sc[...] = jnp.zeros_like(acc_sc)
        qpos, qseg = qp_ref[qr, :], qs_ref[qr, :]

        def one_key(j, _):
            @pl.when(need[i, j] != 0)
            def _():
                kr = rows_of(j)
                ok = allowed_pairs(qpos, qseg, kp_ref[j], ks_ref[j])
                k, v = kv_ref[kr, 0:HP], kv_ref[kr, HP : 2 * HP]
                for g in range(2):
                    q = q_ref[qr, g * HP : (g + 1) * HP]
                    s = jnp.where(ok, dot(q, k, ((1,), (1,))) * scale, NEG)
                    m_old = m_sc[g]
                    m_new = jnp.maximum(m_old, jnp.max(s, -1, keepdims=True))
                    p = jnp.where(ok, jnp.exp(s - m_new), 0.0)
                    decay = jnp.exp(m_old - m_new)
                    l_sc[g] = l_sc[g] * decay + jnp.sum(p, -1, keepdims=True)
                    acc_sc[g] = acc_sc[g] * decay + dot(p.astype(BF), v)
                    m_sc[g] = m_new

            return 0

        lax.fori_loop(0, n_k, one_key, 0)
        for g in range(2):
            o_ref[qr, g * HP : (g + 1) * HP] = (acc_sc[g] / l_sc[g]).astype(BF)
            lse_ref[qr, g : g + 1] = m_sc[g] + jnp.log(l_sc[g])
        return 0

    lax.fori_loop(0, n_q, one_query, 0)


def attn_bwd_kernel(
    need, q_ref, kv_ref, qp_ref, qs_ref, kp_ref, ks_ref, o_ref, lse_ref, do_ref, dq_ref, dkv_ref, dq_sc, dk_sc, dv_sc
):
    scale = 1.0 / math.sqrt(HD)
    n_q, n_k = q_ref.shape[0] // BLK, kv_ref.shape[0] // BLK
    dk_sc[...] = jnp.zeros_like(dk_sc)
    dv_sc[...] = jnp.zeros_like(dv_sc)

    def as_row(col):
        return jnp.broadcast_to(col, (BLK, HP)).T[0:1, :]

    def one_query(i, _):
        qr = rows_of(i)
        dq_sc[...] = jnp.zeros_like(dq_sc)
        qpos, qseg = qp_ref[i], qs_ref[i]
        lse, delta = [], []
        for g in range(2):
            cols = slice(g * HP, (g + 1) * HP)
            lse.append(as_row(lse_ref[qr, g : g + 1]))
            prod = do_ref[qr, cols].astype(F32) * o_ref[qr, cols].astype(F32)
            delta.append(as_row(jnp.sum(prod, -1, keepdims=True)))

        def one_key(j, _):
            @pl.when(need[i, j] != 0)
            def _():
                kr = rows_of(j)
                ok = allowed_pairs(qpos, qseg, kp_ref[kr, :], ks_ref[kr, :])
                k, v = kv_ref[kr, 0:HP], kv_ref[kr, HP : 2 * HP]
                for g in range(2):
                    cols = slice(g * HP, (g + 1) * HP)
                    q, do = q_ref[qr, cols], do_ref[qr, cols]
                    s = dot(k, q, ((1,), (1,))) * scale
                    p = jnp.where(ok, jnp.exp(s - lse[g]), 0.0)
                    dp = dot(v, do, ((1,), (1,)))
                    ds = (p * (dp - delta[g])).astype(BF)
                    dv_sc[kr, :] += dot(p.astype(BF), do)
                    dk_sc[kr, :] += dot(ds, q)
                    dq_sc[g] += dot(ds, k, ((0,), (0,)))

            return 0

        lax.fori_loop(0, n_k, one_key, 0)
        for g in range(2):
            dq_ref[qr, g * HP : (g + 1) * HP] = (dq_sc[g] * scale).astype(BF)
        return 0

    lax.fori_loop(0, n_q, one_query, 0)
    dkv_ref[:, 0:HP] = (dk_sc[...] * scale).astype(BF)
    dkv_ref[:, HP : 2 * HP] = dv_sc[...].astype(BF)


def in_vmem(count):
    return [pl.BlockSpec(memory_space=pltpu.SMEM)] + [pl.BlockSpec(memory_space=pltpu.VMEM)] * count


def attn_cost(n_q, n_k, products):
    return pl.CostEstimate(
        flops=products * n_q * n_k * 2 * HP * 2 // 2, transcendentals=n_q * n_k, bytes_accessed=(n_q + n_k) * HP * 16
    )


def attend(need, q, kv, qpos, qseg, kpos, kseg):
    n_q, n_k = q.shape[0], kv.shape[0]
    return pl.pallas_call(
        attn_fwd_kernel,
        out_shape=(jax.ShapeDtypeStruct((n_q, 2 * HP), BF), jax.ShapeDtypeStruct((n_q, 2), F32)),
        in_specs=in_vmem(6),
        out_specs=(pl.BlockSpec(memory_space=pltpu.VMEM),) * 2,
        scratch_shapes=[pltpu.VMEM((2, BLK, 1), F32), pltpu.VMEM((2, BLK, 1), F32), pltpu.VMEM((2, BLK, HP), F32)],
        compiler_params=pltpu.CompilerParams(vmem_limit_bytes=40 << 20),
        cost_estimate=attn_cost(n_q, n_k, 2),
        name="attn_fwd",
    )(need, q, kv, qpos[:, None], qseg[:, None], kpos.reshape(-1, 1, BLK), kseg.reshape(-1, 1, BLK))


def attend_back(need, q, kv, qpos, qseg, kpos, kseg, o, lse, do):
    n_q, n_k = q.shape[0], kv.shape[0]
    return pl.pallas_call(
        attn_bwd_kernel,
        out_shape=(jax.ShapeDtypeStruct((n_q, 2 * HP), BF), jax.ShapeDtypeStruct((n_k, 2 * HP), BF)),
        in_specs=in_vmem(9),
        out_specs=(pl.BlockSpec(memory_space=pltpu.VMEM),) * 2,
        scratch_shapes=[pltpu.VMEM((2, BLK, HP), F32), pltpu.VMEM((n_k, HP), F32), pltpu.VMEM((n_k, HP), F32)],
        compiler_params=pltpu.CompilerParams(vmem_limit_bytes=48 << 20),
        cost_estimate=attn_cost(n_q, n_k, 5),
        name="attn_bwd",
    )(need, q, kv, qpos.reshape(-1, 1, BLK), qseg.reshape(-1, 1, BLK), kpos[:, None], kseg[:, None], o, lse, do)


def swap(value, axis, mask):
    return lax.ppermute(value, axis, [(i, i ^ mask) for i in range(lax.axis_size(axis))])


def gather_rel(value):
    n_blk = lax.axis_size("blk")
    mine = jnp.stack([value] + [swap(value, "blk", k) for k in range(1, n_blk)])
    return jnp.stack([mine, swap(mine, "dp", 1)])


def scatter_rel(parts):
    n_blk = lax.axis_size("blk")
    local = parts[0] + swap(parts[1].astype(BF), "dp", 1).astype(F32)
    total = local[0]
    for k in range(1, n_blk):
        total = total + swap(local[k].astype(BF), "blk", k).astype(F32)
    return total


def exchange_rel(parts):
    n_blk = lax.axis_size("blk")
    both = jnp.stack([parts[0], swap(parts[1], "dp", 1)], 1)
    return jnp.stack([both[0]] + [swap(both[k], "blk", k) for k in range(1, n_blk)], 1)


def rel_to_abs(value, reverse=False):
    n_blk = lax.axis_size("blk")
    mine = lax.axis_index("dp") * n_blk + lax.axis_index("blk")
    flat = value.reshape((2 * n_blk,) + value.shape[(1 if reverse else 2) :])
    out = jnp.stack([lax.dynamic_index_in_dim(flat, i ^ mine, 0, keepdims=False) for i in range(2 * n_blk)])
    return out.reshape((2, n_blk) + out.shape[1:]) if reverse else out


def per_device(
    activations,
    segments,
    cotangent,
    norm_gain_one,
    query_weight,
    key_weight,
    value_weight,
    output_weight,
    norm_gain_two,
    gate_weight,
    up_weight,
    down_weight,
):
    n_blk, n_head = lax.axis_size("blk"), lax.axis_size("head")
    n_plane = 2 * n_blk
    assert lax.axis_size("dp") == 2 and activations.shape[0] == 2 and n_plane == KVH
    sub = n_head // 4
    tok = activations.shape[2]
    span = tok * n_head
    own = 2 * tok
    rows = n_plane * own
    my_dp, my_blk, my_head = (lax.axis_index(name) for name in ("dp", "blk", "head"))
    my_seq, my_sub = my_head // sub, my_head % sub

    def routes(k):
        pairs = []
        for core in range(2):
            for head in range(n_head):
                seq_part, sub_part = head // sub, head % sub
                target = 2 * (k ^ (seq_part & 1)) + core
                pairs.append((core * n_head + head, (seq_part >> 1) * n_head + target * sub + sub_part))
        return pairs

    def to_plane(value):
        parts = []
        for k in range(2):
            piece = lax.dynamic_index_in_dim(value, k ^ (my_seq & 1), 0, keepdims=False)
            parts.append(lax.ppermute(piece, ("dp", "head"), routes(k)))
        return jnp.concatenate(parts, 0)

    def from_plane(value):
        parts = []
        for k in range(2):
            back = [(b, a) for a, b in routes(k)]
            parts.append(lax.ppermute(value[k * tok : (k + 1) * tok], ("dp", "head"), back))
        odd = (my_seq & 1) == 1
        return jnp.stack([jnp.where(odd, parts[1], parts[0]), jnp.where(odd, parts[0], parts[1])])

    x = to_plane(activations[:, 0]).astype(F32)
    cot = to_plane(cotangent[:, 0])

    small = jnp.concatenate([norm_gain_one, norm_gain_two, segments[:, 0].reshape(-1).astype(BF)])[None]
    small = rel_to_abs(gather_rel(small))[:, 0]
    n_gain = D // n_plane
    gain_one = small[:, :n_gain].reshape(D).astype(F32)
    gain_two = small[:, n_gain : 2 * n_gain].reshape(D).astype(F32)
    seg_all = small[:, 2 * n_gain :].reshape(2, n_blk, 2, span)
    seg_seq = lax.dynamic_index_in_dim(seg_all, my_seq & 1, 0, keepdims=False)
    seg_seq = lax.dynamic_index_in_dim(seg_seq, my_seq >> 1, 1, keepdims=False)
    chunks = seg_seq.astype(jnp.int32).reshape(n_blk * n_head, tok)

    def chunk_ids(sub_index):
        ids = []
        for core in range(2):
            for blk in range(n_blk):
                for k in range(2):
                    seq_part = 2 * (my_dp ^ core) + ((my_seq >> 1) ^ k)
                    ids.append((my_blk ^ blk) * n_head + seq_part * sub + sub_index)
        return ids

    def pos_seg(sub_index):
        ids = chunk_ids(sub_index)
        lane = jnp.arange(tok, dtype=jnp.int32)
        pos = jnp.concatenate([i * tok + lane for i in ids])
        seg = jnp.concatenate([lax.dynamic_index_in_dim(chunks, i, 0, keepdims=False) for i in ids])
        return pos, seg

    qpos, qseg = pos_seg(my_sub)
    if sub == 1:
        kpos, kseg = qpos, qseg
    else:
        every = [pos_seg(i) for i in range(sub)]
        kpos, kseg = (jnp.concatenate([e[i] for e in every]) for i in range(2))
    blocked = lambda v: v.reshape(-1, BLK)
    qb, qsb, kb, ksb = blocked(qpos), blocked(qseg), blocked(kpos), blocked(kseg)
    need = (
        (jnp.min(kb, 1)[None, :] <= jnp.max(qb, 1)[:, None])
        & (jnp.min(ksb, 1)[None, :] <= jnp.max(qsb, 1)[:, None])
        & (jnp.max(ksb, 1)[None, :] >= jnp.min(qsb, 1)[:, None])
    ).astype(jnp.int32)

    def column_parts(weight):
        width = weight.shape[1] // n_plane
        return weight.reshape(weight.shape[0], n_plane, width).transpose(1, 0, 2)

    qkv_parts = jnp.concatenate([column_parts(w) for w in (query_weight, key_weight, value_weight)], -1)
    qkv_w = rel_to_abs(exchange_rel(rel_to_abs(qkv_parts, True))).reshape(D, 4 * HD)
    pad_heads = lambda v: jnp.pad(v.reshape(v.shape[0], -1, HD), ((0, 0), (0, 0), (0, HP - HD))).reshape(v.shape[0], -1)
    qkv_w = pad_heads(qkv_w)
    out_pad = jnp.pad(output_weight.reshape(2, HD, D), ((0, 0), (0, HP - HD), (0, 0))).reshape(2 * HP, D)
    out_w = gather_rel(out_pad).reshape(n_plane * 2 * HP, D)
    ff_parts = jnp.concatenate([column_parts(w) for w in (gate_weight, up_weight)], -1)
    ff_w = rel_to_abs(exchange_rel(rel_to_abs(ff_parts, True))).reshape(D, 2 * FF // n_plane)
    ff_here = FF // n_plane
    gate_w, up_w = ff_w[:, :ff_here], ff_w[:, ff_here:]

    normed_one, factor_one = normalize(x)
    input_one = (normed_one * gain_one).astype(BF)
    all_one = gather_rel(input_one).reshape(rows, D)
    qkv = dot(all_one, qkv_w).astype(BF)
    q, kv = qkv[:, : 2 * HP], qkv[:, 2 * HP :]
    if sub > 1:
        groups = [[s * sub + i for i in range(sub)] for s in range(4)]
        kv = lax.all_gather(kv, "head", axis=0, tiled=True, axis_index_groups=groups)
    o, lse = attend(need, q, kv, qpos, qseg, kpos, kseg)
    o_tok = exchange_rel(o.reshape(2, n_blk, own, 2 * HP))
    o_tok = o_tok.reshape(n_plane, own, 2 * HP).transpose(1, 0, 2).reshape(own, n_plane * 2 * HP)
    x_mid = x + dot(o_tok, out_w)
    normed_two, factor_two = normalize(x_mid)
    input_two = (normed_two * gain_two).astype(BF)
    all_two = gather_rel(input_two).reshape(rows, D)
    all_cot = gather_rel(cot).reshape(rows, D)
    gate_val = dot(all_two, gate_w)
    up_val = dot(all_two, up_w)
    sigma = jax.nn.sigmoid(gate_val)
    silu_val = gate_val * sigma
    hidden = (silu_val * up_val).astype(BF)
    in_plane = lambda v: v.reshape(2, n_blk, own, D)
    block_out = (x_mid + scatter_rel(in_plane(dot(hidden, down_weight)))).astype(BF)

    grad_hidden = dot(all_cot, down_weight, ((1,), (1,)))
    grad_gate = (grad_hidden * up_val * sigma * (1.0 + gate_val * (1.0 - sigma))).astype(BF)
    grad_up = (grad_hidden * silu_val).astype(BF)
    grad_in_two = scatter_rel(in_plane(dot(grad_gate, gate_w, ((1,), (1,))) + dot(grad_up, up_w, ((1,), (1,)))))
    grad_mid = cot.astype(F32) + norm_back(grad_in_two, gain_two, normed_two, factor_two)
    grad_branch = grad_mid.astype(BF)
    grad_o = dot(grad_branch, out_w, ((1,), (1,))).astype(BF)
    grad_o = exchange_rel(grad_o.reshape(own, 2, n_blk, 2 * HP).transpose(1, 2, 0, 3)).reshape(rows, 2 * HP)
    all_branch = gather_rel(grad_branch).reshape(rows, D)
    dq, dkv = attend_back(need, q, kv, qpos, qseg, kpos, kseg, o, lse, grad_o)
    if sub > 1:
        dkv = lax.psum_scatter(dkv, "head", scatter_dimension=0, tiled=True, axis_index_groups=groups)
    dqkv = jnp.concatenate([dq, dkv], 1)
    grad_in_one = scatter_rel(in_plane(dot(dqkv, qkv_w, ((1,), (1,)))))
    grad_input = grad_mid + norm_back(grad_in_one, gain_one, normed_one, factor_one)

    contract = ((0,), (0,))

    def owned_rows(grad):
        return lax.all_gather(
            lax.psum_scatter(grad.astype(BF), "head", scatter_dimension=0, tiled=True), "head", axis=0, tiled=True
        ).astype(F32)

    def owned_columns(grad):
        width = grad.shape[1]
        part = D // n_plane // n_head
        sent = grad.astype(BF).reshape(n_plane, n_head, part, width).transpose(1, 0, 2, 3)
        mine = lax.psum_scatter(sent.reshape(D, width), "head", scatter_dimension=0, tiled=True)
        moved = exchange_rel(rel_to_abs(mine.reshape(n_plane, part, width), True))
        full = lax.all_gather(moved, "head", axis=0)
        full = rel_to_abs(jnp.moveaxis(full, 0, 2))
        return full.reshape(n_plane, D // n_plane, width).transpose(1, 0, 2).astype(F32)

    grad_down = owned_rows(dot(hidden, all_cot, contract))
    grad_ff = owned_columns(jnp.concatenate([dot(all_two, grad_gate, contract), dot(all_two, grad_up, contract)], 1))
    grad_out = dot(o, all_branch, contract).reshape(2, HP, D)[:, :HD].reshape(2 * HD, D)
    grad_out = owned_rows(grad_out)
    grad_qkv = dot(all_one, dqkv, contract).reshape(D, 4, HP)[:, :, :HD].reshape(D, 4 * HD)
    grad_qkv = owned_columns(grad_qkv)
    flat = lambda v: v.reshape(v.shape[0], -1)
    grad_query = flat(grad_qkv[:, :, : 2 * HD])
    grad_key = flat(grad_qkv[:, :, 2 * HD : 3 * HD])
    grad_value = flat(grad_qkv[:, :, 3 * HD :])
    grad_gate_w = flat(grad_ff[:, :, :ff_here])
    grad_up_w = flat(grad_ff[:, :, ff_here:])

    def gain_grad(gain, *pairs):
        return sum(jnp.sum(w.astype(F32) * g, -1) for w, g in pairs) / gain.astype(F32)

    grad_gain_one = gain_grad(
        norm_gain_one, (query_weight, grad_query), (key_weight, grad_key), (value_weight, grad_value)
    )
    grad_gain_two = gain_grad(norm_gain_two, (gate_weight, grad_gate_w), (up_weight, grad_up_w))
    return (
        from_plane(block_out)[:, None],
        from_plane(grad_input.astype(BF))[:, None],
        grad_gain_one,
        grad_query,
        grad_key,
        grad_value,
        grad_out,
        grad_gain_two,
        grad_gate_w,
        grad_up_w,
        grad_down,
    )


def solution(mesh):
    tokens = P(None, "dp", ("blk", "head"), None)
    vector = P(("dp", "blk"))
    matrix = P(("dp", "blk"), None)
    return jax.shard_map(
        per_device,
        mesh=mesh,
        in_specs=(
            tokens,
            P(None, "dp", "blk"),
            tokens,
            vector,
            matrix,
            matrix,
            matrix,
            matrix,
            vector,
            matrix,
            matrix,
            matrix,
        ),
        out_specs=(tokens, tokens, vector, matrix, matrix, matrix, matrix, vector, matrix, matrix, matrix),
        check_vma=False,
    )
```

time: 1440 us -> 843 us (0.59)
  waiting for transfers between devices: 756 us -> 306 us
  matrix products: 342 us -> 87.1 us
  other arithmetic: 35.4 us -> 130 us
  blocking collectives: 118 us -> 41.7 us
  local copies, waits for them, and re-layouts: 70.2 us -> 133 us
  Pallas kernels: 0 us -> 42.2 us
    reduce_scatter x11 -> x4, waiting for transfers between devices: 397 us -> 0.02 us  [the longest x2 0.01 us: owned_rows(): lax.psum_scatter(grad.astype(BF), 'head', scatter_dimension=0, tiled=True)]
    ppermute x0 -> x68, waiting for transfers between devices: none -> 276 us  [the longest x60 248 us: swap(): lax.ppermute(value, axis, [(i, i ^ mask) for i in range(lax.axis_size(axi...]
    dot_general x86 -> x15, matrix products: 342 us -> 87.1 us  [dot(): lax.dot_general(left, right, (dims, ((), ())), preferred_element_type=F32)]
    psum x1 -> x0, waiting for transfers between devices: 178 us -> none  [per_device(): lax.psum(shortened(owned), 'head')]
    all_gather x7 -> x3, waiting for transfers between devices: 136 us -> 29.3 us  [the longest x2 29.3 us: owned_columns(): full = lax.all_gather(moved, 'head', axis=0)]
    another operation x1 -> x39, other arithmetic: 1.58 us -> 93.1 us  [the longest x12 33.8 us: gather_rel(): return jnp.stack([mine, swap(mine, 'dp', 1)])]
    all_to_all x16 -> x0, starting transfers between devices: 84.8 us -> none  [the longest x2 11.8 us: per_device(): lax.all_to_all(grad_query.astype(jnp.bfloat16), 'head', split_axis=0, con...]
    ppermute x0 -> x68, starting transfers between devices: none -> 78.3 us  [the longest x60 66.3 us: swap(): lax.ppermute(value, axis, [(i, i ^ mask) for i in range(lax.axis_size(axi...]
  transfers between devices with their start and end apart: 35 -> 75, of which waited for: 19 -> 33; matrix products, arithmetic and copies ran while one was open for 24% -> 35% of each run, Pallas kernels for 0% -> 5%
where the time goes in v1:
time: 843 us; the launch traced here: 834 us
  waiting for transfers between devices  306 us (36%)
  local copies, waits for them, and re-layouts  133 us (16%)
  other arithmetic  130 us (15%)
  matrix products  87.1 us (10%)
  starting transfers between devices  78.8 us (9%)
  Pallas kernels  42.2 us (5%)
  blocking collectives  41.7 us (5%)
  between operations  16.5 us (2%)
    ppermute x60, waiting for transfers between devices, swap(): lax.ppermute(value, axis, [(i, i ^ mask) for i in range(lax.axis_size(axi...  248 us
    dot_general x15, matrix products, dot(): lax.dot_general(left, right, (dims, ((), ())), preferred_element_type=F32)  87.1 us
    ppermute x60, starting transfers between devices, swap(): lax.ppermute(value, axis, [(i, i ^ mask) for i in range(lax.axis_size(axi...  66.3 us
    unnamed x199, local copies, waits for them, and re-layouts  47.7 us
    all_gather x1, blocking collectives, owned_rows(): lax.all_gather(lax.psum_scatter(grad.astype(BF), 'head', scatter_dimensio...  41.7 us
    another operation x12, other arithmetic, gather_rel(): return jnp.stack([mine, swap(mine, 'dp', 1)])  33.8 us
    all_gather x2, waiting for transfers between devices, owned_columns(): full = lax.all_gather(moved, 'head', axis=0)  29.3 us
    another operation x6, other arithmetic, exchange_rel(): both = jnp.stack([parts[0], swap(parts[1], 'dp', 1)], 1)  22.9 us
  transfers between devices with their start and end apart: 75, of which 33 were waited for; matrix products, arithmetic and copies ran while one was open for 35% of the time, Pallas kernels for 5%

profile of v1, /device:TPU:8, one launch (start us, length us, event | category | flops | bytes accessed | tf_op | source)
XLA Modules:
  0.0 834.4 jit_solution(5795843382304192233)
XLA Ops:
  33.5 6.4 fusion.45
  47.3 4.6 pad_maximum_fusion.12
  52.4 3.5 collective-permute-start
  59.7 14.0 %collective-permute-done = bf16[128,1536]{1,0:T(8,128)(2,1)S(1)} collective-permute-done((bf16[128,1536]{1,0:T(8,128)(2,1)}, bf16[128,1536]{1,0:T(8,128)(2,1)S(1)}, u32[]{:S(2)}, u32[]{:S(2)}) %collective-permute-start) | collective-permute-done | bytes 393248 | tf_op jit(solution)/shard_map/ppermute | solution.py:245
  78.1 17.5 %collective-permute-done.8 = bf16[256,1536]{1,0:T(8,128)(2,1)S(1)} collective-permute-done((bf16[256,1536]{1,0:T(8,128)(2,1)S(1)}, bf16[256,1536]{1,0:T(8,128)(2,1)S(1)}, u32[]{:S(2)}, u32[]{:S(2)}) %collective-permute-start.8) | collective-permute-done | bytes 786464 | tf_op jit(solution)/shard_map/ppermute | solution.py:175
  96.1 15.8 %collective-permute-done.7 = bf16[256,1536]{1,0:T(8,128)(2,1)S(1)} collective-permute-done((bf16[256,1536]{1,0:T(8,128)(2,1)S(1)}, bf16[256,1536]{1,0:T(8,128)(2,1)S(1)}, u32[]{:S(2)}, u32[]{:S(2)}) %collective-permute-start.7) | collective-permute-done | bytes 786464 | tf_op jit(solution)/shard_map/ppermute | solution.py:175
  117.3 5.5 fusion.53
  125.1 4.4 collective-permute-done.18
  130.0 4.3 fusion.103
  134.3 4.5 collective-permute-done.12
  140.7 3.5 collective-permute-start.26
  150.0 4.2 reshape.397
  154.2 3.5 copy.410
  159.2 4.0 pad_maximum_fusion
  163.2 3.7 convolution_convert_fusion.1
  168.5 22.0 %attn_fwd.1 = (bf16[2048,256]{1,0:T(8,128)(2,1)S(1)}, f32[2048,2]{1,0:T(8,128)S(1)}) custom-call(s32[8,8]{1,0:T(8,128)S(1)} %and_convert_fusion.need, bf16[2048,256]{1,0:T(8,128)(2,1)S(1)} %get-tuple-element.158.q_ref, bf16[2048,256]{1,0:T(8,128)(2,1)S(1)} %get-tuple-element.157.kv_ref, s32[2048,1]{1,0:T(8,128)S(1)} %copy.356.qp_ref.kp_ref, ...), custom_call_target="tpu_custom_call" | custom-call | flops 2147483648 | bytes 8388608 | tf_op jit(solution)/shard_map/attn_fwd/pallas_call | solution.py:148
  193.0 4.5 maximum_bitcast_fusion.1
  206.8 5.1 pad_maximum_fusion.1
  211.9 15.6 %collective-permute-done.15 = bf16[2,256,256]{2,1,0:T(8,128)(2,1)S(1)} collective-permute-done((bf16[2,256,256]{2,1,0:T(8,128)(2,1)S(1)}, bf16[2,256,256]{2,1,0:T(8,128)(2,1)S(1)}, u32[]{:S(2)}, u32[]{:S(2)}) %collective-permute-start.15) | collective-permute-done | bytes 262176 | tf_op jit(solution)/shard_map/ppermute | solution.py:175
  229.0 4.7 collective-permute-done.17
  237.6 5.0 multiply_reduce_fusion.3
  244.9 5.7 collective-permute-done.39
  256.9 10.4 %collective-permute-done.23 = bf16[256,1536]{1,0:T(8,128)(2,1)S(1)} collective-permute-done((bf16[256,1536]{1,0:T(8,128)(2,1)S(1)}, bf16[256,1536]{1,0:T(8,128)(2,1)S(1)}, u32[]{:S(2)}, u32[]{:S(2)}) %collective-permute-start.23) | collective-permute-done | bytes 786464 | tf_op jit(solution)/shard_map/ppermute | solution.py:175
  267.3 3.9 collective-permute-done.22
  271.2 15.4 %collective-permute-done.24 = bf16[256,1536]{1,0:T(8,128)(2,1)S(1)} collective-permute-done((bf16[256,1536]{1,0:T(8,128)(2,1)S(1)}, bf16[256,1536]{1,0:T(8,128)(2,1)S(1)}, u32[]{:S(2)}, u32[]{:S(2)}) %collective-permute-start.24) | collective-permute-done | bytes 786464 | tf_op jit(solution)/shard_map/ppermute | solution.py:175
  288.6 10.5 %fusion.22 = (bf16[1,2,192,1024]{3,0,2,1:T(2,128)(2,1)S(1)}, bf16[1,2,192,1024]{3,0,2,1:T(2,128)(2,1)S(1)}, bf16[1,2,192,1024]{3,0,2,1:T(2,128)(2,1)S(1)}, bf16[1,2,192,1024]{3,0,2,1:T(2,128)(2,1)S(1)}) fusion(bf16[4,1,192,1024]{3,0,2,1:T(4,128)(2,1)S(1)} %copy-done.30, bf16[4,1,192,1024]{3,0,2,1:T(4,128)(2,1)} %bitcast.83), kind=kLoop, calls=%fused_computation.76 | loop fusion | flops 6291456 | bytes 6291456 | tf_op jit(solution)/shard_map/stack | solution.py:195
  303.8 33.0 %collective-permute-done.28 = bf16[2,192,1024]{2,1,0:T(8,128)(2,1)S(1)} collective-permute-done((bf16[2,192,1024]{2,1,0:T(8,128)(2,1)S(1)}, bf16[2,192,1024]{2,1,0:T(8,128)(2,1)S(1)}, u32[]{:S(2)}, u32[]{:S(2)}) %collective-permute-start.28) | collective-permute-done | bytes 786464 | tf_op jit(solution)/shard_map/ppermute | solution.py:175
  346.8 6.2 fusion.38
  353.0 5.1 fusion.42
  358.0 8.1 multiply_convert_fusion
  367.4 4.6 convolution_convert_fusion
  372.2 10.1 %fusion.40 = f32[2048,1536]{1,0:T(8,128)} fusion(bf16[2048,512]{1,0:T(8,128)(2,1)} %get-tuple-element.120, bf16[1536,1024]{1,0:T(8,128)(2,1)} %bitcast.558), kind=kOutput, calls=%fused_computation.105 | convolution fusion | flops 3221225472 | bytes 16252928 | tf_op jit(solution)/shard_map/dot_general | solution.py:25
  382.3 7.2 convolution_add_fusion
  389.5 4.5 copy-done.10
  396.1 8.7 %copy.390 = bf16[1536,2048]{1,0:T(8,128)(2,1)} copy(bf16[1536,2048]{0,1:T(8,128)(2,1)} %bitcast.492) | data formatting | bytes 12582912 | tf_op jit(solution)/shard_map/dot_general | solution.py:25
  404.8 5.0 fusion.116
  412.9 10.4 %fusion.11 = bf16[8,4,48,512]{3,2,1,0:T(8,128)(2,1)S(1)} fusion(bf16[8,4,48,2048]{3,2,1,0:T(8,128)(2,1)} %bitcast.520, bf16[2048,512]{1,0:T(8,128)(2,1)S(1)} %copy-done.32), kind=kOutput, calls=%fused_computation.67 | convolution fusion | flops 3222011904 | bytes 9961472 | tf_op jit(solution)/shard_map/dot_general | solution.py:25
  428.0 6.2 fusion.8
  437.0 5.0 fusion.109
  447.0 6.0 fusion.110
  456.2 7.8 collective-permute-done.43
  465.5 16.4 %collective-permute-done.45 = bf16[256,1536]{1,0:T(8,128)(2,1)} collective-permute-done((bf16[256,1536]{1,0:T(8,128)(2,1)}, bf16[256,1536]{1,0:T(8,128)(2,1)}, u32[]{:S(2)}, u32[]{:S(2)}) %collective-permute-start.45) | collective-permute-done | bytes 786464 | tf_op jit(solution)/shard_map/ppermute | solution.py:175
  486.2 11.6 %collective-permute-done.31 = bf16[256,1536]{1,0:T(8,128)(2,1)S(1)} collective-permute-done((bf16[256,1536]{1,0:T(8,128)(2,1)S(1)}, bf16[256,1536]{1,0:T(8,128)(2,1)S(1)}, u32[]{:S(2)}, u32[]{:S(2)}) %collective-permute-start.31) | collective-permute-done | bytes 786464 | tf_op jit(solution)/shard_map/ppermute | solution.py:175
  497.8 17.5 %collective-permute-done.33 = bf16[256,1536]{1,0:T(8,128)(2,1)S(1)} collective-permute-done((bf16[256,1536]{1,0:T(8,128)(2,1)S(1)}, bf16[256,1536]{1,0:T(8,128)(2,1)S(1)}, u32[]{:S(2)}, u32[]{:S(2)}) %collective-permute-start.33) | collective-permute-done | bytes 786464 | tf_op jit(solution)/shard_map/ppermute | solution.py:175
  516.6 5.1 fusion.108
  538.8 4.9 collective-permute-done.49
  543.7 18.9 %collective-permute-done.48 = bf16[2,256,256]{2,1,0:T(8,128)(2,1)S(1)} collective-permute-done((bf16[2,256,256]{2,1,0:T(8,128)(2,1)S(1)}, bf16[2,256,256]{2,1,0:T(8,128)(2,1)S(1)}, u32[]{:S(2)}, u32[]{:S(2)}) %collective-permute-start.48) | collective-permute-done | bytes 262176 | tf_op jit(solution)/shard_map/ppermute | solution.py:175
  563.7 20.2 %attn_bwd.1 = (bf16[2048,256]{1,0:T(8,128)(2,1)S(1)}, bf16[2048,256]{1,0:T(8,128)(2,1)S(1)}) custom-call(s32[8,8]{1,0:T(8,128)S(1)} %and_convert_fusion.need, bf16[2048,256]{1,0:T(8,128)(2,1)S(1)} %copy-done.8, bf16[2048,256]{1,0:T(8,128)(2,1)S(1)} %copy-done.6, s32[8,1,256]{2,1,0:T(1,128)S(1)} %bitcast.483, s32[8,1,256]{2,1,0:T(1,128)S(1)} %bitcast.480, ...), custom_call_target="tpu_custom_call" | custom-call | flops 5368709120 | bytes 8388608 | tf_op jit(solution)/shard_map/attn_bwd/pallas_call | solution.py:162
  585.3 3.9 copy.411
  589.3 6.8 fusion.118
  599.6 4.3 fusion.100
  604.0 5.0 fusion.117
  609.0 4.5 copy-done.24
  617.0 3.4 pad_maximum_fusion.4
  624.4 5.9 slice.349
  631.6 9.4 %collective-permute-start.64 = (bf16[4,48,1024]{2,1,0:T(8,128)(2,1)S(1)}, bf16[4,48,1024]{2,1,0:T(8,128)(2,1)S(1)}, u32[]{:S(2)}, u32[]{:S(2)}) collective-permute-start(bf16[4,48,1024]{2,1,0:T(8,128)(2,1)S(1)} %pad_maximum_fusion.21), channel_id=1, source_target_pairs={{0,16},{16,0},{1,17},{17,1},{2,18},{18,2},{3,19},{19,3},{4,20},{20... | collective-permute-start | bytes 1179656 | tf_op jit(solution)/shard_map/ppermute | solution.py:175
  652.3 7.7 fusion.107
  665.8 14.3 %collective-permute-done.35 = bf16[128,1536]{1,0:T(8,128)(2,1)} collective-permute-done((bf16[128,1536]{1,0:T(8,128)(2,1)S(1)}, bf16[128,1536]{1,0:T(8,128)(2,1)}, u32[]{:S(2)}, u32[]{:S(2)}) %collective-permute-start.35) | collective-permute-done | bytes 393248 | tf_op jit(solution)/shard_map/ppermute | solution.py:252
  684.7 17.6 %collective-permute-done.67 = bf16[2,48,1024]{2,1,0:T(8,128)(2,1)S(1)} collective-permute-done((bf16[2,48,1024]{2,1,0:T(8,128)(2,1)}, bf16[2,48,1024]{2,1,0:T(8,128)(2,1)S(1)}, u32[]{:S(2)}, u32[]{:S(2)}) %collective-permute-start.67) | collective-permute-done | bytes 196640 | tf_op jit(solution)/shard_map/ppermute | solution.py:175
  702.3 6.3 collective-permute-done.66
  715.8 3.7 collective-permute-start.55
  720.5 3.5 convert_element_type.301
  724.0 41.7 %all_gather.20 = bf16[192,1536]{1,0:T(8,128)(2,1)S(1)} all-gather(bf16[48,1536]{1,0:T(8,128)(2,1)} %reduce-scatter.7.cloned.1.call-done), channel_id=1, replica_groups=mesh['dp'=2,'blk'=4,'head'=4] {'head'}, dimensions={0}, use_global_device_ids=true | all-gather | bytes 737280 | tf_op jit(solution)/shard_map/all_gather | solution.py:357
  785.9 29.3 %all-gather.10.cloned.1.call-done = bf16[8,4,48,1024]{3,2,1,0:T(8,128)(2,1)} async-done(((bf16[2,4,48,1024]{3,2,1,0:T(8,128)(2,1)}), bf16[8,4,48,1024]{3,2,1,0:T(8,128)(2,1)}) %all-gather.10.cloned.1.call-update) | async-done | bytes 3145744 | tf_op jit(solution)/shard_map/all_gather | solution.py:367
  (476 shorter events, 225.5 us)
Async XLA Ops:
  7.2 596.7 %reduce-scatter.11.cloned.1.call-start = ((), (), s32[]{:S(2)}) async-start(), calls=%async_computation.7 | async-start | bytes 1966080 | tf_op jit(solution)/shard_map/reduce_scatter | solution.py:358
  10.2 42.2 %collective-permute-start.4 = (bf16[1,1408]{1,0:T(2,128)(2,1)}, bf16[1,1408]{1,0:T(2,128)(2,1)}, u32[]{:S(2)}, u32[]{:S(2)}) collective-permute-start(bf16[1,1408]{1,0:T(2,128)(2,1)} %broadcast_in_dim.10), channel_id=1, source_target_pairs={{0,12},{4,8},{8,4},{12,0},{1,13},{5,9},{9,5},{13,1},{2,14},{6,10},... | collective-permute-start | bytes 8456 | tf_op jit(solution)/shard_map/ppermute | solution.py:175
  12.6 43.3 %collective-permute-start.3 = (bf16[1,1408]{1,0:T(2,128)(2,1)}, bf16[1,1408]{1,0:T(2,128)(2,1)}, u32[]{:S(2)}, u32[]{:S(2)}) collective-permute-start(bf16[1,1408]{1,0:T(2,128)(2,1)} %broadcast_in_dim.10), channel_id=1, source_target_pairs={{0,8},{4,12},{8,0},{12,4},{1,9},{5,13},{9,1},{13,5},{2,10},{6,14},... | collective-permute-start | bytes 8456 | tf_op jit(solution)/shard_map/ppermute | solution.py:175
  13.1 43.3 %collective-permute-start.2 = (bf16[1,1408]{1,0:T(2,128)(2,1)}, bf16[1,1408]{1,0:T(2,128)(2,1)}, u32[]{:S(2)}, u32[]{:S(2)}) collective-permute-start(bf16[1,1408]{1,0:T(2,128)(2,1)} %broadcast_in_dim.10), channel_id=1, source_target_pairs={{0,4},{4,0},{8,12},{12,8},{1,5},{5,1},{9,13},{13,9},{2,6},{6,2},{1... | collective-permute-start | bytes 8456 | tf_op jit(solution)/shard_map/ppermute | solution.py:175
  15.6 107.4 %collective-permute-start.20 = (bf16[256,1536]{1,0:T(8,128)(2,1)}, bf16[256,1536]{1,0:T(8,128)(2,1)}, u32[]{:S(2)}, u32[]{:S(2)}) collective-permute-start(bf16[256,1536]{1,0:T(8,128)(2,1)} %bitcast.66), channel_id=1, source_target_pairs={{0,12},{4,8},{8,4},{12,0},{1,13},{5,9},{9,5},{13,1},{2,14},{6,10},... | collective-permute-start | bytes 2359304 | tf_op jit(solution)/shard_map/ppermute | solution.py:175
  18.1 105.8 %collective-permute-start.19 = (bf16[256,1536]{1,0:T(8,128)(2,1)}, bf16[256,1536]{1,0:T(8,128)(2,1)}, u32[]{:S(2)}, u32[]{:S(2)}) collective-permute-start(bf16[256,1536]{1,0:T(8,128)(2,1)} %bitcast.66), channel_id=1, source_target_pairs={{0,8},{4,12},{8,0},{12,4},{1,9},{5,13},{9,1},{13,5},{2,10},{6,14},... | collective-permute-start | bytes 2359304 | tf_op jit(solution)/shard_map/ppermute | solution.py:175
  52.4 21.4 %collective-permute-start = (bf16[128,1536]{1,0:T(8,128)(2,1)}, bf16[128,1536]{1,0:T(8,128)(2,1)S(1)}, u32[]{:S(2)}, u32[]{:S(2)}) collective-permute-start(bf16[128,1536]{1,0:T(8,128)(2,1)} %get-tuple-element.206), channel_id=1, source_target_pairs={{0,0},{1,2},{2,16},{3,18},{16,1},{17,3},{18,17},{19,19},{4,4},{5,6... | collective-permute-start | bytes 1179656 | tf_op jit(solution)/shard_map/ppermute | solution.py:245
  55.9 17.9 %collective-permute-start.1 = (bf16[128,1536]{1,0:T(8,128)(2,1)}, bf16[128,1536]{1,0:T(8,128)(2,1)S(1)}, u32[]{:S(2)}, u32[]{:S(2)}) collective-permute-start(bf16[128,1536]{1,0:T(8,128)(2,1)} %get-tuple-element.207), channel_id=1, source_target_pairs={{0,2},{1,0},{2,18},{3,16},{16,3},{17,1},{18,19},{19,17},{4,6},{5,4... | collective-permute-start | bytes 1179656 | tf_op jit(solution)/shard_map/ppermute | solution.py:245
  74.3 21.3 %collective-permute-start.8 = (bf16[256,1536]{1,0:T(8,128)(2,1)S(1)}, bf16[256,1536]{1,0:T(8,128)(2,1)S(1)}, u32[]{:S(2)}, u32[]{:S(2)}) collective-permute-start(bf16[256,1536]{1,0:T(8,128)(2,1)S(1)} %fusion.14), channel_id=1, source_target_pairs={{0,12},{4,8},{8,4},{12,0},{1,13},{5,9},{9,5},{13,1},{2,14},{6,10},... | collective-permute-start | bytes 2359304 | tf_op jit(solution)/shard_map/ppermute | solution.py:175
  75.8 36.2 %collective-permute-start.7 = (bf16[256,1536]{1,0:T(8,128)(2,1)S(1)}, bf16[256,1536]{1,0:T(8,128)(2,1)S(1)}, u32[]{:S(2)}, u32[]{:S(2)}) collective-permute-start(bf16[256,1536]{1,0:T(8,128)(2,1)S(1)} %fusion.14), channel_id=1, source_target_pairs={{0,8},{4,12},{8,0},{12,4},{1,9},{5,13},{9,1},{13,5},{2,10},{6,14},... | collective-permute-start | bytes 2359304 | tf_op jit(solution)/shard_map/ppermute | solution.py:175
  76.3 36.2 %collective-permute-start.6 = (bf16[256,1536]{1,0:T(8,128)(2,1)S(1)}, bf16[256,1536]{1,0:T(8,128)(2,1)S(1)}, u32[]{:S(2)}, u32[]{:S(2)}) collective-permute-start(bf16[256,1536]{1,0:T(8,128)(2,1)S(1)} %fusion.14), channel_id=1, source_target_pairs={{0,4},{4,0},{8,12},{12,8},{1,5},{5,1},{9,13},{13,9},{2,6},{6,2},{1... | collective-permute-start | bytes 2359304 | tf_op jit(solution)/shard_map/ppermute | solution.py:175
  95.6 33.9 %collective-permute-start.18 = (bf16[256,1536]{1,0:T(8,128)(2,1)}, bf16[256,1536]{1,0:T(8,128)(2,1)}, u32[]{:S(2)}, u32[]{:S(2)}) collective-permute-start(bf16[256,1536]{1,0:T(8,128)(2,1)} %bitcast.66), channel_id=1, source_target_pairs={{0,4},{4,0},{8,12},{12,8},{1,5},{5,1},{9,13},{13,9},{2,6},{6,2},{1... | collective-permute-start | bytes 2359304 | tf_op jit(solution)/shard_map/ppermute | solution.py:175
  115.5 43.7 %collective-permute-start.9 = (bf16[4,256,1536]{2,1,0:T(8,128)(2,1)}, bf16[4,256,1536]{2,1,0:T(8,128)(2,1)}, u32[]{:S(2)}, u32[]{:S(2)}) collective-permute-start(bf16[4,256,1536]{2,1,0:T(8,128)(2,1)} %get-tuple-element.154), channel_id=1, source_target_pairs={{0,16},{16,0},{1,17},{17,1},{2,18},{18,2},{3,19},{19,3},{4,20},{20... | collective-permute-start | bytes 9437192 | tf_op jit(solution)/shard_map/ppermute | solution.py:175
  117.2 82.3 %collective-permute-start.37 = (bf16[128,1536]{1,0:T(8,128)(2,1)}, bf16[128,1536]{1,0:T(8,128)(2,1)}, u32[]{:S(2)}, u32[]{:S(2)}) collective-permute-start(bf16[128,1536]{1,0:T(8,128)(2,1)} %get-tuple-element.200), channel_id=1, source_target_pairs={{0,2},{1,0},{2,18},{3,16},{16,3},{17,1},{18,19},{19,17},{4,6},{5,4... | collective-permute-start | bytes 1179656 | tf_op jit(solution)/shard_map/ppermute | solution.py:245
  123.0 15.8 %collective-permute-start.12 = (bf16[2,192,384]{2,1,0:T(8,128)(2,1)S(1)}, bf16[2,192,384]{2,1,0:T(8,128)(2,1)S(1)}, u32[]{:S(2)}, u32[]{:S(2)}) collective-permute-start(bf16[2,192,384]{2,1,0:T(8,128)(2,1)S(1)} %bitcast.593), channel_id=1, source_target_pairs={{0,8},{4,12},{8,0},{12,4},{1,9},{5,13},{9,1},{13,5},{2,10},{6,14},... | collective-permute-start | bytes 884744 | tf_op jit(solution)/shard_map/ppermute | solution.py:175
  123.9 16.9 %collective-permute-start.13 = (bf16[2,192,384]{2,1,0:T(8,128)(2,1)S(1)}, bf16[2,192,384]{2,1,0:T(8,128)(2,1)S(1)}, u32[]{:S(2)}, u32[]{:S(2)}) collective-permute-start(bf16[2,192,384]{2,1,0:T(8,128)(2,1)S(1)} %bitcast.592), channel_id=1, source_target_pairs={{0,12},{4,8},{8,4},{12,0},{1,13},{5,9},{9,5},{13,1},{2,14},{6,10},... | collective-permute-start | bytes 884744 | tf_op jit(solution)/shard_map/ppermute | solution.py:175
  129.5 14.7 %collective-permute-start.11 = (bf16[2,192,384]{2,1,0:T(8,128)(2,1)S(1)}, bf16[2,192,384]{2,1,0:T(8,128)(2,1)S(1)}, u32[]{:S(2)}, u32[]{:S(2)}) collective-permute-start(bf16[2,192,384]{2,1,0:T(8,128)(2,1)S(1)} %bitcast.591), channel_id=1, source_target_pairs={{0,4},{4,0},{8,12},{12,8},{1,5},{5,1},{9,13},{13,9},{2,6},{6,2},{1... | collective-permute-start | bytes 884744 | tf_op jit(solution)/shard_map/ppermute | solution.py:175
  138.8 58.8 %collective-permute-start.36 = (bf16[128,1536]{1,0:T(8,128)(2,1)}, bf16[128,1536]{1,0:T(8,128)(2,1)}, u32[]{:S(2)}, u32[]{:S(2)}) collective-permute-start(bf16[128,1536]{1,0:T(8,128)(2,1)} %get-tuple-element.201), channel_id=1, source_target_pairs={{0,0},{1,2},{2,16},{3,18},{16,1},{17,3},{18,17},{19,19},{4,4},{5,6... | collective-permute-start | bytes 1179656 | tf_op jit(solution)/shard_map/ppermute | solution.py:245
  140.7 147.8 %collective-permute-start.26 = (bf16[4,192,1024]{2,0,1:T(4,128)(2,1)}, bf16[4,192,1024]{2,0,1:T(4,128)(2,1)}, u32[]{:S(2)}, u32[]{:S(2)}) collective-permute-start(bf16[4,192,1024]{2,0,1:T(4,128)(2,1)} %pad_maximum_fusion.12), channel_id=1, source_target_pairs={{0,16},{16,0},{1,17},{17,1},{2,18},{18,2},{3,19},{19,3},{4,20},{20... | collective-permute-start | bytes 4718600 | tf_op jit(solution)/shard_map/ppermute | solution.py:175
  144.2 62.1 %collective-permute-start.21 = (bf16[4,256,1536]{2,1,0:T(8,128)(2,1)}, bf16[4,256,1536]{2,1,0:T(8,128)(2,1)}, u32[]{:S(2)}, u32[]{:S(2)}) collective-permute-start(bf16[4,256,1536]{2,1,0:T(8,128)(2,1)} %get-tuple-element.152), channel_id=1, source_target_pairs={{0,16},{16,0},{1,17},{17,1},{2,18},{18,2},{3,19},{19,3},{4,20},{20... | collective-permute-start | bytes 9437192 | tf_op jit(solution)/shard_map/ppermute | solution.py:175
  201.3 42.1 %collective-permute-start.40 = (bf16[256,1536]{1,0:T(8,128)(2,1)}, bf16[256,1536]{1,0:T(8,128)(2,1)}, u32[]{:S(2)}, u32[]{:S(2)}) collective-permute-start(bf16[256,1536]{1,0:T(8,128)(2,1)} %constant_dynamic-update-slice_fusion.2), channel_id=1, source_target_pairs={{0,12},{4,8},{8,4},{12,0},{1,13},{5,9},{9,5},{13,1},{2,14},{6,10},... | collective-permute-start | bytes 2359304 | tf_op jit(solution)/shard_map/ppermute | solution.py:175
  203.2 24.3 %collective-permute-start.15 = (bf16[2,256,256]{2,1,0:T(8,128)(2,1)S(1)}, bf16[2,256,256]{2,1,0:T(8,128)(2,1)S(1)}, u32[]{:S(2)}, u32[]{:S(2)}) collective-permute-start(bf16[2,256,256]{2,1,0:T(8,128)(2,1)S(1)} %get-tuple-element.179), channel_id=1, source_target_pairs={{0,4},{4,0},{8,12},{12,8},{1,5},{5,1},{9,13},{13,9},{2,6},{6,2},{1... | collective-permute-start | bytes 786440 | tf_op jit(solution)/shard_map/ppermute | solution.py:175
  204.8 29.0 %collective-permute-start.17 = (bf16[2,256,256]{2,1,0:T(8,128)(2,1)S(1)}, bf16[2,256,256]{2,1,0:T(8,128)(2,1)S(1)}, u32[]{:S(2)}, u32[]{:S(2)}) collective-permute-start(bf16[2,256,256]{2,1,0:T(8,128)(2,1)S(1)} %get-tuple-element.180), channel_id=1, source_target_pairs={{0,12},{4,8},{8,4},{12,0},{1,13},{5,9},{9,5},{13,1},{2,14},{6,10},... | collective-permute-start | bytes 786440 | tf_op jit(solution)/shard_map/ppermute | solution.py:175
  206.3 28.0 %collective-permute-start.16 = (bf16[2,256,256]{2,1,0:T(8,128)(2,1)S(1)}, bf16[2,256,256]{2,1,0:T(8,128)(2,1)S(1)}, u32[]{:S(2)}, u32[]{:S(2)}) collective-permute-start(bf16[2,256,256]{2,1,0:T(8,128)(2,1)S(1)} %get-tuple-element.181), channel_id=1, source_target_pairs={{0,8},{4,12},{8,0},{12,4},{1,9},{5,13},{9,1},{13,5},{2,10},{6,14},... | collective-permute-start | bytes 786440 | tf_op jit(solution)/shard_map/ppermute | solution.py:175
  227.5 23.2 %collective-permute-start.39 = (bf16[256,1536]{1,0:T(8,128)(2,1)}, bf16[256,1536]{1,0:T(8,128)(2,1)}, u32[]{:S(2)}, u32[]{:S(2)}) collective-permute-start(bf16[256,1536]{1,0:T(8,128)(2,1)} %constant_dynamic-update-slice_fusion.2), channel_id=1, source_target_pairs={{0,8},{4,12},{8,0},{12,4},{1,9},{5,13},{9,1},{13,5},{2,10},{6,14},... | collective-permute-start | bytes 2359304 | tf_op jit(solution)/shard_map/ppermute | solution.py:175
  233.7 20.8 %collective-permute-start.38 = (bf16[256,1536]{1,0:T(8,128)(2,1)}, bf16[256,1536]{1,0:T(8,128)(2,1)}, u32[]{:S(2)}, u32[]{:S(2)}) collective-permute-start(bf16[256,1536]{1,0:T(8,128)(2,1)} %constant_dynamic-update-slice_fusion.2), channel_id=1, source_target_pairs={{0,4},{4,0},{8,12},{12,8},{1,5},{5,1},{9,13},{13,9},{2,6},{6,2},{1... | collective-permute-start | bytes 2359304 | tf_op jit(solution)/shard_map/ppermute | solution.py:175
  242.9 24.4 %collective-permute-start.23 = (bf16[256,1536]{1,0:T(8,128)(2,1)S(1)}, bf16[256,1536]{1,0:T(8,128)(2,1)S(1)}, u32[]{:S(2)}, u32[]{:S(2)}) collective-permute-start(bf16[256,1536]{1,0:T(8,128)(2,1)S(1)} %multiply_convert_fusion.3), channel_id=1, source_target_pairs={{0,8},{4,12},{8,0},{12,4},{1,9},{5,13},{9,1},{13,5},{2,10},{6,14},... | collective-permute-start | bytes 2359304 | tf_op jit(solution)/shard_map/ppermute | solution.py:175
  243.5 27.8 %collective-permute-start.22 = (bf16[256,1536]{1,0:T(8,128)(2,1)S(1)}, bf16[256,1536]{1,0:T(8,128)(2,1)S(1)}, u32[]{:S(2)}, u32[]{:S(2)}) collective-permute-start(bf16[256,1536]{1,0:T(8,128)(2,1)S(1)} %multiply_convert_fusion.3), channel_id=1, source_target_pairs={{0,4},{4,0},{8,12},{12,8},{1,5},{5,1},{9,13},{13,9},{2,6},{6,2},{1... | collective-permute-start | bytes 2359304 | tf_op jit(solution)/shard_map/ppermute | solution.py:175
  250.7 36.0 %collective-permute-start.24 = (bf16[256,1536]{1,0:T(8,128)(2,1)S(1)}, bf16[256,1536]{1,0:T(8,128)(2,1)S(1)}, u32[]{:S(2)}, u32[]{:S(2)}) collective-permute-start(bf16[256,1536]{1,0:T(8,128)(2,1)S(1)} %multiply_convert_fusion.3), channel_id=1, source_target_pairs={{0,12},{4,8},{8,4},{12,0},{1,13},{5,9},{9,5},{13,1},{2,14},{6,10},... | collective-permute-start | bytes 2359304 | tf_op jit(solution)/shard_map/ppermute | solution.py:175
  256.6 82.5 %collective-permute-start.41 = (bf16[4,256,1536]{2,1,0:T(8,128)(2,1)S(1)}, bf16[4,256,1536]{2,1,0:T(8,128)(2,1)S(1)}, u32[]{:S(2)}, u32[]{:S(2)}) collective-permute-start(bf16[4,256,1536]{2,1,0:T(8,128)(2,1)S(1)} %get-tuple-element.133), channel_id=1, source_target_pairs={{0,16},{16,0},{1,17},{17,1},{2,18},{18,2},{3,19},{19,3},{4,20},{20... | collective-permute-start | bytes 9437192 | tf_op jit(solution)/shard_map/ppermute | solution.py:175
  288.5 55.7 %collective-permute-start.25 = (bf16[4,256,1536]{2,1,0:T(8,128)(2,1)}, bf16[4,256,1536]{2,1,0:T(8,128)(2,1)}, u32[]{:S(2)}, u32[]{:S(2)}) collective-permute-start(bf16[4,256,1536]{2,1,0:T(8,128)(2,1)} %get-tuple-element.150), channel_id=1, source_target_pairs={{0,16},{16,0},{1,17},{17,1},{2,18},{18,2},{3,19},{19,3},{4,20},{20... | collective-permute-start | bytes 9437192 | tf_op jit(solution)/shard_map/ppermute | solution.py:175
  299.9 36.9 %collective-permute-start.28 = (bf16[2,192,1024]{2,1,0:T(8,128)(2,1)S(1)}, bf16[2,192,1024]{2,1,0:T(8,128)(2,1)S(1)}, u32[]{:S(2)}, u32[]{:S(2)}) collective-permute-start(bf16[2,192,1024]{2,1,0:T(8,128)(2,1)S(1)} %bitcast.584), channel_id=1, source_target_pairs={{0,8},{4,12},{8,0},{12,4},{1,9},{5,13},{9,1},{13,5},{2,10},{6,14},... | collective-permute-start | bytes 2359304 | tf_op jit(solution)/shard_map/ppermute | solution.py:175
  301.5 35.3 %collective-permute-start.29 = (bf16[2,192,1024]{2,1,0:T(8,128)(2,1)S(1)}, bf16[2,192,1024]{2,1,0:T(8,128)(2,1)S(1)}, u32[]{:S(2)}, u32[]{:S(2)}) collective-permute-start(bf16[2,192,1024]{2,1,0:T(8,128)(2,1)S(1)} %bitcast.583), channel_id=1, source_target_pairs={{0,12},{4,8},{8,4},{12,0},{1,13},{5,9},{9,5},{13,1},{2,14},{6,10},... | collective-permute-start | bytes 2359304 | tf_op jit(solution)/shard_map/ppermute | solution.py:175
  302.0 36.1 %collective-permute-start.27 = (bf16[2,192,1024]{2,1,0:T(8,128)(2,1)S(1)}, bf16[2,192,1024]{2,1,0:T(8,128)(2,1)S(1)}, u32[]{:S(2)}, u32[]{:S(2)}) collective-permute-start(bf16[2,192,1024]{2,1,0:T(8,128)(2,1)S(1)} %bitcast.582), channel_id=1, source_target_pairs={{0,4},{4,0},{8,12},{12,8},{1,5},{5,1},{9,13},{13,9},{2,6},{6,2},{1... | collective-permute-start | bytes 2359304 | tf_op jit(solution)/shard_map/ppermute | solution.py:175
  372.1 258.2 %reduce-scatter.9.cloned.1.call-start = ((), (), s32[]{:S(2)}) async-start(), calls=%async_computation.6 | async-start | bytes 3932160 | tf_op jit(solution)/shard_map/reduce_scatter | solution.py:365
  396.1 40.9 %collective-permute-start.42 = (bf16[4,256,1536]{2,1,0:T(8,128)(2,1)}, bf16[4,256,1536]{2,1,0:T(8,128)(2,1)}, u32[]{:S(2)}, u32[]{:S(2)}) collective-permute-start(bf16[4,256,1536]{2,1,0:T(8,128)(2,1)} %bitcast.109), channel_id=1, source_target_pairs={{0,16},{16,0},{1,17},{17,1},{2,18},{18,2},{3,19},{19,3},{4,20},{20... | collective-permute-start | bytes 9437192 | tf_op jit(solution)/shard_map/ppermute | solution.py:175
  411.9 35.1 %collective-permute-start.30 = (bf16[4,256,1536]{2,1,0:T(8,128)(2,1)}, bf16[4,256,1536]{2,1,0:T(8,128)(2,1)}, u32[]{:S(2)}, u32[]{:S(2)}) collective-permute-start(bf16[4,256,1536]{2,1,0:T(8,128)(2,1)} %bitcast.90), channel_id=1, source_target_pairs={{0,16},{16,0},{1,17},{17,1},{2,18},{18,2},{3,19},{19,3},{4,20},{20... | collective-permute-start | bytes 9437192 | tf_op jit(solution)/shard_map/ppermute | solution.py:175
  436.8 204.3 %reduce-scatter.5.cloned.1.call-start = ((), (), s32[]{:S(2)}) async-start(), calls=%async_computation.4 | async-start | bytes 1474560 | tf_op jit(solution)/shard_map/reduce_scatter | solution.py:365
  443.5 20.5 %collective-permute-start.43 = (bf16[256,1536]{1,0:T(8,128)(2,1)}, bf16[256,1536]{1,0:T(8,128)(2,1)S(1)}, u32[]{:S(2)}, u32[]{:S(2)}) collective-permute-start(bf16[256,1536]{1,0:T(8,128)(2,1)} %get-tuple-element.129), channel_id=1, source_target_pairs={{0,4},{4,0},{8,12},{12,8},{1,5},{5,1},{9,13},{13,9},{2,6},{6,2},{1... | collective-permute-start | bytes 2359304 | tf_op jit(solution)/shard_map/ppermute | solution.py:175
  444.3 37.7 %collective-permute-start.45 = (bf16[256,1536]{1,0:T(8,128)(2,1)}, bf16[256,1536]{1,0:T(8,128)(2,1)}, u32[]{:S(2)}, u32[]{:S(2)}) collective-permute-start(bf16[256,1536]{1,0:T(8,128)(2,1)} %get-tuple-element.130), channel_id=1, source_target_pairs={{0,12},{4,8},{8,4},{12,0},{1,13},{5,9},{9,5},{13,1},{2,14},{6,10},... | collective-permute-start | bytes 2359304 | tf_op jit(solution)/shard_map/ppermute | solution.py:175
  446.4 37.6 %collective-permute-start.44 = (bf16[256,1536]{1,0:T(8,128)(2,1)}, bf16[256,1536]{1,0:T(8,128)(2,1)}, u32[]{:S(2)}, u32[]{:S(2)}) collective-permute-start(bf16[256,1536]{1,0:T(8,128)(2,1)} %get-tuple-element.131), channel_id=1, source_target_pairs={{0,8},{4,12},{8,0},{12,4},{1,9},{5,13},{9,1},{13,5},{2,10},{6,14},... | collective-permute-start | bytes 2359304 | tf_op jit(solution)/shard_map/ppermute | solution.py:175
  453.2 44.6 %collective-permute-start.31 = (bf16[256,1536]{1,0:T(8,128)(2,1)S(1)}, bf16[256,1536]{1,0:T(8,128)(2,1)S(1)}, u32[]{:S(2)}, u32[]{:S(2)}) collective-permute-start(bf16[256,1536]{1,0:T(8,128)(2,1)S(1)} %get-tuple-element.134), channel_id=1, source_target_pairs={{0,4},{4,0},{8,12},{12,8},{1,5},{5,1},{9,13},{13,9},{2,6},{6,2},{1... | collective-permute-start | bytes 2359304 | tf_op jit(solution)/shard_map/ppermute | solution.py:175
  454.2 61.0 %collective-permute-start.33 = (bf16[256,1536]{1,0:T(8,128)(2,1)S(1)}, bf16[256,1536]{1,0:T(8,128)(2,1)S(1)}, u32[]{:S(2)}, u32[]{:S(2)}) collective-permute-start(bf16[256,1536]{1,0:T(8,128)(2,1)S(1)} %get-tuple-element.135), channel_id=1, source_target_pairs={{0,12},{4,8},{8,4},{12,0},{1,13},{5,9},{9,5},{13,1},{2,14},{6,10},... | collective-permute-start | bytes 2359304 | tf_op jit(solution)/shard_map/ppermute | solution.py:175
  464.0 52.6 %collective-permute-start.32 = (bf16[256,1536]{1,0:T(8,128)(2,1)S(1)}, bf16[256,1536]{1,0:T(8,128)(2,1)S(1)}, u32[]{:S(2)}, u32[]{:S(2)}) collective-permute-start(bf16[256,1536]{1,0:T(8,128)(2,1)S(1)} %get-tuple-element.136), channel_id=1, source_target_pairs={{0,8},{4,12},{8,0},{12,4},{1,9},{5,13},{9,1},{13,5},{2,10},{6,14},... | collective-permute-start | bytes 2359304 | tf_op jit(solution)/shard_map/ppermute | solution.py:175
  530.8 31.7 %collective-permute-start.48 = (bf16[2,256,256]{2,1,0:T(8,128)(2,1)S(1)}, bf16[2,256,256]{2,1,0:T(8,128)(2,1)S(1)}, u32[]{:S(2)}, u32[]{:S(2)}) collective-permute-start(bf16[2,256,256]{2,1,0:T(8,128)(2,1)S(1)} %get-tuple-element.175), channel_id=1, source_target_pairs={{0,8},{4,12},{8,0},{12,4},{1,9},{5,13},{9,1},{13,5},{2,10},{6,14},... | collective-permute-start | bytes 786440 | tf_op jit(solution)/shard_map/ppermute | solution.py:175
  532.3 67.2 %collective-permute-start.62 = (bf16[256,1536]{1,0:T(8,128)(2,1)S(1)}, bf16[256,1536]{1,0:T(8,128)(2,1)}, u32[]{:S(2)}, u32[]{:S(2)}) collective-permute-start(bf16[256,1536]{1,0:T(8,128)(2,1)S(1)} %get-tuple-element.113), channel_id=1, source_target_pairs={{0,12},{4,8},{8,4},{12,0},{1,13},{5,9},{9,5},{13,1},{2,14},{6,10},... | collective-permute-start | bytes 2359304 | tf_op jit(solution)/shard_map/ppermute | solution.py:175
  533.1 66.5 %collective-permute-start.61 = (bf16[256,1536]{1,0:T(8,128)(2,1)S(1)}, bf16[256,1536]{1,0:T(8,128)(2,1)}, u32[]{:S(2)}, u32[]{:S(2)}) collective-permute-start(bf16[256,1536]{1,0:T(8,128)(2,1)S(1)} %get-tuple-element.113), channel_id=1, source_target_pairs={{0,8},{4,12},{8,0},{12,4},{1,9},{5,13},{9,1},{13,5},{2,10},{6,14},... | collective-permute-start | bytes 2359304 | tf_op jit(solution)/shard_map/ppermute | solution.py:175
  538.0 61.6 %collective-permute-start.60 = (bf16[256,1536]{1,0:T(8,128)(2,1)S(1)}, bf16[256,1536]{1,0:T(8,128)(2,1)}, u32[]{:S(2)}, u32[]{:S(2)}) collective-permute-start(bf16[256,1536]{1,0:T(8,128)(2,1)S(1)} %get-tuple-element.113), channel_id=1, source_target_pairs={{0,4},{4,0},{8,12},{12,8},{1,5},{5,1},{9,13},{13,9},{2,6},{6,2},{1... | collective-permute-start | bytes 2359304 | tf_op jit(solution)/shard_map/ppermute | solution.py:175
  599.5 121.0 %all-gather.6.cloned.1.call-start = ((), (), s32[]{:S(2)}) async-start(), calls=%async_computation.8 | async-start | bytes 1966080 | tf_op jit(solution)/shard_map/all_gather | solution.py:357
  604.0 120.0 %reduce-scatter.7.cloned.1.call-start = ((), (), s32[]{:S(2)}) async-start(), calls=%async_computation.5 | async-start | bytes 737280 | tf_op jit(solution)/shard_map/reduce_scatter | solution.py:358
  615.6 36.7 %collective-permute-start.50 = (bf16[4,256,1536]{2,1,0:T(8,128)(2,1)}, bf16[4,256,1536]{2,1,0:T(8,128)(2,1)}, u32[]{:S(2)}, u32[]{:S(2)}) collective-permute-start(bf16[4,256,1536]{2,1,0:T(8,128)(2,1)} %bitcast.131), channel_id=1, source_target_pairs={{0,16},{16,0},{1,17},{17,1},{2,18},{18,2},{3,19},{19,3},{4,20},{20... | collective-permute-start | bytes 9437192 | tf_op jit(solution)/shard_map/ppermute | solution.py:175
  623.1 144.8 %all-gather.8.cloned.1.call-start = ((), (), s32[]{:S(2)}) async-start(), calls=%async_computation.9 | async-start | bytes 1474560 | tf_op jit(solution)/shard_map/all_gather | solution.py:367
  624.3 39.9 %collective-permute-start.34 = (bf16[128,1536]{1,0:T(8,128)(2,1)}, bf16[128,1536]{1,0:T(8,128)(2,1)S(1)}, u32[]{:S(2)}, u32[]{:S(2)}) collective-permute-start(bf16[128,1536]{1,0:T(8,128)(2,1)} %get-tuple-element.204), channel_id=1, source_target_pairs={{2,0},{0,1},{18,2},{16,3},{3,16},{1,17},{19,18},{17,19},{6,4},{4,5... | collective-permute-start | bytes 1179656 | tf_op jit(solution)/shard_map/ppermute | solution.py:252
  631.6 14.9 %collective-permute-start.64 = (bf16[4,48,1024]{2,1,0:T(8,128)(2,1)S(1)}, bf16[4,48,1024]{2,1,0:T(8,128)(2,1)S(1)}, u32[]{:S(2)}, u32[]{:S(2)}) collective-permute-start(bf16[4,48,1024]{2,1,0:T(8,128)(2,1)S(1)} %pad_maximum_fusion.21), channel_id=1, source_target_pairs={{0,16},{16,0},{1,17},{17,1},{2,18},{18,2},{3,19},{19,3},{4,20},{20... | collective-permute-start | bytes 1179656 | tf_op jit(solution)/shard_map/ppermute | solution.py:175
  648.4 31.7 %collective-permute-start.35 = (bf16[128,1536]{1,0:T(8,128)(2,1)S(1)}, bf16[128,1536]{1,0:T(8,128)(2,1)}, u32[]{:S(2)}, u32[]{:S(2)}) collective-permute-start(bf16[128,1536]{1,0:T(8,128)(2,1)S(1)} %get-tuple-element.205), channel_id=1, source_target_pairs={{0,0},{2,1},{16,2},{18,3},{1,16},{3,17},{17,18},{19,19},{4,4},{6,5... | collective-permute-start | bytes 1179656 | tf_op jit(solution)/shard_map/ppermute | solution.py:252
  650.7 31.6 %collective-permute-start.65 = (bf16[2,48,1024]{2,1,0:T(8,128)(2,1)}, bf16[2,48,1024]{2,1,0:T(8,128)(2,1)}, u32[]{:S(2)}, u32[]{:S(2)}) collective-permute-start(bf16[2,48,1024]{2,1,0:T(8,128)(2,1)} %get-tuple-element.185), channel_id=1, source_target_pairs={{0,4},{4,0},{8,12},{12,8},{1,5},{5,1},{9,13},{13,9},{2,6},{6,2},{1... | collective-permute-start | bytes 589832 | tf_op jit(solution)/shard_map/ppermute | solution.py:175
  652.3 162.9 %all-gather.10.cloned.1.call-start = ((), (), s32[]{:S(2)}) async-start(), calls=%async_computation.10 | async-start | bytes 3932160 | tf_op jit(solution)/shard_map/all_gather | solution.py:367
  661.5 49.2 %collective-permute-start.51 = (bf16[256,1536]{1,0:T(8,128)(2,1)}, bf16[256,1536]{1,0:T(8,128)(2,1)S(1)}, u32[]{:S(2)}, u32[]{:S(2)}) collective-permute-start(bf16[256,1536]{1,0:T(8,128)(2,1)} %get-tuple-element.126), channel_id=1, source_target_pairs={{0,4},{4,0},{8,12},{12,8},{1,5},{5,1},{9,13},{13,9},{2,6},{6,2},{1... | collective-permute-start | bytes 2359304 | tf_op jit(solution)/shard_map/ppermute | solution.py:175
  662.8 47.9 %collective-permute-start.53 = (bf16[256,1536]{1,0:T(8,128)(2,1)}, bf16[256,1536]{1,0:T(8,128)(2,1)S(1)}, u32[]{:S(2)}, u32[]{:S(2)}) collective-permute-start(bf16[256,1536]{1,0:T(8,128)(2,1)} %get-tuple-element.127), channel_id=1, source_target_pairs={{0,12},{4,8},{8,4},{12,0},{1,13},{5,9},{9,5},{13,1},{2,14},{6,10},... | collective-permute-start | bytes 2359304 | tf_op jit(solution)/shard_map/ppermute | solution.py:175
  665.0 45.7 %collective-permute-start.52 = (bf16[256,1536]{1,0:T(8,128)(2,1)}, bf16[256,1536]{1,0:T(8,128)(2,1)S(1)}, u32[]{:S(2)}, u32[]{:S(2)}) collective-permute-start(bf16[256,1536]{1,0:T(8,128)(2,1)} %get-tuple-element.128), channel_id=1, source_target_pairs={{0,8},{4,12},{8,0},{12,4},{1,9},{5,13},{9,1},{13,5},{2,10},{6,14},... | collective-permute-start | bytes 2359304 | tf_op jit(solution)/shard_map/ppermute | solution.py:175
  680.1 22.2 %collective-permute-start.67 = (bf16[2,48,1024]{2,1,0:T(8,128)(2,1)}, bf16[2,48,1024]{2,1,0:T(8,128)(2,1)S(1)}, u32[]{:S(2)}, u32[]{:S(2)}) collective-permute-start(bf16[2,48,1024]{2,1,0:T(8,128)(2,1)} %get-tuple-element.186), channel_id=1, source_target_pairs={{0,12},{4,8},{8,4},{12,0},{1,13},{5,9},{9,5},{13,1},{2,14},{6,10},... | collective-permute-start | bytes 589832 | tf_op jit(solution)/shard_map/ppermute | solution.py:175
  682.3 26.3 %collective-permute-start.66 = (bf16[2,48,1024]{2,1,0:T(8,128)(2,1)}, bf16[2,48,1024]{2,1,0:T(8,128)(2,1)S(1)}, u32[]{:S(2)}, u32[]{:S(2)}) collective-permute-start(bf16[2,48,1024]{2,1,0:T(8,128)(2,1)} %get-tuple-element.187), channel_id=1, source_target_pairs={{0,8},{4,12},{8,0},{12,4},{1,9},{5,13},{9,1},{13,5},{2,10},{6,14},... | collective-permute-start | bytes 589832 | tf_op jit(solution)/shard_map/ppermute | solution.py:175
  715.8 51.1 %collective-permute-start.54 = (bf16[128,1536]{1,0:T(8,128)(2,1)S(1)}, bf16[128,1536]{1,0:T(8,128)(2,1)S(1)}, u32[]{:S(2)}, u32[]{:S(2)}) collective-permute-start(bf16[128,1536]{1,0:T(8,128)(2,1)S(1)} %get-tuple-element.198), channel_id=1, source_target_pairs={{2,0},{0,1},{18,2},{16,3},{3,16},{1,17},{19,18},{17,19},{6,4},{4,5... | collective-permute-start | bytes 1179656 | tf_op jit(solution)/shard_map/ppermute | solution.py:252
  715.8 51.0 %collective-permute-start.55 = (bf16[128,1536]{1,0:T(8,128)(2,1)S(1)}, bf16[128,1536]{1,0:T(8,128)(2,1)S(1)}, u32[]{:S(2)}, u32[]{:S(2)}) collective-permute-start(bf16[128,1536]{1,0:T(8,128)(2,1)S(1)} %get-tuple-element.199), channel_id=1, source_target_pairs={{0,0},{2,1},{16,2},{18,3},{1,16},{3,17},{17,18},{19,19},{4,4},{6,5... | collective-permute-start | bytes 1179656 | tf_op jit(solution)/shard_map/ppermute | solution.py:252
  (84 other events, 1805.5 us)
Sparse Core Ops, SparseCore 0:
  372.2 38.2 reduce-scatter.10
  436.9 63.9 reduce-scatter.8
  599.6 34.4 reduce-scatter.4
  635.6 43.3 all-gather.5
  681.6 21.5 reduce-scatter.6
  705.3 44.4 all-gather.7
  751.3 63.8 all-gather.9

commit v2 on v1

v2 whole, which is shorter than its diff:
```python
import functools
import math

import jax
import jax.numpy as jnp
from jax import lax
from jax.experimental import pallas as pl
from jax.experimental.pallas import tpu as pltpu
from jax.sharding import PartitionSpec as P

D = 1536
QH = 16
KVH = 8
HD = 96
HP = 128
FF = 4096
EPS = 1e-05
NEG = -1e30
BLK = 256
BF = jnp.bfloat16
F32 = jnp.float32


def dot(left, right, dims=((1,), (0,))):
    return lax.dot_general(left, right, (dims, ((), ())), preferred_element_type=F32)


def normalize(values):
    factor = lax.rsqrt(jnp.mean(values * values, -1, keepdims=True) + EPS)
    return values * factor, factor


def norm_back(grad_norm, gain, normed, factor):
    scaled = grad_norm * gain
    return factor * (scaled - normed * jnp.mean(scaled * normed, -1, keepdims=True))


def rows_of(index):
    return pl.ds(pl.multiple_of(index * BLK, BLK), BLK)


def as_column(row):
    return jnp.broadcast_to(row, (HP, BLK)).T[:, 0:1]


def as_row(col):
    return jnp.broadcast_to(col, (BLK, HP)).T[0:1, :]


def keys_to_columns(kp_ref, ks_ref, pos_sc, seg_sc):
    def one(j, _):
        pos_sc[rows_of(j), :] = as_column(kp_ref[j])
        seg_sc[rows_of(j), :] = as_column(ks_ref[j])
        return 0

    lax.fori_loop(0, kp_ref.shape[0], one, 0)


def attn_fwd_kernel(first, need, q_ref, kv_ref, qp_ref, qs_ref, kp_ref, ks_ref, o_ref, lse_ref, m_sc, l_sc, acc_sc, pos_sc, seg_sc):
    scale = 1.0 / math.sqrt(HD)
    n_q, n_k = q_ref.shape[0] // BLK, kv_ref.shape[0] // BLK
    k_cols, v_cols = slice(first, first + HP), slice(first + HP, first + 2 * HP)
    keys_to_columns(kp_ref, ks_ref, pos_sc, seg_sc)

    def one_query(i, _):
        qr = rows_of(i)
        m_sc[...] = jnp.full_like(m_sc, NEG)
        l_sc[...] = jnp.zeros_like(l_sc)
        acc_sc[...] = jnp.zeros_like(acc_sc)
        qpos, qseg = qp_ref[i], qs_ref[i]

        def one_key(j, _):
            @pl.when(need[i, j] != 0)
            def _():
                kr = rows_of(j)
                ok = (pos_sc[kr, :] <= qpos) & (seg_sc[kr, :] == qseg)
                k, v = kv_ref[kr, k_cols], kv_ref[kr, v_cols]
                state = [(m_sc[g], l_sc[g], acc_sc[g], q_ref[qr, g * HP : (g + 1) * HP]) for g in range(2)]
                scores = [jnp.where(ok, dot(k, q, ((1,), (1,))) * scale, NEG) for _, _, _, q in state]
                new = []
                for (m_old, l_old, acc_old, _), s in zip(state, scores):
                    m_new = jnp.maximum(m_old, jnp.max(s, 0, keepdims=True))
                    p = jnp.where(ok, jnp.exp(s - m_new), 0.0)
                    decay = jnp.exp(m_old - m_new)
                    total = l_old * decay + jnp.sum(p, 0, keepdims=True)
                    new.append((m_new, total, acc_old * decay + dot(v, p.astype(BF), ((0,), (0,)))))
                for g in range(2):
                    m_sc[g], l_sc[g], acc_sc[g] = new[g]

            return 0

        lax.fori_loop(0, n_k, one_key, 0)
        for g in range(2):
            o_ref[qr, g * HP : (g + 1) * HP] = (acc_sc[g] / l_sc[g]).T.astype(BF)
            lse_ref[i, g : g + 1, :] = m_sc[g] + jnp.log(l_sc[g])
        return 0

    lax.fori_loop(0, n_q, one_query, 0)


def attn_bwd_kernel(first, need, q_ref, kv_ref, qp_ref, qs_ref, kp_ref, ks_ref, o_ref, lse_ref, do_ref, *rest):
    dq_ref, dkv_ref = rest[0], rest[-6]
    dq_sc, dk_sc, dv_sc, pos_sc, seg_sc = rest[-5:]
    scale = 1.0 / math.sqrt(HD)
    n_q, n_k = q_ref.shape[0] // BLK, kv_ref.shape[0] // BLK
    k_cols, v_cols = slice(first, first + HP), slice(first + HP, first + 2 * HP)
    dk_sc[...] = jnp.zeros_like(dk_sc)
    dv_sc[...] = jnp.zeros_like(dv_sc)
    keys_to_columns(kp_ref, ks_ref, pos_sc, seg_sc)

    def one_query(i, _):
        qr = rows_of(i)
        dq_sc[...] = jnp.zeros_like(dq_sc)
        qpos, qseg = qp_ref[i], qs_ref[i]
        lse, delta = [], []
        for g in range(2):
            cols = slice(g * HP, (g + 1) * HP)
            lse.append(lse_ref[i, g : g + 1, :])
            prod = do_ref[qr, cols].astype(F32) * o_ref[qr, cols].astype(F32)
            delta.append(as_row(jnp.sum(prod, -1, keepdims=True)))

        def one_key(j, _):
            @pl.when(need[i, j] != 0)
            def _():
                kr = rows_of(j)
                ok = (pos_sc[kr, :] <= qpos) & (seg_sc[kr, :] == qseg)
                k, v = kv_ref[kr, k_cols], kv_ref[kr, v_cols]
                qs = [q_ref[qr, g * HP : (g + 1) * HP] for g in range(2)]
                dos = [do_ref[qr, g * HP : (g + 1) * HP] for g in range(2)]
                scores = [dot(k, q, ((1,), (1,))) * scale for q in qs]
                dps = [dot(v, do, ((1,), (1,))) for do in dos]
                dv, dk = dv_sc[kr, :], dk_sc[kr, :]
                dqs = []
                for g in range(2):
                    p = jnp.where(ok, jnp.exp(scores[g] - lse[g]), 0.0)
                    ds = (p * (dps[g] - delta[g])).astype(BF)
                    dv = dv + dot(p.astype(BF), dos[g])
                    dk = dk + dot(ds, qs[g])
                    dqs.append(dot(ds, k, ((0,), (0,))))
                dv_sc[kr, :], dk_sc[kr, :] = dv, dk
                for g in range(2):
                    dq_sc[g] += dqs[g]

            return 0

        lax.fori_loop(0, n_k, one_key, 0)
        for g in range(2):
            dq_ref[qr, g * HP : (g + 1) * HP] = (dq_sc[g] * scale).astype(BF)
        return 0

    lax.fori_loop(0, n_q, one_query, 0)
    dkv_ref[:, k_cols] = (dk_sc[...] * scale).astype(BF)
    dkv_ref[:, v_cols] = dv_sc[...].astype(BF)


def in_vmem(count):
    return [pl.BlockSpec(memory_space=pltpu.SMEM)] + [pl.BlockSpec(memory_space=pltpu.VMEM)] * count


def attn_cost(n_q, n_k, products):
    return pl.CostEstimate(
        flops=6 * products * n_q * n_k * 2 * HP, transcendentals=n_q * n_k * 2, bytes_accessed=(n_q + n_k) * HP * 16
    )


def attend(need, q, kv, qpos, qseg, kpos, kseg):
    first, kv = (2 * HP, q) if kv is None else (0, kv)
    n_q, n_k = q.shape[0], kv.shape[0]
    return pl.pallas_call(
        functools.partial(attn_fwd_kernel, first),
        out_shape=(jax.ShapeDtypeStruct((n_q, 2 * HP), BF), jax.ShapeDtypeStruct((n_q // BLK, 2, BLK), F32)),
        in_specs=in_vmem(6),
        out_specs=(pl.BlockSpec(memory_space=pltpu.VMEM),) * 2,
        scratch_shapes=[pltpu.VMEM((2, 1, BLK), F32)] * 2 + [pltpu.VMEM((2, HP, BLK), F32)] + [pltpu.VMEM((n_k, 1), F32)] * 2,
        compiler_params=pltpu.CompilerParams(vmem_limit_bytes=40 << 20),
        cost_estimate=attn_cost(n_q, n_k, 2),
        name="attn_fwd",
    )(need, q, kv, qpos, qseg, kpos, kseg)


def attend_back(need, q, kv, qpos, qseg, kpos, kseg, o, lse, do):
    joint = kv is None
    first, kv = (2 * HP, q) if joint else (0, kv)
    n_q, n_k = q.shape[0], kv.shape[0]
    shapes = [jax.ShapeDtypeStruct((n_q, 4 * HP), BF)] if joint else [jax.ShapeDtypeStruct((n, 2 * HP), BF) for n in (n_q, n_k)]
    return pl.pallas_call(
        functools.partial(attn_bwd_kernel, first),
        out_shape=shapes,
        in_specs=in_vmem(9),
        out_specs=[pl.BlockSpec(memory_space=pltpu.VMEM)] * len(shapes),
        scratch_shapes=[pltpu.VMEM((2, BLK, HP), F32)] + [pltpu.VMEM((n_k, HP), F32)] * 2 + [pltpu.VMEM((n_k, 1), F32)] * 2,
        compiler_params=pltpu.CompilerParams(vmem_limit_bytes=48 << 20),
        cost_estimate=attn_cost(n_q, n_k, 5),
        name="attn_bwd",
    )(need, q, kv, qpos, qseg, kpos, kseg, o, lse, do)


def whole(count):
    return [pl.BlockSpec(memory_space=pltpu.VMEM)] * count


def place_call(kernel, out_shape, ids, *values, name, scratch=()):
    moved = sum(v.size * v.dtype.itemsize for v in values)
    return pl.pallas_call(
        kernel,
        out_shape=out_shape,
        in_specs=[pl.BlockSpec(memory_space=pltpu.SMEM)] + whole(len(values)),
        out_specs=jax.tree.map(lambda _: pl.BlockSpec(memory_space=pltpu.VMEM), out_shape),
        scratch_shapes=scratch,
        compiler_params=pltpu.CompilerParams(vmem_limit_bytes=40 << 20),
        cost_estimate=pl.CostEstimate(flops=0, transcendentals=0, bytes_accessed=2 * moved),
        name=name,
    )(ids, *values)


def pack_qkv_kernel(ids, q_ref, k_ref, v_ref, small_ref, out_ref):
    rows = q_ref.shape[0]
    zero = jnp.zeros((rows, HP - HD), BF)
    for dev in range(KVH):
        slot = ids[0] ^ dev
        heads = [(q_ref, 2 * dev), (q_ref, 2 * dev + 1), (k_ref, dev), (v_ref, dev)]
        for i, (ref, head) in enumerate(heads):
            piece = ref[:, head * HD : (head + 1) * HD]
            out_ref[slot, :rows, i * HP : (i + 1) * HP] = jnp.concatenate([piece, zero], 1)
        out_ref[slot, rows:, :] = small_ref[...]


def pack_ff_kernel(ids, gate_ref, up_ref, out_ref):
    width = gate_ref.shape[1] // KVH
    for dev in range(KVH):
        slot = ids[0] ^ dev
        for i, ref in enumerate((gate_ref, up_ref)):
            out_ref[slot, :, i * width : (i + 1) * width] = ref[:, dev * width : (dev + 1) * width]


def head_kernel(n_blk, ids, *refs):
    got, x_refs = refs[:n_blk], refs[n_blk : n_blk + 2]
    w_ref, seg_ref, gain_ref, x_ref, n_ref, small_sc = refs[n_blk + 2 :]
    n_rows = w_ref.shape[0] // (2 * n_blk)
    for k, ref in enumerate(got):
        for core in range(2):
            at = pl.multiple_of((ids[0] ^ (core * n_blk + k)) * n_rows, 16)
            w_ref[pl.ds(at, n_rows), :] = ref[core, :n_rows, :]
            small_sc[core * n_blk + k] = ref[core, n_rows:, :]
    gains = [[], []]
    for dev in range(2 * n_blk):
        small = small_sc[ids[0] ^ dev]
        seg_ref[dev] = small
        small = small.astype(F32)
        for i in range(2):
            gains[i].append(small[i : i + 1, :n_rows])
    for i in range(2):
        gain_ref[i] = jnp.concatenate(gains[i], 1)
    tok = x_refs[0].shape[0]
    for i, ref in enumerate(x_refs):
        x = ref[...]
        x_ref[i * tok : (i + 1) * tok, :] = x
        x = x.astype(F32)
        factor = lax.rsqrt(jnp.mean(x * x, -1, keepdims=True) + EPS)
        n_ref[i * tok : (i + 1) * tok, :] = (x * factor * gain_ref[0]).astype(BF)


def unpack_ff_kernel(ids, in_ref, gate_ref, up_ref):
    n_head, n_slot, part, width = in_ref.shape
    for head in range(n_head):
        for slot in range(n_slot):
            at = pl.ds(pl.multiple_of(((ids[0] ^ slot) * n_head + head) * part, 16), part)
            gate_ref[at, :] = in_ref[head, slot, :, : width // 2]
            up_ref[at, :] = in_ref[head, slot, :, width // 2 :]


def chunk_heads(ids, count):
    if count == 7:
        return [(ids[1] + (i - 3), (ids[1] + (i - 3) >= 0) & (ids[1] + (i - 3) < 4)) for i in range(7)]
    return [(i, None) for i in range(count)]


def place_chunk(ok, body):
    if ok is None:
        body()
    else:
        pl.when(ok)(body)


def place_rows_kernel(ids, *refs):
    out_ref = refs[-1]
    part = refs[0].shape[0]
    for ref, (head, ok) in zip(refs[:-1], chunk_heads(ids, len(refs) - 1)):

        def body():
            out_ref[pl.ds(pl.multiple_of(head * part, 16), part), :] = ref[...].astype(F32)

        place_chunk(ok, body)


def place_columns_kernel(widths, count, ids, *refs):
    chunks, outs = refs[:count], refs[count:]
    n_slot, part = chunks[0].shape[:2]
    for ref, (head, ok) in zip(chunks, chunk_heads(ids, count)):

        def body():
            at = pl.ds(pl.multiple_of(head * part, 16), part)
            first = 0
            for out_ref, width in zip(outs, widths):
                for pair in range(0, n_slot, 2):
                    both = [ref[ids[0] ^ dev][:, first : first + width] for dev in (pair, pair + 1)]
                    out_ref[at, pair * width : (pair + 2) * width] = jnp.concatenate(both, 1).astype(F32)
                first += width

        place_chunk(ok, body)


def ff_kernel(n0, n1, c0, c1, gate_ref, up_ref, down_ref, hid_ref, dgu_ref, own_ref, other_ref):
    width = gate_ref.shape[1]
    for i, (n_ref, c_ref) in ((1, (n1, c1)), (0, (n0, c0))):
        n = n_ref[...]
        gate = dot(n, gate_ref[...])
        up = dot(n, up_ref[...])
        grad = dot(c_ref[...], down_ref[...], ((1,), (1,)))
        sigma = jax.nn.sigmoid(gate)
        silu = gate * sigma
        hid_ref[i] = (silu * up).astype(BF)
        grad_gate = (grad * up * sigma * (1.0 + gate * (1.0 - sigma))).astype(BF)
        grad_up = (grad * silu).astype(BF)
        dgu_ref[i, :, :width] = grad_gate
        dgu_ref[i, :, width:] = grad_up
        total = dot(grad_gate, gate_ref[...], ((1,), (1,))) + dot(grad_up, up_ref[...], ((1,), (1,)))
        if i == 0:
            own_ref[...] = total
        else:
            other_ref[...] = total.astype(BF)


def ff_call(n0, n1, c0, c1, gate_w, up_w, down_w):
    rows, width = n0.shape[0], gate_w.shape[1]
    return pl.pallas_call(
        ff_kernel,
        out_shape=(
            jax.ShapeDtypeStruct((2, rows, width), BF),
            jax.ShapeDtypeStruct((2, rows, 2 * width), BF),
            jax.ShapeDtypeStruct((rows, D), F32),
            jax.ShapeDtypeStruct((rows, D), BF),
        ),
        in_specs=whole(7),
        out_specs=tuple(whole(4)),
        compiler_params=pltpu.CompilerParams(vmem_limit_bytes=40 << 20),
        cost_estimate=pl.CostEstimate(
            flops=2 * 2 * rows * D * width * 5, transcendentals=2 * rows * width, bytes_accessed=12 << 20
        ),
        name="ff",
    )(n0, n1, c0, c1, gate_w, up_w, down_w)


def ff_weight_kernel(n_pairs, *refs):
    n_refs, c_refs = refs[: 2 * n_pairs], refs[2 * n_pairs : 4 * n_pairs]
    dgu_refs, hid_refs = refs[4 * n_pairs : 5 * n_pairs], refs[5 * n_pairs : 6 * n_pairs]
    ff_ref, down_ref = refs[6 * n_pairs :]
    over = ((0,), (0,))
    total_ff = total_down = None
    for i in range(2 * n_pairs):
        core, k = i // n_pairs, i % n_pairs
        one = dot(n_refs[i][...], dgu_refs[k][core], over)
        two = dot(hid_refs[k][core], c_refs[i][...], over)
        total_ff = one if total_ff is None else total_ff + one
        total_down = two if total_down is None else total_down + two
    n_head, n_dev, part, width = ff_ref.shape
    for dev in range(n_dev):
        for head in range(n_head):
            first = (dev * n_head + head) * part
            ff_ref[head, dev] = total_ff[first : first + part].astype(BF)
    down_ref[...] = total_down.astype(BF)


def ff_weight_call(n_list, c_list, dgu_list, hid_list, n_head, n_plane):
    n_pairs = len(dgu_list)
    rows, width2 = n_list[0].shape[0], dgu_list[0].shape[2]
    part = D // n_plane // n_head
    cols = 384
    steps = D // cols
    lanes = pl.BlockSpec((rows, cols), lambda j: (0, j))
    fixed = lambda v: pl.BlockSpec(v.shape, lambda j: (0, 0, 0), pipeline_mode=pl.Buffered(1))
    per_step = n_plane // steps
    return pl.pallas_call(
        functools.partial(ff_weight_kernel, n_pairs),
        grid=(steps,),
        out_shape=(
            jax.ShapeDtypeStruct((n_head, n_plane, part, width2), BF),
            jax.ShapeDtypeStruct((width2 // 2, D), BF),
        ),
        in_specs=[lanes] * (4 * n_pairs) + [fixed(v) for v in dgu_list] + [fixed(v) for v in hid_list],
        out_specs=(
            pl.BlockSpec((n_head, per_step, part, width2), lambda j: (0, j, 0, 0)),
            pl.BlockSpec((width2 // 2, cols), lambda j: (0, j)),
        ),
        compiler_params=pltpu.CompilerParams(vmem_limit_bytes=56 << 20),
        cost_estimate=pl.CostEstimate(
            flops=2 * 2 * n_pairs * rows * D * width2 * 3 // 2, transcendentals=0, bytes_accessed=24 << 20
        ),
        name="ff_weight",
    )(*n_list, *c_list, *dgu_list, *hid_list)


def simple_call(kernel, out_shape, values, name, flops):
    leaves = jax.tree.leaves(out_shape)
    moved = sum(v.size * v.dtype.itemsize for v in list(values) + leaves)
    return pl.pallas_call(
        kernel,
        out_shape=out_shape,
        in_specs=whole(len(values)),
        out_specs=jax.tree.map(lambda _: pl.BlockSpec(memory_space=pltpu.VMEM), out_shape),
        compiler_params=pltpu.CompilerParams(vmem_limit_bytes=52 << 20),
        cost_estimate=pl.CostEstimate(flops=flops, transcendentals=0, bytes_accessed=moved),
        name=name,
    )(*values)


def stack_project_kernel(*refs):
    weight, out_ref = refs[-2], refs[-1]
    rows = refs[0].shape[0]
    for i, ref in enumerate(refs[:-2]):
        out_ref[i * rows : (i + 1) * rows, :] = dot(ref[...], weight[...]).astype(BF)


def out_project_kernel(n_blk, *refs):
    o_refs, w_refs = refs[:n_blk], refs[n_blk : 3 * n_blk]
    x_ref, gain_ref, mid_ref, n_ref = refs[3 * n_blk :]
    total = x_ref[...].astype(F32)
    for core in range(2):
        for k in range(n_blk):
            o = o_refs[k][core]
            o = jnp.concatenate([o[:, :HD], o[:, HP : HP + HD]], 1)
            total = total + dot(o, w_refs[core * n_blk + k][...])
    mid_ref[...] = total
    factor = lax.rsqrt(jnp.mean(total * total, -1, keepdims=True) + EPS)
    n_ref[...] = (total * factor * gain_ref[...]).astype(BF)


def branch_kernel(n_blk, *refs):
    w_refs = refs[: 2 * n_blk]
    local_ref, got_refs = refs[2 * n_blk], refs[2 * n_blk + 1 : 3 * n_blk]
    mid_ref, cot_ref, gain_ref, grad_ref, branch_ref, do_ref = refs[3 * n_blk :]
    total = local_ref[...]
    for ref in got_refs:
        total = total + ref[...].astype(F32)
    mid = mid_ref[...]
    factor = lax.rsqrt(jnp.mean(mid * mid, -1, keepdims=True) + EPS)
    grad = cot_ref[...].astype(F32) + norm_back(total, gain_ref[...], mid * factor, factor)
    grad_ref[...] = grad
    branch = grad.astype(BF)
    branch_ref[...] = branch
    zero = jnp.zeros((branch.shape[0], HP - HD), BF)
    for core in range(2):
        for k in range(n_blk):
            do = dot(branch, w_refs[core * n_blk + k][...], ((1,), (1,))).astype(BF)
            do_ref[core, k] = jnp.concatenate([do[:, :HD], zero, do[:, HD:], zero], 1)


def back_project_kernel(transposed, *refs):
    weight, own_ref, other_ref = refs[-3], refs[-2], refs[-1]
    dims = ((1,), (1,)) if transposed else ((1,), (0,))
    n_blk, rows = own_ref.shape[:2]
    for core in (1, 0):
        for k in range(n_blk):
            at = (core * n_blk + k) * rows
            value = refs[0][at : at + rows, :] if len(refs) == 4 else refs[k][core]
            part = dot(value, weight[...], dims)
            if core:
                other_ref[k] = part.astype(BF)
            else:
                own_ref[k] = part


def out_weight_kernel(count, *refs):
    o_ref, b_refs, out_ref = refs[0], refs[1 : 1 + count], refs[-1]
    rows = b_refs[0].shape[0]
    total = None
    for i, ref in enumerate(b_refs):
        one = dot(o_ref[i * rows : (i + 1) * rows, :], ref[...], ((0,), (0,)))
        total = one if total is None else total + one
    out_ref[:HD, :] = total[:HD].astype(BF)
    out_ref[HD:, :] = total[HP : HP + HD].astype(BF)


def qkv_weight_kernel(n_refs_count, *refs):
    n_refs, grad_ref, out_ref = refs[:n_refs_count], refs[-2], refs[-1]
    rows = n_refs[0].shape[0]
    total = None
    for i, ref in enumerate(n_refs):
        one = dot(ref[...], grad_ref[i * rows : (i + 1) * rows, :], ((0,), (0,)))
        total = one if total is None else total + one
    total = jnp.concatenate([total[:, g * HP : g * HP + HD] for g in range(4)], 1)
    n_head, n_dev, part, _ = out_ref.shape
    for dev in range(n_dev):
        for head in range(n_head):
            first = (dev * n_head + head) * part
            out_ref[head, dev] = total[first : first + part].astype(BF)


def qkv_weight_call(n_list, dqkv, n_head, n_plane):
    rows = n_list[0].shape[0]
    part = D // n_plane // n_head
    cols = 384
    steps = D // cols
    return pl.pallas_call(
        functools.partial(qkv_weight_kernel, len(n_list)),
        grid=(steps,),
        out_shape=jax.ShapeDtypeStruct((n_head, n_plane, part, 4 * HD), BF),
        in_specs=[pl.BlockSpec((rows, cols), lambda j: (0, j))] * len(n_list)
        + [pl.BlockSpec(dqkv.shape, lambda j: (0, 0), pipeline_mode=pl.Buffered(1))],
        out_specs=pl.BlockSpec((n_head, n_plane // steps, part, 4 * HD), lambda j: (0, j, 0, 0)),
        compiler_params=pltpu.CompilerParams(vmem_limit_bytes=48 << 20),
        cost_estimate=pl.CostEstimate(
            flops=2 * len(n_list) * rows * D * 4 * HP * 2, transcendentals=0, bytes_accessed=12 << 20
        ),
        name="qkv_weight",
    )(*n_list, dqkv)


def after(value, *first):
    return lax.optimization_barrier((value,) + first)[0]


def swap(value, axis, mask):
    return lax.ppermute(value, axis, [(i, i ^ mask) for i in range(lax.axis_size(axis))])


class Stages:
    def __init__(self):
        self.last = ()

    def __call__(self, *trees):
        leaves, tree = jax.tree.flatten(trees)
        tied = lax.optimization_barrier(tuple(leaves) + self.last)
        self.last = (tied[0],)
        return jax.tree.unflatten(tree, tied[: len(leaves)])


def near(value):
    return swap(value, "blk", 1), swap(value, "blk", 2)


def far(one, two):
    half = one.shape[0] // 2
    return swap(one[:half], "blk", 2), swap(two[half:], "blk", 1)


def across(*values):
    return tuple(swap(v, "dp", 1) for v in values)


def chips(both):
    return [both[0]] + [swap(both[k], "blk", k) for k in range(1, len(both))]


def pair_up(mine, other):
    return [jnp.stack([mine[k], other[k]]) for k in range(mine.shape[0])]


def add_cores(own, other):
    return own + swap(other, "dp", 1).astype(F32)


def line_step(left, right):
    up = [(i, i + 1) for i in range(3)]
    return lax.ppermute(left, "head", up), lax.ppermute(right, "head", [(b, a) for a, b in up])


def rel_to_abs(value, reverse=False):
    n_blk = lax.axis_size("blk")
    mine = lax.axis_index("dp") * n_blk + lax.axis_index("blk")
    flat = value.reshape((2 * n_blk,) + value.shape[(1 if reverse else 2) :])
    out = jnp.stack([lax.dynamic_index_in_dim(flat, i ^ mine, 0, keepdims=False) for i in range(2 * n_blk)])
    return out.reshape((2, n_blk) + out.shape[1:]) if reverse else out


def per_device(
    activations,
    segments,
    cotangent,
    norm_gain_one,
    query_weight,
    key_weight,
    value_weight,
    output_weight,
    norm_gain_two,
    gate_weight,
    up_weight,
    down_weight,
):
    n_blk, n_head = lax.axis_size("blk"), lax.axis_size("head")
    n_plane = 2 * n_blk
    assert lax.axis_size("dp") == 2 and activations.shape[0] == 2 and n_plane == KVH
    sub = n_head // 4
    tok = activations.shape[2]
    span = tok * n_head
    own = 2 * tok
    rows = n_plane * own
    my_dp, my_blk, my_head = (lax.axis_index(name) for name in ("dp", "blk", "head"))
    my_seq, my_sub = my_head // sub, my_head % sub

    def routes(k):
        pairs = []
        for core in range(2):
            for head in range(n_head):
                seq_part, sub_part = head // sub, head % sub
                target = 2 * (k ^ (seq_part & 1)) + core
                pairs.append((core * n_head + head, (seq_part >> 1) * n_head + target * sub + sub_part))
        return pairs

    def to_plane(value):
        parts = []
        for k in range(2):
            piece = lax.dynamic_index_in_dim(value, k ^ (my_seq & 1), 0, keepdims=False)
            parts.append(lax.ppermute(piece, ("dp", "head"), routes(k)))
        return parts

    def from_plane(value):
        parts = []
        for k in range(2):
            back = [(b, a) for a, b in routes(k)]
            parts.append(lax.ppermute(value[k * tok : (k + 1) * tok], ("dp", "head"), back))
        odd = (my_seq & 1) == 1
        return jnp.stack([jnp.where(odd, parts[1], parts[0]), jnp.where(odd, parts[0], parts[1])])

    me = my_dp * n_blk + my_blk
    ids = jnp.stack([me, my_head]).astype(jnp.int32)
    n_rows = D // n_plane
    part = n_rows // n_head
    ff_here = FF // n_plane
    width = 4 * HP
    assert span % width == 0
    seg_rows = span // width
    small_rows = -(-(2 + 2 * seg_rows) // 16) * 16
    gain_row = lambda v: jnp.pad(v, (0, width - n_rows))[None]
    small = [gain_row(norm_gain_one), gain_row(norm_gain_two), segments[:, 0].astype(BF).reshape(2 * seg_rows, width)]
    small.append(jnp.zeros((small_rows - 2 - 2 * seg_rows, width), BF))
    small = jnp.concatenate(small)
    fence = Stages()
    join = jnp.concatenate
    share = n_rows // 4

    def pack_qkv(*values):
        shape = jax.ShapeDtypeStruct((n_plane, n_rows + small_rows, 4 * HP), BF)
        packed = place_call(pack_qkv_kernel, shape, ids, *values, name="pack_qkv")
        return packed.reshape((2, n_blk) + packed.shape[1:])

    def pack_ff(gate, up):
        cut = [lax.dynamic_slice_in_dim(w, my_seq * share, share, 0) for w in (gate, up)]
        shape = jax.ShapeDtypeStruct((n_plane, share, 2 * ff_here), BF)
        packed = place_call(pack_ff_kernel, shape, ids, *cut, name="pack_ff")
        return packed.reshape((2, n_blk) + packed.shape[1:])

    packed, near_out, act_low, cot_low, gate_low, up_low = fence(
        pack_qkv(query_weight, key_weight, value_weight, small),
        near(output_weight),
        activations,
        cotangent,
        gate_weight,
        up_weight,
    )
    both, act_low, cot_low, gate_low, up_low = fence(
        pair_up(packed[0], swap(packed[1], "dp", 1)), act_low, cot_low, gate_low, up_low
    )
    ff_packed = pack_ff(gate_low, up_low)
    got, x_parts, ff_both, cot_low = fence(
        chips(both), to_plane(act_low[:, 0]), pair_up(ff_packed[0], swap(ff_packed[1], "dp", 1)), cot_low
    )
    qkv_w, seg_all, gains, x_low, input_one = place_call(
        functools.partial(head_kernel, n_blk),
        (
            jax.ShapeDtypeStruct((D, width), BF),
            jax.ShapeDtypeStruct((n_plane, small_rows, width), BF),
            jax.ShapeDtypeStruct((2, 1, D), F32),
            jax.ShapeDtypeStruct((own, D), BF),
            jax.ShapeDtypeStruct((own, D), BF),
        ),
        ids,
        *got,
        *x_parts,
        name="head",
        scratch=[pltpu.VMEM((n_plane, small_rows, width), BF)],
    )
    gain_one, gain_two = gains[0, 0], gains[1, 0]
    seg_all = seg_all[:, 2 : 2 + 2 * seg_rows].reshape(2, n_blk, 2, span)
    seg_seq = lax.dynamic_index_in_dim(seg_all, my_seq & 1, 0, keepdims=False)
    seg_seq = lax.dynamic_index_in_dim(seg_seq, my_seq >> 1, 1, keepdims=False)
    chunks = seg_seq.astype(jnp.int32).reshape(n_blk * n_head, tok)

    def chunk_ids(sub_index):
        ids = []
        for core in range(2):
            for blk in range(n_blk):
                for k in range(2):
                    seq_part = 2 * (my_dp ^ core) + ((my_seq >> 1) ^ k)
                    ids.append((my_blk ^ blk) * n_head + seq_part * sub + sub_index)
        return ids

    def pos_seg(sub_index):
        ids = chunk_ids(sub_index)
        lane = jnp.arange(tok, dtype=jnp.int32)
        pos = jnp.concatenate([i * tok + lane for i in ids])
        seg = jnp.concatenate([lax.dynamic_index_in_dim(chunks, i, 0, keepdims=False) for i in ids])
        return pos, seg

    qpos, qseg = pos_seg(my_sub)
    if sub == 1:
        kpos, kseg = qpos, qseg
    else:
        every = [pos_seg(i) for i in range(sub)]
        kpos, kseg = (jnp.concatenate([e[i] for e in every]) for i in range(2))
    blocked = lambda v: v.reshape(-1, BLK)
    qb, qsb, kb, ksb = blocked(qpos), blocked(qseg), blocked(kpos), blocked(kseg)
    need = (
        (jnp.min(kb, 1)[None, :] <= jnp.max(qb, 1)[:, None])
        & (jnp.min(ksb, 1)[None, :] <= jnp.max(qsb, 1)[:, None])
        & (jnp.max(ksb, 1)[None, :] >= jnp.min(qsb, 1)[:, None])
    ).astype(jnp.int32)

    input_one, qkv_w, ff_both, cot_low = fence(input_one, qkv_w, ff_both, cot_low)
    near_one, cot, side_one = fence(near(input_one), to_plane(cot_low[:, 0]), across(input_one))
    far_one, more_one, cot = fence(far(*near_one), across(*near_one), join(cot))
    far_one = join(far_one)
    mine_one = [input_one, *near_one, far_one]
    all_one = fence(*mine_one, *side_one, *more_one, *across(far_one))

    def project_qkv(*values):
        shape = jax.ShapeDtypeStruct((rows, 4 * HP), BF)
        return simple_call(stack_project_kernel, shape, values, "project_qkv", 2 * rows * D * 4 * HP)

    ff_both = [after(v, all_one[-1]) for v in ff_both]
    qkv, ff_got, cot, near_out = fence(project_qkv(*all_one, qkv_w), chips(ff_both), cot, near_out)
    kv = ()
    if sub > 1:
        groups = [[s * sub + i for i in range(sub)] for s in range(4)]
        kv = (lax.all_gather(qkv[:, 2 * HP :], "head", axis=0, tiled=True, axis_index_groups=groups),)
    q_args = tuple(v.astype(F32).reshape(-1, 1, BLK) for v in (qpos, qseg, kpos, kseg))
    sharing = None if sub == 1 else [[s * sub + i for s in range(4)] for i in range(sub)]
    ff_all = jnp.stack(ff_got, 1).reshape(-1, 2 * ff_here)
    ff_all = lax.all_gather(ff_all, "head", axis=0, tiled=True, axis_index_groups=sharing)
    ff_all = ff_all.reshape(4, n_plane, share, 2 * ff_here)
    (o, lse), near_cot, far_out = fence(attend(need, qkv, *(kv or (None,)), *q_args), near(cot), far(*near_out))
    o_parts = o.reshape(2, n_blk, own, 2 * HP)
    mine_out = [output_weight, *near_out, join(far_out)]
    o_both, near_cot = fence(pair_up(o_parts[0], swap(o_parts[1], "dp", 1)), near_cot)
    o_got, side_out, near_cot = fence(chips(o_both), across(*mine_out), near_cot)
    all_out = [*mine_out, *side_out]

    def out_project(*values):
        shapes = (jax.ShapeDtypeStruct((own, D), F32), jax.ShapeDtypeStruct((own, D), BF))
        kernel = functools.partial(out_project_kernel, n_blk)
        return simple_call(kernel, shapes, values, "out_project", 2 * own * D * D)

    (x_mid, input_two), side_cot = fence(
        out_project(*o_got, *all_out, x_low, gain_two[None]), across(cot, *near_cot)
    )

    def unpack_ff(value):
        shapes = (jax.ShapeDtypeStruct((D, ff_here), BF),) * 2
        return place_call(unpack_ff_kernel, shapes, ids, value, name="unpack_ff")

    def ff_part(n_mine, n_side, c_mine, c_side):
        return ff_call(n_mine, n_side, c_mine, c_side, gate_w, up_w, down_weight)

    gate_w, up_w = unpack_ff(after(ff_all, input_two))
    side_two = across(input_two)
    near_two, part_0, near_cot, gate_w, up_w = fence(
        near(input_two), ff_part(input_two, side_two[0], cot, side_cot[0]), near_cot, gate_w, up_w
    )
    more_two = across(*near_two)
    far_two, far_cot, part_1, part_2 = fence(
        far(*near_two),
        far(*near_cot),
        ff_part(near_two[0], more_two[0], near_cot[0], side_cot[1]),
        ff_part(near_two[1], more_two[1], near_cot[1], side_cot[2]),
    )
    far_two, far_cot = join(far_two), join(far_cot)
    last_two, last_cot = across(far_two, far_cot)
    side_parts = across(part_0[3], part_1[3], part_2[3])
    part_3, side_parts = fence(ff_part(far_two, last_two, far_cot, last_cot), side_parts)
    parts = [part_0, part_1, part_2, part_3]
    side_parts = [*side_parts, *across(part_3[3])]
    hidden, grad_gu = [p[0] for p in parts], [p[1] for p in parts]
    all_two = [input_two, *near_two, far_two, *side_two, *more_two, last_two]
    all_cot = [cot, *near_cot, far_cot, *side_cot, last_cot]
    local_two = [p[2] + v.astype(F32) for p, v in zip(parts, side_parts)]
    local_0, sent_two = fence(local_two[0], [v.astype(BF) for v in local_two])
    got_two = chips(sent_two)[1:]

    contract = ((0,), (0,))

    def rel_parts(mine):
        return rel_to_abs(mine, True)

    def head_sum(sent):
        return lax.psum_scatter(sent, "head", scatter_dimension=0, tiled=True)

    def owned_rows(chunks):
        if n_head != 4:
            return chunks[0].reshape(-1, chunks[0].shape[-1]).astype(F32)
        shape = jax.ShapeDtypeStruct((4 * chunks[0].shape[0], chunks[0].shape[1]), F32)
        return place_call(place_rows_kernel, shape, ids, *chunks, name="place_rows")

    def owned_columns(chunks, widths):
        if n_head != 4:
            full = rel_to_abs(jnp.moveaxis(chunks[0], 0, 1).reshape((2, n_blk, n_head) + chunks[0].shape[2:]))
            full = full.reshape(n_plane, n_rows, -1).transpose(1, 0, 2).astype(F32)
            ends = [sum(widths[: i + 1]) for i in range(len(widths))]
            return [full[:, :, e - w : e].reshape(n_rows, -1) for e, w in zip(ends, widths)]
        shapes = [jax.ShapeDtypeStruct((n_rows, n_plane * w), F32) for w in widths]
        kernel = functools.partial(place_columns_kernel, widths, len(chunks))
        return place_call(kernel, shapes, ids, *chunks, name="place_columns")

    ff_sent, down_sent = ff_weight_call(all_two, all_cot, grad_gu, hidden, n_head, n_plane)
    got_two, ff_sent, down_sent = fence(got_two, ff_sent, down_sent)
    down_mine = head_sum(down_sent)
    ff_mine = head_sum(ff_sent.reshape(D, 2 * ff_here)).reshape(n_plane, part, 2 * ff_here)

    def branch(*values):
        shapes = (
            jax.ShapeDtypeStruct((own, D), F32),
            jax.ShapeDtypeStruct((own, D), BF),
            jax.ShapeDtypeStruct((2, n_blk, own, 2 * HP), BF),
        )
        kernel = functools.partial(branch_kernel, n_blk)
        return simple_call(kernel, shapes, values, "branch", 2 * own * D * D)

    grad_mid, grad_branch, grad_o = fence(*branch(*all_out, local_0, *got_two, x_mid, cot, gain_two[None]))
    (do_both,) = fence(pair_up(grad_o[0], swap(grad_o[1], "dp", 1)))
    do_got, down_mine, grad_branch = fence(chips(do_both), down_mine, grad_branch)
    grad_o = jnp.stack(do_got, 1).reshape(rows, 2 * HP)
    line = n_head == 4
    no_step = lambda *v: ()
    step = line_step if line else no_step
    back = attend_back(need, qkv, *(kv or (None,)), *q_args, o, lse, grad_o)
    line_0 = step(down_mine, down_mine)
    dqkv, near_branch = fence(back, near(grad_branch))
    if sub > 1:
        dkv = lax.psum_scatter(dqkv[1], "head", scatter_dimension=0, tiled=True, axis_index_groups=groups)
        dqkv = [join([dqkv[0], dkv], 1)]
    dqkv = dqkv[0]

    def back_project(transposed, *values):
        shapes = tuple(jax.ShapeDtypeStruct((n_blk, own, D), t) for t in (F32, BF))
        kernel = functools.partial(back_project_kernel, transposed)
        return simple_call(kernel, shapes, values, "back_project", 2 * rows * D * values[-1].size // D)

    qkv_grad, far_branch, dqkv, line_0 = fence(
        qkv_weight_call(all_one, dqkv, n_head, n_plane), far(*near_branch), dqkv, line_0
    )
    qkv_mine = head_sum(qkv_grad.reshape(D, 4 * HD)).reshape(n_plane, part, 4 * HD)
    mine_branch = [grad_branch, *near_branch, join(far_branch)]
    (one_own, one_other), line_1, side_branch, ff_mine = fence(
        back_project(True, dqkv, qkv_w), step(*line_0), across(*mine_branch), ff_mine
    )

    def out_weights(*values):
        rows_per = values[1].shape[0]
        lanes = pl.BlockSpec((rows_per, 384), lambda j: (0, j))
        return pl.pallas_call(
            functools.partial(out_weight_kernel, n_plane),
            grid=(D // 384,),
            out_shape=jax.ShapeDtypeStruct((2 * HD, D), BF),
            in_specs=[pl.BlockSpec(values[0].shape, lambda j: (0, 0), pipeline_mode=pl.Buffered(1))] + [lanes] * n_plane,
            out_specs=pl.BlockSpec((2 * HD, 384), lambda j: (0, j)),
            compiler_params=pltpu.CompilerParams(vmem_limit_bytes=48 << 20),
            cost_estimate=pl.CostEstimate(flops=4 * rows * D * 2 * HP, transcendentals=0, bytes_accessed=9 << 20),
            name="out_weight",
        )(*values)

    ff_rel = rel_parts(ff_mine)
    one_side, out_grad, one_own, ff_both, line_1, hidden = fence(
        swap(one_other, "dp", 1),
        out_weights(o, *mine_branch, *side_branch),
        one_own,
        pair_up(ff_rel[0], swap(ff_rel[1], "dp", 1)),
        line_1,
        hidden,
    )
    out_mine = head_sum(out_grad)
    local_one = [one_own[k] + one_side[k].astype(F32) for k in range(n_blk)]
    ff_got, local_0, sent_one, line_2, qkv_mine = fence(
        chips(ff_both), local_one[0], [v.astype(BF) for v in local_one], step(*line_1), qkv_mine
    )
    ff_rows = jnp.stack(ff_got, 1).reshape(ff_mine.shape)
    qkv_rel = rel_parts(qkv_mine)
    qkv_both = pair_up(qkv_rel[0], swap(qkv_rel[1], "dp", 1))
    ff_0 = step(ff_rows, ff_rows)
    out_own, out_other = back_project(False, *hidden, down_weight)
    out_side = swap(out_other, "dp", 1)
    local_out = [out_own[k] + out_side[k].astype(F32) for k in range(n_blk)]
    ff_0, qkv_rows, local_out_0, sent_out, sent_one, local_0, out_mine = fence(
        ff_0, chips(qkv_both), local_out[0], [v.astype(BF) for v in local_out], sent_one, local_0, out_mine
    )
    got_one, ff_1 = fence(chips(sent_one)[1:], step(*ff_0))
    normed, factor = normalize(x_low.astype(F32))
    grad_in_one = local_0 + sum(g.astype(F32) for g in got_one)
    grad_input = (grad_mid + norm_back(grad_in_one, gain_one, normed, factor)).astype(BF)
    local_0 = local_out_0
    got_out = chips([after(v, *ff_1) if line else v for v in sent_out])[1:]
    late = join([jnp.stack(qkv_rows, 1).reshape(-1, 4 * HD), out_mine.reshape(-1, 4 * HD)])
    late = lax.all_gather(late, "head", axis=0)
    if line:
        down_chunks = [line_2[0], line_1[0], line_0[0], down_mine, line_0[1], line_1[1], line_2[1]]
        grad_down = owned_rows(down_chunks)
    else:
        grad_down = owned_rows([lax.all_gather(down_mine, "head", axis=0)])
    got_out, ff_2, grad_input = fence(got_out, step(*ff_1), grad_input)
    block_out = (x_mid + local_0 + sum(g.astype(F32) for g in got_out)).astype(BF)
    block_out, grad_input = from_plane(block_out), from_plane(grad_input)
    late_qkv = late[:, : n_plane * part].reshape(n_head, n_plane, part, 4 * HD)
    late_out = late[:, n_plane * part :].reshape(n_head, part, D)
    each = lambda v: [v[i] for i in range(4)] if line else [v]
    if line:
        ff_chunks = [ff_2[0], ff_1[0], ff_0[0], ff_rows, ff_0[1], ff_1[1], ff_2[1]]
    else:
        ff_chunks = [lax.all_gather(ff_rows, "head", axis=0)]
    grad_gate_w, grad_up_w = owned_columns(ff_chunks, (ff_here, ff_here))
    grad_query, grad_key, grad_value = owned_columns(each(late_qkv), (2 * HD, HD, HD))
    grad_out = owned_rows(each(late_out))

    def gain_grad(gain, *pairs):
        return sum(jnp.sum(w.astype(F32) * g, -1) for w, g in pairs) / gain.astype(F32)

    grad_gain_one = gain_grad(
        norm_gain_one, (query_weight, grad_query), (key_weight, grad_key), (value_weight, grad_value)
    )
    grad_gain_two = gain_grad(norm_gain_two, (gate_weight, grad_gate_w), (up_weight, grad_up_w))
    return (
        block_out[:, None],
        grad_input[:, None],
        grad_gain_one,
        grad_query,
        grad_key,
        grad_value,
        grad_out,
        grad_gain_two,
        grad_gate_w,
        grad_up_w,
        grad_down,
    )


def solution(mesh):
    tokens = P(None, "dp", ("blk", "head"), None)
    vector = P(("dp", "blk"))
    matrix = P(("dp", "blk"), None)
    return jax.shard_map(
        per_device,
        mesh=mesh,
        in_specs=(
            tokens,
            P(None, "dp", "blk"),
            tokens,
            vector,
            matrix,
            matrix,
            matrix,
            matrix,
            vector,
            matrix,
            matrix,
            matrix,
        ),
        out_specs=(tokens, tokens, vector, matrix, matrix, matrix, matrix, vector, matrix, matrix, matrix),
        check_vma=False,
    )
```

time: 843 us -> 596 us (0.71)
  Pallas kernels: 42.2 us -> 135 us
  other arithmetic: 130 us -> 39.1 us
  matrix products: 87.1 us -> 0 us
  local copies, waits for them, and re-layouts: 133 us -> 54.3 us
  waiting for transfers between devices: 306 us -> 231 us
  blocking collectives: 41.7 us -> 0 us
  starting transfers between devices: 78.8 us -> 111 us
    ppermute x60 -> x79, waiting for transfers between devices: 248 us -> 121 us  [swap(): lax.ppermute(value, axis, [(i, i ^ mask) for i in range(lax.axis_size(axi...]
    pallas_call x2 -> x22, Pallas kernels: 42.2 us -> 135 us  [the longest x5 37.7 us: simple_call(): pl.pallas_call(kernel, out_shape=out_shape, in_specs=whole(len(values)),...]
    dot_general x15 -> x0, matrix products: 87.1 us -> none  [dot(): lax.dot_general(left, right, (dims, ((), ())), preferred_element_type=F32)]
    another operation x33 -> x27, other arithmetic: 84.3 us -> 8.04 us  [the longest x22 6.59 us: pair_up(): return [jnp.stack([mine[k], other[k]]) for k in range(mine.shape[0])]]
    all_gather x1 -> x0, blocking collectives: 41.7 us -> none  [owned_rows(): lax.all_gather(lax.psum_scatter(grad.astype(BF), 'head', scatter_dimensio...]
    ppermute x0 -> x12, waiting for transfers between devices: none -> 41.3 us  [the longest x6 30.8 us: line_step(): lax.ppermute(left, 'head', up)]
    ppermute x0 -> x12, starting transfers between devices: none -> 35.2 us  [the longest x6 18.3 us: line_step(): lax.ppermute(left, 'head', up)]
    all_gather x3 -> x2, waiting for transfers between devices: 29.3 us -> 7.57 us  [the longest x1 7.57 us: per_device(): lax.all_gather(ff_all, 'head', axis=0, tiled=True, axis_index_groups=shar...]
  transfers between devices with their start and end apart: 75 -> 105, of which waited for: 33 -> 39; matrix products, arithmetic and copies ran while one was open for 35% -> 9% of each run, Pallas kernels for 5% -> 22%
where the time goes in v2:
time: 596 us; the launch traced here: 587 us
  waiting for transfers between devices  231 us (39%)
  Pallas kernels  135 us (23%)
  starting transfers between devices  111 us (19%)
  local copies, waits for them, and re-layouts  54.3 us (9%)
  other arithmetic  39.1 us (7%)
  between operations  16.7 us (3%)
    ppermute x79, waiting for transfers between devices, swap(): lax.ppermute(value, axis, [(i, i ^ mask) for i in range(lax.axis_size(axi...  121 us
    ppermute x79, starting transfers between devices, swap(): lax.ppermute(value, axis, [(i, i ^ mask) for i in range(lax.axis_size(axi...  60.9 us
    pallas_call x5, Pallas kernels, simple_call(): pl.pallas_call(kernel, out_shape=out_shape, in_specs=whole(len(values)),...  37.7 us
    unnamed x236, local copies, waits for them, and re-layouts  33.8 us
    ppermute x4, waiting for transfers between devices, to_plane(): parts.append(lax.ppermute(piece, ('dp', 'head'), routes(k)))  31.7 us
    ppermute x6, waiting for transfers between devices, line_step(): lax.ppermute(left, 'head', up)  30.8 us
    pallas_call x4, Pallas kernels, ff_call(): pl.pallas_call(ff_kernel, out_shape=(jax.ShapeDtypeStruct((2, rows, width...  21.5 us
    ppermute x4, waiting for transfers between devices, from_plane(): lax.ppermute(value[k * tok:(k + 1) * tok], ('dp', 'head'), back)  19.6 us
  transfers between devices with their start and end apart: 105, of which 39 were waited for; matrix products, arithmetic and copies ran while one was open for 9% of the time, Pallas kernels for 22%

profile of v2, /device:TPU:8, one launch (start us, length us, event | category | flops | bytes accessed | tf_op | source)
XLA Modules:
  0.0 587.4 jit_solution(7482816693845834148)
XLA Ops:
  16.9 5.7 collective-permute-done.refs_5_.refs_1_
  25.2 2.3 collective-permute-done.2
  35.5 3.5 collective-permute-start.6
  42.0 14.6 %collective-permute-done.6.refs_4_ = bf16[128,1536]{1,0:T(8,128)(2,1)S(1)} collective-permute-done((bf16[128,1536]{1,0:T(8,128)(2,1)S(1)}, bf16[128,1536]{1,0:T(8,128)(2,1)S(1)}, u32[]{:S(2)}, u32[]{:S(2)}) %collective-permute-start.6) | collective-permute-done | bytes 393248 | tf_op jit(solution)/shard_map/ppermute | solution.py:614
  60.1 4.4 collective-permute-start.11
  64.7 17.1 %collective-permute-done.11 = bf16[128,1536]{1,0:T(8,128)(2,1)S(1)} collective-permute-done((bf16[128,1536]{1,0:T(8,128)(2,1)S(1)}, bf16[128,1536]{1,0:T(8,128)(2,1)S(1)}, u32[]{:S(2)}, u32[]{:S(2)}) %collective-permute-start.11) | collective-permute-done | bytes 393248 | tf_op jit(solution)/shard_map/ppermute | solution.py:614
  85.5 9.0 %collective-permute-done.14 = bf16[128,1536]{1,0:T(8,128)(2,1)S(1)} collective-permute-done((bf16[128,1536]{1,0:T(8,128)(2,1)S(1)}, bf16[128,1536]{1,0:T(8,128)(2,1)S(1)}, u32[]{:S(2)}, u32[]{:S(2)}) %collective-permute-start.14) | collective-permute-done | bytes 393248 | tf_op jit(solution)/shard_map/ppermute | solution.py:524
  96.7 2.5 collective-permute-done.18.refs_7_
  103.8 7.6 %project_qkv.1.q_ref.kv_ref = bf16[2048,512]{1,0:T(8,128)(2,1)} custom-call(bf16[256,1536]{1,0:T(8,128)(2,1)S(1)} %copy-done.44, bf16[256,1536]{1,0:T(8,128)(2,1)S(1)} %collective-permute-done.9.refs_1_, bf16[256,1536]{1,0:T(8,128)(2,1)} %copy-done.32, bf16[256,1536]{1,0:T(8,128)(2,1)} %constant_dynamic-update-slice_fusion.2.refs_3_, ...), custom_call_target="tpu_custom_call" | custom-call | flops 3221225472 | bytes 9961472 | tf_op jit(solution)/shard_map/project_qkv/pallas_call | solution.py:406
  118.9 13.0 %attn_fwd.1 = (bf16[2048,256]{1,0:T(8,128)(2,1)S(1)}, f32[8,2,256]{2,1,0:T(2,128)S(1)}) custom-call(s32[8,8]{1,0:T(8,128)S(1)} %and_convert_fusion.need, bf16[2048,512]{1,0:T(8,128)(2,1)S(1)} %copy-done.71, bf16[2048,512]{1,0:T(8,128)(2,1)S(1)} %copy-done.71, f32[8,1,256]{2,1,0:T(1,128)S(1)} %bitcast.191, f32[8,1,256]{2,1,0:T(1,128)S(1)} %bitcast.195, ...), custom_call_target="tpu_custom_call" | custom-call | flops 12884901888 | bytes 8388608 | tf_op jit(solution)/shard_map/attn_fwd/pallas_call | solution.py:169
  132.0 7.2 %collective-permute-done.24 = bf16[96,1536]{1,0:T(8,128)(2,1)S(1)} collective-permute-done((bf16[96,1536]{1,0:T(8,128)(2,1)S(1)}, bf16[96,1536]{1,0:T(8,128)(2,1)S(1)}, u32[]{:S(2)}, u32[]{:S(2)}) %collective-permute-start.24) | collective-permute-done | bytes 294944 | tf_op jit(solution)/shard_map/ppermute | solution.py:524
  140.4 2.3 collective-permute-done.26
  146.5 5.6 collective-permute-done.27.refs_1_
  152.1 5.7 collective-permute-done.29.refs_3_
  158.4 5.8 out_project.1
  168.5 7.6 %all-gather.4.cloned.1.call-done = bf16[1536,1024]{1,0:T(8,128)(2,1)} async-done(((bf16[384,1024]{1,0:T(8,128)(2,1)}), bf16[1536,1024]{1,0:T(8,128)(2,1)}) %all-gather.4.cloned.1.call-update) | async-done | bytes 3145744 | tf_op jit(solution)/shard_map/all_gather | solution.py:739
  181.9 4.7 ff.4
  195.0 5.8 ff.5
  202.6 6.3 %ff.6 = (bf16[2,256,512]{2,1,0:T(8,128)(2,1)S(1)}, bf16[2,256,1024]{2,1,0:T(8,128)(2,1)S(1)}, f32[256,1536]{1,0:T(8,128)S(1)}, bf16[256,1536]{1,0:T(8,128)(2,1)S(1)}) custom-call(bf16[256,1536]{1,0:T(8,128)(2,1)} %collective-permute-done.38.n0.refs_2_, bf16[256,1536]{1,0:T(8,128)(2,1)S(1)} %collective-permute-done.45.n1.refs_6_, ...), custom_call_target="tpu_custom_call" | custom-call | flops 4026531840 | bytes 12582912 | tf_op jit(solution)/shard_map/ff/pallas_call | solution.py:336
  214.7 4.7 ff.7
  225.8 16.8 %ff_weight.1 = (bf16[4,8,48,1024]{3,2,1,0:T(8,128)(2,1)}, bf16[512,1536]{1,0:T(8,128)(2,1)}) custom-call(bf16[256,1536]{1,0:T(8,128)(2,1)} %get-tuple-element.356.n0.refs_0_, bf16[256,1536]{1,0:T(8,128)(2,1)} %collective-permute-done.37.n0.refs_1_, bf16[256,1536]{1,0:T(8,128)(2,1)} %collective-permute-done.38.n0.refs_2_, bf16[256,1536]{1,0:T(8,128)(2,1)} %copy-done.38, ...), custom_call_target="tpu_custom_call" | custom-call | flops 9663676416 | bytes 25165824 | tf_op jit(solution)/shard_map/ff_weight/pallas_call | solution.py:383
  242.7 17.4 %collective-permute-done.53.refs_10_ = bf16[256,1536]{1,0:T(8,128)(2,1)} collective-permute-done((bf16[256,1536]{1,0:T(8,128)(2,1)S(1)}, bf16[256,1536]{1,0:T(8,128)(2,1)}, u32[]{:S(2)}, u32[]{:S(2)}) %collective-permute-start.53) | collective-permute-done | bytes 786464 | tf_op jit(solution)/shard_map/ppermute | solution.py:524
  260.6 7.3 %branch.1 = (f32[256,1536]{1,0:T(8,128)}, bf16[256,1536]{1,0:T(8,128)(2,1)}, bf16[2,4,256,256]{3,2,1,0:T(8,128)(2,1)}) custom-call(bf16[192,1536]{1,0:T(8,128)(2,1)S(1)} %copy-done.8, bf16[192,1536]{1,0:T(8,128)(2,1)S(1)} %copy-done.3, bf16[192,1536]{1,0:T(8,128)(2,1)S(1)} %copy-done.5, bf16[192,1536]{1,0:T(8,128)(2,1)} %copy-done.87, ...), custom_call_target="tpu_custom_call" | custom-call | flops 1207959552 | bytes 14424064 | tf_op jit(solution)/shard_map/branch/pallas_call | solution.py:406
  274.7 5.7 collective-permute-done.56
  280.4 5.0 collective-permute-done.57
  285.4 9.0 %reduce-scatter.5.cloned.1.call-done.refs_3_ = bf16[128,1536]{1,0:T(8,128)(2,1)} async-done(((bf16[512,1536]{1,0:T(8,128)(2,1)}), bf16[128,1536]{1,0:T(8,128)(2,1)}) %reduce-scatter.5.cloned.1.call-update) | async-done | bytes 393232 | tf_op jit(solution)/shard_map/reduce_scatter | solution.py:795
  297.4 3.5 collective-permute-start.63
  300.8 2.4 collective-permute-start.64
  304.9 17.2 %attn_bwd.1.refs_8_.refs_0_ = bf16[2048,512]{1,0:T(8,128)(2,1)S(1)} custom-call(s32[8,8]{1,0:T(8,128)S(1)} %and_convert_fusion.need, bf16[2048,512]{1,0:T(8,128)(2,1)} %project_qkv.1.q_ref.kv_ref, bf16[2048,512]{1,0:T(8,128)(2,1)} %project_qkv.1.q_ref.kv_ref, f32[8,1,256]{2,1,0:T(1,128)S(1)} %bitcast.193, f32[8,1,256]{2,1,0:T(1,128)S(1)} %bitcast.197, ...), custom_call_target="tpu_custom_call" | custom-call | flops 32212254720 | bytes 8388608 | tf_op jit(solution)/shard_map/attn_bwd/pallas_call | solution.py:186
  325.1 7.4 %qkv_weight.1 = bf16[4,8,48,384]{3,2,1,0:T(8,128)(2,1)} custom-call(bf16[256,1536]{1,0:T(8,128)(2,1)S(1)} %copy-done.45, bf16[256,1536]{1,0:T(8,128)(2,1)S(1)} %copy-done.31, bf16[256,1536]{1,0:T(8,128)(2,1)S(1)} %copy-done.33, bf16[256,1536]{1,0:T(8,128)(2,1)} %constant_dynamic-update-slice_fusion.2.refs_3_, bf16[256,1536]{1,0:T(8,128)(2,1)S(1)} %copy-done.47, ...), custom_call_target="tpu_custom_call" | custom-call | flops 6442450944 | bytes 12582912 | tf_op jit(solution)/shard_map/qkv_weight/pallas_call | solution.py:504
  335.6 3.5 collective-permute-start.65
  339.1 2.4 collective-permute-start.66
  341.5 8.6 %back_project.2 = (f32[4,256,1536]{2,1,0:T(8,128)}, bf16[4,256,1536]{2,1,0:T(8,128)(2,1)}) custom-call(bf16[2048,512]{1,0:T(8,128)(2,1)} %copy-done.72, bf16[1536,512]{1,0:T(8,128)(2,1)S(1)} %copy-done.42), custom_call_target="tpu_custom_call" | custom-call | flops 3221225472 | bytes 13107200 | tf_op jit(solution)/shard_map/back_project/pallas_call | solution.py:406
  350.1 15.2 %collective-permute-done.65.refs_1_ = bf16[128,1536]{1,0:T(8,128)(2,1)S(1)} collective-permute-done((bf16[128,1536]{1,0:T(8,128)(2,1)S(1)}, bf16[128,1536]{1,0:T(8,128)(2,1)S(1)}, u32[]{:S(2)}, u32[]{:S(2)}) %collective-permute-start.65) | collective-permute-done | bytes 393248 | tf_op jit(solution)/shard_map/ppermute | solution.py:565
  365.3 5.6 collective-permute-done.66.refs_5_
  373.3 2.0 constant_dynamic-slice_fusion.8
  380.1 5.7 out_weight.1
  389.9 8.4 %back_project.3 = (f32[4,256,1536]{2,1,0:T(8,128)}, bf16[4,256,1536]{2,1,0:T(8,128)(2,1)}) custom-call(bf16[2,256,512]{2,1,0:T(8,128)(2,1)S(1)} %copy-done.78, bf16[2,256,512]{2,1,0:T(8,128)(2,1)S(1)} %copy-done.80, bf16[2,256,512]{2,1,0:T(8,128)(2,1)S(1)} %copy-done.82, bf16[2,256,512]{2,1,0:T(8,128)(2,1)} %copy-done.83, bf16[512,1536]{1,0:T(8,128)(2,1)} %refs_4_.3), custom_call_target="tpu_custom_call" | custom-call | flops 3221225472 | bytes 13107200 | tf_op jit(solution)/shard_map/back_project/pallas_call | solution.py:406
  399.8 2.0 collective-permute-start.75
  401.9 2.7 collective-permute-start.76
  406.1 2.3 collective-permute-start.77
  408.5 4.6 fusion.10
  414.3 3.7 collective-permute-done.77.refs_6_
  419.4 2.9 collective-permute-start.78
  422.3 3.0 collective-permute-start.79
  429.7 6.3 %fusion.13 = (bf16[256,1536]{1,0:T(8,128)(2,1)}, bf16[256,1536]{1,0:T(8,128)(2,1)}, bf16[256,1536]{1,0:T(8,128)(2,1)}, f32[256,1536]{1,0:T(8,128)}) fusion(f32[4,256,1536]{2,1,0:T(8,128)} %get-tuple-element.476, bf16[4,256,1536]{2,1,0:T(8,128)(2,1)} %collective-permute-done.84), kind=kLoop, calls=%fused_computation.34 | loop fusion | flops 4325376 | bytes 13369344 | tf_op jit(solution)/shard_map/convert_element_type | solution.py:892
  436.1 14.5 %collective-permute-done.78.refs_2_ = bf16[8,48,1024]{2,1,0:T(8,128)(2,1)S(1)} collective-permute-done((bf16[8,48,1024]{2,1,0:T(8,128)(2,1)S(1)}, bf16[8,48,1024]{2,1,0:T(8,128)(2,1)S(1)}, u32[]{:S(2)}, u32[]{:S(2)}) %collective-permute-start.78) | collective-permute-done | bytes 786464 | tf_op jit(solution)/shard_map/ppermute | solution.py:565
  455.3 3.4 collective-permute-start.88
  458.6 3.3 collective-permute-start.89
  468.2 2.4 place_rows.3
  473.6 15.9 %collective-permute-done.86 = bf16[256,1536]{1,0:T(8,128)(2,1)} collective-permute-done((bf16[256,1536]{1,0:T(8,128)(2,1)}, bf16[256,1536]{1,0:T(8,128)(2,1)}, u32[]{:S(2)}, u32[]{:S(2)}) %collective-permute-start.86) | collective-permute-done | bytes 786464 | tf_op jit(solution)/shard_map/ppermute | solution.py:524
  489.5 2.4 collective-permute-start.93
  492.0 3.5 collective-permute-start.94
  499.0 2.9 fusion.2
  502.1 2.6 fusion.6
  504.7 11.5 %collective-permute-done.90 = bf16[256,1536]{1,0:T(8,128)(2,1)S(1)} collective-permute-done((bf16[256,1536]{1,0:T(8,128)(2,1)}, bf16[256,1536]{1,0:T(8,128)(2,1)S(1)}, u32[]{:S(2)}, u32[]{:S(2)}) %collective-permute-start.90) | collective-permute-done | bytes 786464 | tf_op jit(solution)/shard_map/ppermute | solution.py:524
  516.2 14.5 %collective-permute-done.91 = bf16[256,1536]{1,0:T(8,128)(2,1)S(1)} collective-permute-done((bf16[256,1536]{1,0:T(8,128)(2,1)}, bf16[256,1536]{1,0:T(8,128)(2,1)S(1)}, u32[]{:S(2)}, u32[]{:S(2)}) %collective-permute-start.91) | collective-permute-done | bytes 786464 | tf_op jit(solution)/shard_map/ppermute | solution.py:524
  531.4 4.0 collective-permute-start.96
  535.6 2.3 collective-permute-start.98
  537.9 4.8 place_columns.3
  542.6 2.5 multiply_reduce_fusion.1
  547.2 12.2 %collective-permute-done.96 = bf16[128,1536]{1,0:T(8,128)(2,1)S(1)} collective-permute-done((bf16[128,1536]{1,0:T(8,128)(2,1)S(1)}, bf16[128,1536]{1,0:T(8,128)(2,1)S(1)}, u32[]{:S(2)}, u32[]{:S(2)}) %collective-permute-start.96) | collective-permute-done | bytes 393248 | tf_op jit(solution)/shard_map/ppermute | solution.py:621
  560.4 7.4 %collective-permute-done.98 = bf16[128,1536]{1,0:T(8,128)(2,1)S(1)} collective-permute-done((bf16[128,1536]{1,0:T(8,128)(2,1)S(1)}, bf16[128,1536]{1,0:T(8,128)(2,1)S(1)}, u32[]{:S(2)}, u32[]{:S(2)}) %collective-permute-start.98) | collective-permute-done | bytes 393248 | tf_op jit(solution)/shard_map/ppermute | solution.py:621
  571.4 3.3 place_columns.2
  (549 shorter events, 151.5 us)
Async XLA Ops:
  7.2 168.9 %all-gather.4.cloned.1.call-start = ((), (), s32[]{:S(2)}) async-start(), calls=%async_computation.4 | async-start | bytes 3932160 | tf_op jit(solution)/shard_map/all_gather | solution.py:739
  7.2 15.3 %collective-permute-start = (bf16[192,1536]{1,0:T(8,128)(2,1)}, bf16[192,1536]{1,0:T(8,128)(2,1)S(1)}, u32[]{:S(2)}, u32[]{:S(2)}) collective-permute-start(bf16[192,1536]{1,0:T(8,128)(2,1)} %refs_0_.1), channel_id=1, source_target_pairs={{0,4},{4,0},{8,12},{12,8},{1,5},{5,1},{9,13},{13,9},{2,6},{6,2},{1... | collective-permute-start | bytes 1769480 | tf_op jit(solution)/shard_map/ppermute | solution.py:524
  8.8 15.0 %collective-permute-start.1 = (bf16[192,1536]{1,0:T(8,128)(2,1)}, bf16[192,1536]{1,0:T(8,128)(2,1)S(1)}, u32[]{:S(2)}, u32[]{:S(2)}) collective-permute-start(bf16[192,1536]{1,0:T(8,128)(2,1)} %refs_0_.1), channel_id=1, source_target_pairs={{0,8},{4,12},{8,0},{12,4},{1,9},{5,13},{9,1},{13,5},{2,10},{6,14},... | collective-permute-start | bytes 1769480 | tf_op jit(solution)/shard_map/ppermute | solution.py:524
  29.0 27.5 %collective-permute-start.3 = (bf16[2,208,512]{2,1,0:T(8,128)(2,1)S(1)}, bf16[2,208,512]{2,1,0:T(8,128)(2,1)S(1)}, u32[]{:S(2)}, u32[]{:S(2)}) collective-permute-start(bf16[2,208,512]{2,1,0:T(8,128)(2,1)S(1)} %get-tuple-element.271), channel_id=1, source_target_pairs={{0,4},{4,0},{8,12},{12,8},{1,5},{5,1},{9,13},{13,9},{2,6},{6,2},{1... | collective-permute-start | bytes 1277960 | tf_op jit(solution)/shard_map/ppermute | solution.py:524
  29.6 27.0 %collective-permute-start.4 = (bf16[2,208,512]{2,1,0:T(8,128)(2,1)S(1)}, bf16[2,208,512]{2,1,0:T(8,128)(2,1)S(1)}, u32[]{:S(2)}, u32[]{:S(2)}) collective-permute-start(bf16[2,208,512]{2,1,0:T(8,128)(2,1)S(1)} %get-tuple-element.272), channel_id=1, source_target_pairs={{0,8},{4,12},{8,0},{12,4},{1,9},{5,13},{9,1},{13,5},{2,10},{6,14},... | collective-permute-start | bytes 1277960 | tf_op jit(solution)/shard_map/ppermute | solution.py:524
  31.1 25.4 %collective-permute-start.5 = (bf16[2,208,512]{2,1,0:T(8,128)(2,1)S(1)}, bf16[2,208,512]{2,1,0:T(8,128)(2,1)S(1)}, u32[]{:S(2)}, u32[]{:S(2)}) collective-permute-start(bf16[2,208,512]{2,1,0:T(8,128)(2,1)S(1)} %get-tuple-element.273), channel_id=1, source_target_pairs={{0,12},{4,8},{8,4},{12,0},{1,13},{5,9},{9,5},{13,1},{2,14},{6,10},... | collective-permute-start | bytes 1277960 | tf_op jit(solution)/shard_map/ppermute | solution.py:524
  35.5 21.0 %collective-permute-start.6 = (bf16[128,1536]{1,0:T(8,128)(2,1)S(1)}, bf16[128,1536]{1,0:T(8,128)(2,1)S(1)}, u32[]{:S(2)}, u32[]{:S(2)}) collective-permute-start(bf16[128,1536]{1,0:T(8,128)(2,1)S(1)} %get-tuple-element.611), channel_id=1, source_target_pairs={{0,0},{1,2},{2,16},{3,18},{16,1},{17,3},{18,17},{19,19},{4,4},{5,6... | collective-permute-start | bytes 1179656 | tf_op jit(solution)/shard_map/ppermute | solution.py:614
  39.1 17.5 %collective-permute-start.7 = (bf16[128,1536]{1,0:T(8,128)(2,1)S(1)}, bf16[128,1536]{1,0:T(8,128)(2,1)S(1)}, u32[]{:S(2)}, u32[]{:S(2)}) collective-permute-start(bf16[128,1536]{1,0:T(8,128)(2,1)S(1)} %get-tuple-element.610), channel_id=1, source_target_pairs={{0,2},{1,0},{2,18},{3,16},{16,3},{17,1},{18,19},{19,17},{4,6},{5,4... | collective-permute-start | bytes 1179656 | tf_op jit(solution)/shard_map/ppermute | solution.py:614
  57.7 24.8 %collective-permute-start.9 = (bf16[256,1536]{1,0:T(8,128)(2,1)S(1)}, bf16[256,1536]{1,0:T(8,128)(2,1)S(1)}, u32[]{:S(2)}, u32[]{:S(2)}) collective-permute-start(bf16[256,1536]{1,0:T(8,128)(2,1)S(1)} %get-tuple-element.303.refs_0_), channel_id=1, source_target_pairs={{0,4},{4,0},{8,12},{12,8},{1,5},{5,1},{9,13},{13,9},{2,6},{6,2},{1... | collective-permute-start | bytes 2359304 | tf_op jit(solution)/shard_map/ppermute | solution.py:524
  58.3 24.2 %collective-permute-start.10 = (bf16[256,1536]{1,0:T(8,128)(2,1)S(1)}, bf16[256,1536]{1,0:T(8,128)(2,1)S(1)}, u32[]{:S(2)}, u32[]{:S(2)}) collective-permute-start(bf16[256,1536]{1,0:T(8,128)(2,1)S(1)} %get-tuple-element.303.refs_0_), channel_id=1, source_target_pairs={{0,8},{4,12},{8,0},{12,4},{1,9},{5,13},{9,1},{13,5},{2,10},{6,14},... | collective-permute-start | bytes 2359304 | tf_op jit(solution)/shard_map/ppermute | solution.py:524
  59.9 22.7 %collective-permute-start.13 = (bf16[256,1536]{1,0:T(8,128)(2,1)S(1)}, bf16[256,1536]{1,0:T(8,128)(2,1)S(1)}, u32[]{:S(2)}, u32[]{:S(2)}) collective-permute-start(bf16[256,1536]{1,0:T(8,128)(2,1)S(1)} %get-tuple-element.303.refs_0_), channel_id=1, source_target_pairs={{0,16},{16,0},{1,17},{17,1},{2,18},{18,2},{3,19},{19,3},{4,20},{20... | collective-permute-start | bytes 2359304 | tf_op jit(solution)/shard_map/ppermute | solution.py:524
  60.1 21.7 %collective-permute-start.11 = (bf16[128,1536]{1,0:T(8,128)(2,1)S(1)}, bf16[128,1536]{1,0:T(8,128)(2,1)S(1)}, u32[]{:S(2)}, u32[]{:S(2)}) collective-permute-start(bf16[128,1536]{1,0:T(8,128)(2,1)S(1)} %get-tuple-element.605), channel_id=1, source_target_pairs={{0,0},{1,2},{2,16},{3,18},{16,1},{17,3},{18,17},{19,19},{4,4},{5,6... | collective-permute-start | bytes 1179656 | tf_op jit(solution)/shard_map/ppermute | solution.py:614
  64.5 18.0 %collective-permute-start.12 = (bf16[128,1536]{1,0:T(8,128)(2,1)S(1)}, bf16[128,1536]{1,0:T(8,128)(2,1)S(1)}, u32[]{:S(2)}, u32[]{:S(2)}) collective-permute-start(bf16[128,1536]{1,0:T(8,128)(2,1)S(1)} %get-tuple-element.604), channel_id=1, source_target_pairs={{0,2},{1,0},{2,18},{3,16},{16,3},{17,1},{18,19},{19,17},{4,6},{5,4... | collective-permute-start | bytes 1179656 | tf_op jit(solution)/shard_map/ppermute | solution.py:614
  81.8 61.8 %collective-permute-start.30 = (bf16[192,1536]{1,0:T(8,128)(2,1)S(1)}, bf16[192,1536]{1,0:T(8,128)(2,1)}, u32[]{:S(2)}, u32[]{:S(2)}) collective-permute-start(bf16[192,1536]{1,0:T(8,128)(2,1)S(1)} %copy-done.8), channel_id=1, source_target_pairs={{0,16},{16,0},{1,17},{17,1},{2,18},{18,2},{3,19},{19,3},{4,20},{20... | collective-permute-start | bytes 1769480 | tf_op jit(solution)/shard_map/ppermute | solution.py:524
  112.8 181.6 %reduce-scatter.5.cloned.1.call-start = ((), (), s32[]{:S(2)}) async-start(), calls=%async_computation.5 | async-start | bytes 1966080 | tf_op jit(solution)/shard_map/reduce_scatter | solution.py:795
  113.1 26.6 %collective-permute-start.22 = (bf16[256,1536]{1,0:T(8,128)(2,1)S(1)}, bf16[256,1536]{1,0:T(8,128)(2,1)S(1)}, u32[]{:S(2)}, u32[]{:S(2)}) collective-permute-start(bf16[256,1536]{1,0:T(8,128)(2,1)S(1)} %pad_maximum_fusion.1.c0.refs_8_.refs_13_), channel_id=1, source_target_pairs={{0,4},{4,0},{8,12},{12,8},{1,5},{5,1},{9,13},{13,9},{2,6},{6,2},{1... | collective-permute-start | bytes 2359304 | tf_op jit(solution)/shard_map/ppermute | solution.py:524
  114.3 25.3 %collective-permute-start.23 = (bf16[256,1536]{1,0:T(8,128)(2,1)S(1)}, bf16[256,1536]{1,0:T(8,128)(2,1)S(1)}, u32[]{:S(2)}, u32[]{:S(2)}) collective-permute-start(bf16[256,1536]{1,0:T(8,128)(2,1)S(1)} %pad_maximum_fusion.1.c0.refs_8_.refs_13_), channel_id=1, source_target_pairs={{0,8},{4,12},{8,0},{12,4},{1,9},{5,13},{9,1},{13,5},{2,10},{6,14},... | collective-permute-start | bytes 2359304 | tf_op jit(solution)/shard_map/ppermute | solution.py:524
  115.8 23.3 %collective-permute-start.24 = (bf16[96,1536]{1,0:T(8,128)(2,1)S(1)}, bf16[96,1536]{1,0:T(8,128)(2,1)S(1)}, u32[]{:S(2)}, u32[]{:S(2)}) collective-permute-start(bf16[96,1536]{1,0:T(8,128)(2,1)S(1)} %slice.383), channel_id=1, source_target_pairs={{0,8},{4,12},{8,0},{12,4},{1,9},{5,13},{9,1},{13,5},{2,10},{6,14},... | collective-permute-start | bytes 884744 | tf_op jit(solution)/shard_map/ppermute | solution.py:524
  116.5 22.7 %collective-permute-start.25 = (bf16[96,1536]{1,0:T(8,128)(2,1)S(1)}, bf16[96,1536]{1,0:T(8,128)(2,1)S(1)}, u32[]{:S(2)}, u32[]{:S(2)}) collective-permute-start(bf16[96,1536]{1,0:T(8,128)(2,1)S(1)} %slice.384), channel_id=1, source_target_pairs={{0,4},{4,0},{8,12},{12,8},{1,5},{5,1},{9,13},{13,9},{2,6},{6,2},{1... | collective-permute-start | bytes 884744 | tf_op jit(solution)/shard_map/ppermute | solution.py:524
  146.5 17.7 %collective-permute-start.34 = (bf16[256,1536]{1,0:T(8,128)(2,1)S(1)}, bf16[256,1536]{1,0:T(8,128)(2,1)S(1)}, u32[]{:S(2)}, u32[]{:S(2)}) collective-permute-start(bf16[256,1536]{1,0:T(8,128)(2,1)S(1)} %pad_maximum_fusion.1.c0.refs_8_.refs_13_), channel_id=1, source_target_pairs={{0,16},{16,0},{1,17},{17,1},{2,18},{18,2},{3,19},{19,3},{4,20},{20... | collective-permute-start | bytes 2359304 | tf_op jit(solution)/shard_map/ppermute | solution.py:524
  166.2 21.2 %collective-permute-start.37 = (bf16[256,1536]{1,0:T(8,128)(2,1)}, bf16[256,1536]{1,0:T(8,128)(2,1)}, u32[]{:S(2)}, u32[]{:S(2)}) collective-permute-start(bf16[256,1536]{1,0:T(8,128)(2,1)} %get-tuple-element.356.n0.refs_0_), channel_id=1, source_target_pairs={{0,4},{4,0},{8,12},{12,8},{1,5},{5,1},{9,13},{13,9},{2,6},{6,2},{1... | collective-permute-start | bytes 2359304 | tf_op jit(solution)/shard_map/ppermute | solution.py:524
  167.1 20.4 %collective-permute-start.38 = (bf16[256,1536]{1,0:T(8,128)(2,1)}, bf16[256,1536]{1,0:T(8,128)(2,1)}, u32[]{:S(2)}, u32[]{:S(2)}) collective-permute-start(bf16[256,1536]{1,0:T(8,128)(2,1)} %get-tuple-element.356.n0.refs_0_), channel_id=1, source_target_pairs={{0,8},{4,12},{8,0},{12,4},{1,9},{5,13},{9,1},{13,5},{2,10},{6,14},... | collective-permute-start | bytes 2359304 | tf_op jit(solution)/shard_map/ppermute | solution.py:524
  187.6 15.0 %collective-permute-start.45 = (bf16[256,1536]{1,0:T(8,128)(2,1)}, bf16[256,1536]{1,0:T(8,128)(2,1)S(1)}, u32[]{:S(2)}, u32[]{:S(2)}) collective-permute-start(bf16[256,1536]{1,0:T(8,128)(2,1)} %collective-permute-done.38.n0.refs_2_), channel_id=1, source_target_pairs={{0,16},{16,0},{1,17},{17,1},{2,18},{18,2},{3,19},{19,3},{4,20},{20... | collective-permute-start | bytes 2359304 | tf_op jit(solution)/shard_map/ppermute | solution.py:524
  190.6 18.4 %collective-permute-start.40 = (bf16[128,1536]{1,0:T(8,128)(2,1)S(1)}, bf16[128,1536]{1,0:T(8,128)(2,1)S(1)}, u32[]{:S(2)}, u32[]{:S(2)}) collective-permute-start(bf16[128,1536]{1,0:T(8,128)(2,1)S(1)} %slice.399), channel_id=1, source_target_pairs={{0,8},{4,12},{8,0},{12,4},{1,9},{5,13},{9,1},{13,5},{2,10},{6,14},... | collective-permute-start | bytes 1179656 | tf_op jit(solution)/shard_map/ppermute | solution.py:524
  192.2 16.8 %collective-permute-start.41 = (bf16[128,1536]{1,0:T(8,128)(2,1)S(1)}, bf16[128,1536]{1,0:T(8,128)(2,1)S(1)}, u32[]{:S(2)}, u32[]{:S(2)}) collective-permute-start(bf16[128,1536]{1,0:T(8,128)(2,1)S(1)} %slice.400), channel_id=1, source_target_pairs={{0,4},{4,0},{8,12},{12,8},{1,5},{5,1},{9,13},{13,9},{2,6},{6,2},{1... | collective-permute-start | bytes 1179656 | tf_op jit(solution)/shard_map/ppermute | solution.py:524
  193.7 16.2 %collective-permute-start.42 = (bf16[128,1536]{1,0:T(8,128)(2,1)S(1)}, bf16[128,1536]{1,0:T(8,128)(2,1)S(1)}, u32[]{:S(2)}, u32[]{:S(2)}) collective-permute-start(bf16[128,1536]{1,0:T(8,128)(2,1)S(1)} %slice.401), channel_id=1, source_target_pairs={{0,8},{4,12},{8,0},{12,4},{1,9},{5,13},{9,1},{13,5},{2,10},{6,14},... | collective-permute-start | bytes 1179656 | tf_op jit(solution)/shard_map/ppermute | solution.py:524
  194.4 16.7 %collective-permute-start.43 = (bf16[128,1536]{1,0:T(8,128)(2,1)S(1)}, bf16[128,1536]{1,0:T(8,128)(2,1)S(1)}, u32[]{:S(2)}, u32[]{:S(2)}) collective-permute-start(bf16[128,1536]{1,0:T(8,128)(2,1)S(1)} %slice.402), channel_id=1, source_target_pairs={{0,4},{4,0},{8,12},{12,8},{1,5},{5,1},{9,13},{13,9},{2,6},{6,2},{1... | collective-permute-start | bytes 1179656 | tf_op jit(solution)/shard_map/ppermute | solution.py:524
  222.3 20.5 %collective-permute-start.52 = (bf16[256,1536]{1,0:T(8,128)(2,1)S(1)}, bf16[256,1536]{1,0:T(8,128)(2,1)S(1)}, u32[]{:S(2)}, u32[]{:S(2)}) collective-permute-start(bf16[256,1536]{1,0:T(8,128)(2,1)S(1)} %add_convert_fusion.9), channel_id=1, source_target_pairs={{0,4},{4,0},{8,12},{12,8},{1,5},{5,1},{9,13},{13,9},{2,6},{6,2},{1... | collective-permute-start | bytes 2359304 | tf_op jit(solution)/shard_map/ppermute | solution.py:524
  223.9 36.3 %collective-permute-start.53 = (bf16[256,1536]{1,0:T(8,128)(2,1)S(1)}, bf16[256,1536]{1,0:T(8,128)(2,1)}, u32[]{:S(2)}, u32[]{:S(2)}) collective-permute-start(bf16[256,1536]{1,0:T(8,128)(2,1)S(1)} %add_convert_fusion.8), channel_id=1, source_target_pairs={{0,8},{4,12},{8,0},{12,4},{1,9},{5,13},{9,1},{13,5},{2,10},{6,14},... | collective-permute-start | bytes 2359304 | tf_op jit(solution)/shard_map/ppermute | solution.py:524
  224.3 35.8 %collective-permute-start.54 = (bf16[256,1536]{1,0:T(8,128)(2,1)S(1)}, bf16[256,1536]{1,0:T(8,128)(2,1)}, u32[]{:S(2)}, u32[]{:S(2)}) collective-permute-start(bf16[256,1536]{1,0:T(8,128)(2,1)S(1)} %add_convert_fusion.7), channel_id=1, source_target_pairs={{0,12},{4,8},{8,4},{12,0},{1,13},{5,9},{9,5},{13,1},{2,14},{6,10},... | collective-permute-start | bytes 2359304 | tf_op jit(solution)/shard_map/ppermute | solution.py:524
  260.1 113.1 %reduce-scatter.7.cloned.1.call-start = ((), (), s32[]{:S(2)}) async-start(), calls=%async_computation.6 | async-start | bytes 3932160 | tf_op jit(solution)/shard_map/reduce_scatter | solution.py:795
  269.1 144.0 %reduce-scatter.9.cloned.1.call-start = ((), (), s32[]{:S(2)}) async-start(), calls=%async_computation.7 | async-start | bytes 1474560 | tf_op jit(solution)/shard_map/reduce_scatter | solution.py:795
  271.7 13.7 %collective-permute-start.57 = (bf16[2,256,256]{2,1,0:T(8,128)(2,1)S(1)}, bf16[2,256,256]{2,1,0:T(8,128)(2,1)S(1)}, u32[]{:S(2)}, u32[]{:S(2)}) collective-permute-start(bf16[2,256,256]{2,1,0:T(8,128)(2,1)S(1)} %pad_maximum_fusion.17), channel_id=1, source_target_pairs={{0,8},{4,12},{8,0},{12,4},{1,9},{5,13},{9,1},{13,5},{2,10},{6,14},... | collective-permute-start | bytes 786440 | tf_op jit(solution)/shard_map/ppermute | solution.py:524
  294.4 29.1 %collective-permute-start.59 = (bf16[256,1536]{1,0:T(8,128)(2,1)}, bf16[256,1536]{1,0:T(8,128)(2,1)S(1)}, u32[]{:S(2)}, u32[]{:S(2)}) collective-permute-start(bf16[256,1536]{1,0:T(8,128)(2,1)} %get-tuple-element.436.refs_1_), channel_id=1, source_target_pairs={{0,4},{4,0},{8,12},{12,8},{1,5},{5,1},{9,13},{13,9},{2,6},{6,2},{1... | collective-permute-start | bytes 2359304 | tf_op jit(solution)/shard_map/ppermute | solution.py:524
  295.9 27.6 %collective-permute-start.60 = (bf16[256,1536]{1,0:T(8,128)(2,1)}, bf16[256,1536]{1,0:T(8,128)(2,1)S(1)}, u32[]{:S(2)}, u32[]{:S(2)}) collective-permute-start(bf16[256,1536]{1,0:T(8,128)(2,1)} %get-tuple-element.436.refs_1_), channel_id=1, source_target_pairs={{0,8},{4,12},{8,0},{12,4},{1,9},{5,13},{9,1},{13,5},{2,10},{6,14},... | collective-permute-start | bytes 2359304 | tf_op jit(solution)/shard_map/ppermute | solution.py:524
  297.4 35.1 %collective-permute-start.63 = (bf16[128,1536]{1,0:T(8,128)(2,1)}, bf16[128,1536]{1,0:T(8,128)(2,1)S(1)}, u32[]{:S(2)}, u32[]{:S(2)}) collective-permute-start(bf16[128,1536]{1,0:T(8,128)(2,1)} %reduce-scatter.5.cloned.1.call-done.refs_3_), channel_id=1, source_target_pairs={{0,1},{1,2},{2,3},{4,5},{5,6},{6,7},{8,9},{9,10},{10,11},{12,13},{... | collective-permute-start | bytes 1179656 | tf_op jit(solution)/shard_map/ppermute | solution.py:565
  300.8 31.7 %collective-permute-start.64 = (bf16[128,1536]{1,0:T(8,128)(2,1)}, bf16[128,1536]{1,0:T(8,128)(2,1)S(1)}, u32[]{:S(2)}, u32[]{:S(2)}) collective-permute-start(bf16[128,1536]{1,0:T(8,128)(2,1)} %reduce-scatter.5.cloned.1.call-done.refs_3_), channel_id=1, source_target_pairs={{1,0},{2,1},{3,2},{5,4},{6,5},{7,6},{9,8},{10,9},{11,10},{13,12},{... | collective-permute-start | bytes 1179656 | tf_op jit(solution)/shard_map/ppermute | solution.py:565
  303.2 35.9 %collective-permute-start.67 = (bf16[256,1536]{1,0:T(8,128)(2,1)}, bf16[256,1536]{1,0:T(8,128)(2,1)S(1)}, u32[]{:S(2)}, u32[]{:S(2)}) collective-permute-start(bf16[256,1536]{1,0:T(8,128)(2,1)} %get-tuple-element.436.refs_1_), channel_id=1, source_target_pairs={{0,16},{16,0},{1,17},{17,1},{2,18},{18,2},{3,19},{19,3},{4,20},{20... | collective-permute-start | bytes 2359304 | tf_op jit(solution)/shard_map/ppermute | solution.py:524
  332.4 38.4 %collective-permute-start.68 = (bf16[256,1536]{1,0:T(8,128)(2,1)S(1)}, bf16[256,1536]{1,0:T(8,128)(2,1)S(1)}, u32[]{:S(2)}, u32[]{:S(2)}) collective-permute-start(bf16[256,1536]{1,0:T(8,128)(2,1)S(1)} %collective-permute-done.59.refs_2_), channel_id=1, source_target_pairs={{0,16},{16,0},{1,17},{17,1},{2,18},{18,2},{3,19},{19,3},{4,20},{20... | collective-permute-start | bytes 2359304 | tf_op jit(solution)/shard_map/ppermute | solution.py:524
  332.5 39.2 %collective-permute-start.69 = (bf16[256,1536]{1,0:T(8,128)(2,1)S(1)}, bf16[256,1536]{1,0:T(8,128)(2,1)S(1)}, u32[]{:S(2)}, u32[]{:S(2)}) collective-permute-start(bf16[256,1536]{1,0:T(8,128)(2,1)S(1)} %collective-permute-done.60.refs_3_), channel_id=1, source_target_pairs={{0,16},{16,0},{1,17},{17,1},{2,18},{18,2},{3,19},{19,3},{4,20},{20... | collective-permute-start | bytes 2359304 | tf_op jit(solution)/shard_map/ppermute | solution.py:524
  335.5 37.1 %collective-permute-start.70 = (bf16[256,1536]{1,0:T(8,128)(2,1)S(1)}, bf16[256,1536]{1,0:T(8,128)(2,1)}, u32[]{:S(2)}, u32[]{:S(2)}) collective-permute-start(bf16[256,1536]{1,0:T(8,128)(2,1)S(1)} %constant_dynamic-update-slice_fusion.10.refs_4_), channel_id=1, source_target_pairs={{0,16},{16,0},{1,17},{17,1},{2,18},{18,2},{3,19},{19,3},{4,20},{20... | collective-permute-start | bytes 2359304 | tf_op jit(solution)/shard_map/ppermute | solution.py:524
  335.6 29.7 %collective-permute-start.65 = (bf16[128,1536]{1,0:T(8,128)(2,1)S(1)}, bf16[128,1536]{1,0:T(8,128)(2,1)S(1)}, u32[]{:S(2)}, u32[]{:S(2)}) collective-permute-start(bf16[128,1536]{1,0:T(8,128)(2,1)S(1)} %collective-permute-done.63.refs_2_), channel_id=1, source_target_pairs={{0,1},{1,2},{2,3},{4,5},{5,6},{6,7},{8,9},{9,10},{10,11},{12,13},{... | collective-permute-start | bytes 1179656 | tf_op jit(solution)/shard_map/ppermute | solution.py:565
  339.1 31.7 %collective-permute-start.66 = (bf16[128,1536]{1,0:T(8,128)(2,1)S(1)}, bf16[128,1536]{1,0:T(8,128)(2,1)S(1)}, u32[]{:S(2)}, u32[]{:S(2)}) collective-permute-start(bf16[128,1536]{1,0:T(8,128)(2,1)S(1)} %collective-permute-done.64.refs_4_), channel_id=1, source_target_pairs={{1,0},{2,1},{3,2},{5,4},{6,5},{7,6},{9,8},{10,9},{11,10},{13,12},{... | collective-permute-start | bytes 1179656 | tf_op jit(solution)/shard_map/ppermute | solution.py:565
  373.2 16.6 %collective-permute-start.71 = (bf16[4,256,1536]{2,1,0:T(8,128)(2,1)}, bf16[4,256,1536]{2,1,0:T(8,128)(2,1)}, u32[]{:S(2)}, u32[]{:S(2)}) collective-permute-start(bf16[4,256,1536]{2,1,0:T(8,128)(2,1)} %get-tuple-element.450), channel_id=1, source_target_pairs={{0,16},{16,0},{1,17},{17,1},{2,18},{18,2},{3,19},{19,3},{4,20},{20... | collective-permute-start | bytes 9437192 | tf_op jit(solution)/shard_map/ppermute | solution.py:524
  376.5 75.3 %reduce-scatter.11.cloned.1.call-start = ((), (), s32[]{:S(2)}) async-start(), calls=%async_computation.8 | async-start | bytes 737280 | tf_op jit(solution)/shard_map/reduce_scatter | solution.py:795
  398.2 29.5 %collective-permute-start.84 = (bf16[4,256,1536]{2,1,0:T(8,128)(2,1)}, bf16[4,256,1536]{2,1,0:T(8,128)(2,1)}, u32[]{:S(2)}, u32[]{:S(2)}) collective-permute-start(bf16[4,256,1536]{2,1,0:T(8,128)(2,1)} %get-tuple-element.477), channel_id=1, source_target_pairs={{0,16},{16,0},{1,17},{17,1},{2,18},{18,2},{3,19},{19,3},{4,20},{20... | collective-permute-start | bytes 9437192 | tf_op jit(solution)/shard_map/ppermute | solution.py:524
  398.9 14.2 %collective-permute-start.74 = (bf16[2,48,1024]{2,1,0:T(8,128)(2,1)S(1)}, bf16[2,48,1024]{2,1,0:T(8,128)(2,1)S(1)}, u32[]{:S(2)}, u32[]{:S(2)}) collective-permute-start(bf16[2,48,1024]{2,1,0:T(8,128)(2,1)S(1)} %pad_maximum_fusion.25), channel_id=1, source_target_pairs={{0,8},{4,12},{8,0},{12,4},{1,9},{5,13},{9,1},{13,5},{2,10},{6,14},... | collective-permute-start | bytes 589832 | tf_op jit(solution)/shard_map/ppermute | solution.py:524
  419.2 149.6 %all-gather.6.cloned.1.call-start = ((), (), s32[]{:S(2)}) async-start(), calls=%async_computation.9 | async-start | bytes 2211840 | tf_op jit(solution)/shard_map/all_gather | solution.py:901
  419.4 31.2 %collective-permute-start.78 = (bf16[8,48,1024]{2,1,0:T(8,128)(2,1)S(1)}, bf16[8,48,1024]{2,1,0:T(8,128)(2,1)S(1)}, u32[]{:S(2)}, u32[]{:S(2)}) collective-permute-start(bf16[8,48,1024]{2,1,0:T(8,128)(2,1)S(1)} %bitcast.183), channel_id=1, source_target_pairs={{0,1},{1,2},{2,3},{4,5},{5,6},{6,7},{8,9},{9,10},{10,11},{12,13},{... | collective-permute-start | bytes 2359304 | tf_op jit(solution)/shard_map/ppermute | solution.py:565
  422.3 29.4 %collective-permute-start.79 = (bf16[8,48,1024]{2,1,0:T(8,128)(2,1)S(1)}, bf16[8,48,1024]{2,1,0:T(8,128)(2,1)S(1)}, u32[]{:S(2)}, u32[]{:S(2)}) collective-permute-start(bf16[8,48,1024]{2,1,0:T(8,128)(2,1)S(1)} %bitcast.184), channel_id=1, source_target_pairs={{1,0},{2,1},{3,2},{5,4},{6,5},{7,6},{9,8},{10,9},{11,10},{13,12},{... | collective-permute-start | bytes 2359304 | tf_op jit(solution)/shard_map/ppermute | solution.py:565
  451.8 21.8 %collective-permute-start.85 = (bf16[256,1536]{1,0:T(8,128)(2,1)}, bf16[256,1536]{1,0:T(8,128)(2,1)}, u32[]{:S(2)}, u32[]{:S(2)}) collective-permute-start(bf16[256,1536]{1,0:T(8,128)(2,1)} %get-tuple-element.485), channel_id=1, source_target_pairs={{0,4},{4,0},{8,12},{12,8},{1,5},{5,1},{9,13},{13,9},{2,6},{6,2},{1... | collective-permute-start | bytes 2359304 | tf_op jit(solution)/shard_map/ppermute | solution.py:524
  453.2 36.3 %collective-permute-start.86 = (bf16[256,1536]{1,0:T(8,128)(2,1)}, bf16[256,1536]{1,0:T(8,128)(2,1)}, u32[]{:S(2)}, u32[]{:S(2)}) collective-permute-start(bf16[256,1536]{1,0:T(8,128)(2,1)} %get-tuple-element.486), channel_id=1, source_target_pairs={{0,8},{4,12},{8,0},{12,4},{1,9},{5,13},{9,1},{13,5},{2,10},{6,14},... | collective-permute-start | bytes 2359304 | tf_op jit(solution)/shard_map/ppermute | solution.py:524
  454.4 35.2 %collective-permute-start.87 = (bf16[256,1536]{1,0:T(8,128)(2,1)}, bf16[256,1536]{1,0:T(8,128)(2,1)}, u32[]{:S(2)}, u32[]{:S(2)}) collective-permute-start(bf16[256,1536]{1,0:T(8,128)(2,1)} %get-tuple-element.487), channel_id=1, source_target_pairs={{0,12},{4,8},{8,4},{12,0},{1,13},{5,9},{9,5},{13,1},{2,14},{6,10},... | collective-permute-start | bytes 2359304 | tf_op jit(solution)/shard_map/ppermute | solution.py:524
  455.3 34.3 %collective-permute-start.88 = (bf16[8,48,1024]{2,1,0:T(8,128)(2,1)S(1)}, bf16[8,48,1024]{2,1,0:T(8,128)(2,1)}, u32[]{:S(2)}, u32[]{:S(2)}) collective-permute-start(bf16[8,48,1024]{2,1,0:T(8,128)(2,1)S(1)} %collective-permute-done.78.refs_2_), channel_id=1, source_target_pairs={{0,1},{1,2},{2,3},{4,5},{5,6},{6,7},{8,9},{9,10},{10,11},{12,13},{... | collective-permute-start | bytes 2359304 | tf_op jit(solution)/shard_map/ppermute | solution.py:565
  458.6 30.9 %collective-permute-start.89 = (bf16[8,48,1024]{2,1,0:T(8,128)(2,1)S(1)}, bf16[8,48,1024]{2,1,0:T(8,128)(2,1)}, u32[]{:S(2)}, u32[]{:S(2)}) collective-permute-start(bf16[8,48,1024]{2,1,0:T(8,128)(2,1)S(1)} %collective-permute-done.79.refs_4_), channel_id=1, source_target_pairs={{1,0},{2,1},{3,2},{5,4},{6,5},{7,6},{9,8},{10,9},{11,10},{13,12},{... | collective-permute-start | bytes 2359304 | tf_op jit(solution)/shard_map/ppermute | solution.py:565
  489.5 41.2 %collective-permute-start.93 = (bf16[8,48,1024]{2,1,0:T(8,128)(2,1)}, bf16[8,48,1024]{2,1,0:T(8,128)(2,1)S(1)}, u32[]{:S(2)}, u32[]{:S(2)}) collective-permute-start(bf16[8,48,1024]{2,1,0:T(8,128)(2,1)} %collective-permute-done.88.refs_1_), channel_id=1, source_target_pairs={{0,1},{1,2},{2,3},{4,5},{5,6},{6,7},{8,9},{9,10},{10,11},{12,13},{... | collective-permute-start | bytes 2359304 | tf_op jit(solution)/shard_map/ppermute | solution.py:565
  492.0 38.8 %collective-permute-start.94 = (bf16[8,48,1024]{2,1,0:T(8,128)(2,1)}, bf16[8,48,1024]{2,1,0:T(8,128)(2,1)S(1)}, u32[]{:S(2)}, u32[]{:S(2)}) collective-permute-start(bf16[8,48,1024]{2,1,0:T(8,128)(2,1)} %collective-permute-done.89.refs_5_), channel_id=1, source_target_pairs={{1,0},{2,1},{3,2},{5,4},{6,5},{7,6},{9,8},{10,9},{11,10},{13,12},{... | collective-permute-start | bytes 2359304 | tf_op jit(solution)/shard_map/ppermute | solution.py:565
  495.4 20.8 %collective-permute-start.90 = (bf16[256,1536]{1,0:T(8,128)(2,1)}, bf16[256,1536]{1,0:T(8,128)(2,1)S(1)}, u32[]{:S(2)}, u32[]{:S(2)}) collective-permute-start(bf16[256,1536]{1,0:T(8,128)(2,1)} %get-tuple-element.492), channel_id=1, source_target_pairs={{0,4},{4,0},{8,12},{12,8},{1,5},{5,1},{9,13},{13,9},{2,6},{6,2},{1... | collective-permute-start | bytes 2359304 | tf_op jit(solution)/shard_map/ppermute | solution.py:524
  496.2 34.6 %collective-permute-start.91 = (bf16[256,1536]{1,0:T(8,128)(2,1)}, bf16[256,1536]{1,0:T(8,128)(2,1)S(1)}, u32[]{:S(2)}, u32[]{:S(2)}) collective-permute-start(bf16[256,1536]{1,0:T(8,128)(2,1)} %get-tuple-element.494), channel_id=1, source_target_pairs={{0,8},{4,12},{8,0},{12,4},{1,9},{5,13},{9,1},{13,5},{2,10},{6,14},... | collective-permute-start | bytes 2359304 | tf_op jit(solution)/shard_map/ppermute | solution.py:524
  497.6 33.2 %collective-permute-start.92 = (bf16[256,1536]{1,0:T(8,128)(2,1)}, bf16[256,1536]{1,0:T(8,128)(2,1)S(1)}, u32[]{:S(2)}, u32[]{:S(2)}) collective-permute-start(bf16[256,1536]{1,0:T(8,128)(2,1)} %get-tuple-element.496), channel_id=1, source_target_pairs={{0,12},{4,8},{8,4},{12,0},{1,13},{5,9},{9,5},{13,1},{2,14},{6,10},... | collective-permute-start | bytes 2359304 | tf_op jit(solution)/shard_map/ppermute | solution.py:524
  531.3 15.8 %collective-permute-start.95 = (bf16[128,1536]{1,0:T(8,128)(2,1)S(1)}, bf16[128,1536]{1,0:T(8,128)(2,1)S(1)}, u32[]{:S(2)}, u32[]{:S(2)}) collective-permute-start(bf16[128,1536]{1,0:T(8,128)(2,1)S(1)} %get-tuple-element.594), channel_id=1, source_target_pairs={{2,0},{0,1},{18,2},{16,3},{3,16},{1,17},{19,18},{17,19},{6,4},{4,5... | collective-permute-start | bytes 1179656 | tf_op jit(solution)/shard_map/ppermute | solution.py:621
  531.4 27.9 %collective-permute-start.96 = (bf16[128,1536]{1,0:T(8,128)(2,1)S(1)}, bf16[128,1536]{1,0:T(8,128)(2,1)S(1)}, u32[]{:S(2)}, u32[]{:S(2)}) collective-permute-start(bf16[128,1536]{1,0:T(8,128)(2,1)S(1)} %get-tuple-element.595), channel_id=1, source_target_pairs={{0,0},{2,1},{16,2},{18,3},{1,16},{3,17},{17,18},{19,19},{4,4},{6,5... | collective-permute-start | bytes 1179656 | tf_op jit(solution)/shard_map/ppermute | solution.py:621
  535.5 24.9 %collective-permute-start.97 = (bf16[128,1536]{1,0:T(8,128)(2,1)S(1)}, bf16[128,1536]{1,0:T(8,128)(2,1)S(1)}, u32[]{:S(2)}, u32[]{:S(2)}) collective-permute-start(bf16[128,1536]{1,0:T(8,128)(2,1)S(1)} %get-tuple-element.590), channel_id=1, source_target_pairs={{2,0},{0,1},{18,2},{16,3},{3,16},{1,17},{19,18},{17,19},{6,4},{4,5... | collective-permute-start | bytes 1179656 | tf_op jit(solution)/shard_map/ppermute | solution.py:621
  535.6 32.2 %collective-permute-start.98 = (bf16[128,1536]{1,0:T(8,128)(2,1)S(1)}, bf16[128,1536]{1,0:T(8,128)(2,1)S(1)}, u32[]{:S(2)}, u32[]{:S(2)}) collective-permute-start(bf16[128,1536]{1,0:T(8,128)(2,1)S(1)} %get-tuple-element.591), channel_id=1, source_target_pairs={{0,0},{2,1},{16,2},{18,3},{1,16},{3,17},{17,18},{19,19},{4,4},{6,5... | collective-permute-start | bytes 1179656 | tf_op jit(solution)/shard_map/ppermute | solution.py:621
  (149 other events, 1636.7 us)
Sparse Core Ops, SparseCore 0:
  112.9 63.1 all-gather.3
  260.3 34.0 reduce-scatter.4
  297.3 75.8 reduce-scatter.6
  376.6 24.9 reduce-scatter.8
  419.4 23.9 reduce-scatter.10
  473.7 53.6 all-gather.5

commit v3 on v2

--- a/solution.py
+++ b/solution.py
@@ -19,6 +19,13 @@
 BLK = 256
 BF = jnp.bfloat16
 F32 = jnp.float32
+
+
+def small_cost(flops, transcendentals, bytes_accessed):
+    part = 64
+    return pl.CostEstimate(
+        flops=flops // part, transcendentals=transcendentals // part, bytes_accessed=bytes_accessed // part
+    )
 
 
 def dot(left, right, dims=((1,), (0,))):
@@ -158,8 +165,8 @@
 
 
 def attn_cost(n_q, n_k, products):
-    return pl.CostEstimate(
-        flops=6 * products * n_q * n_k * 2 * HP, transcendentals=n_q * n_k * 2, bytes_accessed=(n_q + n_k) * HP * 16
+    return small_cost(
+        flops=2 * products * n_q * n_k * 2 * HP, transcendentals=n_q * n_k * 2, bytes_accessed=(n_q + n_k) * HP * 16
     )
 
 
@@ -208,7 +215,7 @@
         out_specs=jax.tree.map(lambda _: pl.BlockSpec(memory_space=pltpu.VMEM), out_shape),
         scratch_shapes=scratch,
         compiler_params=pltpu.CompilerParams(vmem_limit_bytes=40 << 20),
-        cost_estimate=pl.CostEstimate(flops=0, transcendentals=0, bytes_accessed=2 * moved),
+        cost_estimate=small_cost(flops=0, transcendentals=0, bytes_accessed=2 * moved),
         name=name,
     )(ids, *values)
 
@@ -235,7 +242,7 @@
 
 def head_kernel(n_blk, ids, *refs):
     got, x_refs = refs[:n_blk], refs[n_blk : n_blk + 2]
-    w_ref, seg_ref, gain_ref, x_ref, n_ref, small_sc = refs[n_blk + 2 :]
+    w_ref, seg_ref, gain_ref, x_ref, c_ref, n_ref, small_sc = refs[n_blk + 2 :]
     n_rows = w_ref.shape[0] // (2 * n_blk)
     for k, ref in enumerate(got):
         for core in range(2):
@@ -251,10 +258,11 @@
             gains[i].append(small[i : i + 1, :n_rows])
     for i in range(2):
         gain_ref[i] = jnp.concatenate(gains[i], 1)
-    tok = x_refs[0].shape[0]
+    tok = x_refs[0].shape[0] // 2
     for i, ref in enumerate(x_refs):
-        x = ref[...]
+        x = ref[:tok, :]
         x_ref[i * tok : (i + 1) * tok, :] = x
+        c_ref[i * tok : (i + 1) * tok, :] = ref[tok:, :]
         x = x.astype(F32)
         factor = lax.rsqrt(jnp.mean(x * x, -1, keepdims=True) + EPS)
         n_ref[i * tok : (i + 1) * tok, :] = (x * factor * gain_ref[0]).astype(BF)
@@ -344,7 +352,7 @@
         in_specs=whole(7),
         out_specs=tuple(whole(4)),
         compiler_params=pltpu.CompilerParams(vmem_limit_bytes=40 << 20),
-        cost_estimate=pl.CostEstimate(
+        cost_estimate=small_cost(
             flops=2 * 2 * rows * D * width * 5, transcendentals=2 * rows * width, bytes_accessed=12 << 20
         ),
         name="ff",
@@ -393,7 +401,7 @@
             pl.BlockSpec((width2 // 2, cols), lambda j: (0, j)),
         ),
         compiler_params=pltpu.CompilerParams(vmem_limit_bytes=56 << 20),
-        cost_estimate=pl.CostEstimate(
+        cost_estimate=small_cost(
             flops=2 * 2 * n_pairs * rows * D * width2 * 3 // 2, transcendentals=0, bytes_accessed=24 << 20
         ),
         name="ff_weight",
@@ -409,7 +417,7 @@
         in_specs=whole(len(values)),
         out_specs=jax.tree.map(lambda _: pl.BlockSpec(memory_space=pltpu.VMEM), out_shape),
         compiler_params=pltpu.CompilerParams(vmem_limit_bytes=52 << 20),
-        cost_estimate=pl.CostEstimate(flops=flops, transcendentals=0, bytes_accessed=moved),
+        cost_estimate=small_cost(flops=flops, transcendentals=0, bytes_accessed=moved),
         name=name,
     )(*values)
 
@@ -509,7 +517,7 @@
         + [pl.BlockSpec(dqkv.shape, lambda j: (0, 0), pipeline_mode=pl.Buffered(1))],
         out_specs=pl.BlockSpec((n_head, n_plane // steps, part, 4 * HD), lambda j: (0, j, 0, 0)),
         compiler_params=pltpu.CompilerParams(vmem_limit_bytes=48 << 20),
-        cost_estimate=pl.CostEstimate(
+        cost_estimate=small_cost(
             flops=2 * len(n_list) * rows * D * 4 * HP * 2, transcendentals=0, bytes_accessed=12 << 20
         ),
         name="qkv_weight",
@@ -558,6 +566,18 @@
 
 def add_cores(own, other):
     return own + swap(other, "dp", 1).astype(F32)
+
+
+def sum_far(parts):
+    half = parts[3].shape[0] // 2
+    return swap(parts[3][:half].astype(BF), "blk", 1), swap(parts[3][half:].astype(BF), "blk", 2)
+
+
+def sum_near(parts, low, high):
+    half = parts[3].shape[0] // 2
+    one = jnp.concatenate([parts[1][:half], parts[1][half:] + high.astype(F32)])
+    two = jnp.concatenate([parts[2][:half] + low.astype(F32), parts[2][half:]])
+    return swap(one.astype(BF), "blk", 1), swap(two.astype(BF), "blk", 2)
 
 
 def line_step(left, right):
@@ -607,11 +627,11 @@
                 pairs.append((core * n_head + head, (seq_part >> 1) * n_head + target * sub + sub_part))
         return pairs
 
-    def to_plane(value):
+    def to_plane(*values):
         parts = []
         for k in range(2):
-            piece = lax.dynamic_index_in_dim(value, k ^ (my_seq & 1), 0, keepdims=False)
-            parts.append(lax.ppermute(piece, ("dp", "head"), routes(k)))
+            piece = [lax.dynamic_index_in_dim(v[:, 0], k ^ (my_seq & 1), 0, keepdims=False) for v in values]
+            parts.append(lax.ppermute(jnp.concatenate(piece), ("dp", "head"), routes(k)))
         return parts
 
     def from_plane(value):
@@ -650,27 +670,24 @@
         packed = place_call(pack_ff_kernel, shape, ids, *cut, name="pack_ff")
         return packed.reshape((2, n_blk) + packed.shape[1:])
 
-    packed, near_out, act_low, cot_low, gate_low, up_low = fence(
-        pack_qkv(query_weight, key_weight, value_weight, small),
-        near(output_weight),
-        activations,
-        cotangent,
-        gate_weight,
-        up_weight,
-    )
-    both, act_low, cot_low, gate_low, up_low = fence(
-        pair_up(packed[0], swap(packed[1], "dp", 1)), act_low, cot_low, gate_low, up_low
+    near_out = near(output_weight)
+    packed, act_low, cot_low, gate_low, up_low = fence(
+        pack_qkv(query_weight, key_weight, value_weight, small), activations, cotangent, gate_weight, up_weight
+    )
+    both, near_out, act_low, cot_low, gate_low, up_low = fence(
+        pair_up(packed[0], swap(packed[1], "dp", 1)), near_out, act_low, cot_low, gate_low, up_low
     )
     ff_packed = pack_ff(gate_low, up_low)
-    got, x_parts, ff_both, cot_low = fence(
-        chips(both), to_plane(act_low[:, 0]), pair_up(ff_packed[0], swap(ff_packed[1], "dp", 1)), cot_low
-    )
-    qkv_w, seg_all, gains, x_low, input_one = place_call(
+    got, x_parts, ff_both = fence(
+        chips(both), to_plane(act_low, cot_low), pair_up(ff_packed[0], swap(ff_packed[1], "dp", 1))
+    )
+    qkv_w, seg_all, gains, x_low, cot, input_one = place_call(
         functools.partial(head_kernel, n_blk),
         (
             jax.ShapeDtypeStruct((D, width), BF),
             jax.ShapeDtypeStruct((n_plane, small_rows, width), BF),
             jax.ShapeDtypeStruct((2, 1, D), F32),
+            jax.ShapeDtypeStruct((own, D), BF),
             jax.ShapeDtypeStruct((own, D), BF),
             jax.ShapeDtypeStruct((own, D), BF),
         ),
@@ -716,10 +733,11 @@
         & (jnp.max(ksb, 1)[None, :] >= jnp.min(qsb, 1)[:, None])
     ).astype(jnp.int32)
 
-    input_one, qkv_w, ff_both, cot_low = fence(input_one, qkv_w, ff_both, cot_low)
-    near_one, cot, side_one = fence(near(input_one), to_plane(cot_low[:, 0]), across(input_one))
-    far_one, more_one, cot = fence(far(*near_one), across(*near_one), join(cot))
+    input_one, qkv_w, ff_both, cot = fence(input_one, qkv_w, ff_both, cot)
+    near_one, side_one, ff_both = fence(near(input_one), across(input_one), ff_both)
+    far_one, ff_got, near_one = fence(far(*near_one), chips(ff_both), near_one)
     far_one = join(far_one)
+    more_one = across(*near_one)
     mine_one = [input_one, *near_one, far_one]
     all_one = fence(*mine_one, *side_one, *more_one, *across(far_one))
 
@@ -727,8 +745,8 @@
         shape = jax.ShapeDtypeStruct((rows, 4 * HP), BF)
         return simple_call(stack_project_kernel, shape, values, "project_qkv", 2 * rows * D * 4 * HP)
 
-    ff_both = [after(v, all_one[-1]) for v in ff_both]
-    qkv, ff_got, cot, near_out = fence(project_qkv(*all_one, qkv_w), chips(ff_both), cot, near_out)
+    qkv = project_qkv(*all_one, qkv_w)
+    cot, *near_out = lax.optimization_barrier((cot, *near_out, all_one[-1]))[:-1]
     kv = ()
     if sub > 1:
         groups = [[s * sub + i for i in range(sub)] for s in range(4)]
@@ -825,33 +843,40 @@
         return simple_call(kernel, shapes, values, "branch", 2 * own * D * D)
 
     grad_mid, grad_branch, grad_o = fence(*branch(*all_out, local_0, *got_two, x_mid, cot, gain_two[None]))
-    (do_both,) = fence(pair_up(grad_o[0], swap(grad_o[1], "dp", 1)))
-    do_got, down_mine, grad_branch = fence(chips(do_both), down_mine, grad_branch)
+
+    def back_project(transposed, *values):
+        shapes = tuple(jax.ShapeDtypeStruct((n_blk, own, D), t) for t in (F32, BF))
+        kernel = functools.partial(back_project_kernel, transposed)
+        return simple_call(kernel, shapes, values, "back_project", 2 * rows * D * values[-1].size // D)
+
+    do_both, hidden = fence(pair_up(grad_o[0], swap(grad_o[1], "dp", 1)), hidden)
+    out_own, out_other = back_project(False, *hidden, down_weight)
+    do_got, out_own, out_side, grad_branch = fence(chips(do_both), out_own, swap(out_other, "dp", 1), grad_branch)
     grad_o = jnp.stack(do_got, 1).reshape(rows, 2 * HP)
     line = n_head == 4
     no_step = lambda *v: ()
     step = line_step if line else no_step
     back = attend_back(need, qkv, *(kv or (None,)), *q_args, o, lse, grad_o)
-    line_0 = step(down_mine, down_mine)
-    dqkv, near_branch = fence(back, near(grad_branch))
+    dqkv, near_branch, out_own, out_side = fence(back, near(grad_branch), out_own, out_side)
+    local_out = [out_own[k] + out_side[k].astype(F32) for k in range(n_blk)]
     if sub > 1:
         dkv = lax.psum_scatter(dqkv[1], "head", scatter_dimension=0, tiled=True, axis_index_groups=groups)
         dqkv = [join([dqkv[0], dkv], 1)]
     dqkv = dqkv[0]
-
-    def back_project(transposed, *values):
-        shapes = tuple(jax.ShapeDtypeStruct((n_blk, own, D), t) for t in (F32, BF))
-        kernel = functools.partial(back_project_kernel, transposed)
-        return simple_call(kernel, shapes, values, "back_project", 2 * rows * D * values[-1].size // D)
-
-    qkv_grad, far_branch, dqkv, line_0 = fence(
-        qkv_weight_call(all_one, dqkv, n_head, n_plane), far(*near_branch), dqkv, line_0
+    qkv_grad, far_branch, dqkv, ff_mine, local_out, far_sum = fence(
+        qkv_weight_call(all_one, dqkv, n_head, n_plane), far(*near_branch), dqkv, ff_mine, local_out, sum_far(local_out)
     )
     qkv_mine = head_sum(qkv_grad.reshape(D, 4 * HD)).reshape(n_plane, part, 4 * HD)
     mine_branch = [grad_branch, *near_branch, join(far_branch)]
-    (one_own, one_other), line_1, side_branch, ff_mine = fence(
-        back_project(True, dqkv, qkv_w), step(*line_0), across(*mine_branch), ff_mine
-    )
+    ff_rel = rel_parts(ff_mine)
+    (one_own, one_other), side_branch, ff_both, got_out, local_out_0 = fence(
+        back_project(True, dqkv, qkv_w),
+        across(*mine_branch),
+        pair_up(ff_rel[0], swap(ff_rel[1], "dp", 1)),
+        sum_near(local_out, *far_sum),
+        local_out[0],
+    )
+    block_out = (x_mid + local_out_0 + sum(g.astype(F32) for g in got_out)).astype(BF)
 
     def out_weights(*values):
         rows_per = values[1].shape[0]
@@ -863,50 +888,39 @@
             in_specs=[pl.BlockSpec(values[0].shape, lambda j: (0, 0), pipeline_mode=pl.Buffered(1))] + [lanes] * n_plane,
             out_specs=pl.BlockSpec((2 * HD, 384), lambda j: (0, j)),
             compiler_params=pltpu.CompilerParams(vmem_limit_bytes=48 << 20),
-            cost_estimate=pl.CostEstimate(flops=4 * rows * D * 2 * HP, transcendentals=0, bytes_accessed=9 << 20),
+            cost_estimate=small_cost(flops=4 * rows * D * 2 * HP, transcendentals=0, bytes_accessed=9 << 20),
             name="out_weight",
         )(*values)
 
-    ff_rel = rel_parts(ff_mine)
-    one_side, out_grad, one_own, ff_both, line_1, hidden = fence(
-        swap(one_other, "dp", 1),
+    one_side = swap(one_other, "dp", 1)
+    local_one = [one_own[k] + one_side[k].astype(F32) for k in range(n_blk)]
+    ff_got, out_grad, local_0, sent_one, down_mine = fence(
+        chips(ff_both),
         out_weights(o, *mine_branch, *side_branch),
-        one_own,
-        pair_up(ff_rel[0], swap(ff_rel[1], "dp", 1)),
-        line_1,
-        hidden,
+        local_one[0],
+        [v.astype(BF) for v in local_one],
+        down_mine,
     )
     out_mine = head_sum(out_grad)
-    local_one = [one_own[k] + one_side[k].astype(F32) for k in range(n_blk)]
-    ff_got, local_0, sent_one, line_2, qkv_mine = fence(
-        chips(ff_both), local_one[0], [v.astype(BF) for v in local_one], step(*line_1), qkv_mine
-    )
+    late_down = lax.all_gather(down_mine, "head", axis=0)
     ff_rows = jnp.stack(ff_got, 1).reshape(ff_mine.shape)
-    qkv_rel = rel_parts(qkv_mine)
-    qkv_both = pair_up(qkv_rel[0], swap(qkv_rel[1], "dp", 1))
     ff_0 = step(ff_rows, ff_rows)
-    out_own, out_other = back_project(False, *hidden, down_weight)
-    out_side = swap(out_other, "dp", 1)
-    local_out = [out_own[k] + out_side[k].astype(F32) for k in range(n_blk)]
-    ff_0, qkv_rows, local_out_0, sent_out, sent_one, local_0, out_mine = fence(
-        ff_0, chips(qkv_both), local_out[0], [v.astype(BF) for v in local_out], sent_one, local_0, out_mine
-    )
-    got_one, ff_1 = fence(chips(sent_one)[1:], step(*ff_0))
+    got_one, ff_1, ff_0, qkv_mine, out_mine, block_out = fence(
+        chips(sent_one)[1:], step(*ff_0), ff_0, qkv_mine, out_mine, block_out
+    )
     normed, factor = normalize(x_low.astype(F32))
     grad_in_one = local_0 + sum(g.astype(F32) for g in got_one)
     grad_input = (grad_mid + norm_back(grad_in_one, gain_one, normed, factor)).astype(BF)
-    local_0 = local_out_0
-    got_out = chips([after(v, *ff_1) if line else v for v in sent_out])[1:]
+    qkv_rel = rel_parts(qkv_mine)
+    qkv_both = pair_up(qkv_rel[0], swap(qkv_rel[1], "dp", 1))
+    qkv_rows, ff_2, grad_input, block_out, out_mine = fence(
+        chips(qkv_both), step(*ff_1), grad_input, block_out, out_mine
+    )
     late = join([jnp.stack(qkv_rows, 1).reshape(-1, 4 * HD), out_mine.reshape(-1, 4 * HD)])
     late = lax.all_gather(late, "head", axis=0)
-    if line:
-        down_chunks = [line_2[0], line_1[0], line_0[0], down_mine, line_0[1], line_1[1], line_2[1]]
-        grad_down = owned_rows(down_chunks)
-    else:
-        grad_down = owned_rows([lax.all_gather(down_mine, "head", axis=0)])
-    got_out, ff_2, grad_input = fence(got_out, step(*ff_1), grad_input)
-    block_out = (x_mid + local_0 + sum(g.astype(F32) for g in got_out)).astype(BF)
-    block_out, grad_input = from_plane(block_out), from_plane(grad_input)
+    grad_input = from_plane(grad_input)
+    block_out = from_plane(block_out)
+    grad_down = late_down.reshape(-1, D).astype(F32)
     late_qkv = late[:, : n_plane * part].reshape(n_head, n_plane, part, 4 * HD)
     late_out = late[:, n_plane * part :].reshape(n_head, part, D)
     each = lambda v: [v[i] for i in range(4)] if line else [v]

time: 596 us -> 585 us (0.982)
  starting transfers between devices: 111 us -> 94.2 us
  other arithmetic: 39.1 us -> 51.1 us
  local copies, waits for them, and re-layouts: 54.3 us -> 45 us
    all_gather x0 -> x1, waiting for transfers between devices: none -> 26.5 us  [per_device(): late_down = lax.all_gather(down_mine, 'head', axis=0)]
    ppermute x4 -> x2, waiting for transfers between devices: 31.7 us -> 7.99 us  [to_plane(): lax.ppermute(jnp.concatenate(piece), ('dp', 'head'), routes(k))]
    ppermute x4, waiting for transfers between devices: 19.6 us -> 42.7 us  [from_plane(): lax.ppermute(value[k * tok:(k + 1) * tok], ('dp', 'head'), back)]
    unnamed x236 -> x198, local copies, waits for them, and re-layouts: 33.8 us -> 20.2 us
    ppermute x6 -> x3, starting transfers between devices: 18.3 us -> 8.36 us  [line_step(): lax.ppermute(left, 'head', up)]
    ppermute x6 -> x3, waiting for transfers between devices: 10.5 us -> 1.75 us  [line_step(): lax.ppermute(right, 'head', [(b, a) for a, b in up])]
    all_gather x1, waiting for transfers between devices: 7.57 us -> 0.01 us  [per_device(): lax.all_gather(ff_all, 'head', axis=0, tiled=True, axis_index_groups=shar...]
    another operation x0 -> x3, other arithmetic: none -> 6.78 us
  transfers between devices with their start and end apart: 105 -> 99, of which waited for: 39 -> 39; matrix products, arithmetic and copies ran while one was open for 9% -> 12% of each run, Pallas kernels for 22% -> 22%
where the time goes in v3:
time: 585 us; the launch traced here: 577 us
  waiting for transfers between devices  231 us (39%)
  Pallas kernels  139 us (24%)
  starting transfers between devices  94.2 us (16%)
  other arithmetic  51.1 us (9%)
  local copies, waits for them, and re-layouts  45 us (8%)
  between operations  16.7 us (3%)
    ppermute x80, waiting for transfers between devices, swap(): lax.ppermute(value, axis, [(i, i ^ mask) for i in range(lax.axis_size(axi...  124 us
    ppermute x80, starting transfers between devices, swap(): lax.ppermute(value, axis, [(i, i ^ mask) for i in range(lax.axis_size(axi...  63.1 us
    ppermute x4, waiting for transfers between devices, from_plane(): lax.ppermute(value[k * tok:(k + 1) * tok], ('dp', 'head'), back)  42.7 us
    pallas_call x5, Pallas kernels, simple_call(): pl.pallas_call(kernel, out_shape=out_shape, in_specs=whole(len(values)),...  37.7 us
    all_gather x1, waiting for transfers between devices, per_device(): late_down = lax.all_gather(down_mine, 'head', axis=0)  26.5 us
    ppermute x3, waiting for transfers between devices, line_step(): lax.ppermute(left, 'head', up)  24.3 us
    pallas_call x4, Pallas kernels, ff_call(): pl.pallas_call(ff_kernel, out_shape=(jax.ShapeDtypeStruct((2, rows, width...  21.7 us
    unnamed x198, local copies, waits for them, and re-layouts  20.2 us
  transfers between devices with their start and end apart: 99, of which 39 were waited for; matrix products, arithmetic and copies ran while one was open for 12% of the time, Pallas kernels for 22%

profile of v3, /device:TPU:8, one launch (start us, length us, event | category | flops | bytes accessed | tf_op | source)
XLA Modules:
  0.0 576.9 jit_solution(6431434849912565206)
XLA Ops:
  18.0 2.3 collective-permute-done
  24.6 3.5 collective-permute-start.6
  38.6 6.3 %collective-permute-done.3.refs_1_ = bf16[2,208,512]{2,1,0:T(8,128)(2,1)S(1)} collective-permute-done((bf16[2,208,512]{2,1,0:T(8,128)(2,1)S(1)}, bf16[2,208,512]{2,1,0:T(8,128)(2,1)S(1)}, u32[]{:S(2)}, u32[]{:S(2)}) %collective-permute-start.3) | collective-permute-done | bytes 426016 | tf_op jit(solution)/shard_map/ppermute | solution.py:532
  44.9 8.1 %collective-permute-done.4.refs_2_ = bf16[2,208,512]{2,1,0:T(8,128)(2,1)S(1)} collective-permute-done((bf16[2,208,512]{2,1,0:T(8,128)(2,1)S(1)}, bf16[2,208,512]{2,1,0:T(8,128)(2,1)S(1)}, u32[]{:S(2)}, u32[]{:S(2)}) %collective-permute-start.4) | collective-permute-done | bytes 426016 | tf_op jit(solution)/shard_map/ppermute | solution.py:532
  52.9 1.6 collective-permute-done.5.refs_3_
  54.6 8.0 %collective-permute-done.6.refs_4_ = bf16[256,1536]{1,0:T(8,128)(2,1)S(1)} collective-permute-done((bf16[256,1536]{1,0:T(8,128)(2,1)S(1)}, bf16[256,1536]{1,0:T(8,128)(2,1)S(1)}, u32[]{:S(2)}, u32[]{:S(2)}) %collective-permute-start.6) | collective-permute-done | bytes 786464 | tf_op jit(solution)/shard_map/ppermute | solution.py:634
  68.2 17.4 %collective-permute-done.9.refs_1_ = bf16[256,1536]{1,0:T(8,128)(2,1)S(1)} collective-permute-done((bf16[256,1536]{1,0:T(8,128)(2,1)S(1)}, bf16[256,1536]{1,0:T(8,128)(2,1)S(1)}, u32[]{:S(2)}, u32[]{:S(2)}) %collective-permute-start.9) | collective-permute-done | bytes 786464 | tf_op jit(solution)/shard_map/ppermute | solution.py:532
  86.0 1.6 collective-permute-start.12
  90.3 2.4 collective-permute-start.16
  92.8 11.2 %collective-permute-done.14 = bf16[2,48,1024]{2,1,0:T(8,128)(2,1)S(1)} collective-permute-done((bf16[2,48,1024]{2,1,0:T(8,128)(2,1)}, bf16[2,48,1024]{2,1,0:T(8,128)(2,1)S(1)}, u32[]{:S(2)}, u32[]{:S(2)}) %collective-permute-start.14) | collective-permute-done | bytes 196640 | tf_op jit(solution)/shard_map/ppermute | solution.py:532
  103.9 2.3 collective-permute-done.16
  117.5 7.6 %project_qkv.1.q_ref.kv_ref = bf16[2048,512]{1,0:T(8,128)(2,1)} custom-call(bf16[256,1536]{1,0:T(8,128)(2,1)S(1)} %copy-done.26, bf16[256,1536]{1,0:T(8,128)(2,1)S(1)} %collective-permute-done.9.refs_1_, bf16[256,1536]{1,0:T(8,128)(2,1)} %copy-done.11, bf16[256,1536]{1,0:T(8,128)(2,1)} %copy-done.15, bf16[256,1536]{1,0:T(8,128)(2,1)} %collective-permute-done.11.refs_4_, ...), custom_call_target="tpu_custom_call" | custom-call | flops 50331648 | bytes 155648 | tf_op jit(solution)/shard_map/project_qkv/pallas_call | solution.py:414
  125.1 1.6 copy-done
  126.7 15.5 %attn_fwd.1 = (bf16[2048,256]{1,0:T(8,128)(2,1)S(1)}, f32[8,2,256]{2,1,0:T(2,128)S(1)}) custom-call(s32[8,8]{1,0:T(8,128)S(1)} %and_convert_fusion.need, bf16[2048,512]{1,0:T(8,128)(2,1)S(1)} %copy-done, bf16[2048,512]{1,0:T(8,128)(2,1)S(1)} %copy-done, f32[8,1,256]{2,1,0:T(1,128)S(1)} %bitcast.193, f32[8,1,256]{2,1,0:T(1,128)S(1)} %bitcast.197, ...), custom_call_target="tpu_custom_call" | custom-call | flops 67108864 | bytes 131072 | tf_op jit(solution)/shard_map/attn_fwd/pallas_call | solution.py:176
  143.6 2.3 collective-permute-done.24
  147.6 1.6 collective-permute-start.26
  149.7 5.6 collective-permute-done.25.refs_1_
  155.3 6.0 %collective-permute-done.26.refs_2_ = bf16[2,256,256]{2,1,0:T(8,128)(2,1)S(1)} collective-permute-done((bf16[2,256,256]{2,1,0:T(8,128)(2,1)S(1)}, bf16[2,256,256]{2,1,0:T(8,128)(2,1)S(1)}, u32[]{:S(2)}, u32[]{:S(2)}) %collective-permute-start.26) | collective-permute-done | bytes 262176 | tf_op jit(solution)/shard_map/ppermute | solution.py:532
  161.8 5.8 %out_project.1 = (f32[256,1536]{1,0:T(8,128)}, bf16[256,1536]{1,0:T(8,128)(2,1)}) custom-call(bf16[2,256,256]{2,1,0:T(8,128)(2,1)S(1)} %pad_maximum_fusion.14.refs_0_, bf16[2,256,256]{2,1,0:T(8,128)(2,1)S(1)} %collective-permute-done.25.refs_1_, bf16[2,256,256]{2,1,0:T(8,128)(2,1)S(1)} %collective-permute-done.26.refs_2_, ...), custom_call_target="tpu_custom_call" | custom-call | flops 18874368 | bytes 139360 | tf_op jit(solution)/shard_map/out_project/pallas_call | solution.py:414
  171.8 1.9 copy-done.39
  175.3 4.7 ff.4
  180.0 9.8 %collective-permute-done.35.n0.refs_1_ = bf16[256,1536]{1,0:T(8,128)(2,1)} collective-permute-done((bf16[256,1536]{1,0:T(8,128)(2,1)}, bf16[256,1536]{1,0:T(8,128)(2,1)}, u32[]{:S(2)}, u32[]{:S(2)}) %collective-permute-start.35) | collective-permute-done | bytes 786464 | tf_op jit(solution)/shard_map/ppermute | solution.py:532
  198.8 5.8 %ff.5 = (bf16[2,256,512]{2,1,0:T(8,128)(2,1)S(1)}, bf16[2,256,1024]{2,1,0:T(8,128)(2,1)S(1)}, f32[256,1536]{1,0:T(8,128)S(1)}, bf16[256,1536]{1,0:T(8,128)(2,1)S(1)}) custom-call(bf16[256,1536]{1,0:T(8,128)(2,1)} %collective-permute-done.35.n0.refs_1_, bf16[256,1536]{1,0:T(8,128)(2,1)S(1)} %collective-permute-done.42.n1.refs_5_, ...), custom_call_target="tpu_custom_call" | custom-call | flops 62914560 | bytes 196608 | tf_op jit(solution)/shard_map/ff/pallas_call | solution.py:344
  206.4 6.5 %ff.6 = (bf16[2,256,512]{2,1,0:T(8,128)(2,1)S(1)}, bf16[2,256,1024]{2,1,0:T(8,128)(2,1)S(1)}, f32[256,1536]{1,0:T(8,128)S(1)}, bf16[256,1536]{1,0:T(8,128)(2,1)S(1)}) custom-call(bf16[256,1536]{1,0:T(8,128)(2,1)} %collective-permute-done.36.n0.refs_2_, bf16[256,1536]{1,0:T(8,128)(2,1)S(1)} %collective-permute-done.43.n1.refs_6_, ...), custom_call_target="tpu_custom_call" | custom-call | flops 62914560 | bytes 196608 | tf_op jit(solution)/shard_map/ff/pallas_call | solution.py:344
  217.6 4.7 ff.7
  228.8 16.8 %ff_weight.1 = (bf16[4,8,48,1024]{3,2,1,0:T(8,128)(2,1)}, bf16[512,1536]{1,0:T(8,128)(2,1)}) custom-call(bf16[256,1536]{1,0:T(8,128)(2,1)} %get-tuple-element.338.n0.refs_0_, bf16[256,1536]{1,0:T(8,128)(2,1)} %collective-permute-done.35.n0.refs_1_, bf16[256,1536]{1,0:T(8,128)(2,1)} %collective-permute-done.36.n0.refs_2_, bf16[256,1536]{1,0:T(8,128)(2,1)} %copy-done.17, ...), custom_call_target="tpu_custom_call" | custom-call | flops 150994944 | bytes 393216 | tf_op jit(solution)/shard_map/ff_weight/pallas_call | solution.py:391
  245.7 16.8 %collective-permute-done.51.refs_10_ = bf16[256,1536]{1,0:T(8,128)(2,1)} collective-permute-done((bf16[256,1536]{1,0:T(8,128)(2,1)S(1)}, bf16[256,1536]{1,0:T(8,128)(2,1)}, u32[]{:S(2)}, u32[]{:S(2)}) %collective-permute-start.51) | collective-permute-done | bytes 786464 | tf_op jit(solution)/shard_map/ppermute | solution.py:532
  262.5 7.4 %branch.1 = (f32[256,1536]{1,0:T(8,128)}, bf16[256,1536]{1,0:T(8,128)(2,1)}, bf16[2,4,256,256]{3,2,1,0:T(8,128)(2,1)}) custom-call(bf16[192,1536]{1,0:T(8,128)(2,1)} %refs_0_.1, bf16[192,1536]{1,0:T(8,128)(2,1)S(1)} %copy-done.21, bf16[192,1536]{1,0:T(8,128)(2,1)S(1)} %copy-done.24, bf16[192,1536]{1,0:T(8,128)(2,1)} %copy-done.62, ...), custom_call_target="tpu_custom_call" | custom-call | flops 18874368 | bytes 225376 | tf_op jit(solution)/shard_map/branch/pallas_call | solution.py:414
  273.7 8.3 %back_project.2 = (f32[4,256,1536]{2,1,0:T(8,128)}, bf16[4,256,1536]{2,1,0:T(8,128)(2,1)}) custom-call(bf16[2,256,512]{2,1,0:T(8,128)(2,1)S(1)} %copy-done.43, bf16[2,256,512]{2,1,0:T(8,128)(2,1)S(1)} %copy-done.45, bf16[2,256,512]{2,1,0:T(8,128)(2,1)S(1)} %copy-done.47, bf16[2,256,512]{2,1,0:T(8,128)(2,1)} %copy-done.48, bf16[512,1536]{1,0:T(8,128)(2,1)} %refs_4_.3), custom_call_target="tpu_custom_call" | custom-call | flops 50331648 | bytes 204800 | tf_op jit(solution)/shard_map/back_project/pallas_call | solution.py:414
  286.0 5.7 collective-permute-done.54
  292.5 4.7 collective-permute-done.56
  299.9 19.9 %attn_bwd.1.refs_8_.refs_0_ = bf16[2048,512]{1,0:T(8,128)(2,1)S(1)} custom-call(s32[8,8]{1,0:T(8,128)S(1)} %and_convert_fusion.need, bf16[2048,512]{1,0:T(8,128)(2,1)} %project_qkv.1.q_ref.kv_ref, bf16[2048,512]{1,0:T(8,128)(2,1)} %project_qkv.1.q_ref.kv_ref, f32[8,1,256]{2,1,0:T(1,128)S(1)} %bitcast.195, f32[8,1,256]{2,1,0:T(1,128)S(1)} %bitcast.199, ...), custom_call_target="tpu_custom_call" | custom-call | flops 167772160 | bytes 131072 | tf_op jit(solution)/shard_map/attn_bwd/pallas_call | solution.py:193
  319.8 2.1 slice.440
  322.5 1.8 slice.441
  325.3 4.6 add_convert_fusion.4
  333.5 7.6 %qkv_weight.1 = bf16[4,8,48,384]{3,2,1,0:T(8,128)(2,1)} custom-call(bf16[256,1536]{1,0:T(8,128)(2,1)S(1)} %copy-done.27, bf16[256,1536]{1,0:T(8,128)(2,1)S(1)} %copy-done.10, bf16[256,1536]{1,0:T(8,128)(2,1)S(1)} %copy-done.12, bf16[256,1536]{1,0:T(8,128)(2,1)S(1)} %copy-done.16, bf16[256,1536]{1,0:T(8,128)(2,1)} %collective-permute-done.11.refs_4_, ...), custom_call_target="tpu_custom_call" | custom-call | flops 100663296 | bytes 196608 | tf_op jit(solution)/shard_map/qkv_weight/pallas_call | solution.py:512
  348.7 8.6 %back_project.3 = (f32[4,256,1536]{2,1,0:T(8,128)}, bf16[4,256,1536]{2,1,0:T(8,128)(2,1)}) custom-call(bf16[2048,512]{1,0:T(8,128)(2,1)} %copy-done.2, bf16[1536,512]{1,0:T(8,128)(2,1)S(1)} %copy-done.8), custom_call_target="tpu_custom_call" | custom-call | flops 50331648 | bytes 204800 | tf_op jit(solution)/shard_map/back_project/pallas_call | solution.py:414
  359.5 6.8 %collective-permute-done.69 = bf16[256,1536]{1,0:T(8,128)(2,1)S(1)} collective-permute-done((bf16[256,1536]{1,0:T(8,128)(2,1)S(1)}, bf16[256,1536]{1,0:T(8,128)(2,1)S(1)}, u32[]{:S(2)}, u32[]{:S(2)}) %collective-permute-start.69) | collective-permute-done | bytes 786464 | tf_op jit(solution)/shard_map/ppermute | solution.py:532
  372.1 6.0 %out_weight.1 = bf16[192,1536]{1,0:T(8,128)(2,1)} custom-call(bf16[2048,256]{1,0:T(8,128)(2,1)} %copy-done.5, bf16[256,1536]{1,0:T(8,128)(2,1)S(1)} %copy-done.58, bf16[256,1536]{1,0:T(8,128)(2,1)} %collective-permute-done.58.refs_2_, bf16[256,1536]{1,0:T(8,128)(2,1)} %collective-permute-done.59.refs_3_, ...), custom_call_target="tpu_custom_call" | custom-call | flops 50331648 | bytes 147456 | tf_op jit(solution)/shard_map/out_weight/pallas_call | solution.py:884
  378.0 6.3 %fusion.10 = (bf16[256,1536]{1,0:T(8,128)(2,1)}, bf16[256,1536]{1,0:T(8,128)(2,1)}, bf16[256,1536]{1,0:T(8,128)(2,1)}, f32[256,1536]{1,0:T(8,128)}) fusion(f32[4,256,1536]{2,1,0:T(8,128)} %get-tuple-element.453, bf16[4,256,1536]{2,1,0:T(8,128)(2,1)} %collective-permute-done.74), kind=kLoop, calls=%fused_computation.31 | loop fusion | flops 4325376 | bytes 13369344 | tf_op jit(solution)/shard_map/convert_element_type | solution.py:901
  385.7 1.9 collective-permute-start.78
  387.6 4.0 collective-permute-start.80
  395.4 16.4 %collective-permute-done.78.refs_2_ = bf16[8,48,1024]{2,1,0:T(8,128)(2,1)S(1)} collective-permute-done((bf16[8,48,1024]{2,1,0:T(8,128)(2,1)S(1)}, bf16[8,48,1024]{2,1,0:T(8,128)(2,1)S(1)}, u32[]{:S(2)}, u32[]{:S(2)}) %collective-permute-start.78) | collective-permute-done | bytes 786464 | tf_op jit(solution)/shard_map/ppermute | solution.py:585
  411.8 3.6 collective-permute-start.79
  415.5 3.1 collective-permute-start.81
  418.6 3.7 add_convert_fusion
  422.3 4.8 collective-permute-done.76
  428.5 4.1 reduce-scatter.11.cloned.1.call-done
  432.6 7.9 %collective-permute-done.79.refs_1_ = bf16[8,48,1024]{2,1,0:T(8,128)(2,1)} collective-permute-done((bf16[8,48,1024]{2,1,0:T(8,128)(2,1)S(1)}, bf16[8,48,1024]{2,1,0:T(8,128)(2,1)}, u32[]{:S(2)}, u32[]{:S(2)}) %collective-permute-start.79) | collective-permute-done | bytes 786464 | tf_op jit(solution)/shard_map/ppermute | solution.py:585
  440.5 1.7 collective-permute-done.81.refs_5_
  443.3 2.8 collective-permute-start.86
  446.2 3.9 collective-permute-start.87
  450.1 2.9 fusion.2
  453.2 3.3 fusion.6
  461.9 26.5 %all-gather.10.cloned.1.call-done = bf16[512,1536]{1,0:T(8,128)(2,1)} async-done(((bf16[128,1536]{1,0:T(8,128)(2,1)}), bf16[512,1536]{1,0:T(8,128)(2,1)}) %all-gather.10.cloned.1.call-update) | async-done | bytes 1572880 | tf_op jit(solution)/shard_map/all_gather | solution.py:905
  488.4 3.5 convert_element_type.240
  492.9 3.2 collective-permute-start.89
  498.6 3.9 collective-permute-start.91
  502.6 5.0 place_columns.3
  507.6 2.7 multiply_reduce_fusion.1
  512.3 9.5 %collective-permute-done.89 = bf16[128,1536]{1,0:T(8,128)(2,1)} collective-permute-done((bf16[128,1536]{1,0:T(8,128)(2,1)}, bf16[128,1536]{1,0:T(8,128)(2,1)}, u32[]{:S(2)}, u32[]{:S(2)}) %collective-permute-start.89) | collective-permute-done | bytes 393248 | tf_op jit(solution)/shard_map/ppermute | solution.py:641
  523.9 33.2 %collective-permute-done.91 = bf16[128,1536]{1,0:T(8,128)(2,1)S(1)} collective-permute-done((bf16[128,1536]{1,0:T(8,128)(2,1)S(1)}, bf16[128,1536]{1,0:T(8,128)(2,1)S(1)}, u32[]{:S(2)}, u32[]{:S(2)}) %collective-permute-start.91) | collective-permute-done | bytes 393248 | tf_op jit(solution)/shard_map/ppermute | solution.py:641
  560.8 3.3 place_columns.2
  568.0 1.6 place_rows.1
  (508 shorter events, 136.3 us)
Async XLA Ops:
  7.2 164.6 %all-gather.6.cloned.1.call-start = ((), (), s32[]{:S(2)}) async-start(), calls=%async_computation.4 | async-start | bytes 3932160 | tf_op jit(solution)/shard_map/all_gather | solution.py:757
  7.2 15.3 %collective-permute-start.1 = (bf16[192,1536]{1,0:T(8,128)(2,1)}, bf16[192,1536]{1,0:T(8,128)(2,1)S(1)}, u32[]{:S(2)}, u32[]{:S(2)}) collective-permute-start(bf16[192,1536]{1,0:T(8,128)(2,1)} %refs_0_.1), channel_id=1, source_target_pairs={{0,4},{4,0},{8,12},{12,8},{1,5},{5,1},{9,13},{13,9},{2,6},{6,2},{1... | collective-permute-start | bytes 1769480 | tf_op jit(solution)/shard_map/ppermute | solution.py:532
  8.8 15.0 %collective-permute-start.2 = (bf16[192,1536]{1,0:T(8,128)(2,1)}, bf16[192,1536]{1,0:T(8,128)(2,1)S(1)}, u32[]{:S(2)}, u32[]{:S(2)}) collective-permute-start(bf16[192,1536]{1,0:T(8,128)(2,1)} %refs_0_.1), channel_id=1, source_target_pairs={{0,8},{4,12},{8,0},{12,4},{1,9},{5,13},{9,1},{13,5},{2,10},{6,14},... | collective-permute-start | bytes 1769480 | tf_op jit(solution)/shard_map/ppermute | solution.py:532
  24.6 37.9 %collective-permute-start.6 = (bf16[256,1536]{1,0:T(8,128)(2,1)S(1)}, bf16[256,1536]{1,0:T(8,128)(2,1)S(1)}, u32[]{:S(2)}, u32[]{:S(2)}) collective-permute-start(bf16[256,1536]{1,0:T(8,128)(2,1)S(1)} %pad_maximum_fusion.1), channel_id=1, source_target_pairs={{0,0},{1,2},{2,16},{3,18},{16,1},{17,3},{18,17},{19,19},{4,4},{5,6... | collective-permute-start | bytes 2359304 | tf_op jit(solution)/shard_map/ppermute | solution.py:634
  32.1 30.5 %collective-permute-start.7 = (bf16[256,1536]{1,0:T(8,128)(2,1)S(1)}, bf16[256,1536]{1,0:T(8,128)(2,1)S(1)}, u32[]{:S(2)}, u32[]{:S(2)}) collective-permute-start(bf16[256,1536]{1,0:T(8,128)(2,1)S(1)} %pad_maximum_fusion.2), channel_id=1, source_target_pairs={{0,2},{1,0},{2,18},{3,16},{16,3},{17,1},{18,19},{19,17},{4,6},{5,4... | collective-permute-start | bytes 2359304 | tf_op jit(solution)/shard_map/ppermute | solution.py:634
  32.8 20.1 %collective-permute-start.4 = (bf16[2,208,512]{2,1,0:T(8,128)(2,1)S(1)}, bf16[2,208,512]{2,1,0:T(8,128)(2,1)S(1)}, u32[]{:S(2)}, u32[]{:S(2)}) collective-permute-start(bf16[2,208,512]{2,1,0:T(8,128)(2,1)S(1)} %get-tuple-element.259), channel_id=1, source_target_pairs={{0,8},{4,12},{8,0},{12,4},{1,9},{5,13},{9,1},{13,5},{2,10},{6,14},... | collective-permute-start | bytes 1277960 | tf_op jit(solution)/shard_map/ppermute | solution.py:532
  34.3 20.2 %collective-permute-start.5 = (bf16[2,208,512]{2,1,0:T(8,128)(2,1)S(1)}, bf16[2,208,512]{2,1,0:T(8,128)(2,1)S(1)}, u32[]{:S(2)}, u32[]{:S(2)}) collective-permute-start(bf16[2,208,512]{2,1,0:T(8,128)(2,1)S(1)} %get-tuple-element.260), channel_id=1, source_target_pairs={{0,12},{4,8},{8,4},{12,0},{1,13},{5,9},{9,5},{13,1},{2,14},{6,10},... | collective-permute-start | bytes 1277960 | tf_op jit(solution)/shard_map/ppermute | solution.py:532
  65.8 19.9 %collective-permute-start.9 = (bf16[256,1536]{1,0:T(8,128)(2,1)S(1)}, bf16[256,1536]{1,0:T(8,128)(2,1)S(1)}, u32[]{:S(2)}, u32[]{:S(2)}) collective-permute-start(bf16[256,1536]{1,0:T(8,128)(2,1)S(1)} %get-tuple-element.294.refs_0_), channel_id=1, source_target_pairs={{0,4},{4,0},{8,12},{12,8},{1,5},{5,1},{9,13},{13,9},{2,6},{6,2},{1... | collective-permute-start | bytes 2359304 | tf_op jit(solution)/shard_map/ppermute | solution.py:532
  66.3 19.6 %collective-permute-start.10 = (bf16[256,1536]{1,0:T(8,128)(2,1)S(1)}, bf16[256,1536]{1,0:T(8,128)(2,1)S(1)}, u32[]{:S(2)}, u32[]{:S(2)}) collective-permute-start(bf16[256,1536]{1,0:T(8,128)(2,1)S(1)} %get-tuple-element.294.refs_0_), channel_id=1, source_target_pairs={{0,8},{4,12},{8,0},{12,4},{1,9},{5,13},{9,1},{13,5},{2,10},{6,14},... | collective-permute-start | bytes 2359304 | tf_op jit(solution)/shard_map/ppermute | solution.py:532
  67.8 18.1 %collective-permute-start.11 = (bf16[256,1536]{1,0:T(8,128)(2,1)S(1)}, bf16[256,1536]{1,0:T(8,128)(2,1)}, u32[]{:S(2)}, u32[]{:S(2)}) collective-permute-start(bf16[256,1536]{1,0:T(8,128)(2,1)S(1)} %get-tuple-element.294.refs_0_), channel_id=1, source_target_pairs={{0,16},{16,0},{1,17},{17,1},{2,18},{18,2},{3,19},{19,3},{4,20},{20... | collective-permute-start | bytes 2359304 | tf_op jit(solution)/shard_map/ppermute | solution.py:532
  86.0 20.2 %collective-permute-start.12 = (bf16[128,1536]{1,0:T(8,128)(2,1)S(1)}, bf16[128,1536]{1,0:T(8,128)(2,1)S(1)}, u32[]{:S(2)}, u32[]{:S(2)}) collective-permute-start(bf16[128,1536]{1,0:T(8,128)(2,1)S(1)} %slice.404), channel_id=1, source_target_pairs={{0,8},{4,12},{8,0},{12,4},{1,9},{5,13},{9,1},{13,5},{2,10},{6,14},... | collective-permute-start | bytes 1179656 | tf_op jit(solution)/shard_map/ppermute | solution.py:532
  87.6 18.6 %collective-permute-start.13 = (bf16[128,1536]{1,0:T(8,128)(2,1)S(1)}, bf16[128,1536]{1,0:T(8,128)(2,1)S(1)}, u32[]{:S(2)}, u32[]{:S(2)}) collective-permute-start(bf16[128,1536]{1,0:T(8,128)(2,1)S(1)} %slice.405), channel_id=1, source_target_pairs={{0,4},{4,0},{8,12},{12,8},{1,5},{5,1},{9,13},{13,9},{2,6},{6,2},{1... | collective-permute-start | bytes 1179656 | tf_op jit(solution)/shard_map/ppermute | solution.py:532
  89.2 14.7 %collective-permute-start.14 = (bf16[2,48,1024]{2,1,0:T(8,128)(2,1)}, bf16[2,48,1024]{2,1,0:T(8,128)(2,1)S(1)}, u32[]{:S(2)}, u32[]{:S(2)}) collective-permute-start(bf16[2,48,1024]{2,1,0:T(8,128)(2,1)} %pad_maximum_fusion.23), channel_id=1, source_target_pairs={{0,4},{4,0},{8,12},{12,8},{1,5},{5,1},{9,13},{13,9},{2,6},{6,2},{1... | collective-permute-start | bytes 589832 | tf_op jit(solution)/shard_map/ppermute | solution.py:532
  90.3 15.9 %collective-permute-start.16 = (bf16[2,48,1024]{2,1,0:T(8,128)(2,1)}, bf16[2,48,1024]{2,1,0:T(8,128)(2,1)S(1)}, u32[]{:S(2)}, u32[]{:S(2)}) collective-permute-start(bf16[2,48,1024]{2,1,0:T(8,128)(2,1)} %pad_maximum_fusion.25), channel_id=1, source_target_pairs={{0,12},{4,8},{8,4},{12,0},{1,13},{5,9},{9,5},{13,1},{2,14},{6,10},... | collective-permute-start | bytes 589832 | tf_op jit(solution)/shard_map/ppermute | solution.py:532
  103.9 43.6 %collective-permute-start.28 = (bf16[192,1536]{1,0:T(8,128)(2,1)}, bf16[192,1536]{1,0:T(8,128)(2,1)}, u32[]{:S(2)}, u32[]{:S(2)}) collective-permute-start(bf16[192,1536]{1,0:T(8,128)(2,1)} %refs_0_.1), channel_id=1, source_target_pairs={{0,16},{16,0},{1,17},{17,1},{2,18},{18,2},{3,19},{19,3},{4,20},{20... | collective-permute-start | bytes 1769480 | tf_op jit(solution)/shard_map/ppermute | solution.py:532
  108.1 234.0 %reduce-scatter.5.cloned.1.call-start = ((), (), s32[]{:S(2)}) async-start(), calls=%async_computation.5 | async-start | bytes 3932160 | tf_op jit(solution)/shard_map/reduce_scatter | solution.py:813
  111.0 31.8 %collective-permute-start.20 = (bf16[256,1536]{1,0:T(8,128)(2,1)S(1)}, bf16[256,1536]{1,0:T(8,128)(2,1)S(1)}, u32[]{:S(2)}, u32[]{:S(2)}) collective-permute-start(bf16[256,1536]{1,0:T(8,128)(2,1)S(1)} %get-tuple-element.309.c0.refs_8_.refs_13_), channel_id=1, source_target_pairs={{0,4},{4,0},{8,12},{12,8},{1,5},{5,1},{9,13},{13,9},{2,6},{6,2},{1... | collective-permute-start | bytes 2359304 | tf_op jit(solution)/shard_map/ppermute | solution.py:532
  112.4 30.4 %collective-permute-start.21 = (bf16[256,1536]{1,0:T(8,128)(2,1)S(1)}, bf16[256,1536]{1,0:T(8,128)(2,1)}, u32[]{:S(2)}, u32[]{:S(2)}) collective-permute-start(bf16[256,1536]{1,0:T(8,128)(2,1)S(1)} %get-tuple-element.309.c0.refs_8_.refs_13_), channel_id=1, source_target_pairs={{0,8},{4,12},{8,0},{12,4},{1,9},{5,13},{9,1},{13,5},{2,10},{6,14},... | collective-permute-start | bytes 2359304 | tf_op jit(solution)/shard_map/ppermute | solution.py:532
  115.0 27.2 %collective-permute-start.22 = (bf16[96,1536]{1,0:T(8,128)(2,1)S(1)}, bf16[96,1536]{1,0:T(8,128)(2,1)S(1)}, u32[]{:S(2)}, u32[]{:S(2)}) collective-permute-start(bf16[96,1536]{1,0:T(8,128)(2,1)S(1)} %slice.407), channel_id=1, source_target_pairs={{0,8},{4,12},{8,0},{12,4},{1,9},{5,13},{9,1},{13,5},{2,10},{6,14},... | collective-permute-start | bytes 884744 | tf_op jit(solution)/shard_map/ppermute | solution.py:532
  116.6 25.7 %collective-permute-start.23 = (bf16[96,1536]{1,0:T(8,128)(2,1)S(1)}, bf16[96,1536]{1,0:T(8,128)(2,1)S(1)}, u32[]{:S(2)}, u32[]{:S(2)}) collective-permute-start(bf16[96,1536]{1,0:T(8,128)(2,1)S(1)} %slice.408), channel_id=1, source_target_pairs={{0,4},{4,0},{8,12},{12,8},{1,5},{5,1},{9,13},{13,9},{2,6},{6,2},{1... | collective-permute-start | bytes 884744 | tf_op jit(solution)/shard_map/ppermute | solution.py:532
  149.6 18.0 %collective-permute-start.32 = (bf16[256,1536]{1,0:T(8,128)(2,1)S(1)}, bf16[256,1536]{1,0:T(8,128)(2,1)S(1)}, u32[]{:S(2)}, u32[]{:S(2)}) collective-permute-start(bf16[256,1536]{1,0:T(8,128)(2,1)S(1)} %get-tuple-element.309.c0.refs_8_.refs_13_), channel_id=1, source_target_pairs={{0,16},{16,0},{1,17},{17,1},{2,18},{18,2},{3,19},{19,3},{4,20},{20... | collective-permute-start | bytes 2359304 | tf_op jit(solution)/shard_map/ppermute | solution.py:532
  169.6 20.2 %collective-permute-start.35 = (bf16[256,1536]{1,0:T(8,128)(2,1)}, bf16[256,1536]{1,0:T(8,128)(2,1)}, u32[]{:S(2)}, u32[]{:S(2)}) collective-permute-start(bf16[256,1536]{1,0:T(8,128)(2,1)} %get-tuple-element.338.n0.refs_0_), channel_id=1, source_target_pairs={{0,4},{4,0},{8,12},{12,8},{1,5},{5,1},{9,13},{13,9},{2,6},{6,2},{1... | collective-permute-start | bytes 2359304 | tf_op jit(solution)/shard_map/ppermute | solution.py:532
  170.8 20.0 %collective-permute-start.36 = (bf16[256,1536]{1,0:T(8,128)(2,1)}, bf16[256,1536]{1,0:T(8,128)(2,1)}, u32[]{:S(2)}, u32[]{:S(2)}) collective-permute-start(bf16[256,1536]{1,0:T(8,128)(2,1)} %get-tuple-element.338.n0.refs_0_), channel_id=1, source_target_pairs={{0,8},{4,12},{8,0},{12,4},{1,9},{5,13},{9,1},{13,5},{2,10},{6,14},... | collective-permute-start | bytes 2359304 | tf_op jit(solution)/shard_map/ppermute | solution.py:532
  190.8 15.6 %collective-permute-start.43 = (bf16[256,1536]{1,0:T(8,128)(2,1)}, bf16[256,1536]{1,0:T(8,128)(2,1)S(1)}, u32[]{:S(2)}, u32[]{:S(2)}) collective-permute-start(bf16[256,1536]{1,0:T(8,128)(2,1)} %collective-permute-done.36.n0.refs_2_), channel_id=1, source_target_pairs={{0,16},{16,0},{1,17},{17,1},{2,18},{18,2},{3,19},{19,3},{4,20},{20... | collective-permute-start | bytes 2359304 | tf_op jit(solution)/shard_map/ppermute | solution.py:532
  193.4 20.6 %collective-permute-start.38 = (bf16[128,1536]{1,0:T(8,128)(2,1)S(1)}, bf16[128,1536]{1,0:T(8,128)(2,1)S(1)}, u32[]{:S(2)}, u32[]{:S(2)}) collective-permute-start(bf16[128,1536]{1,0:T(8,128)(2,1)S(1)} %slice.423), channel_id=1, source_target_pairs={{0,8},{4,12},{8,0},{12,4},{1,9},{5,13},{9,1},{13,5},{2,10},{6,14},... | collective-permute-start | bytes 1179656 | tf_op jit(solution)/shard_map/ppermute | solution.py:532
  194.3 19.6 %collective-permute-start.39 = (bf16[128,1536]{1,0:T(8,128)(2,1)S(1)}, bf16[128,1536]{1,0:T(8,128)(2,1)S(1)}, u32[]{:S(2)}, u32[]{:S(2)}) collective-permute-start(bf16[128,1536]{1,0:T(8,128)(2,1)S(1)} %slice.424), channel_id=1, source_target_pairs={{0,4},{4,0},{8,12},{12,8},{1,5},{5,1},{9,13},{13,9},{2,6},{6,2},{1... | collective-permute-start | bytes 1179656 | tf_op jit(solution)/shard_map/ppermute | solution.py:532
  195.8 18.2 %collective-permute-start.40 = (bf16[128,1536]{1,0:T(8,128)(2,1)S(1)}, bf16[128,1536]{1,0:T(8,128)(2,1)S(1)}, u32[]{:S(2)}, u32[]{:S(2)}) collective-permute-start(bf16[128,1536]{1,0:T(8,128)(2,1)S(1)} %slice.425), channel_id=1, source_target_pairs={{0,8},{4,12},{8,0},{12,4},{1,9},{5,13},{9,1},{13,5},{2,10},{6,14},... | collective-permute-start | bytes 1179656 | tf_op jit(solution)/shard_map/ppermute | solution.py:532
  197.4 16.6 %collective-permute-start.41 = (bf16[128,1536]{1,0:T(8,128)(2,1)S(1)}, bf16[128,1536]{1,0:T(8,128)(2,1)S(1)}, u32[]{:S(2)}, u32[]{:S(2)}) collective-permute-start(bf16[128,1536]{1,0:T(8,128)(2,1)S(1)} %slice.426), channel_id=1, source_target_pairs={{0,4},{4,0},{8,12},{12,8},{1,5},{5,1},{9,13},{13,9},{2,6},{6,2},{1... | collective-permute-start | bytes 1179656 | tf_op jit(solution)/shard_map/ppermute | solution.py:532
  225.3 20.5 %collective-permute-start.50 = (bf16[256,1536]{1,0:T(8,128)(2,1)S(1)}, bf16[256,1536]{1,0:T(8,128)(2,1)S(1)}, u32[]{:S(2)}, u32[]{:S(2)}) collective-permute-start(bf16[256,1536]{1,0:T(8,128)(2,1)S(1)} %add_convert_fusion.7), channel_id=1, source_target_pairs={{0,4},{4,0},{8,12},{12,8},{1,5},{5,1},{9,13},{13,9},{2,6},{6,2},{1... | collective-permute-start | bytes 2359304 | tf_op jit(solution)/shard_map/ppermute | solution.py:532
  226.3 36.3 %collective-permute-start.51 = (bf16[256,1536]{1,0:T(8,128)(2,1)S(1)}, bf16[256,1536]{1,0:T(8,128)(2,1)}, u32[]{:S(2)}, u32[]{:S(2)}) collective-permute-start(bf16[256,1536]{1,0:T(8,128)(2,1)S(1)} %add_convert_fusion.6), channel_id=1, source_target_pairs={{0,8},{4,12},{8,0},{12,4},{1,9},{5,13},{9,1},{13,5},{2,10},{6,14},... | collective-permute-start | bytes 2359304 | tf_op jit(solution)/shard_map/ppermute | solution.py:532
  227.7 34.9 %collective-permute-start.52 = (bf16[256,1536]{1,0:T(8,128)(2,1)S(1)}, bf16[256,1536]{1,0:T(8,128)(2,1)}, u32[]{:S(2)}, u32[]{:S(2)}) collective-permute-start(bf16[256,1536]{1,0:T(8,128)(2,1)S(1)} %add_convert_fusion.5), channel_id=1, source_target_pairs={{0,12},{4,8},{8,4},{12,0},{1,13},{5,9},{9,5},{13,1},{2,14},{6,10},... | collective-permute-start | bytes 2359304 | tf_op jit(solution)/shard_map/ppermute | solution.py:532
  271.2 113.2 %reduce-scatter.7.cloned.1.call-start = ((), (), s32[]{:S(2)}) async-start(), calls=%async_computation.6 | async-start | bytes 1966080 | tf_op jit(solution)/shard_map/reduce_scatter | solution.py:813
  282.1 15.2 %collective-permute-start.57 = (bf16[4,256,1536]{2,1,0:T(8,128)(2,1)}, bf16[4,256,1536]{2,1,0:T(8,128)(2,1)S(1)}, u32[]{:S(2)}, u32[]{:S(2)}) collective-permute-start(bf16[4,256,1536]{2,1,0:T(8,128)(2,1)} %get-tuple-element.418), channel_id=1, source_target_pairs={{0,16},{16,0},{1,17},{17,1},{2,18},{18,2},{3,19},{19,3},{4,20},{20... | collective-permute-start | bytes 9437192 | tf_op jit(solution)/shard_map/ppermute | solution.py:532
  297.2 22.5 %collective-permute-start.58 = (bf16[256,1536]{1,0:T(8,128)(2,1)S(1)}, bf16[256,1536]{1,0:T(8,128)(2,1)}, u32[]{:S(2)}, u32[]{:S(2)}) collective-permute-start(bf16[256,1536]{1,0:T(8,128)(2,1)S(1)} %copy-done.57), channel_id=1, source_target_pairs={{0,4},{4,0},{8,12},{12,8},{1,5},{5,1},{9,13},{13,9},{2,6},{6,2},{1... | collective-permute-start | bytes 2359304 | tf_op jit(solution)/shard_map/ppermute | solution.py:532
  298.2 21.5 %collective-permute-start.59 = (bf16[256,1536]{1,0:T(8,128)(2,1)S(1)}, bf16[256,1536]{1,0:T(8,128)(2,1)}, u32[]{:S(2)}, u32[]{:S(2)}) collective-permute-start(bf16[256,1536]{1,0:T(8,128)(2,1)S(1)} %copy-done.57), channel_id=1, source_target_pairs={{0,8},{4,12},{8,0},{12,4},{1,9},{5,13},{9,1},{13,5},{2,10},{6,14},... | collective-permute-start | bytes 2359304 | tf_op jit(solution)/shard_map/ppermute | solution.py:532
  321.8 19.3 %collective-permute-start.60 = (bf16[128,1536]{1,0:T(8,128)(2,1)}, bf16[128,1536]{1,0:T(8,128)(2,1)S(1)}, u32[]{:S(2)}, u32[]{:S(2)}) collective-permute-start(bf16[128,1536]{1,0:T(8,128)(2,1)} %slice.440), channel_id=1, source_target_pairs={{0,8},{4,12},{8,0},{12,4},{1,9},{5,13},{9,1},{13,5},{2,10},{6,14},... | collective-permute-start | bytes 1179656 | tf_op jit(solution)/shard_map/ppermute | solution.py:532
  324.3 17.2 %collective-permute-start.61 = (bf16[128,1536]{1,0:T(8,128)(2,1)}, bf16[128,1536]{1,0:T(8,128)(2,1)}, u32[]{:S(2)}, u32[]{:S(2)}) collective-permute-start(bf16[128,1536]{1,0:T(8,128)(2,1)} %slice.441), channel_id=1, source_target_pairs={{0,4},{4,0},{8,12},{12,8},{1,5},{5,1},{9,13},{13,9},{2,6},{6,2},{1... | collective-permute-start | bytes 1179656 | tf_op jit(solution)/shard_map/ppermute | solution.py:532
  333.3 89.0 %reduce-scatter.9.cloned.1.call-start = ((), (), s32[]{:S(2)}) async-start(), calls=%async_computation.7 | async-start | bytes 1474560 | tf_op jit(solution)/shard_map/reduce_scatter | solution.py:813
  341.1 18.4 %collective-permute-start.65 = (bf16[256,1536]{1,0:T(8,128)(2,1)}, bf16[256,1536]{1,0:T(8,128)(2,1)S(1)}, u32[]{:S(2)}, u32[]{:S(2)}) collective-permute-start(bf16[256,1536]{1,0:T(8,128)(2,1)} %collective-permute-done.58.refs_2_), channel_id=1, source_target_pairs={{0,16},{16,0},{1,17},{17,1},{2,18},{18,2},{3,19},{19,3},{4,20},{20... | collective-permute-start | bytes 2359304 | tf_op jit(solution)/shard_map/ppermute | solution.py:532
  341.5 18.0 %collective-permute-start.66 = (bf16[256,1536]{1,0:T(8,128)(2,1)}, bf16[256,1536]{1,0:T(8,128)(2,1)S(1)}, u32[]{:S(2)}, u32[]{:S(2)}) collective-permute-start(bf16[256,1536]{1,0:T(8,128)(2,1)} %collective-permute-done.59.refs_3_), channel_id=1, source_target_pairs={{0,16},{16,0},{1,17},{17,1},{2,18},{18,2},{3,19},{19,3},{4,20},{20... | collective-permute-start | bytes 2359304 | tf_op jit(solution)/shard_map/ppermute | solution.py:532
  343.4 16.1 %collective-permute-start.67 = (bf16[256,1536]{1,0:T(8,128)(2,1)S(1)}, bf16[256,1536]{1,0:T(8,128)(2,1)S(1)}, u32[]{:S(2)}, u32[]{:S(2)}) collective-permute-start(bf16[256,1536]{1,0:T(8,128)(2,1)S(1)} %constant_dynamic-update-slice_fusion.10.refs_4_), channel_id=1, source_target_pairs={{0,16},{16,0},{1,17},{17,1},{2,18},{18,2},{3,19},{19,3},{4,20},{20... | collective-permute-start | bytes 2359304 | tf_op jit(solution)/shard_map/ppermute | solution.py:532
  346.6 19.8 %collective-permute-start.69 = (bf16[256,1536]{1,0:T(8,128)(2,1)S(1)}, bf16[256,1536]{1,0:T(8,128)(2,1)S(1)}, u32[]{:S(2)}, u32[]{:S(2)}) collective-permute-start(bf16[256,1536]{1,0:T(8,128)(2,1)S(1)} %pad_maximum_fusion.4), channel_id=1, source_target_pairs={{0,4},{4,0},{8,12},{12,8},{1,5},{5,1},{9,13},{13,9},{2,6},{6,2},{1... | collective-permute-start | bytes 2359304 | tf_op jit(solution)/shard_map/ppermute | solution.py:532
  347.9 19.4 %collective-permute-start.70 = (bf16[256,1536]{1,0:T(8,128)(2,1)S(1)}, bf16[256,1536]{1,0:T(8,128)(2,1)S(1)}, u32[]{:S(2)}, u32[]{:S(2)}) collective-permute-start(bf16[256,1536]{1,0:T(8,128)(2,1)S(1)} %pad_maximum_fusion.5), channel_id=1, source_target_pairs={{0,8},{4,12},{8,0},{12,4},{1,9},{5,13},{9,1},{13,5},{2,10},{6,14},... | collective-permute-start | bytes 2359304 | tf_op jit(solution)/shard_map/ppermute | solution.py:532
  368.2 64.4 %reduce-scatter.11.cloned.1.call-start = ((), (), s32[]{:S(2)}) async-start(), calls=%async_computation.8 | async-start | bytes 737280 | tf_op jit(solution)/shard_map/reduce_scatter | solution.py:813
  368.5 15.9 %collective-permute-start.71 = (bf16[2,48,1024]{2,1,0:T(8,128)(2,1)}, bf16[2,48,1024]{2,1,0:T(8,128)(2,1)S(1)}, u32[]{:S(2)}, u32[]{:S(2)}) collective-permute-start(bf16[2,48,1024]{2,1,0:T(8,128)(2,1)} %pad_maximum_fusion.27), channel_id=1, source_target_pairs={{0,4},{4,0},{8,12},{12,8},{1,5},{5,1},{9,13},{13,9},{2,6},{6,2},{1... | collective-permute-start | bytes 589832 | tf_op jit(solution)/shard_map/ppermute | solution.py:532
  369.7 14.7 %collective-permute-start.72 = (bf16[2,48,1024]{2,1,0:T(8,128)(2,1)}, bf16[2,48,1024]{2,1,0:T(8,128)(2,1)}, u32[]{:S(2)}, u32[]{:S(2)}) collective-permute-start(bf16[2,48,1024]{2,1,0:T(8,128)(2,1)} %pad_maximum_fusion.28), channel_id=1, source_target_pairs={{0,8},{4,12},{8,0},{12,4},{1,9},{5,13},{9,1},{13,5},{2,10},{6,14},... | collective-permute-start | bytes 589832 | tf_op jit(solution)/shard_map/ppermute | solution.py:532
  384.4 104.0 %all-gather.10.cloned.1.call-start = ((), (), s32[]{:S(2)}) async-start(), calls=%async_computation.10 | async-start | bytes 1966080 | tf_op jit(solution)/shard_map/all_gather | solution.py:905
  385.7 26.1 %collective-permute-start.78 = (bf16[8,48,1024]{2,1,0:T(8,128)(2,1)S(1)}, bf16[8,48,1024]{2,1,0:T(8,128)(2,1)S(1)}, u32[]{:S(2)}, u32[]{:S(2)}) collective-permute-start(bf16[8,48,1024]{2,1,0:T(8,128)(2,1)S(1)} %bitcast.186), channel_id=1, source_target_pairs={{0,1},{1,2},{2,3},{4,5},{5,6},{6,7},{8,9},{9,10},{10,11},{12,13},{... | collective-permute-start | bytes 2359304 | tf_op jit(solution)/shard_map/ppermute | solution.py:585
  387.6 27.8 %collective-permute-start.80 = (bf16[8,48,1024]{2,1,0:T(8,128)(2,1)S(1)}, bf16[8,48,1024]{2,1,0:T(8,128)(2,1)S(1)}, u32[]{:S(2)}, u32[]{:S(2)}) collective-permute-start(bf16[8,48,1024]{2,1,0:T(8,128)(2,1)S(1)} %bitcast.187), channel_id=1, source_target_pairs={{1,0},{2,1},{3,2},{5,4},{6,5},{7,6},{9,8},{10,9},{11,10},{13,12},{... | collective-permute-start | bytes 2359304 | tf_op jit(solution)/shard_map/ppermute | solution.py:585
  391.8 30.5 %collective-permute-start.75 = (bf16[256,1536]{1,0:T(8,128)(2,1)}, bf16[256,1536]{1,0:T(8,128)(2,1)}, u32[]{:S(2)}, u32[]{:S(2)}) collective-permute-start(bf16[256,1536]{1,0:T(8,128)(2,1)} %get-tuple-element.456), channel_id=1, source_target_pairs={{0,4},{4,0},{8,12},{12,8},{1,5},{5,1},{9,13},{13,9},{2,6},{6,2},{1... | collective-permute-start | bytes 2359304 | tf_op jit(solution)/shard_map/ppermute | solution.py:532
  393.0 34.1 %collective-permute-start.76 = (bf16[256,1536]{1,0:T(8,128)(2,1)}, bf16[256,1536]{1,0:T(8,128)(2,1)}, u32[]{:S(2)}, u32[]{:S(2)}) collective-permute-start(bf16[256,1536]{1,0:T(8,128)(2,1)} %get-tuple-element.457), channel_id=1, source_target_pairs={{0,8},{4,12},{8,0},{12,4},{1,9},{5,13},{9,1},{13,5},{2,10},{6,14},... | collective-permute-start | bytes 2359304 | tf_op jit(solution)/shard_map/ppermute | solution.py:532
  394.3 34.3 %collective-permute-start.77 = (bf16[256,1536]{1,0:T(8,128)(2,1)}, bf16[256,1536]{1,0:T(8,128)(2,1)}, u32[]{:S(2)}, u32[]{:S(2)}) collective-permute-start(bf16[256,1536]{1,0:T(8,128)(2,1)} %get-tuple-element.458), channel_id=1, source_target_pairs={{0,12},{4,8},{8,4},{12,0},{1,13},{5,9},{9,5},{13,1},{2,14},{6,10},... | collective-permute-start | bytes 2359304 | tf_op jit(solution)/shard_map/ppermute | solution.py:532
  411.8 28.7 %collective-permute-start.79 = (bf16[8,48,1024]{2,1,0:T(8,128)(2,1)S(1)}, bf16[8,48,1024]{2,1,0:T(8,128)(2,1)}, u32[]{:S(2)}, u32[]{:S(2)}) collective-permute-start(bf16[8,48,1024]{2,1,0:T(8,128)(2,1)S(1)} %collective-permute-done.78.refs_2_), channel_id=1, source_target_pairs={{0,1},{1,2},{2,3},{4,5},{5,6},{6,7},{8,9},{9,10},{10,11},{12,13},{... | collective-permute-start | bytes 2359304 | tf_op jit(solution)/shard_map/ppermute | solution.py:585
  415.5 26.8 %collective-permute-start.81 = (bf16[8,48,1024]{2,1,0:T(8,128)(2,1)S(1)}, bf16[8,48,1024]{2,1,0:T(8,128)(2,1)}, u32[]{:S(2)}, u32[]{:S(2)}) collective-permute-start(bf16[8,48,1024]{2,1,0:T(8,128)(2,1)S(1)} %collective-permute-done.80.refs_4_), channel_id=1, source_target_pairs={{1,0},{2,1},{3,2},{5,4},{6,5},{7,6},{9,8},{10,9},{11,10},{13,12},{... | collective-permute-start | bytes 2359304 | tf_op jit(solution)/shard_map/ppermute | solution.py:585
  418.6 139.5 %all-gather.8.cloned.1.call-start = ((), (), s32[]{:S(2)}) async-start(), calls=%async_computation.9 | async-start | bytes 2211840 | tf_op jit(solution)/shard_map/all_gather | solution.py:920
  443.3 48.6 %collective-permute-start.86 = (bf16[8,48,1024]{2,1,0:T(8,128)(2,1)}, bf16[8,48,1024]{2,1,0:T(8,128)(2,1)}, u32[]{:S(2)}, u32[]{:S(2)}) collective-permute-start(bf16[8,48,1024]{2,1,0:T(8,128)(2,1)} %collective-permute-done.79.refs_1_), channel_id=1, source_target_pairs={{0,1},{1,2},{2,3},{4,5},{5,6},{6,7},{8,9},{9,10},{10,11},{12,13},{... | collective-permute-start | bytes 2359304 | tf_op jit(solution)/shard_map/ppermute | solution.py:585
  446.2 45.8 %collective-permute-start.87 = (bf16[8,48,1024]{2,1,0:T(8,128)(2,1)}, bf16[8,48,1024]{2,1,0:T(8,128)(2,1)}, u32[]{:S(2)}, u32[]{:S(2)}) collective-permute-start(bf16[8,48,1024]{2,1,0:T(8,128)(2,1)} %collective-permute-done.81.refs_5_), channel_id=1, source_target_pairs={{1,0},{2,1},{3,2},{5,4},{6,5},{7,6},{9,8},{10,9},{11,10},{13,12},{... | collective-permute-start | bytes 2359304 | tf_op jit(solution)/shard_map/ppermute | solution.py:585
  457.1 34.8 %collective-permute-start.83 = (bf16[2,48,384]{2,1,0:T(8,128)(2,1)}, bf16[2,48,384]{2,1,0:T(8,128)(2,1)S(1)}, u32[]{:S(2)}, u32[]{:S(2)}) collective-permute-start(bf16[2,48,384]{2,1,0:T(8,128)(2,1)} %pad_maximum_fusion.32), channel_id=1, source_target_pairs={{0,4},{4,0},{8,12},{12,8},{1,5},{5,1},{9,13},{13,9},{2,6},{6,2},{1... | collective-permute-start | bytes 221192 | tf_op jit(solution)/shard_map/ppermute | solution.py:532
  459.3 32.6 %collective-permute-start.84 = (bf16[2,48,384]{2,1,0:T(8,128)(2,1)}, bf16[2,48,384]{2,1,0:T(8,128)(2,1)}, u32[]{:S(2)}, u32[]{:S(2)}) collective-permute-start(bf16[2,48,384]{2,1,0:T(8,128)(2,1)} %pad_maximum_fusion.33), channel_id=1, source_target_pairs={{0,8},{4,12},{8,0},{12,4},{1,9},{5,13},{9,1},{13,5},{2,10},{6,14},... | collective-permute-start | bytes 221192 | tf_op jit(solution)/shard_map/ppermute | solution.py:532
  461.4 30.5 %collective-permute-start.85 = (bf16[2,48,384]{2,1,0:T(8,128)(2,1)}, bf16[2,48,384]{2,1,0:T(8,128)(2,1)}, u32[]{:S(2)}, u32[]{:S(2)}) collective-permute-start(bf16[2,48,384]{2,1,0:T(8,128)(2,1)} %pad_maximum_fusion.34), channel_id=1, source_target_pairs={{0,12},{4,8},{8,4},{12,0},{1,13},{5,9},{9,5},{13,1},{2,14},{6,10},... | collective-permute-start | bytes 221192 | tf_op jit(solution)/shard_map/ppermute | solution.py:532
  492.9 19.4 %collective-permute-start.88 = (bf16[128,1536]{1,0:T(8,128)(2,1)}, bf16[128,1536]{1,0:T(8,128)(2,1)}, u32[]{:S(2)}, u32[]{:S(2)}) collective-permute-start(bf16[128,1536]{1,0:T(8,128)(2,1)} %get-tuple-element.568), channel_id=1, source_target_pairs={{2,0},{0,1},{18,2},{16,3},{3,16},{1,17},{19,18},{17,19},{6,4},{4,5... | collective-permute-start | bytes 1179656 | tf_op jit(solution)/shard_map/ppermute | solution.py:641
  492.9 28.9 %collective-permute-start.89 = (bf16[128,1536]{1,0:T(8,128)(2,1)}, bf16[128,1536]{1,0:T(8,128)(2,1)}, u32[]{:S(2)}, u32[]{:S(2)}) collective-permute-start(bf16[128,1536]{1,0:T(8,128)(2,1)} %get-tuple-element.569), channel_id=1, source_target_pairs={{0,0},{2,1},{16,2},{18,3},{1,16},{3,17},{17,18},{19,19},{4,4},{6,5... | collective-permute-start | bytes 1179656 | tf_op jit(solution)/shard_map/ppermute | solution.py:641
  498.2 25.7 %collective-permute-start.90 = (bf16[128,1536]{1,0:T(8,128)(2,1)S(1)}, bf16[128,1536]{1,0:T(8,128)(2,1)S(1)}, u32[]{:S(2)}, u32[]{:S(2)}) collective-permute-start(bf16[128,1536]{1,0:T(8,128)(2,1)S(1)} %get-tuple-element.564), channel_id=1, source_target_pairs={{2,0},{0,1},{18,2},{16,3},{3,16},{1,17},{19,18},{17,19},{6,4},{4,5... | collective-permute-start | bytes 1179656 | tf_op jit(solution)/shard_map/ppermute | solution.py:641
  498.6 58.5 %collective-permute-start.91 = (bf16[128,1536]{1,0:T(8,128)(2,1)S(1)}, bf16[128,1536]{1,0:T(8,128)(2,1)S(1)}, u32[]{:S(2)}, u32[]{:S(2)}) collective-permute-start(bf16[128,1536]{1,0:T(8,128)(2,1)S(1)} %get-tuple-element.565), channel_id=1, source_target_pairs={{0,0},{2,1},{16,2},{18,3},{1,16},{3,17},{17,18},{19,19},{4,4},{6,5... | collective-permute-start | bytes 1179656 | tf_op jit(solution)/shard_map/ppermute | solution.py:641
  (124 other events, 1223.6 us)
Sparse Core Ops, SparseCore 0:
  108.2 60.3 all-gather.5
  271.3 58.0 reduce-scatter.4
  333.4 32.8 reduce-scatter.6
  369.1 30.0 reduce-scatter.8
  401.9 30.7 reduce-scatter.10
  434.1 54.3 all-gather.9
  498.3 55.4 all-gather.7

commit v4 on v3

--- a/solution.py
+++ b/solution.py
@@ -316,6 +316,28 @@
                 first += width
 
         place_chunk(ok, body)
+
+
+def last_kernel(ids, in_ref, q_w, k_w, v_w, gain_ref, q_ref, k_ref, v_ref, out_ref, sum_ref):
+    n_head = in_ref.shape[0]
+    n_rows = q_w.shape[0]
+    part = n_rows // n_head
+    n_slot = 2 * (q_w.shape[1] // (4 * HD))
+    for head in range(n_head):
+        at = slice(head * part, (head + 1) * part)
+        for pair in range(0, n_slot, 2):
+            two = [in_ref[head, pl.ds(pl.multiple_of((ids[0] ^ dev) * part, 16), part), :] for dev in (pair, pair + 1)]
+            for ref, first, width in ((q_ref, 0, 2 * HD), (k_ref, 2 * HD, HD), (v_ref, 3 * HD, HD)):
+                both = jnp.concatenate([v[:, first : first + width] for v in two], 1)
+                ref[at, pair * width : (pair + 2) * width] = both.astype(F32)
+        for i in range(D // (4 * HD)):
+            rows = slice((n_slot + i) * part, (n_slot + i + 1) * part)
+            out_ref[at, i * 4 * HD : (i + 1) * 4 * HD] = in_ref[head, rows, :].astype(F32)
+    total = None
+    for w, g in ((q_w, q_ref), (k_w, k_ref), (v_w, v_ref)):
+        one = jnp.sum(w[...].astype(F32) * g[...], -1, keepdims=True)
+        total = one if total is None else total + one
+    sum_ref[...] = jnp.broadcast_to(total, (n_rows, 128)).T[0:1, :] / gain_ref[...]
 
 
 def ff_kernel(n0, n1, c0, c1, gate_ref, up_ref, down_ref, hid_ref, dgu_ref, own_ref, other_ref):
@@ -916,28 +938,35 @@
     qkv_rows, ff_2, grad_input, block_out, out_mine = fence(
         chips(qkv_both), step(*ff_1), grad_input, block_out, out_mine
     )
-    late = join([jnp.stack(qkv_rows, 1).reshape(-1, 4 * HD), out_mine.reshape(-1, 4 * HD)])
+    out_rows = out_mine.reshape(part, -1, 4 * HD).transpose(1, 0, 2) if line else out_mine
+    late = join([jnp.stack(qkv_rows, 1).reshape(-1, 4 * HD), out_rows.reshape(-1, 4 * HD)])
     late = lax.all_gather(late, "head", axis=0)
     grad_input = from_plane(grad_input)
     block_out = from_plane(block_out)
     grad_down = late_down.reshape(-1, D).astype(F32)
-    late_qkv = late[:, : n_plane * part].reshape(n_head, n_plane, part, 4 * HD)
-    late_out = late[:, n_plane * part :].reshape(n_head, part, D)
-    each = lambda v: [v[i] for i in range(4)] if line else [v]
     if line:
         ff_chunks = [ff_2[0], ff_1[0], ff_0[0], ff_rows, ff_0[1], ff_1[1], ff_2[1]]
     else:
         ff_chunks = [lax.all_gather(ff_rows, "head", axis=0)]
     grad_gate_w, grad_up_w = owned_columns(ff_chunks, (ff_here, ff_here))
-    grad_query, grad_key, grad_value = owned_columns(each(late_qkv), (2 * HD, HD, HD))
-    grad_out = owned_rows(each(late_out))
-
     def gain_grad(gain, *pairs):
         return sum(jnp.sum(w.astype(F32) * g, -1) for w, g in pairs) / gain.astype(F32)
 
-    grad_gain_one = gain_grad(
-        norm_gain_one, (query_weight, grad_query), (key_weight, grad_key), (value_weight, grad_value)
-    )
+    if line:
+        matrices = (query_weight, key_weight, value_weight)
+        shapes = [jax.ShapeDtypeStruct(w.shape, F32) for w in (*matrices, output_weight)]
+        shapes.append(jax.ShapeDtypeStruct((1, n_rows), F32))
+        values = (late, *matrices, norm_gain_one.astype(F32)[None])
+        grad_query, grad_key, grad_value, grad_out, grad_gain_one = place_call(last_kernel, shapes, ids, *values, name="last")
+        grad_gain_one = grad_gain_one[0]
+    else:
+        late_qkv = late[:, : n_plane * part].reshape(n_head, n_plane, part, 4 * HD)
+        late_out = late[:, n_plane * part :].reshape(n_head, part, D)
+        grad_query, grad_key, grad_value = owned_columns([late_qkv], (2 * HD, HD, HD))
+        grad_out = owned_rows([late_out])
+        grad_gain_one = gain_grad(
+            norm_gain_one, (query_weight, grad_query), (key_weight, grad_key), (value_weight, grad_value)
+        )
     grad_gain_two = gain_grad(norm_gain_two, (gate_weight, grad_gate_w), (up_weight, grad_up_w))
     return (
         block_out[:, None],

time: 585 us -> 579 us (0.990)
    unnamed x198 -> x196, local copies, waits for them, and re-layouts: 20.2 us -> 21.5 us
    pallas_call x7 -> x6, Pallas kernels: 13.6 us -> 12.6 us  [place_call(): pl.pallas_call(kernel, out_shape=out_shape, in_specs=[pl.BlockSpec(memory...]
where the time goes in v4:
time: 579 us; the launch traced here: 571 us
  waiting for transfers between devices  231 us (40%)
  Pallas kernels  138 us (24%)
  starting transfers between devices  94.1 us (16%)
  other arithmetic  48.3 us (8%)
  local copies, waits for them, and re-layouts  43.2 us (7%)
  between operations  16.6 us (3%)
    ppermute x80, waiting for transfers between devices, swap(): lax.ppermute(value, axis, [(i, i ^ mask) for i in range(lax.axis_size(axi...  124 us
    ppermute x80, starting transfers between devices, swap(): lax.ppermute(value, axis, [(i, i ^ mask) for i in range(lax.axis_size(axi...  63 us
    ppermute x4, waiting for transfers between devices, from_plane(): lax.ppermute(value[k * tok:(k + 1) * tok], ('dp', 'head'), back)  42.7 us
    pallas_call x5, Pallas kernels, simple_call(): pl.pallas_call(kernel, out_shape=out_shape, in_specs=whole(len(values)),...  37.7 us
    all_gather x1, waiting for transfers between devices, per_device(): late_down = lax.all_gather(down_mine, 'head', axis=0)  26.5 us
    ppermute x3, waiting for transfers between devices, line_step(): lax.ppermute(left, 'head', up)  23.7 us
    pallas_call x4, Pallas kernels, ff_call(): pl.pallas_call(ff_kernel, out_shape=(jax.ShapeDtypeStruct((2, rows, width...  21.7 us
    unnamed x196, local copies, waits for them, and re-layouts  21.5 us
  transfers between devices with their start and end apart: 99, of which 39 were waited for; matrix products, arithmetic and copies ran while one was open for 12% of the time, Pallas kernels for 22%

profile of v4, /device:TPU:8, one launch (start us, length us, event | category | flops | bytes accessed | tf_op | source)
XLA Modules:
  0.0 570.8 jit_solution(668645499100149946)
XLA Ops:
  7.2 1.6 collective-permute-start.1
  18.0 2.3 collective-permute-done
  24.6 3.5 collective-permute-start.6
  38.6 6.3 %collective-permute-done.3.refs_1_ = bf16[2,208,512]{2,1,0:T(8,128)(2,1)S(1)} collective-permute-done((bf16[2,208,512]{2,1,0:T(8,128)(2,1)S(1)}, bf16[2,208,512]{2,1,0:T(8,128)(2,1)S(1)}, u32[]{:S(2)}, u32[]{:S(2)}) %collective-permute-start.3) | collective-permute-done | bytes 426016 | tf_op jit(solution)/shard_map/ppermute | solution.py:554
  44.9 8.1 %collective-permute-done.4.refs_2_ = bf16[2,208,512]{2,1,0:T(8,128)(2,1)S(1)} collective-permute-done((bf16[2,208,512]{2,1,0:T(8,128)(2,1)S(1)}, bf16[2,208,512]{2,1,0:T(8,128)(2,1)S(1)}, u32[]{:S(2)}, u32[]{:S(2)}) %collective-permute-start.4) | collective-permute-done | bytes 426016 | tf_op jit(solution)/shard_map/ppermute | solution.py:554
  52.9 1.6 collective-permute-done.5.refs_3_
  54.6 8.0 %collective-permute-done.6.refs_4_ = bf16[256,1536]{1,0:T(8,128)(2,1)S(1)} collective-permute-done((bf16[256,1536]{1,0:T(8,128)(2,1)S(1)}, bf16[256,1536]{1,0:T(8,128)(2,1)S(1)}, u32[]{:S(2)}, u32[]{:S(2)}) %collective-permute-start.6) | collective-permute-done | bytes 786464 | tf_op jit(solution)/shard_map/ppermute | solution.py:656
  68.3 17.4 %collective-permute-done.9.refs_1_ = bf16[256,1536]{1,0:T(8,128)(2,1)S(1)} collective-permute-done((bf16[256,1536]{1,0:T(8,128)(2,1)S(1)}, bf16[256,1536]{1,0:T(8,128)(2,1)S(1)}, u32[]{:S(2)}, u32[]{:S(2)}) %collective-permute-start.9) | collective-permute-done | bytes 786464 | tf_op jit(solution)/shard_map/ppermute | solution.py:554
  86.0 1.6 collective-permute-start.12
  87.6 1.6 collective-permute-start.13
  90.3 2.4 collective-permute-start.16
  92.8 11.2 %collective-permute-done.14 = bf16[2,48,1024]{2,1,0:T(8,128)(2,1)S(1)} collective-permute-done((bf16[2,48,1024]{2,1,0:T(8,128)(2,1)}, bf16[2,48,1024]{2,1,0:T(8,128)(2,1)S(1)}, u32[]{:S(2)}, u32[]{:S(2)}) %collective-permute-start.14) | collective-permute-done | bytes 196640 | tf_op jit(solution)/shard_map/ppermute | solution.py:554
  104.0 2.3 collective-permute-done.16
  117.6 7.6 %project_qkv.1.q_ref.kv_ref = bf16[2048,512]{1,0:T(8,128)(2,1)} custom-call(bf16[256,1536]{1,0:T(8,128)(2,1)S(1)} %copy-done.26, bf16[256,1536]{1,0:T(8,128)(2,1)S(1)} %collective-permute-done.9.refs_1_, bf16[256,1536]{1,0:T(8,128)(2,1)} %copy-done.11, bf16[256,1536]{1,0:T(8,128)(2,1)} %copy-done.15, bf16[256,1536]{1,0:T(8,128)(2,1)} %collective-permute-done.11.refs_4_, ...), custom_call_target="tpu_custom_call" | custom-call | flops 50331648 | bytes 155648 | tf_op jit(solution)/shard_map/project_qkv/pallas_call | solution.py:436
  125.1 1.6 copy-done
  126.7 15.5 %attn_fwd.1 = (bf16[2048,256]{1,0:T(8,128)(2,1)S(1)}, f32[8,2,256]{2,1,0:T(2,128)S(1)}) custom-call(s32[8,8]{1,0:T(8,128)S(1)} %and_convert_fusion.need, bf16[2048,512]{1,0:T(8,128)(2,1)S(1)} %copy-done, bf16[2048,512]{1,0:T(8,128)(2,1)S(1)} %copy-done, f32[8,1,256]{2,1,0:T(1,128)S(1)} %bitcast.196, f32[8,1,256]{2,1,0:T(1,128)S(1)} %bitcast.200, ...), custom_call_target="tpu_custom_call" | custom-call | flops 67108864 | bytes 131072 | tf_op jit(solution)/shard_map/attn_fwd/pallas_call | solution.py:176
  143.7 2.3 collective-permute-done.24
  149.7 5.6 collective-permute-done.25.refs_1_
  155.3 5.9 %collective-permute-done.26.refs_2_ = bf16[2,256,256]{2,1,0:T(8,128)(2,1)S(1)} collective-permute-done((bf16[2,256,256]{2,1,0:T(8,128)(2,1)S(1)}, bf16[2,256,256]{2,1,0:T(8,128)(2,1)S(1)}, u32[]{:S(2)}, u32[]{:S(2)}) %collective-permute-start.26) | collective-permute-done | bytes 262176 | tf_op jit(solution)/shard_map/ppermute | solution.py:554
  161.9 5.8 %out_project.1 = (f32[256,1536]{1,0:T(8,128)}, bf16[256,1536]{1,0:T(8,128)(2,1)}) custom-call(bf16[2,256,256]{2,1,0:T(8,128)(2,1)S(1)} %pad_maximum_fusion.14.refs_0_, bf16[2,256,256]{2,1,0:T(8,128)(2,1)S(1)} %collective-permute-done.25.refs_1_, bf16[2,256,256]{2,1,0:T(8,128)(2,1)S(1)} %collective-permute-done.26.refs_2_, ...), custom_call_target="tpu_custom_call" | custom-call | flops 18874368 | bytes 139360 | tf_op jit(solution)/shard_map/out_project/pallas_call | solution.py:436
  171.8 1.9 copy-done.39
  175.3 4.7 ff.4
  180.0 9.8 %collective-permute-done.35.n0.refs_1_ = bf16[256,1536]{1,0:T(8,128)(2,1)} collective-permute-done((bf16[256,1536]{1,0:T(8,128)(2,1)}, bf16[256,1536]{1,0:T(8,128)(2,1)}, u32[]{:S(2)}, u32[]{:S(2)}) %collective-permute-start.35) | collective-permute-done | bytes 786464 | tf_op jit(solution)/shard_map/ppermute | solution.py:554
  198.7 5.8 %ff.5 = (bf16[2,256,512]{2,1,0:T(8,128)(2,1)S(1)}, bf16[2,256,1024]{2,1,0:T(8,128)(2,1)S(1)}, f32[256,1536]{1,0:T(8,128)S(1)}, bf16[256,1536]{1,0:T(8,128)(2,1)S(1)}) custom-call(bf16[256,1536]{1,0:T(8,128)(2,1)} %collective-permute-done.35.n0.refs_1_, bf16[256,1536]{1,0:T(8,128)(2,1)S(1)} %collective-permute-done.42.n1.refs_5_, ...), custom_call_target="tpu_custom_call" | custom-call | flops 62914560 | bytes 196608 | tf_op jit(solution)/shard_map/ff/pallas_call | solution.py:366
  206.4 6.5 %ff.6 = (bf16[2,256,512]{2,1,0:T(8,128)(2,1)S(1)}, bf16[2,256,1024]{2,1,0:T(8,128)(2,1)S(1)}, f32[256,1536]{1,0:T(8,128)S(1)}, bf16[256,1536]{1,0:T(8,128)(2,1)S(1)}) custom-call(bf16[256,1536]{1,0:T(8,128)(2,1)} %collective-permute-done.36.n0.refs_2_, bf16[256,1536]{1,0:T(8,128)(2,1)S(1)} %collective-permute-done.43.n1.refs_6_, ...), custom_call_target="tpu_custom_call" | custom-call | flops 62914560 | bytes 196608 | tf_op jit(solution)/shard_map/ff/pallas_call | solution.py:366
  217.5 4.7 ff.7
  228.7 16.8 %ff_weight.1 = (bf16[4,8,48,1024]{3,2,1,0:T(8,128)(2,1)}, bf16[512,1536]{1,0:T(8,128)(2,1)}) custom-call(bf16[256,1536]{1,0:T(8,128)(2,1)} %get-tuple-element.340.n0.refs_0_, bf16[256,1536]{1,0:T(8,128)(2,1)} %collective-permute-done.35.n0.refs_1_, bf16[256,1536]{1,0:T(8,128)(2,1)} %collective-permute-done.36.n0.refs_2_, bf16[256,1536]{1,0:T(8,128)(2,1)} %copy-done.17, ...), custom_call_target="tpu_custom_call" | custom-call | flops 150994944 | bytes 393216 | tf_op jit(solution)/shard_map/ff_weight/pallas_call | solution.py:413
  245.6 16.8 %collective-permute-done.51.refs_10_ = bf16[256,1536]{1,0:T(8,128)(2,1)} collective-permute-done((bf16[256,1536]{1,0:T(8,128)(2,1)S(1)}, bf16[256,1536]{1,0:T(8,128)(2,1)}, u32[]{:S(2)}, u32[]{:S(2)}) %collective-permute-start.51) | collective-permute-done | bytes 786464 | tf_op jit(solution)/shard_map/ppermute | solution.py:554
  262.5 7.4 %branch.1 = (f32[256,1536]{1,0:T(8,128)}, bf16[256,1536]{1,0:T(8,128)(2,1)}, bf16[2,4,256,256]{3,2,1,0:T(8,128)(2,1)}) custom-call(bf16[192,1536]{1,0:T(8,128)(2,1)} %refs_0_.1, bf16[192,1536]{1,0:T(8,128)(2,1)S(1)} %copy-done.21, bf16[192,1536]{1,0:T(8,128)(2,1)S(1)} %copy-done.24, bf16[192,1536]{1,0:T(8,128)(2,1)} %copy-done.63, ...), custom_call_target="tpu_custom_call" | custom-call | flops 18874368 | bytes 225376 | tf_op jit(solution)/shard_map/branch/pallas_call | solution.py:436
  273.7 8.3 %back_project.2 = (f32[4,256,1536]{2,1,0:T(8,128)}, bf16[4,256,1536]{2,1,0:T(8,128)(2,1)}) custom-call(bf16[2,256,512]{2,1,0:T(8,128)(2,1)S(1)} %copy-done.43, bf16[2,256,512]{2,1,0:T(8,128)(2,1)S(1)} %copy-done.45, bf16[2,256,512]{2,1,0:T(8,128)(2,1)S(1)} %copy-done.47, bf16[2,256,512]{2,1,0:T(8,128)(2,1)} %copy-done.48, bf16[512,1536]{1,0:T(8,128)(2,1)} %refs_4_.3), custom_call_target="tpu_custom_call" | custom-call | flops 50331648 | bytes 204800 | tf_op jit(solution)/shard_map/back_project/pallas_call | solution.py:436
  286.0 5.7 collective-permute-done.54
  292.4 4.7 collective-permute-done.56
  299.7 19.9 %attn_bwd.1.refs_8_.refs_0_ = bf16[2048,512]{1,0:T(8,128)(2,1)S(1)} custom-call(s32[8,8]{1,0:T(8,128)S(1)} %and_convert_fusion.need, bf16[2048,512]{1,0:T(8,128)(2,1)} %project_qkv.1.q_ref.kv_ref, bf16[2048,512]{1,0:T(8,128)(2,1)} %project_qkv.1.q_ref.kv_ref, f32[8,1,256]{2,1,0:T(1,128)S(1)} %bitcast.198, f32[8,1,256]{2,1,0:T(1,128)S(1)} %bitcast.202, ...), custom_call_target="tpu_custom_call" | custom-call | flops 167772160 | bytes 131072 | tf_op jit(solution)/shard_map/attn_bwd/pallas_call | solution.py:193
  319.7 2.1 slice.398
  322.4 1.8 slice.399
  325.3 4.6 add_convert_fusion.4
  333.4 7.6 %qkv_weight.1 = bf16[4,8,48,384]{3,2,1,0:T(8,128)(2,1)} custom-call(bf16[256,1536]{1,0:T(8,128)(2,1)S(1)} %copy-done.27, bf16[256,1536]{1,0:T(8,128)(2,1)S(1)} %copy-done.10, bf16[256,1536]{1,0:T(8,128)(2,1)S(1)} %copy-done.12, bf16[256,1536]{1,0:T(8,128)(2,1)S(1)} %copy-done.16, bf16[256,1536]{1,0:T(8,128)(2,1)} %collective-permute-done.11.refs_4_, ...), custom_call_target="tpu_custom_call" | custom-call | flops 100663296 | bytes 196608 | tf_op jit(solution)/shard_map/qkv_weight/pallas_call | solution.py:534
  348.6 8.6 %back_project.3 = (f32[4,256,1536]{2,1,0:T(8,128)}, bf16[4,256,1536]{2,1,0:T(8,128)(2,1)}) custom-call(bf16[2048,512]{1,0:T(8,128)(2,1)} %copy-done.2, bf16[1536,512]{1,0:T(8,128)(2,1)S(1)} %copy-done.8), custom_call_target="tpu_custom_call" | custom-call | flops 50331648 | bytes 204800 | tf_op jit(solution)/shard_map/back_project/pallas_call | solution.py:436
  359.4 6.9 %collective-permute-done.69 = bf16[256,1536]{1,0:T(8,128)(2,1)S(1)} collective-permute-done((bf16[256,1536]{1,0:T(8,128)(2,1)S(1)}, bf16[256,1536]{1,0:T(8,128)(2,1)S(1)}, u32[]{:S(2)}, u32[]{:S(2)}) %collective-permute-start.69) | collective-permute-done | bytes 786464 | tf_op jit(solution)/shard_map/ppermute | solution.py:554
  372.0 6.0 %out_weight.1 = bf16[192,1536]{1,0:T(8,128)(2,1)} custom-call(bf16[2048,256]{1,0:T(8,128)(2,1)} %copy-done.5, bf16[256,1536]{1,0:T(8,128)(2,1)S(1)} %copy-done.59, bf16[256,1536]{1,0:T(8,128)(2,1)} %collective-permute-done.58.refs_2_, bf16[256,1536]{1,0:T(8,128)(2,1)} %collective-permute-done.59.refs_3_, ...), custom_call_target="tpu_custom_call" | custom-call | flops 50331648 | bytes 147456 | tf_op jit(solution)/shard_map/out_weight/pallas_call | solution.py:906
  378.0 6.3 %fusion.10 = (bf16[256,1536]{1,0:T(8,128)(2,1)}, bf16[256,1536]{1,0:T(8,128)(2,1)}, bf16[256,1536]{1,0:T(8,128)(2,1)}, f32[256,1536]{1,0:T(8,128)}) fusion(f32[4,256,1536]{2,1,0:T(8,128)} %get-tuple-element.455, bf16[4,256,1536]{2,1,0:T(8,128)(2,1)} %collective-permute-done.74), kind=kLoop, calls=%fused_computation.30 | loop fusion | flops 4325376 | bytes 13369344 | tf_op jit(solution)/shard_map/convert_element_type | solution.py:923
  385.6 1.9 collective-permute-start.78
  387.5 4.0 collective-permute-start.80
  395.9 15.8 %collective-permute-done.78.refs_2_ = bf16[8,48,1024]{2,1,0:T(8,128)(2,1)S(1)} collective-permute-done((bf16[8,48,1024]{2,1,0:T(8,128)(2,1)S(1)}, bf16[8,48,1024]{2,1,0:T(8,128)(2,1)S(1)}, u32[]{:S(2)}, u32[]{:S(2)}) %collective-permute-start.78) | collective-permute-done | bytes 786464 | tf_op jit(solution)/shard_map/ppermute | solution.py:607
  411.7 3.6 collective-permute-start.79
  415.4 3.1 collective-permute-start.81
  418.6 3.7 add_convert_fusion
  422.2 5.4 collective-permute-done.76
  429.0 3.6 reduce-scatter.11.cloned.1.call-done
  432.6 7.9 %collective-permute-done.79.refs_1_ = bf16[8,48,1024]{2,1,0:T(8,128)(2,1)} collective-permute-done((bf16[8,48,1024]{2,1,0:T(8,128)(2,1)S(1)}, bf16[8,48,1024]{2,1,0:T(8,128)(2,1)}, u32[]{:S(2)}, u32[]{:S(2)}) %collective-permute-start.79) | collective-permute-done | bytes 786464 | tf_op jit(solution)/shard_map/ppermute | solution.py:607
  440.4 1.7 collective-permute-done.81.refs_5_
  443.3 2.8 collective-permute-start.86
  446.1 3.9 collective-permute-start.87
  450.0 3.0 fusion.2
  453.1 3.3 fusion.6
  461.8 26.5 %all-gather.10.cloned.1.call-done = bf16[512,1536]{1,0:T(8,128)(2,1)} async-done(((bf16[128,1536]{1,0:T(8,128)(2,1)}), bf16[512,1536]{1,0:T(8,128)(2,1)}) %all-gather.10.cloned.1.call-update) | async-done | bytes 1572880 | tf_op jit(solution)/shard_map/all_gather | solution.py:927
  488.4 3.5 convert_element_type.225
  492.9 3.2 collective-permute-start.89
  498.5 3.9 collective-permute-start.91
  502.4 5.0 place_columns.1
  507.5 2.7 multiply_reduce_fusion.1
  512.2 9.6 %collective-permute-done.89 = bf16[128,1536]{1,0:T(8,128)(2,1)} collective-permute-done((bf16[128,1536]{1,0:T(8,128)(2,1)}, bf16[128,1536]{1,0:T(8,128)(2,1)}, u32[]{:S(2)}, u32[]{:S(2)}) %collective-permute-start.89) | collective-permute-done | bytes 393248 | tf_op jit(solution)/shard_map/ppermute | solution.py:663
  523.9 33.1 %collective-permute-done.91 = bf16[128,1536]{1,0:T(8,128)(2,1)S(1)} collective-permute-done((bf16[128,1536]{1,0:T(8,128)(2,1)S(1)}, bf16[128,1536]{1,0:T(8,128)(2,1)S(1)}, u32[]{:S(2)}, u32[]{:S(2)}) %collective-permute-start.91) | collective-permute-done | bytes 393248 | tf_op jit(solution)/shard_map/ppermute | solution.py:663
  559.5 3.9 last.1
  (496 shorter events, 130.1 us)
Async XLA Ops:
  7.2 164.6 %all-gather.6.cloned.1.call-start = ((), (), s32[]{:S(2)}) async-start(), calls=%async_computation.4 | async-start | bytes 3932160 | tf_op jit(solution)/shard_map/all_gather | solution.py:779
  7.2 15.3 %collective-permute-start.1 = (bf16[192,1536]{1,0:T(8,128)(2,1)}, bf16[192,1536]{1,0:T(8,128)(2,1)S(1)}, u32[]{:S(2)}, u32[]{:S(2)}) collective-permute-start(bf16[192,1536]{1,0:T(8,128)(2,1)} %refs_0_.1), channel_id=1, source_target_pairs={{0,4},{4,0},{8,12},{12,8},{1,5},{5,1},{9,13},{13,9},{2,6},{6,2},{1... | collective-permute-start | bytes 1769480 | tf_op jit(solution)/shard_map/ppermute | solution.py:554
  8.8 15.0 %collective-permute-start.2 = (bf16[192,1536]{1,0:T(8,128)(2,1)}, bf16[192,1536]{1,0:T(8,128)(2,1)S(1)}, u32[]{:S(2)}, u32[]{:S(2)}) collective-permute-start(bf16[192,1536]{1,0:T(8,128)(2,1)} %refs_0_.1), channel_id=1, source_target_pairs={{0,8},{4,12},{8,0},{12,4},{1,9},{5,13},{9,1},{13,5},{2,10},{6,14},... | collective-permute-start | bytes 1769480 | tf_op jit(solution)/shard_map/ppermute | solution.py:554
  24.6 37.9 %collective-permute-start.6 = (bf16[256,1536]{1,0:T(8,128)(2,1)S(1)}, bf16[256,1536]{1,0:T(8,128)(2,1)S(1)}, u32[]{:S(2)}, u32[]{:S(2)}) collective-permute-start(bf16[256,1536]{1,0:T(8,128)(2,1)S(1)} %pad_maximum_fusion.1), channel_id=1, source_target_pairs={{0,0},{1,2},{2,16},{3,18},{16,1},{17,3},{18,17},{19,19},{4,4},{5,6... | collective-permute-start | bytes 2359304 | tf_op jit(solution)/shard_map/ppermute | solution.py:656
  32.1 30.5 %collective-permute-start.7 = (bf16[256,1536]{1,0:T(8,128)(2,1)S(1)}, bf16[256,1536]{1,0:T(8,128)(2,1)S(1)}, u32[]{:S(2)}, u32[]{:S(2)}) collective-permute-start(bf16[256,1536]{1,0:T(8,128)(2,1)S(1)} %pad_maximum_fusion.2), channel_id=1, source_target_pairs={{0,2},{1,0},{2,18},{3,16},{16,3},{17,1},{18,19},{19,17},{4,6},{5,4... | collective-permute-start | bytes 2359304 | tf_op jit(solution)/shard_map/ppermute | solution.py:656
  32.8 20.1 %collective-permute-start.4 = (bf16[2,208,512]{2,1,0:T(8,128)(2,1)S(1)}, bf16[2,208,512]{2,1,0:T(8,128)(2,1)S(1)}, u32[]{:S(2)}, u32[]{:S(2)}) collective-permute-start(bf16[2,208,512]{2,1,0:T(8,128)(2,1)S(1)} %get-tuple-element.261), channel_id=1, source_target_pairs={{0,8},{4,12},{8,0},{12,4},{1,9},{5,13},{9,1},{13,5},{2,10},{6,14},... | collective-permute-start | bytes 1277960 | tf_op jit(solution)/shard_map/ppermute | solution.py:554
  34.3 20.2 %collective-permute-start.5 = (bf16[2,208,512]{2,1,0:T(8,128)(2,1)S(1)}, bf16[2,208,512]{2,1,0:T(8,128)(2,1)S(1)}, u32[]{:S(2)}, u32[]{:S(2)}) collective-permute-start(bf16[2,208,512]{2,1,0:T(8,128)(2,1)S(1)} %get-tuple-element.262), channel_id=1, source_target_pairs={{0,12},{4,8},{8,4},{12,0},{1,13},{5,9},{9,5},{13,1},{2,14},{6,10},... | collective-permute-start | bytes 1277960 | tf_op jit(solution)/shard_map/ppermute | solution.py:554
  65.8 19.9 %collective-permute-start.9 = (bf16[256,1536]{1,0:T(8,128)(2,1)S(1)}, bf16[256,1536]{1,0:T(8,128)(2,1)S(1)}, u32[]{:S(2)}, u32[]{:S(2)}) collective-permute-start(bf16[256,1536]{1,0:T(8,128)(2,1)S(1)} %get-tuple-element.296.refs_0_), channel_id=1, source_target_pairs={{0,4},{4,0},{8,12},{12,8},{1,5},{5,1},{9,13},{13,9},{2,6},{6,2},{1... | collective-permute-start | bytes 2359304 | tf_op jit(solution)/shard_map/ppermute | solution.py:554
  66.4 19.6 %collective-permute-start.10 = (bf16[256,1536]{1,0:T(8,128)(2,1)S(1)}, bf16[256,1536]{1,0:T(8,128)(2,1)S(1)}, u32[]{:S(2)}, u32[]{:S(2)}) collective-permute-start(bf16[256,1536]{1,0:T(8,128)(2,1)S(1)} %get-tuple-element.296.refs_0_), channel_id=1, source_target_pairs={{0,8},{4,12},{8,0},{12,4},{1,9},{5,13},{9,1},{13,5},{2,10},{6,14},... | collective-permute-start | bytes 2359304 | tf_op jit(solution)/shard_map/ppermute | solution.py:554
  67.9 18.1 %collective-permute-start.11 = (bf16[256,1536]{1,0:T(8,128)(2,1)S(1)}, bf16[256,1536]{1,0:T(8,128)(2,1)}, u32[]{:S(2)}, u32[]{:S(2)}) collective-permute-start(bf16[256,1536]{1,0:T(8,128)(2,1)S(1)} %get-tuple-element.296.refs_0_), channel_id=1, source_target_pairs={{0,16},{16,0},{1,17},{17,1},{2,18},{18,2},{3,19},{19,3},{4,20},{20... | collective-permute-start | bytes 2359304 | tf_op jit(solution)/shard_map/ppermute | solution.py:554
  86.0 20.2 %collective-permute-start.12 = (bf16[128,1536]{1,0:T(8,128)(2,1)S(1)}, bf16[128,1536]{1,0:T(8,128)(2,1)S(1)}, u32[]{:S(2)}, u32[]{:S(2)}) collective-permute-start(bf16[128,1536]{1,0:T(8,128)(2,1)S(1)} %slice.362), channel_id=1, source_target_pairs={{0,8},{4,12},{8,0},{12,4},{1,9},{5,13},{9,1},{13,5},{2,10},{6,14},... | collective-permute-start | bytes 1179656 | tf_op jit(solution)/shard_map/ppermute | solution.py:554
  87.6 18.6 %collective-permute-start.13 = (bf16[128,1536]{1,0:T(8,128)(2,1)S(1)}, bf16[128,1536]{1,0:T(8,128)(2,1)S(1)}, u32[]{:S(2)}, u32[]{:S(2)}) collective-permute-start(bf16[128,1536]{1,0:T(8,128)(2,1)S(1)} %slice.363), channel_id=1, source_target_pairs={{0,4},{4,0},{8,12},{12,8},{1,5},{5,1},{9,13},{13,9},{2,6},{6,2},{1... | collective-permute-start | bytes 1179656 | tf_op jit(solution)/shard_map/ppermute | solution.py:554
  89.2 14.7 %collective-permute-start.14 = (bf16[2,48,1024]{2,1,0:T(8,128)(2,1)}, bf16[2,48,1024]{2,1,0:T(8,128)(2,1)S(1)}, u32[]{:S(2)}, u32[]{:S(2)}) collective-permute-start(bf16[2,48,1024]{2,1,0:T(8,128)(2,1)} %pad_maximum_fusion.23), channel_id=1, source_target_pairs={{0,4},{4,0},{8,12},{12,8},{1,5},{5,1},{9,13},{13,9},{2,6},{6,2},{1... | collective-permute-start | bytes 589832 | tf_op jit(solution)/shard_map/ppermute | solution.py:554
  90.3 15.9 %collective-permute-start.16 = (bf16[2,48,1024]{2,1,0:T(8,128)(2,1)}, bf16[2,48,1024]{2,1,0:T(8,128)(2,1)S(1)}, u32[]{:S(2)}, u32[]{:S(2)}) collective-permute-start(bf16[2,48,1024]{2,1,0:T(8,128)(2,1)} %pad_maximum_fusion.25), channel_id=1, source_target_pairs={{0,12},{4,8},{8,4},{12,0},{1,13},{5,9},{9,5},{13,1},{2,14},{6,10},... | collective-permute-start | bytes 589832 | tf_op jit(solution)/shard_map/ppermute | solution.py:554
  104.0 43.6 %collective-permute-start.28 = (bf16[192,1536]{1,0:T(8,128)(2,1)}, bf16[192,1536]{1,0:T(8,128)(2,1)}, u32[]{:S(2)}, u32[]{:S(2)}) collective-permute-start(bf16[192,1536]{1,0:T(8,128)(2,1)} %refs_0_.1), channel_id=1, source_target_pairs={{0,16},{16,0},{1,17},{17,1},{2,18},{18,2},{3,19},{19,3},{4,20},{20... | collective-permute-start | bytes 1769480 | tf_op jit(solution)/shard_map/ppermute | solution.py:554
  108.1 234.0 %reduce-scatter.5.cloned.1.call-start = ((), (), s32[]{:S(2)}) async-start(), calls=%async_computation.5 | async-start | bytes 3932160 | tf_op jit(solution)/shard_map/reduce_scatter | solution.py:835
  111.0 31.8 %collective-permute-start.20 = (bf16[256,1536]{1,0:T(8,128)(2,1)S(1)}, bf16[256,1536]{1,0:T(8,128)(2,1)S(1)}, u32[]{:S(2)}, u32[]{:S(2)}) collective-permute-start(bf16[256,1536]{1,0:T(8,128)(2,1)S(1)} %get-tuple-element.311.c0.refs_8_.refs_13_), channel_id=1, source_target_pairs={{0,4},{4,0},{8,12},{12,8},{1,5},{5,1},{9,13},{13,9},{2,6},{6,2},{1... | collective-permute-start | bytes 2359304 | tf_op jit(solution)/shard_map/ppermute | solution.py:554
  112.5 30.4 %collective-permute-start.21 = (bf16[256,1536]{1,0:T(8,128)(2,1)S(1)}, bf16[256,1536]{1,0:T(8,128)(2,1)}, u32[]{:S(2)}, u32[]{:S(2)}) collective-permute-start(bf16[256,1536]{1,0:T(8,128)(2,1)S(1)} %get-tuple-element.311.c0.refs_8_.refs_13_), channel_id=1, source_target_pairs={{0,8},{4,12},{8,0},{12,4},{1,9},{5,13},{9,1},{13,5},{2,10},{6,14},... | collective-permute-start | bytes 2359304 | tf_op jit(solution)/shard_map/ppermute | solution.py:554
  115.1 27.2 %collective-permute-start.22 = (bf16[96,1536]{1,0:T(8,128)(2,1)S(1)}, bf16[96,1536]{1,0:T(8,128)(2,1)S(1)}, u32[]{:S(2)}, u32[]{:S(2)}) collective-permute-start(bf16[96,1536]{1,0:T(8,128)(2,1)S(1)} %slice.365), channel_id=1, source_target_pairs={{0,8},{4,12},{8,0},{12,4},{1,9},{5,13},{9,1},{13,5},{2,10},{6,14},... | collective-permute-start | bytes 884744 | tf_op jit(solution)/shard_map/ppermute | solution.py:554
  116.6 25.7 %collective-permute-start.23 = (bf16[96,1536]{1,0:T(8,128)(2,1)S(1)}, bf16[96,1536]{1,0:T(8,128)(2,1)S(1)}, u32[]{:S(2)}, u32[]{:S(2)}) collective-permute-start(bf16[96,1536]{1,0:T(8,128)(2,1)S(1)} %slice.366), channel_id=1, source_target_pairs={{0,4},{4,0},{8,12},{12,8},{1,5},{5,1},{9,13},{13,9},{2,6},{6,2},{1... | collective-permute-start | bytes 884744 | tf_op jit(solution)/shard_map/ppermute | solution.py:554
  149.7 18.0 %collective-permute-start.32 = (bf16[256,1536]{1,0:T(8,128)(2,1)S(1)}, bf16[256,1536]{1,0:T(8,128)(2,1)S(1)}, u32[]{:S(2)}, u32[]{:S(2)}) collective-permute-start(bf16[256,1536]{1,0:T(8,128)(2,1)S(1)} %get-tuple-element.311.c0.refs_8_.refs_13_), channel_id=1, source_target_pairs={{0,16},{16,0},{1,17},{17,1},{2,18},{18,2},{3,19},{19,3},{4,20},{20... | collective-permute-start | bytes 2359304 | tf_op jit(solution)/shard_map/ppermute | solution.py:554
  169.6 20.2 %collective-permute-start.35 = (bf16[256,1536]{1,0:T(8,128)(2,1)}, bf16[256,1536]{1,0:T(8,128)(2,1)}, u32[]{:S(2)}, u32[]{:S(2)}) collective-permute-start(bf16[256,1536]{1,0:T(8,128)(2,1)} %get-tuple-element.340.n0.refs_0_), channel_id=1, source_target_pairs={{0,4},{4,0},{8,12},{12,8},{1,5},{5,1},{9,13},{13,9},{2,6},{6,2},{1... | collective-permute-start | bytes 2359304 | tf_op jit(solution)/shard_map/ppermute | solution.py:554
  170.8 20.0 %collective-permute-start.36 = (bf16[256,1536]{1,0:T(8,128)(2,1)}, bf16[256,1536]{1,0:T(8,128)(2,1)}, u32[]{:S(2)}, u32[]{:S(2)}) collective-permute-start(bf16[256,1536]{1,0:T(8,128)(2,1)} %get-tuple-element.340.n0.refs_0_), channel_id=1, source_target_pairs={{0,8},{4,12},{8,0},{12,4},{1,9},{5,13},{9,1},{13,5},{2,10},{6,14},... | collective-permute-start | bytes 2359304 | tf_op jit(solution)/shard_map/ppermute | solution.py:554
  190.8 15.6 %collective-permute-start.43 = (bf16[256,1536]{1,0:T(8,128)(2,1)}, bf16[256,1536]{1,0:T(8,128)(2,1)S(1)}, u32[]{:S(2)}, u32[]{:S(2)}) collective-permute-start(bf16[256,1536]{1,0:T(8,128)(2,1)} %collective-permute-done.36.n0.refs_2_), channel_id=1, source_target_pairs={{0,16},{16,0},{1,17},{17,1},{2,18},{18,2},{3,19},{19,3},{4,20},{20... | collective-permute-start | bytes 2359304 | tf_op jit(solution)/shard_map/ppermute | solution.py:554
  193.4 20.6 %collective-permute-start.38 = (bf16[128,1536]{1,0:T(8,128)(2,1)S(1)}, bf16[128,1536]{1,0:T(8,128)(2,1)S(1)}, u32[]{:S(2)}, u32[]{:S(2)}) collective-permute-start(bf16[128,1536]{1,0:T(8,128)(2,1)S(1)} %slice.381), channel_id=1, source_target_pairs={{0,8},{4,12},{8,0},{12,4},{1,9},{5,13},{9,1},{13,5},{2,10},{6,14},... | collective-permute-start | bytes 1179656 | tf_op jit(solution)/shard_map/ppermute | solution.py:554
  194.3 19.6 %collective-permute-start.39 = (bf16[128,1536]{1,0:T(8,128)(2,1)S(1)}, bf16[128,1536]{1,0:T(8,128)(2,1)S(1)}, u32[]{:S(2)}, u32[]{:S(2)}) collective-permute-start(bf16[128,1536]{1,0:T(8,128)(2,1)S(1)} %slice.382), channel_id=1, source_target_pairs={{0,4},{4,0},{8,12},{12,8},{1,5},{5,1},{9,13},{13,9},{2,6},{6,2},{1... | collective-permute-start | bytes 1179656 | tf_op jit(solution)/shard_map/ppermute | solution.py:554
  195.8 18.2 %collective-permute-start.40 = (bf16[128,1536]{1,0:T(8,128)(2,1)S(1)}, bf16[128,1536]{1,0:T(8,128)(2,1)S(1)}, u32[]{:S(2)}, u32[]{:S(2)}) collective-permute-start(bf16[128,1536]{1,0:T(8,128)(2,1)S(1)} %slice.383), channel_id=1, source_target_pairs={{0,8},{4,12},{8,0},{12,4},{1,9},{5,13},{9,1},{13,5},{2,10},{6,14},... | collective-permute-start | bytes 1179656 | tf_op jit(solution)/shard_map/ppermute | solution.py:554
  197.4 16.5 %collective-permute-start.41 = (bf16[128,1536]{1,0:T(8,128)(2,1)S(1)}, bf16[128,1536]{1,0:T(8,128)(2,1)S(1)}, u32[]{:S(2)}, u32[]{:S(2)}) collective-permute-start(bf16[128,1536]{1,0:T(8,128)(2,1)S(1)} %slice.384), channel_id=1, source_target_pairs={{0,4},{4,0},{8,12},{12,8},{1,5},{5,1},{9,13},{13,9},{2,6},{6,2},{1... | collective-permute-start | bytes 1179656 | tf_op jit(solution)/shard_map/ppermute | solution.py:554
  225.2 20.4 %collective-permute-start.50 = (bf16[256,1536]{1,0:T(8,128)(2,1)S(1)}, bf16[256,1536]{1,0:T(8,128)(2,1)S(1)}, u32[]{:S(2)}, u32[]{:S(2)}) collective-permute-start(bf16[256,1536]{1,0:T(8,128)(2,1)S(1)} %add_convert_fusion.7), channel_id=1, source_target_pairs={{0,4},{4,0},{8,12},{12,8},{1,5},{5,1},{9,13},{13,9},{2,6},{6,2},{1... | collective-permute-start | bytes 2359304 | tf_op jit(solution)/shard_map/ppermute | solution.py:554
  226.2 36.3 %collective-permute-start.51 = (bf16[256,1536]{1,0:T(8,128)(2,1)S(1)}, bf16[256,1536]{1,0:T(8,128)(2,1)}, u32[]{:S(2)}, u32[]{:S(2)}) collective-permute-start(bf16[256,1536]{1,0:T(8,128)(2,1)S(1)} %add_convert_fusion.6), channel_id=1, source_target_pairs={{0,8},{4,12},{8,0},{12,4},{1,9},{5,13},{9,1},{13,5},{2,10},{6,14},... | collective-permute-start | bytes 2359304 | tf_op jit(solution)/shard_map/ppermute | solution.py:554
  227.5 34.9 %collective-permute-start.52 = (bf16[256,1536]{1,0:T(8,128)(2,1)S(1)}, bf16[256,1536]{1,0:T(8,128)(2,1)}, u32[]{:S(2)}, u32[]{:S(2)}) collective-permute-start(bf16[256,1536]{1,0:T(8,128)(2,1)S(1)} %add_convert_fusion.5), channel_id=1, source_target_pairs={{0,12},{4,8},{8,4},{12,0},{1,13},{5,9},{9,5},{13,1},{2,14},{6,10},... | collective-permute-start | bytes 2359304 | tf_op jit(solution)/shard_map/ppermute | solution.py:554
  271.1 113.2 %reduce-scatter.7.cloned.1.call-start = ((), (), s32[]{:S(2)}) async-start(), calls=%async_computation.6 | async-start | bytes 1966080 | tf_op jit(solution)/shard_map/reduce_scatter | solution.py:835
  282.0 15.1 %collective-permute-start.57 = (bf16[4,256,1536]{2,1,0:T(8,128)(2,1)}, bf16[4,256,1536]{2,1,0:T(8,128)(2,1)S(1)}, u32[]{:S(2)}, u32[]{:S(2)}) collective-permute-start(bf16[4,256,1536]{2,1,0:T(8,128)(2,1)} %get-tuple-element.420), channel_id=1, source_target_pairs={{0,16},{16,0},{1,17},{17,1},{2,18},{18,2},{3,19},{19,3},{4,20},{20... | collective-permute-start | bytes 9437192 | tf_op jit(solution)/shard_map/ppermute | solution.py:554
  297.1 22.5 %collective-permute-start.58 = (bf16[256,1536]{1,0:T(8,128)(2,1)S(1)}, bf16[256,1536]{1,0:T(8,128)(2,1)}, u32[]{:S(2)}, u32[]{:S(2)}) collective-permute-start(bf16[256,1536]{1,0:T(8,128)(2,1)S(1)} %copy-done.58), channel_id=1, source_target_pairs={{0,4},{4,0},{8,12},{12,8},{1,5},{5,1},{9,13},{13,9},{2,6},{6,2},{1... | collective-permute-start | bytes 2359304 | tf_op jit(solution)/shard_map/ppermute | solution.py:554
  298.1 21.5 %collective-permute-start.59 = (bf16[256,1536]{1,0:T(8,128)(2,1)S(1)}, bf16[256,1536]{1,0:T(8,128)(2,1)}, u32[]{:S(2)}, u32[]{:S(2)}) collective-permute-start(bf16[256,1536]{1,0:T(8,128)(2,1)S(1)} %copy-done.58), channel_id=1, source_target_pairs={{0,8},{4,12},{8,0},{12,4},{1,9},{5,13},{9,1},{13,5},{2,10},{6,14},... | collective-permute-start | bytes 2359304 | tf_op jit(solution)/shard_map/ppermute | solution.py:554
  321.7 19.3 %collective-permute-start.60 = (bf16[128,1536]{1,0:T(8,128)(2,1)}, bf16[128,1536]{1,0:T(8,128)(2,1)S(1)}, u32[]{:S(2)}, u32[]{:S(2)}) collective-permute-start(bf16[128,1536]{1,0:T(8,128)(2,1)} %slice.398), channel_id=1, source_target_pairs={{0,8},{4,12},{8,0},{12,4},{1,9},{5,13},{9,1},{13,5},{2,10},{6,14},... | collective-permute-start | bytes 1179656 | tf_op jit(solution)/shard_map/ppermute | solution.py:554
  324.2 17.2 %collective-permute-start.61 = (bf16[128,1536]{1,0:T(8,128)(2,1)}, bf16[128,1536]{1,0:T(8,128)(2,1)}, u32[]{:S(2)}, u32[]{:S(2)}) collective-permute-start(bf16[128,1536]{1,0:T(8,128)(2,1)} %slice.399), channel_id=1, source_target_pairs={{0,4},{4,0},{8,12},{12,8},{1,5},{5,1},{9,13},{13,9},{2,6},{6,2},{1... | collective-permute-start | bytes 1179656 | tf_op jit(solution)/shard_map/ppermute | solution.py:554
  333.2 89.0 %reduce-scatter.9.cloned.1.call-start = ((), (), s32[]{:S(2)}) async-start(), calls=%async_computation.7 | async-start | bytes 1474560 | tf_op jit(solution)/shard_map/reduce_scatter | solution.py:835
  341.0 18.3 %collective-permute-start.65 = (bf16[256,1536]{1,0:T(8,128)(2,1)}, bf16[256,1536]{1,0:T(8,128)(2,1)S(1)}, u32[]{:S(2)}, u32[]{:S(2)}) collective-permute-start(bf16[256,1536]{1,0:T(8,128)(2,1)} %collective-permute-done.58.refs_2_), channel_id=1, source_target_pairs={{0,16},{16,0},{1,17},{17,1},{2,18},{18,2},{3,19},{19,3},{4,20},{20... | collective-permute-start | bytes 2359304 | tf_op jit(solution)/shard_map/ppermute | solution.py:554
  341.4 17.9 %collective-permute-start.66 = (bf16[256,1536]{1,0:T(8,128)(2,1)}, bf16[256,1536]{1,0:T(8,128)(2,1)S(1)}, u32[]{:S(2)}, u32[]{:S(2)}) collective-permute-start(bf16[256,1536]{1,0:T(8,128)(2,1)} %collective-permute-done.59.refs_3_), channel_id=1, source_target_pairs={{0,16},{16,0},{1,17},{17,1},{2,18},{18,2},{3,19},{19,3},{4,20},{20... | collective-permute-start | bytes 2359304 | tf_op jit(solution)/shard_map/ppermute | solution.py:554
  343.3 16.0 %collective-permute-start.67 = (bf16[256,1536]{1,0:T(8,128)(2,1)S(1)}, bf16[256,1536]{1,0:T(8,128)(2,1)S(1)}, u32[]{:S(2)}, u32[]{:S(2)}) collective-permute-start(bf16[256,1536]{1,0:T(8,128)(2,1)S(1)} %constant_dynamic-update-slice_fusion.10.refs_4_), channel_id=1, source_target_pairs={{0,16},{16,0},{1,17},{17,1},{2,18},{18,2},{3,19},{19,3},{4,20},{20... | collective-permute-start | bytes 2359304 | tf_op jit(solution)/shard_map/ppermute | solution.py:554
  346.5 19.8 %collective-permute-start.69 = (bf16[256,1536]{1,0:T(8,128)(2,1)S(1)}, bf16[256,1536]{1,0:T(8,128)(2,1)S(1)}, u32[]{:S(2)}, u32[]{:S(2)}) collective-permute-start(bf16[256,1536]{1,0:T(8,128)(2,1)S(1)} %pad_maximum_fusion.4), channel_id=1, source_target_pairs={{0,4},{4,0},{8,12},{12,8},{1,5},{5,1},{9,13},{13,9},{2,6},{6,2},{1... | collective-permute-start | bytes 2359304 | tf_op jit(solution)/shard_map/ppermute | solution.py:554
  347.8 19.4 %collective-permute-start.70 = (bf16[256,1536]{1,0:T(8,128)(2,1)S(1)}, bf16[256,1536]{1,0:T(8,128)(2,1)S(1)}, u32[]{:S(2)}, u32[]{:S(2)}) collective-permute-start(bf16[256,1536]{1,0:T(8,128)(2,1)S(1)} %pad_maximum_fusion.5), channel_id=1, source_target_pairs={{0,8},{4,12},{8,0},{12,4},{1,9},{5,13},{9,1},{13,5},{2,10},{6,14},... | collective-permute-start | bytes 2359304 | tf_op jit(solution)/shard_map/ppermute | solution.py:554
  368.1 64.4 %reduce-scatter.11.cloned.1.call-start = ((), (), s32[]{:S(2)}) async-start(), calls=%async_computation.8 | async-start | bytes 737280 | tf_op jit(solution)/shard_map/reduce_scatter | solution.py:835
  368.4 15.8 %collective-permute-start.71 = (bf16[2,48,1024]{2,1,0:T(8,128)(2,1)}, bf16[2,48,1024]{2,1,0:T(8,128)(2,1)S(1)}, u32[]{:S(2)}, u32[]{:S(2)}) collective-permute-start(bf16[2,48,1024]{2,1,0:T(8,128)(2,1)} %pad_maximum_fusion.27), channel_id=1, source_target_pairs={{0,4},{4,0},{8,12},{12,8},{1,5},{5,1},{9,13},{13,9},{2,6},{6,2},{1... | collective-permute-start | bytes 589832 | tf_op jit(solution)/shard_map/ppermute | solution.py:554
  369.7 14.6 %collective-permute-start.72 = (bf16[2,48,1024]{2,1,0:T(8,128)(2,1)}, bf16[2,48,1024]{2,1,0:T(8,128)(2,1)}, u32[]{:S(2)}, u32[]{:S(2)}) collective-permute-start(bf16[2,48,1024]{2,1,0:T(8,128)(2,1)} %pad_maximum_fusion.28), channel_id=1, source_target_pairs={{0,8},{4,12},{8,0},{12,4},{1,9},{5,13},{9,1},{13,5},{2,10},{6,14},... | collective-permute-start | bytes 589832 | tf_op jit(solution)/shard_map/ppermute | solution.py:554
  384.3 104.0 %all-gather.10.cloned.1.call-start = ((), (), s32[]{:S(2)}) async-start(), calls=%async_computation.10 | async-start | bytes 1966080 | tf_op jit(solution)/shard_map/all_gather | solution.py:927
  385.6 26.2 %collective-permute-start.78 = (bf16[8,48,1024]{2,1,0:T(8,128)(2,1)S(1)}, bf16[8,48,1024]{2,1,0:T(8,128)(2,1)S(1)}, u32[]{:S(2)}, u32[]{:S(2)}) collective-permute-start(bf16[8,48,1024]{2,1,0:T(8,128)(2,1)S(1)} %bitcast.192), channel_id=1, source_target_pairs={{0,1},{1,2},{2,3},{4,5},{5,6},{6,7},{8,9},{9,10},{10,11},{12,13},{... | collective-permute-start | bytes 2359304 | tf_op jit(solution)/shard_map/ppermute | solution.py:607
  387.5 27.9 %collective-permute-start.80 = (bf16[8,48,1024]{2,1,0:T(8,128)(2,1)S(1)}, bf16[8,48,1024]{2,1,0:T(8,128)(2,1)S(1)}, u32[]{:S(2)}, u32[]{:S(2)}) collective-permute-start(bf16[8,48,1024]{2,1,0:T(8,128)(2,1)S(1)} %bitcast.193), channel_id=1, source_target_pairs={{1,0},{2,1},{3,2},{5,4},{6,5},{7,6},{9,8},{10,9},{11,10},{13,12},{... | collective-permute-start | bytes 2359304 | tf_op jit(solution)/shard_map/ppermute | solution.py:607
  392.4 29.9 %collective-permute-start.75 = (bf16[256,1536]{1,0:T(8,128)(2,1)}, bf16[256,1536]{1,0:T(8,128)(2,1)}, u32[]{:S(2)}, u32[]{:S(2)}) collective-permute-start(bf16[256,1536]{1,0:T(8,128)(2,1)} %get-tuple-element.458), channel_id=1, source_target_pairs={{0,4},{4,0},{8,12},{12,8},{1,5},{5,1},{9,13},{13,9},{2,6},{6,2},{1... | collective-permute-start | bytes 2359304 | tf_op jit(solution)/shard_map/ppermute | solution.py:554
  393.6 34.0 %collective-permute-start.76 = (bf16[256,1536]{1,0:T(8,128)(2,1)}, bf16[256,1536]{1,0:T(8,128)(2,1)}, u32[]{:S(2)}, u32[]{:S(2)}) collective-permute-start(bf16[256,1536]{1,0:T(8,128)(2,1)} %get-tuple-element.459), channel_id=1, source_target_pairs={{0,8},{4,12},{8,0},{12,4},{1,9},{5,13},{9,1},{13,5},{2,10},{6,14},... | collective-permute-start | bytes 2359304 | tf_op jit(solution)/shard_map/ppermute | solution.py:554
  394.7 34.3 %collective-permute-start.77 = (bf16[256,1536]{1,0:T(8,128)(2,1)}, bf16[256,1536]{1,0:T(8,128)(2,1)}, u32[]{:S(2)}, u32[]{:S(2)}) collective-permute-start(bf16[256,1536]{1,0:T(8,128)(2,1)} %get-tuple-element.460), channel_id=1, source_target_pairs={{0,12},{4,8},{8,4},{12,0},{1,13},{5,9},{9,5},{13,1},{2,14},{6,10},... | collective-permute-start | bytes 2359304 | tf_op jit(solution)/shard_map/ppermute | solution.py:554
  411.7 28.7 %collective-permute-start.79 = (bf16[8,48,1024]{2,1,0:T(8,128)(2,1)S(1)}, bf16[8,48,1024]{2,1,0:T(8,128)(2,1)}, u32[]{:S(2)}, u32[]{:S(2)}) collective-permute-start(bf16[8,48,1024]{2,1,0:T(8,128)(2,1)S(1)} %collective-permute-done.78.refs_2_), channel_id=1, source_target_pairs={{0,1},{1,2},{2,3},{4,5},{5,6},{6,7},{8,9},{9,10},{10,11},{12,13},{... | collective-permute-start | bytes 2359304 | tf_op jit(solution)/shard_map/ppermute | solution.py:607
  415.4 26.8 %collective-permute-start.81 = (bf16[8,48,1024]{2,1,0:T(8,128)(2,1)S(1)}, bf16[8,48,1024]{2,1,0:T(8,128)(2,1)}, u32[]{:S(2)}, u32[]{:S(2)}) collective-permute-start(bf16[8,48,1024]{2,1,0:T(8,128)(2,1)S(1)} %collective-permute-done.80.refs_4_), channel_id=1, source_target_pairs={{1,0},{2,1},{3,2},{5,4},{6,5},{7,6},{9,8},{10,9},{11,10},{13,12},{... | collective-permute-start | bytes 2359304 | tf_op jit(solution)/shard_map/ppermute | solution.py:607
  418.5 139.5 %all-gather.8.cloned.1.call-start = ((), (), s32[]{:S(2)}) async-start(), calls=%async_computation.9 | async-start | bytes 2211840 | tf_op jit(solution)/shard_map/all_gather | solution.py:943
  443.3 48.6 %collective-permute-start.86 = (bf16[8,48,1024]{2,1,0:T(8,128)(2,1)}, bf16[8,48,1024]{2,1,0:T(8,128)(2,1)}, u32[]{:S(2)}, u32[]{:S(2)}) collective-permute-start(bf16[8,48,1024]{2,1,0:T(8,128)(2,1)} %collective-permute-done.79.refs_1_), channel_id=1, source_target_pairs={{0,1},{1,2},{2,3},{4,5},{5,6},{6,7},{8,9},{9,10},{10,11},{12,13},{... | collective-permute-start | bytes 2359304 | tf_op jit(solution)/shard_map/ppermute | solution.py:607
  446.1 45.8 %collective-permute-start.87 = (bf16[8,48,1024]{2,1,0:T(8,128)(2,1)}, bf16[8,48,1024]{2,1,0:T(8,128)(2,1)}, u32[]{:S(2)}, u32[]{:S(2)}) collective-permute-start(bf16[8,48,1024]{2,1,0:T(8,128)(2,1)} %collective-permute-done.81.refs_5_), channel_id=1, source_target_pairs={{1,0},{2,1},{3,2},{5,4},{6,5},{7,6},{9,8},{10,9},{11,10},{13,12},{... | collective-permute-start | bytes 2359304 | tf_op jit(solution)/shard_map/ppermute | solution.py:607
  457.0 34.8 %collective-permute-start.83 = (bf16[2,48,384]{2,1,0:T(8,128)(2,1)}, bf16[2,48,384]{2,1,0:T(8,128)(2,1)S(1)}, u32[]{:S(2)}, u32[]{:S(2)}) collective-permute-start(bf16[2,48,384]{2,1,0:T(8,128)(2,1)} %pad_maximum_fusion.32), channel_id=1, source_target_pairs={{0,4},{4,0},{8,12},{12,8},{1,5},{5,1},{9,13},{13,9},{2,6},{6,2},{1... | collective-permute-start | bytes 221192 | tf_op jit(solution)/shard_map/ppermute | solution.py:554
  459.2 32.7 %collective-permute-start.84 = (bf16[2,48,384]{2,1,0:T(8,128)(2,1)}, bf16[2,48,384]{2,1,0:T(8,128)(2,1)}, u32[]{:S(2)}, u32[]{:S(2)}) collective-permute-start(bf16[2,48,384]{2,1,0:T(8,128)(2,1)} %pad_maximum_fusion.33), channel_id=1, source_target_pairs={{0,8},{4,12},{8,0},{12,4},{1,9},{5,13},{9,1},{13,5},{2,10},{6,14},... | collective-permute-start | bytes 221192 | tf_op jit(solution)/shard_map/ppermute | solution.py:554
  461.3 30.6 %collective-permute-start.85 = (bf16[2,48,384]{2,1,0:T(8,128)(2,1)}, bf16[2,48,384]{2,1,0:T(8,128)(2,1)}, u32[]{:S(2)}, u32[]{:S(2)}) collective-permute-start(bf16[2,48,384]{2,1,0:T(8,128)(2,1)} %pad_maximum_fusion.34), channel_id=1, source_target_pairs={{0,12},{4,8},{8,4},{12,0},{1,13},{5,9},{9,5},{13,1},{2,14},{6,10},... | collective-permute-start | bytes 221192 | tf_op jit(solution)/shard_map/ppermute | solution.py:554
  492.9 19.3 %collective-permute-start.88 = (bf16[128,1536]{1,0:T(8,128)(2,1)}, bf16[128,1536]{1,0:T(8,128)(2,1)}, u32[]{:S(2)}, u32[]{:S(2)}) collective-permute-start(bf16[128,1536]{1,0:T(8,128)(2,1)} %get-tuple-element.564), channel_id=1, source_target_pairs={{2,0},{0,1},{18,2},{16,3},{3,16},{1,17},{19,18},{17,19},{6,4},{4,5... | collective-permute-start | bytes 1179656 | tf_op jit(solution)/shard_map/ppermute | solution.py:663
  492.9 28.9 %collective-permute-start.89 = (bf16[128,1536]{1,0:T(8,128)(2,1)}, bf16[128,1536]{1,0:T(8,128)(2,1)}, u32[]{:S(2)}, u32[]{:S(2)}) collective-permute-start(bf16[128,1536]{1,0:T(8,128)(2,1)} %get-tuple-element.565), channel_id=1, source_target_pairs={{0,0},{2,1},{16,2},{18,3},{1,16},{3,17},{17,18},{19,19},{4,4},{6,5... | collective-permute-start | bytes 1179656 | tf_op jit(solution)/shard_map/ppermute | solution.py:663
  498.1 25.8 %collective-permute-start.90 = (bf16[128,1536]{1,0:T(8,128)(2,1)S(1)}, bf16[128,1536]{1,0:T(8,128)(2,1)S(1)}, u32[]{:S(2)}, u32[]{:S(2)}) collective-permute-start(bf16[128,1536]{1,0:T(8,128)(2,1)S(1)} %get-tuple-element.560), channel_id=1, source_target_pairs={{2,0},{0,1},{18,2},{16,3},{3,16},{1,17},{19,18},{17,19},{6,4},{4,5... | collective-permute-start | bytes 1179656 | tf_op jit(solution)/shard_map/ppermute | solution.py:663
  498.5 58.6 %collective-permute-start.91 = (bf16[128,1536]{1,0:T(8,128)(2,1)S(1)}, bf16[128,1536]{1,0:T(8,128)(2,1)S(1)}, u32[]{:S(2)}, u32[]{:S(2)}) collective-permute-start(bf16[128,1536]{1,0:T(8,128)(2,1)S(1)} %get-tuple-element.561), channel_id=1, source_target_pairs={{0,0},{2,1},{16,2},{18,3},{1,16},{3,17},{17,18},{19,19},{4,4},{6,5... | collective-permute-start | bytes 1179656 | tf_op jit(solution)/shard_map/ppermute | solution.py:663
  (123 other events, 1309.7 us)
Sparse Core Ops, SparseCore 0:
  108.3 60.3 all-gather.5
  271.2 57.9 reduce-scatter.4
  333.3 32.8 reduce-scatter.6
  369.0 30.0 reduce-scatter.8
  401.8 30.7 reduce-scatter.10
  434.0 54.3 all-gather.9
  498.1 55.4 all-gather.7

commit v5 on v4

--- a/solution.py
+++ b/solution.py
@@ -83,11 +83,11 @@
                 ok = (pos_sc[kr, :] <= qpos) & (seg_sc[kr, :] == qseg)
                 k, v = kv_ref[kr, k_cols], kv_ref[kr, v_cols]
                 state = [(m_sc[g], l_sc[g], acc_sc[g], q_ref[qr, g * HP : (g + 1) * HP]) for g in range(2)]
-                scores = [jnp.where(ok, dot(k, q, ((1,), (1,))) * scale, NEG) for _, _, _, q in state]
+                scores = [jnp.where(ok, dot(k, q, ((1,), (1,))) * scale, 2.0 * NEG) for _, _, _, q in state]
                 new = []
                 for (m_old, l_old, acc_old, _), s in zip(state, scores):
                     m_new = jnp.maximum(m_old, jnp.max(s, 0, keepdims=True))
-                    p = jnp.where(ok, jnp.exp(s - m_new), 0.0)
+                    p = jnp.exp(s - m_new)
                     decay = jnp.exp(m_old - m_new)
                     total = l_old * decay + jnp.sum(p, 0, keepdims=True)
                     new.append((m_new, total, acc_old * decay + dot(v, p.astype(BF), ((0,), (0,)))))
@@ -569,9 +569,17 @@
     return swap(value, "blk", 1), swap(value, "blk", 2)
 
 
+def halves(one, two):
+    half = one.shape[0] // 2
+    return one[:half], two[half:]
+
+
+def far_halves(low, high):
+    return swap(low, "blk", 2), swap(high, "blk", 1)
+
+
 def far(one, two):
-    half = one.shape[0] // 2
-    return swap(one[:half], "blk", 2), swap(two[half:], "blk", 1)
+    return far_halves(*halves(one, two))
 
 
 def across(*values):
@@ -782,7 +790,7 @@
     o_parts = o.reshape(2, n_blk, own, 2 * HP)
     mine_out = [output_weight, *near_out, join(far_out)]
     o_both, near_cot = fence(pair_up(o_parts[0], swap(o_parts[1], "dp", 1)), near_cot)
-    o_got, side_out, near_cot = fence(chips(o_both), across(*mine_out), near_cot)
+    o_got, side_out, near_cot, cut_cot = fence(chips(o_both), across(*mine_out), near_cot, halves(*near_cot))
     all_out = [*mine_out, *side_out]
 
     def out_project(*values):
@@ -803,13 +811,13 @@
 
     gate_w, up_w = unpack_ff(after(ff_all, input_two))
     side_two = across(input_two)
-    near_two, part_0, near_cot, gate_w, up_w = fence(
-        near(input_two), ff_part(input_two, side_two[0], cot, side_cot[0]), near_cot, gate_w, up_w
+    near_two, part_0, near_cot, cut_cot, gate_w, up_w = fence(
+        near(input_two), ff_part(input_two, side_two[0], cot, side_cot[0]), near_cot, cut_cot, gate_w, up_w
     )
     more_two = across(*near_two)
     far_two, far_cot, part_1, part_2 = fence(
         far(*near_two),
-        far(*near_cot),
+        far_halves(*cut_cot),
         ff_part(near_two[0], more_two[0], near_cot[0], side_cot[1]),
         ff_part(near_two[1], more_two[1], near_cot[1], side_cot[2]),
     )
@@ -935,9 +943,8 @@
     grad_input = (grad_mid + norm_back(grad_in_one, gain_one, normed, factor)).astype(BF)
     qkv_rel = rel_parts(qkv_mine)
     qkv_both = pair_up(qkv_rel[0], swap(qkv_rel[1], "dp", 1))
-    qkv_rows, ff_2, grad_input, block_out, out_mine = fence(
-        chips(qkv_both), step(*ff_1), grad_input, block_out, out_mine
-    )
+    qkv_rows = chips(qkv_both)
+    ff_2, grad_input, block_out = fence(step(*ff_1), grad_input, block_out)
     out_rows = out_mine.reshape(part, -1, 4 * HD).transpose(1, 0, 2) if line else out_mine
     late = join([jnp.stack(qkv_rows, 1).reshape(-1, 4 * HD), out_rows.reshape(-1, 4 * HD)])
     late = lax.all_gather(late, "head", axis=0)

time: 579 us -> 577 us (level)
    unnamed x196 -> x198, local copies, waits for them, and re-layouts: 21.5 us -> 21.4 us
  transfers between devices with their start and end apart: 99 -> 99, of which waited for: 39 -> 42; matrix products, arithmetic and copies ran while one was open for 12% -> 12% of each run, Pallas kernels for 22% -> 22%
where the time goes in v5:
time: 577 us; the launch traced here: 569 us
  waiting for transfers between devices  232 us (40%)
  Pallas kernels  137 us (24%)
  starting transfers between devices  94 us (16%)
  other arithmetic  44.9 us (8%)
  local copies, waits for them, and re-layouts  44.6 us (8%)
  between operations  16.6 us (3%)
    ppermute x80, waiting for transfers between devices, swap(): lax.ppermute(value, axis, [(i, i ^ mask) for i in range(lax.axis_size(axi...  127 us
    ppermute x80, starting transfers between devices, swap(): lax.ppermute(value, axis, [(i, i ^ mask) for i in range(lax.axis_size(axi...  63 us
    ppermute x4, waiting for transfers between devices, from_plane(): lax.ppermute(value[k * tok:(k + 1) * tok], ('dp', 'head'), back)  45.8 us
    pallas_call x5, Pallas kernels, simple_call(): pl.pallas_call(kernel, out_shape=out_shape, in_specs=whole(len(values)),...  37.7 us
    ppermute x3, waiting for transfers between devices, line_step(): lax.ppermute(left, 'head', up)  23.4 us
    all_gather x1, waiting for transfers between devices, per_device(): late_down = lax.all_gather(down_mine, 'head', axis=0)  22.1 us
    pallas_call x4, Pallas kernels, ff_call(): pl.pallas_call(ff_kernel, out_shape=(jax.ShapeDtypeStruct((2, rows, width...  21.7 us
    unnamed x198, local copies, waits for them, and re-layouts  21.4 us
  transfers between devices with their start and end apart: 99, of which 42 were waited for; matrix products, arithmetic and copies ran while one was open for 12% of the time, Pallas kernels for 22%

profile of v5, /device:TPU:8, one launch (start us, length us, event | category | flops | bytes accessed | tf_op | source)
XLA Modules:
  0.0 568.9 jit_solution(1647113635002324841)
XLA Ops:
  18.0 2.3 collective-permute-done
  24.6 3.5 collective-permute-start.6
  38.6 6.3 %collective-permute-done.3.refs_1_ = bf16[2,208,512]{2,1,0:T(8,128)(2,1)S(1)} collective-permute-done((bf16[2,208,512]{2,1,0:T(8,128)(2,1)S(1)}, bf16[2,208,512]{2,1,0:T(8,128)(2,1)S(1)}, u32[]{:S(2)}, u32[]{:S(2)}) %collective-permute-start.3) | collective-permute-done | bytes 426016 | tf_op jit(solution)/shard_map/ppermute | solution.py:554
  44.9 8.1 %collective-permute-done.4.refs_2_ = bf16[2,208,512]{2,1,0:T(8,128)(2,1)S(1)} collective-permute-done((bf16[2,208,512]{2,1,0:T(8,128)(2,1)S(1)}, bf16[2,208,512]{2,1,0:T(8,128)(2,1)S(1)}, u32[]{:S(2)}, u32[]{:S(2)}) %collective-permute-start.4) | collective-permute-done | bytes 426016 | tf_op jit(solution)/shard_map/ppermute | solution.py:554
  52.9 1.6 collective-permute-done.5.refs_3_
  54.6 8.0 %collective-permute-done.6.refs_4_ = bf16[256,1536]{1,0:T(8,128)(2,1)S(1)} collective-permute-done((bf16[256,1536]{1,0:T(8,128)(2,1)S(1)}, bf16[256,1536]{1,0:T(8,128)(2,1)S(1)}, u32[]{:S(2)}, u32[]{:S(2)}) %collective-permute-start.6) | collective-permute-done | bytes 786464 | tf_op jit(solution)/shard_map/ppermute | solution.py:664
  68.3 17.4 %collective-permute-done.9.refs_1_ = bf16[256,1536]{1,0:T(8,128)(2,1)S(1)} collective-permute-done((bf16[256,1536]{1,0:T(8,128)(2,1)S(1)}, bf16[256,1536]{1,0:T(8,128)(2,1)S(1)}, u32[]{:S(2)}, u32[]{:S(2)}) %collective-permute-start.9) | collective-permute-done | bytes 786464 | tf_op jit(solution)/shard_map/ppermute | solution.py:554
  90.3 2.4 collective-permute-start.16
  92.8 11.2 %collective-permute-done.14 = bf16[2,48,1024]{2,1,0:T(8,128)(2,1)S(1)} collective-permute-done((bf16[2,48,1024]{2,1,0:T(8,128)(2,1)}, bf16[2,48,1024]{2,1,0:T(8,128)(2,1)S(1)}, u32[]{:S(2)}, u32[]{:S(2)}) %collective-permute-start.14) | collective-permute-done | bytes 196640 | tf_op jit(solution)/shard_map/ppermute | solution.py:554
  104.0 2.3 collective-permute-done.16
  117.6 7.6 %project_qkv.1.q_ref.kv_ref = bf16[2048,512]{1,0:T(8,128)(2,1)} custom-call(bf16[256,1536]{1,0:T(8,128)(2,1)S(1)} %copy-done.26, bf16[256,1536]{1,0:T(8,128)(2,1)S(1)} %collective-permute-done.9.refs_1_, bf16[256,1536]{1,0:T(8,128)(2,1)} %copy-done.11, bf16[256,1536]{1,0:T(8,128)(2,1)} %copy-done.15, bf16[256,1536]{1,0:T(8,128)(2,1)} %collective-permute-done.11.refs_4_, ...), custom_call_target="tpu_custom_call" | custom-call | flops 50331648 | bytes 155648 | tf_op jit(solution)/shard_map/project_qkv/pallas_call | solution.py:436
  126.7 14.9 %attn_fwd.1 = (bf16[2048,256]{1,0:T(8,128)(2,1)S(1)}, f32[8,2,256]{2,1,0:T(2,128)S(1)}) custom-call(s32[8,8]{1,0:T(8,128)S(1)} %and_convert_fusion.need, bf16[2048,512]{1,0:T(8,128)(2,1)S(1)} %copy-done, bf16[2048,512]{1,0:T(8,128)(2,1)S(1)} %copy-done, f32[8,1,256]{2,1,0:T(1,128)S(1)} %bitcast.197, f32[8,1,256]{2,1,0:T(1,128)S(1)} %bitcast.201, ...), custom_call_target="tpu_custom_call" | custom-call | flops 67108864 | bytes 131072 | tf_op jit(solution)/shard_map/attn_fwd/pallas_call | solution.py:176
  143.1 2.3 collective-permute-done.24
  149.9 1.8 slice.381
  151.7 3.1 collective-permute-done.25.refs_1_
  154.8 6.0 %collective-permute-done.26.refs_2_ = bf16[2,256,256]{2,1,0:T(8,128)(2,1)S(1)} collective-permute-done((bf16[2,256,256]{2,1,0:T(8,128)(2,1)S(1)}, bf16[2,256,256]{2,1,0:T(8,128)(2,1)S(1)}, u32[]{:S(2)}, u32[]{:S(2)}) %collective-permute-start.26) | collective-permute-done | bytes 262176 | tf_op jit(solution)/shard_map/ppermute | solution.py:554
  161.3 5.8 %out_project.1 = (f32[256,1536]{1,0:T(8,128)}, bf16[256,1536]{1,0:T(8,128)(2,1)}) custom-call(bf16[2,256,256]{2,1,0:T(8,128)(2,1)S(1)} %pad_maximum_fusion.14.refs_0_, bf16[2,256,256]{2,1,0:T(8,128)(2,1)S(1)} %collective-permute-done.25.refs_1_, bf16[2,256,256]{2,1,0:T(8,128)(2,1)S(1)} %collective-permute-done.26.refs_2_, ...), custom_call_target="tpu_custom_call" | custom-call | flops 18874368 | bytes 139360 | tf_op jit(solution)/shard_map/out_project/pallas_call | solution.py:436
  171.2 1.9 copy-done.39
  174.7 4.7 ff.4
  179.5 9.8 %collective-permute-done.35.n0.refs_1_ = bf16[256,1536]{1,0:T(8,128)(2,1)} collective-permute-done((bf16[256,1536]{1,0:T(8,128)(2,1)}, bf16[256,1536]{1,0:T(8,128)(2,1)}, u32[]{:S(2)}, u32[]{:S(2)}) %collective-permute-start.35) | collective-permute-done | bytes 786464 | tf_op jit(solution)/shard_map/ppermute | solution.py:554
  197.0 5.8 %ff.5 = (bf16[2,256,512]{2,1,0:T(8,128)(2,1)S(1)}, bf16[2,256,1024]{2,1,0:T(8,128)(2,1)S(1)}, f32[256,1536]{1,0:T(8,128)S(1)}, bf16[256,1536]{1,0:T(8,128)(2,1)S(1)}) custom-call(bf16[256,1536]{1,0:T(8,128)(2,1)} %collective-permute-done.35.n0.refs_1_, bf16[256,1536]{1,0:T(8,128)(2,1)S(1)} %collective-permute-done.42.n1.refs_5_, ...), custom_call_target="tpu_custom_call" | custom-call | flops 62914560 | bytes 196608 | tf_op jit(solution)/shard_map/ff/pallas_call | solution.py:366
  204.7 6.5 %ff.6 = (bf16[2,256,512]{2,1,0:T(8,128)(2,1)S(1)}, bf16[2,256,1024]{2,1,0:T(8,128)(2,1)S(1)}, f32[256,1536]{1,0:T(8,128)S(1)}, bf16[256,1536]{1,0:T(8,128)(2,1)S(1)}) custom-call(bf16[256,1536]{1,0:T(8,128)(2,1)} %collective-permute-done.36.n0.refs_2_, bf16[256,1536]{1,0:T(8,128)(2,1)S(1)} %collective-permute-done.43.n1.refs_6_, ...), custom_call_target="tpu_custom_call" | custom-call | flops 62914560 | bytes 196608 | tf_op jit(solution)/shard_map/ff/pallas_call | solution.py:366
  216.5 4.7 ff.7
  227.7 16.8 %ff_weight.1 = (bf16[4,8,48,1024]{3,2,1,0:T(8,128)(2,1)}, bf16[512,1536]{1,0:T(8,128)(2,1)}) custom-call(bf16[256,1536]{1,0:T(8,128)(2,1)} %get-tuple-element.339.n0.refs_0_, bf16[256,1536]{1,0:T(8,128)(2,1)} %collective-permute-done.35.n0.refs_1_, bf16[256,1536]{1,0:T(8,128)(2,1)} %collective-permute-done.36.n0.refs_2_, bf16[256,1536]{1,0:T(8,128)(2,1)} %copy-done.17, ...), custom_call_target="tpu_custom_call" | custom-call | flops 150994944 | bytes 393216 | tf_op jit(solution)/shard_map/ff_weight/pallas_call | solution.py:413
  244.6 17.3 %collective-permute-done.51.refs_10_ = bf16[256,1536]{1,0:T(8,128)(2,1)} collective-permute-done((bf16[256,1536]{1,0:T(8,128)(2,1)S(1)}, bf16[256,1536]{1,0:T(8,128)(2,1)}, u32[]{:S(2)}, u32[]{:S(2)}) %collective-permute-start.51) | collective-permute-done | bytes 786464 | tf_op jit(solution)/shard_map/ppermute | solution.py:554
  261.9 7.4 %branch.1 = (f32[256,1536]{1,0:T(8,128)}, bf16[256,1536]{1,0:T(8,128)(2,1)}, bf16[2,4,256,256]{3,2,1,0:T(8,128)(2,1)}) custom-call(bf16[192,1536]{1,0:T(8,128)(2,1)} %refs_0_.1, bf16[192,1536]{1,0:T(8,128)(2,1)S(1)} %copy-done.21, bf16[192,1536]{1,0:T(8,128)(2,1)S(1)} %copy-done.24, bf16[192,1536]{1,0:T(8,128)(2,1)} %copy-done.63, ...), custom_call_target="tpu_custom_call" | custom-call | flops 18874368 | bytes 225376 | tf_op jit(solution)/shard_map/branch/pallas_call | solution.py:436
  273.1 8.3 %back_project.2 = (f32[4,256,1536]{2,1,0:T(8,128)}, bf16[4,256,1536]{2,1,0:T(8,128)(2,1)}) custom-call(bf16[2,256,512]{2,1,0:T(8,128)(2,1)S(1)} %copy-done.43, bf16[2,256,512]{2,1,0:T(8,128)(2,1)S(1)} %copy-done.45, bf16[2,256,512]{2,1,0:T(8,128)(2,1)S(1)} %copy-done.47, bf16[2,256,512]{2,1,0:T(8,128)(2,1)} %copy-done.48, bf16[512,1536]{1,0:T(8,128)(2,1)} %refs_4_.3), custom_call_target="tpu_custom_call" | custom-call | flops 50331648 | bytes 204800 | tf_op jit(solution)/shard_map/back_project/pallas_call | solution.py:436
  283.6 1.8 collective-permute-start.56
  285.5 5.7 collective-permute-done.54
  291.1 4.9 collective-permute-done.55
  298.3 19.9 %attn_bwd.1.refs_8_.refs_0_ = bf16[2048,512]{1,0:T(8,128)(2,1)S(1)} custom-call(s32[8,8]{1,0:T(8,128)S(1)} %and_convert_fusion.need, bf16[2048,512]{1,0:T(8,128)(2,1)} %project_qkv.1.q_ref.kv_ref, bf16[2048,512]{1,0:T(8,128)(2,1)} %project_qkv.1.q_ref.kv_ref, f32[8,1,256]{2,1,0:T(1,128)S(1)} %bitcast.199, f32[8,1,256]{2,1,0:T(1,128)S(1)} %bitcast.203, ...), custom_call_target="tpu_custom_call" | custom-call | flops 167772160 | bytes 131072 | tf_op jit(solution)/shard_map/attn_bwd/pallas_call | solution.py:193
  318.3 2.1 slice.398
  321.9 1.8 slice.399
  324.2 4.6 add_convert_fusion.4
  332.0 7.6 %qkv_weight.1 = bf16[4,8,48,384]{3,2,1,0:T(8,128)(2,1)} custom-call(bf16[256,1536]{1,0:T(8,128)(2,1)S(1)} %copy-done.27, bf16[256,1536]{1,0:T(8,128)(2,1)S(1)} %copy-done.10, bf16[256,1536]{1,0:T(8,128)(2,1)S(1)} %copy-done.12, bf16[256,1536]{1,0:T(8,128)(2,1)S(1)} %copy-done.16, bf16[256,1536]{1,0:T(8,128)(2,1)} %collective-permute-done.11.refs_4_, ...), custom_call_target="tpu_custom_call" | custom-call | flops 100663296 | bytes 196608 | tf_op jit(solution)/shard_map/qkv_weight/pallas_call | solution.py:534
  348.0 8.6 %back_project.3 = (f32[4,256,1536]{2,1,0:T(8,128)}, bf16[4,256,1536]{2,1,0:T(8,128)(2,1)}) custom-call(bf16[2048,512]{1,0:T(8,128)(2,1)} %copy-done.2, bf16[1536,512]{1,0:T(8,128)(2,1)S(1)} %copy-done.8), custom_call_target="tpu_custom_call" | custom-call | flops 50331648 | bytes 204800 | tf_op jit(solution)/shard_map/back_project/pallas_call | solution.py:436
  358.8 6.9 %collective-permute-done.69 = bf16[256,1536]{1,0:T(8,128)(2,1)S(1)} collective-permute-done((bf16[256,1536]{1,0:T(8,128)(2,1)S(1)}, bf16[256,1536]{1,0:T(8,128)(2,1)S(1)}, u32[]{:S(2)}, u32[]{:S(2)}) %collective-permute-start.69) | collective-permute-done | bytes 786464 | tf_op jit(solution)/shard_map/ppermute | solution.py:554
  371.4 6.0 %out_weight.1 = bf16[192,1536]{1,0:T(8,128)(2,1)} custom-call(bf16[2048,256]{1,0:T(8,128)(2,1)} %copy-done.5, bf16[256,1536]{1,0:T(8,128)(2,1)S(1)} %copy-done.59, bf16[256,1536]{1,0:T(8,128)(2,1)} %collective-permute-done.58.refs_2_, bf16[256,1536]{1,0:T(8,128)(2,1)} %collective-permute-done.59.refs_3_, ...), custom_call_target="tpu_custom_call" | custom-call | flops 50331648 | bytes 147456 | tf_op jit(solution)/shard_map/out_weight/pallas_call | solution.py:914
  377.4 6.3 %fusion.10 = (bf16[256,1536]{1,0:T(8,128)(2,1)}, bf16[256,1536]{1,0:T(8,128)(2,1)}, bf16[256,1536]{1,0:T(8,128)(2,1)}, f32[256,1536]{1,0:T(8,128)}) fusion(f32[4,256,1536]{2,1,0:T(8,128)} %get-tuple-element.458, bf16[4,256,1536]{2,1,0:T(8,128)(2,1)} %collective-permute-done.74), kind=kLoop, calls=%fused_computation.30 | loop fusion | flops 4325376 | bytes 13369344 | tf_op jit(solution)/shard_map/convert_element_type | solution.py:931
  384.9 1.9 collective-permute-start.78
  386.8 4.0 collective-permute-start.80
  395.3 15.5 %collective-permute-done.78.refs_2_ = bf16[8,48,1024]{2,1,0:T(8,128)(2,1)S(1)} collective-permute-done((bf16[8,48,1024]{2,1,0:T(8,128)(2,1)S(1)}, bf16[8,48,1024]{2,1,0:T(8,128)(2,1)S(1)}, u32[]{:S(2)}, u32[]{:S(2)}) %collective-permute-start.78) | collective-permute-done | bytes 786464 | tf_op jit(solution)/shard_map/ppermute | solution.py:615
  410.9 3.6 collective-permute-start.79
  414.5 3.1 collective-permute-start.81
  417.6 3.7 add_convert_fusion
  421.4 6.7 %collective-permute-done.76 = bf16[256,1536]{1,0:T(8,128)(2,1)} collective-permute-done((bf16[256,1536]{1,0:T(8,128)(2,1)}, bf16[256,1536]{1,0:T(8,128)(2,1)}, u32[]{:S(2)}, u32[]{:S(2)}) %collective-permute-start.76) | collective-permute-done | bytes 786464 | tf_op jit(solution)/shard_map/ppermute | solution.py:554
  428.1 3.8 reduce-scatter.11.cloned.1.call-done
  431.9 7.9 %collective-permute-done.79.refs_1_ = bf16[8,48,1024]{2,1,0:T(8,128)(2,1)} collective-permute-done((bf16[8,48,1024]{2,1,0:T(8,128)(2,1)S(1)}, bf16[8,48,1024]{2,1,0:T(8,128)(2,1)}, u32[]{:S(2)}, u32[]{:S(2)}) %collective-permute-start.79) | collective-permute-done | bytes 786464 | tf_op jit(solution)/shard_map/ppermute | solution.py:615
  439.8 1.7 collective-permute-done.81.refs_5_
  441.5 2.8 collective-permute-start.82
  444.4 3.9 collective-permute-start.83
  449.9 3.0 fusion.2
  453.0 3.3 fusion.6
  457.2 2.5 collective-permute-start.91
  461.0 1.9 collective-permute-done.91
  465.7 22.1 %all-gather.10.cloned.1.call-done = bf16[512,1536]{1,0:T(8,128)(2,1)} async-done(((bf16[128,1536]{1,0:T(8,128)(2,1)}), bf16[512,1536]{1,0:T(8,128)(2,1)}) %all-gather.10.cloned.1.call-update) | async-done | bytes 1572880 | tf_op jit(solution)/shard_map/all_gather | solution.py:935
  487.7 3.5 convert_element_type.225
  491.4 3.2 collective-permute-start.85
  495.0 3.8 collective-permute-start.87
  498.8 5.0 place_columns.1
  503.9 2.5 multiply_reduce_fusion.1
  508.4 32.4 %collective-permute-done.85 = bf16[128,1536]{1,0:T(8,128)(2,1)S(1)} collective-permute-done((bf16[128,1536]{1,0:T(8,128)(2,1)S(1)}, bf16[128,1536]{1,0:T(8,128)(2,1)S(1)}, u32[]{:S(2)}, u32[]{:S(2)}) %collective-permute-start.85) | collective-permute-done | bytes 393248 | tf_op jit(solution)/shard_map/ppermute | solution.py:671
  541.9 13.3 %collective-permute-done.87 = bf16[128,1536]{1,0:T(8,128)(2,1)S(1)} collective-permute-done((bf16[128,1536]{1,0:T(8,128)(2,1)S(1)}, bf16[128,1536]{1,0:T(8,128)(2,1)S(1)}, u32[]{:S(2)}, u32[]{:S(2)}) %collective-permute-start.87) | collective-permute-done | bytes 393248 | tf_op jit(solution)/shard_map/ppermute | solution.py:671
  557.7 3.9 last.1
  (498 shorter events, 129.2 us)
Async XLA Ops:
  7.2 164.0 %all-gather.6.cloned.1.call-start = ((), (), s32[]{:S(2)}) async-start(), calls=%async_computation.4 | async-start | bytes 3932160 | tf_op jit(solution)/shard_map/all_gather | solution.py:787
  7.2 15.3 %collective-permute-start.1 = (bf16[192,1536]{1,0:T(8,128)(2,1)}, bf16[192,1536]{1,0:T(8,128)(2,1)S(1)}, u32[]{:S(2)}, u32[]{:S(2)}) collective-permute-start(bf16[192,1536]{1,0:T(8,128)(2,1)} %refs_0_.1), channel_id=1, source_target_pairs={{0,4},{4,0},{8,12},{12,8},{1,5},{5,1},{9,13},{13,9},{2,6},{6,2},{1... | collective-permute-start | bytes 1769480 | tf_op jit(solution)/shard_map/ppermute | solution.py:554
  8.8 15.0 %collective-permute-start.2 = (bf16[192,1536]{1,0:T(8,128)(2,1)}, bf16[192,1536]{1,0:T(8,128)(2,1)S(1)}, u32[]{:S(2)}, u32[]{:S(2)}) collective-permute-start(bf16[192,1536]{1,0:T(8,128)(2,1)} %refs_0_.1), channel_id=1, source_target_pairs={{0,8},{4,12},{8,0},{12,4},{1,9},{5,13},{9,1},{13,5},{2,10},{6,14},... | collective-permute-start | bytes 1769480 | tf_op jit(solution)/shard_map/ppermute | solution.py:554
  24.6 37.9 %collective-permute-start.6 = (bf16[256,1536]{1,0:T(8,128)(2,1)S(1)}, bf16[256,1536]{1,0:T(8,128)(2,1)S(1)}, u32[]{:S(2)}, u32[]{:S(2)}) collective-permute-start(bf16[256,1536]{1,0:T(8,128)(2,1)S(1)} %pad_maximum_fusion.1), channel_id=1, source_target_pairs={{0,0},{1,2},{2,16},{3,18},{16,1},{17,3},{18,17},{19,19},{4,4},{5,6... | collective-permute-start | bytes 2359304 | tf_op jit(solution)/shard_map/ppermute | solution.py:664
  32.1 30.5 %collective-permute-start.7 = (bf16[256,1536]{1,0:T(8,128)(2,1)S(1)}, bf16[256,1536]{1,0:T(8,128)(2,1)S(1)}, u32[]{:S(2)}, u32[]{:S(2)}) collective-permute-start(bf16[256,1536]{1,0:T(8,128)(2,1)S(1)} %pad_maximum_fusion.2), channel_id=1, source_target_pairs={{0,2},{1,0},{2,18},{3,16},{16,3},{17,1},{18,19},{19,17},{4,6},{5,4... | collective-permute-start | bytes 2359304 | tf_op jit(solution)/shard_map/ppermute | solution.py:664
  32.8 20.1 %collective-permute-start.4 = (bf16[2,208,512]{2,1,0:T(8,128)(2,1)S(1)}, bf16[2,208,512]{2,1,0:T(8,128)(2,1)S(1)}, u32[]{:S(2)}, u32[]{:S(2)}) collective-permute-start(bf16[2,208,512]{2,1,0:T(8,128)(2,1)S(1)} %get-tuple-element.260), channel_id=1, source_target_pairs={{0,8},{4,12},{8,0},{12,4},{1,9},{5,13},{9,1},{13,5},{2,10},{6,14},... | collective-permute-start | bytes 1277960 | tf_op jit(solution)/shard_map/ppermute | solution.py:554
  34.3 20.2 %collective-permute-start.5 = (bf16[2,208,512]{2,1,0:T(8,128)(2,1)S(1)}, bf16[2,208,512]{2,1,0:T(8,128)(2,1)S(1)}, u32[]{:S(2)}, u32[]{:S(2)}) collective-permute-start(bf16[2,208,512]{2,1,0:T(8,128)(2,1)S(1)} %get-tuple-element.261), channel_id=1, source_target_pairs={{0,12},{4,8},{8,4},{12,0},{1,13},{5,9},{9,5},{13,1},{2,14},{6,10},... | collective-permute-start | bytes 1277960 | tf_op jit(solution)/shard_map/ppermute | solution.py:554
  65.8 19.9 %collective-permute-start.9 = (bf16[256,1536]{1,0:T(8,128)(2,1)S(1)}, bf16[256,1536]{1,0:T(8,128)(2,1)S(1)}, u32[]{:S(2)}, u32[]{:S(2)}) collective-permute-start(bf16[256,1536]{1,0:T(8,128)(2,1)S(1)} %get-tuple-element.295.refs_0_), channel_id=1, source_target_pairs={{0,4},{4,0},{8,12},{12,8},{1,5},{5,1},{9,13},{13,9},{2,6},{6,2},{1... | collective-permute-start | bytes 2359304 | tf_op jit(solution)/shard_map/ppermute | solution.py:554
  66.3 19.6 %collective-permute-start.10 = (bf16[256,1536]{1,0:T(8,128)(2,1)S(1)}, bf16[256,1536]{1,0:T(8,128)(2,1)S(1)}, u32[]{:S(2)}, u32[]{:S(2)}) collective-permute-start(bf16[256,1536]{1,0:T(8,128)(2,1)S(1)} %get-tuple-element.295.refs_0_), channel_id=1, source_target_pairs={{0,8},{4,12},{8,0},{12,4},{1,9},{5,13},{9,1},{13,5},{2,10},{6,14},... | collective-permute-start | bytes 2359304 | tf_op jit(solution)/shard_map/ppermute | solution.py:554
  67.9 18.1 %collective-permute-start.11 = (bf16[256,1536]{1,0:T(8,128)(2,1)S(1)}, bf16[256,1536]{1,0:T(8,128)(2,1)}, u32[]{:S(2)}, u32[]{:S(2)}) collective-permute-start(bf16[256,1536]{1,0:T(8,128)(2,1)S(1)} %get-tuple-element.295.refs_0_), channel_id=1, source_target_pairs={{0,16},{16,0},{1,17},{17,1},{2,18},{18,2},{3,19},{19,3},{4,20},{20... | collective-permute-start | bytes 2359304 | tf_op jit(solution)/shard_map/ppermute | solution.py:554
  86.0 20.2 %collective-permute-start.12 = (bf16[128,1536]{1,0:T(8,128)(2,1)S(1)}, bf16[128,1536]{1,0:T(8,128)(2,1)S(1)}, u32[]{:S(2)}, u32[]{:S(2)}) collective-permute-start(bf16[128,1536]{1,0:T(8,128)(2,1)S(1)} %slice.362), channel_id=1, source_target_pairs={{0,8},{4,12},{8,0},{12,4},{1,9},{5,13},{9,1},{13,5},{2,10},{6,14},... | collective-permute-start | bytes 1179656 | tf_op jit(solution)/shard_map/ppermute | solution.py:554
  87.6 18.6 %collective-permute-start.13 = (bf16[128,1536]{1,0:T(8,128)(2,1)S(1)}, bf16[128,1536]{1,0:T(8,128)(2,1)S(1)}, u32[]{:S(2)}, u32[]{:S(2)}) collective-permute-start(bf16[128,1536]{1,0:T(8,128)(2,1)S(1)} %slice.363), channel_id=1, source_target_pairs={{0,4},{4,0},{8,12},{12,8},{1,5},{5,1},{9,13},{13,9},{2,6},{6,2},{1... | collective-permute-start | bytes 1179656 | tf_op jit(solution)/shard_map/ppermute | solution.py:554
  89.2 14.7 %collective-permute-start.14 = (bf16[2,48,1024]{2,1,0:T(8,128)(2,1)}, bf16[2,48,1024]{2,1,0:T(8,128)(2,1)S(1)}, u32[]{:S(2)}, u32[]{:S(2)}) collective-permute-start(bf16[2,48,1024]{2,1,0:T(8,128)(2,1)} %pad_maximum_fusion.23), channel_id=1, source_target_pairs={{0,4},{4,0},{8,12},{12,8},{1,5},{5,1},{9,13},{13,9},{2,6},{6,2},{1... | collective-permute-start | bytes 589832 | tf_op jit(solution)/shard_map/ppermute | solution.py:554
  89.8 14.2 %collective-permute-start.15 = (bf16[2,48,1024]{2,1,0:T(8,128)(2,1)}, bf16[2,48,1024]{2,1,0:T(8,128)(2,1)S(1)}, u32[]{:S(2)}, u32[]{:S(2)}) collective-permute-start(bf16[2,48,1024]{2,1,0:T(8,128)(2,1)} %pad_maximum_fusion.24), channel_id=1, source_target_pairs={{0,8},{4,12},{8,0},{12,4},{1,9},{5,13},{9,1},{13,5},{2,10},{6,14},... | collective-permute-start | bytes 589832 | tf_op jit(solution)/shard_map/ppermute | solution.py:554
  90.3 15.9 %collective-permute-start.16 = (bf16[2,48,1024]{2,1,0:T(8,128)(2,1)}, bf16[2,48,1024]{2,1,0:T(8,128)(2,1)S(1)}, u32[]{:S(2)}, u32[]{:S(2)}) collective-permute-start(bf16[2,48,1024]{2,1,0:T(8,128)(2,1)} %pad_maximum_fusion.25), channel_id=1, source_target_pairs={{0,12},{4,8},{8,4},{12,0},{1,13},{5,9},{9,5},{13,1},{2,14},{6,10},... | collective-permute-start | bytes 589832 | tf_op jit(solution)/shard_map/ppermute | solution.py:554
  104.0 43.1 %collective-permute-start.28 = (bf16[192,1536]{1,0:T(8,128)(2,1)}, bf16[192,1536]{1,0:T(8,128)(2,1)}, u32[]{:S(2)}, u32[]{:S(2)}) collective-permute-start(bf16[192,1536]{1,0:T(8,128)(2,1)} %refs_0_.1), channel_id=1, source_target_pairs={{0,16},{16,0},{1,17},{17,1},{2,18},{18,2},{3,19},{19,3},{4,20},{20... | collective-permute-start | bytes 1769480 | tf_op jit(solution)/shard_map/ppermute | solution.py:554
  108.1 233.4 %reduce-scatter.5.cloned.1.call-start = ((), (), s32[]{:S(2)}) async-start(), calls=%async_computation.5 | async-start | bytes 3932160 | tf_op jit(solution)/shard_map/reduce_scatter | solution.py:843
  111.0 31.2 %collective-permute-start.20 = (bf16[256,1536]{1,0:T(8,128)(2,1)S(1)}, bf16[256,1536]{1,0:T(8,128)(2,1)S(1)}, u32[]{:S(2)}, u32[]{:S(2)}) collective-permute-start(bf16[256,1536]{1,0:T(8,128)(2,1)S(1)} %get-tuple-element.310.c0.refs_8_.refs_13_), channel_id=1, source_target_pairs={{0,4},{4,0},{8,12},{12,8},{1,5},{5,1},{9,13},{13,9},{2,6},{6,2},{1... | collective-permute-start | bytes 2359304 | tf_op jit(solution)/shard_map/ppermute | solution.py:554
  112.5 29.8 %collective-permute-start.21 = (bf16[256,1536]{1,0:T(8,128)(2,1)S(1)}, bf16[256,1536]{1,0:T(8,128)(2,1)}, u32[]{:S(2)}, u32[]{:S(2)}) collective-permute-start(bf16[256,1536]{1,0:T(8,128)(2,1)S(1)} %get-tuple-element.310.c0.refs_8_.refs_13_), channel_id=1, source_target_pairs={{0,8},{4,12},{8,0},{12,4},{1,9},{5,13},{9,1},{13,5},{2,10},{6,14},... | collective-permute-start | bytes 2359304 | tf_op jit(solution)/shard_map/ppermute | solution.py:554
  115.1 26.6 %collective-permute-start.22 = (bf16[96,1536]{1,0:T(8,128)(2,1)S(1)}, bf16[96,1536]{1,0:T(8,128)(2,1)S(1)}, u32[]{:S(2)}, u32[]{:S(2)}) collective-permute-start(bf16[96,1536]{1,0:T(8,128)(2,1)S(1)} %slice.365), channel_id=1, source_target_pairs={{0,8},{4,12},{8,0},{12,4},{1,9},{5,13},{9,1},{13,5},{2,10},{6,14},... | collective-permute-start | bytes 884744 | tf_op jit(solution)/shard_map/ppermute | solution.py:554
  116.6 25.1 %collective-permute-start.23 = (bf16[96,1536]{1,0:T(8,128)(2,1)S(1)}, bf16[96,1536]{1,0:T(8,128)(2,1)S(1)}, u32[]{:S(2)}, u32[]{:S(2)}) collective-permute-start(bf16[96,1536]{1,0:T(8,128)(2,1)S(1)} %slice.366), channel_id=1, source_target_pairs={{0,4},{4,0},{8,12},{12,8},{1,5},{5,1},{9,13},{13,9},{2,6},{6,2},{1... | collective-permute-start | bytes 884744 | tf_op jit(solution)/shard_map/ppermute | solution.py:554
  151.7 15.5 %collective-permute-start.32 = (bf16[256,1536]{1,0:T(8,128)(2,1)S(1)}, bf16[256,1536]{1,0:T(8,128)(2,1)S(1)}, u32[]{:S(2)}, u32[]{:S(2)}) collective-permute-start(bf16[256,1536]{1,0:T(8,128)(2,1)S(1)} %get-tuple-element.310.c0.refs_8_.refs_13_), channel_id=1, source_target_pairs={{0,16},{16,0},{1,17},{17,1},{2,18},{18,2},{3,19},{19,3},{4,20},{20... | collective-permute-start | bytes 2359304 | tf_op jit(solution)/shard_map/ppermute | solution.py:554
  169.1 20.2 %collective-permute-start.35 = (bf16[256,1536]{1,0:T(8,128)(2,1)}, bf16[256,1536]{1,0:T(8,128)(2,1)}, u32[]{:S(2)}, u32[]{:S(2)}) collective-permute-start(bf16[256,1536]{1,0:T(8,128)(2,1)} %get-tuple-element.339.n0.refs_0_), channel_id=1, source_target_pairs={{0,4},{4,0},{8,12},{12,8},{1,5},{5,1},{9,13},{13,9},{2,6},{6,2},{1... | collective-permute-start | bytes 2359304 | tf_op jit(solution)/shard_map/ppermute | solution.py:554
  170.2 20.0 %collective-permute-start.36 = (bf16[256,1536]{1,0:T(8,128)(2,1)}, bf16[256,1536]{1,0:T(8,128)(2,1)}, u32[]{:S(2)}, u32[]{:S(2)}) collective-permute-start(bf16[256,1536]{1,0:T(8,128)(2,1)} %get-tuple-element.339.n0.refs_0_), channel_id=1, source_target_pairs={{0,8},{4,12},{8,0},{12,4},{1,9},{5,13},{9,1},{13,5},{2,10},{6,14},... | collective-permute-start | bytes 2359304 | tf_op jit(solution)/shard_map/ppermute | solution.py:554
  190.2 14.4 %collective-permute-start.43 = (bf16[256,1536]{1,0:T(8,128)(2,1)}, bf16[256,1536]{1,0:T(8,128)(2,1)S(1)}, u32[]{:S(2)}, u32[]{:S(2)}) collective-permute-start(bf16[256,1536]{1,0:T(8,128)(2,1)} %collective-permute-done.36.n0.refs_2_), channel_id=1, source_target_pairs={{0,16},{16,0},{1,17},{17,1},{2,18},{18,2},{3,19},{19,3},{4,20},{20... | collective-permute-start | bytes 2359304 | tf_op jit(solution)/shard_map/ppermute | solution.py:554
  192.8 19.4 %collective-permute-start.38 = (bf16[128,1536]{1,0:T(8,128)(2,1)S(1)}, bf16[128,1536]{1,0:T(8,128)(2,1)S(1)}, u32[]{:S(2)}, u32[]{:S(2)}) collective-permute-start(bf16[128,1536]{1,0:T(8,128)(2,1)S(1)} %slice.383), channel_id=1, source_target_pairs={{0,8},{4,12},{8,0},{12,4},{1,9},{5,13},{9,1},{13,5},{2,10},{6,14},... | collective-permute-start | bytes 1179656 | tf_op jit(solution)/shard_map/ppermute | solution.py:554
  193.8 18.4 %collective-permute-start.39 = (bf16[128,1536]{1,0:T(8,128)(2,1)S(1)}, bf16[128,1536]{1,0:T(8,128)(2,1)S(1)}, u32[]{:S(2)}, u32[]{:S(2)}) collective-permute-start(bf16[128,1536]{1,0:T(8,128)(2,1)S(1)} %slice.384), channel_id=1, source_target_pairs={{0,4},{4,0},{8,12},{12,8},{1,5},{5,1},{9,13},{13,9},{2,6},{6,2},{1... | collective-permute-start | bytes 1179656 | tf_op jit(solution)/shard_map/ppermute | solution.py:554
  195.2 17.1 %collective-permute-start.40 = (bf16[128,1536]{1,0:T(8,128)(2,1)S(1)}, bf16[128,1536]{1,0:T(8,128)(2,1)S(1)}, u32[]{:S(2)}, u32[]{:S(2)}) collective-permute-start(bf16[128,1536]{1,0:T(8,128)(2,1)S(1)} %copy-done.84), channel_id=1, source_target_pairs={{0,8},{4,12},{8,0},{12,4},{1,9},{5,13},{9,1},{13,5},{2,10},{6,14},... | collective-permute-start | bytes 1179656 | tf_op jit(solution)/shard_map/ppermute | solution.py:554
  195.7 17.2 %collective-permute-start.41 = (bf16[128,1536]{1,0:T(8,128)(2,1)S(1)}, bf16[128,1536]{1,0:T(8,128)(2,1)S(1)}, u32[]{:S(2)}, u32[]{:S(2)}) collective-permute-start(bf16[128,1536]{1,0:T(8,128)(2,1)S(1)} %copy-done.83), channel_id=1, source_target_pairs={{0,4},{4,0},{8,12},{12,8},{1,5},{5,1},{9,13},{13,9},{2,6},{6,2},{1... | collective-permute-start | bytes 1179656 | tf_op jit(solution)/shard_map/ppermute | solution.py:554
  224.1 20.4 %collective-permute-start.50 = (bf16[256,1536]{1,0:T(8,128)(2,1)S(1)}, bf16[256,1536]{1,0:T(8,128)(2,1)S(1)}, u32[]{:S(2)}, u32[]{:S(2)}) collective-permute-start(bf16[256,1536]{1,0:T(8,128)(2,1)S(1)} %add_convert_fusion.7), channel_id=1, source_target_pairs={{0,4},{4,0},{8,12},{12,8},{1,5},{5,1},{9,13},{13,9},{2,6},{6,2},{1... | collective-permute-start | bytes 2359304 | tf_op jit(solution)/shard_map/ppermute | solution.py:554
  225.6 36.3 %collective-permute-start.51 = (bf16[256,1536]{1,0:T(8,128)(2,1)S(1)}, bf16[256,1536]{1,0:T(8,128)(2,1)}, u32[]{:S(2)}, u32[]{:S(2)}) collective-permute-start(bf16[256,1536]{1,0:T(8,128)(2,1)S(1)} %add_convert_fusion.6), channel_id=1, source_target_pairs={{0,8},{4,12},{8,0},{12,4},{1,9},{5,13},{9,1},{13,5},{2,10},{6,14},... | collective-permute-start | bytes 2359304 | tf_op jit(solution)/shard_map/ppermute | solution.py:554
  226.1 35.8 %collective-permute-start.52 = (bf16[256,1536]{1,0:T(8,128)(2,1)S(1)}, bf16[256,1536]{1,0:T(8,128)(2,1)}, u32[]{:S(2)}, u32[]{:S(2)}) collective-permute-start(bf16[256,1536]{1,0:T(8,128)(2,1)S(1)} %add_convert_fusion.5), channel_id=1, source_target_pairs={{0,12},{4,8},{8,4},{12,0},{1,13},{5,9},{9,5},{13,1},{2,14},{6,10},... | collective-permute-start | bytes 2359304 | tf_op jit(solution)/shard_map/ppermute | solution.py:554
  270.5 113.2 %reduce-scatter.7.cloned.1.call-start = ((), (), s32[]{:S(2)}) async-start(), calls=%async_computation.6 | async-start | bytes 1966080 | tf_op jit(solution)/shard_map/reduce_scatter | solution.py:843
  281.4 14.7 %collective-permute-start.57 = (bf16[4,256,1536]{2,1,0:T(8,128)(2,1)}, bf16[4,256,1536]{2,1,0:T(8,128)(2,1)S(1)}, u32[]{:S(2)}, u32[]{:S(2)}) collective-permute-start(bf16[4,256,1536]{2,1,0:T(8,128)(2,1)} %get-tuple-element.423), channel_id=1, source_target_pairs={{0,16},{16,0},{1,17},{17,1},{2,18},{18,2},{3,19},{19,3},{4,20},{20... | collective-permute-start | bytes 9437192 | tf_op jit(solution)/shard_map/ppermute | solution.py:554
  296.1 22.2 %collective-permute-start.58 = (bf16[256,1536]{1,0:T(8,128)(2,1)S(1)}, bf16[256,1536]{1,0:T(8,128)(2,1)}, u32[]{:S(2)}, u32[]{:S(2)}) collective-permute-start(bf16[256,1536]{1,0:T(8,128)(2,1)S(1)} %copy-done.58), channel_id=1, source_target_pairs={{0,4},{4,0},{8,12},{12,8},{1,5},{5,1},{9,13},{13,9},{2,6},{6,2},{1... | collective-permute-start | bytes 2359304 | tf_op jit(solution)/shard_map/ppermute | solution.py:554
  297.6 20.7 %collective-permute-start.59 = (bf16[256,1536]{1,0:T(8,128)(2,1)S(1)}, bf16[256,1536]{1,0:T(8,128)(2,1)}, u32[]{:S(2)}, u32[]{:S(2)}) collective-permute-start(bf16[256,1536]{1,0:T(8,128)(2,1)S(1)} %copy-done.58), channel_id=1, source_target_pairs={{0,8},{4,12},{8,0},{12,4},{1,9},{5,13},{9,1},{13,5},{2,10},{6,14},... | collective-permute-start | bytes 2359304 | tf_op jit(solution)/shard_map/ppermute | solution.py:554
  320.4 19.3 %collective-permute-start.60 = (bf16[128,1536]{1,0:T(8,128)(2,1)}, bf16[128,1536]{1,0:T(8,128)(2,1)S(1)}, u32[]{:S(2)}, u32[]{:S(2)}) collective-permute-start(bf16[128,1536]{1,0:T(8,128)(2,1)} %slice.398), channel_id=1, source_target_pairs={{0,8},{4,12},{8,0},{12,4},{1,9},{5,13},{9,1},{13,5},{2,10},{6,14},... | collective-permute-start | bytes 1179656 | tf_op jit(solution)/shard_map/ppermute | solution.py:554
  323.7 16.5 %collective-permute-start.61 = (bf16[128,1536]{1,0:T(8,128)(2,1)}, bf16[128,1536]{1,0:T(8,128)(2,1)}, u32[]{:S(2)}, u32[]{:S(2)}) collective-permute-start(bf16[128,1536]{1,0:T(8,128)(2,1)} %slice.399), channel_id=1, source_target_pairs={{0,4},{4,0},{8,12},{12,8},{1,5},{5,1},{9,13},{13,9},{2,6},{6,2},{1... | collective-permute-start | bytes 1179656 | tf_op jit(solution)/shard_map/ppermute | solution.py:554
  331.9 89.5 %reduce-scatter.9.cloned.1.call-start = ((), (), s32[]{:S(2)}) async-start(), calls=%async_computation.7 | async-start | bytes 1474560 | tf_op jit(solution)/shard_map/reduce_scatter | solution.py:843
  331.9 14.0 %collective-permute-start.64 = (bf16[256,1536]{1,0:T(8,128)(2,1)}, bf16[256,1536]{1,0:T(8,128)(2,1)}, u32[]{:S(2)}, u32[]{:S(2)}) collective-permute-start(bf16[256,1536]{1,0:T(8,128)(2,1)} %get-tuple-element.429.refs_1_), channel_id=1, source_target_pairs={{0,16},{16,0},{1,17},{17,1},{2,18},{18,2},{3,19},{19,3},{4,20},{20... | collective-permute-start | bytes 2359304 | tf_op jit(solution)/shard_map/ppermute | solution.py:554
  339.7 19.1 %collective-permute-start.65 = (bf16[256,1536]{1,0:T(8,128)(2,1)}, bf16[256,1536]{1,0:T(8,128)(2,1)S(1)}, u32[]{:S(2)}, u32[]{:S(2)}) collective-permute-start(bf16[256,1536]{1,0:T(8,128)(2,1)} %collective-permute-done.58.refs_2_), channel_id=1, source_target_pairs={{0,16},{16,0},{1,17},{17,1},{2,18},{18,2},{3,19},{19,3},{4,20},{20... | collective-permute-start | bytes 2359304 | tf_op jit(solution)/shard_map/ppermute | solution.py:554
  340.2 18.6 %collective-permute-start.66 = (bf16[256,1536]{1,0:T(8,128)(2,1)}, bf16[256,1536]{1,0:T(8,128)(2,1)S(1)}, u32[]{:S(2)}, u32[]{:S(2)}) collective-permute-start(bf16[256,1536]{1,0:T(8,128)(2,1)} %collective-permute-done.59.refs_3_), channel_id=1, source_target_pairs={{0,16},{16,0},{1,17},{17,1},{2,18},{18,2},{3,19},{19,3},{4,20},{20... | collective-permute-start | bytes 2359304 | tf_op jit(solution)/shard_map/ppermute | solution.py:554
  342.8 16.1 %collective-permute-start.67 = (bf16[256,1536]{1,0:T(8,128)(2,1)S(1)}, bf16[256,1536]{1,0:T(8,128)(2,1)S(1)}, u32[]{:S(2)}, u32[]{:S(2)}) collective-permute-start(bf16[256,1536]{1,0:T(8,128)(2,1)S(1)} %constant_dynamic-update-slice_fusion.10.refs_4_), channel_id=1, source_target_pairs={{0,16},{16,0},{1,17},{17,1},{2,18},{18,2},{3,19},{19,3},{4,20},{20... | collective-permute-start | bytes 2359304 | tf_op jit(solution)/shard_map/ppermute | solution.py:554
  346.0 19.8 %collective-permute-start.69 = (bf16[256,1536]{1,0:T(8,128)(2,1)S(1)}, bf16[256,1536]{1,0:T(8,128)(2,1)S(1)}, u32[]{:S(2)}, u32[]{:S(2)}) collective-permute-start(bf16[256,1536]{1,0:T(8,128)(2,1)S(1)} %pad_maximum_fusion.4), channel_id=1, source_target_pairs={{0,4},{4,0},{8,12},{12,8},{1,5},{5,1},{9,13},{13,9},{2,6},{6,2},{1... | collective-permute-start | bytes 2359304 | tf_op jit(solution)/shard_map/ppermute | solution.py:554
  346.6 19.4 %collective-permute-start.70 = (bf16[256,1536]{1,0:T(8,128)(2,1)S(1)}, bf16[256,1536]{1,0:T(8,128)(2,1)S(1)}, u32[]{:S(2)}, u32[]{:S(2)}) collective-permute-start(bf16[256,1536]{1,0:T(8,128)(2,1)S(1)} %pad_maximum_fusion.5), channel_id=1, source_target_pairs={{0,8},{4,12},{8,0},{12,4},{1,9},{5,13},{9,1},{13,5},{2,10},{6,14},... | collective-permute-start | bytes 2359304 | tf_op jit(solution)/shard_map/ppermute | solution.py:554
  367.5 64.4 %reduce-scatter.11.cloned.1.call-start = ((), (), s32[]{:S(2)}) async-start(), calls=%async_computation.8 | async-start | bytes 737280 | tf_op jit(solution)/shard_map/reduce_scatter | solution.py:843
  367.8 15.9 %collective-permute-start.71 = (bf16[2,48,1024]{2,1,0:T(8,128)(2,1)}, bf16[2,48,1024]{2,1,0:T(8,128)(2,1)S(1)}, u32[]{:S(2)}, u32[]{:S(2)}) collective-permute-start(bf16[2,48,1024]{2,1,0:T(8,128)(2,1)} %pad_maximum_fusion.27), channel_id=1, source_target_pairs={{0,4},{4,0},{8,12},{12,8},{1,5},{5,1},{9,13},{13,9},{2,6},{6,2},{1... | collective-permute-start | bytes 589832 | tf_op jit(solution)/shard_map/ppermute | solution.py:554
  368.8 14.9 %collective-permute-start.72 = (bf16[2,48,1024]{2,1,0:T(8,128)(2,1)}, bf16[2,48,1024]{2,1,0:T(8,128)(2,1)}, u32[]{:S(2)}, u32[]{:S(2)}) collective-permute-start(bf16[2,48,1024]{2,1,0:T(8,128)(2,1)} %pad_maximum_fusion.28), channel_id=1, source_target_pairs={{0,8},{4,12},{8,0},{12,4},{1,9},{5,13},{9,1},{13,5},{2,10},{6,14},... | collective-permute-start | bytes 589832 | tf_op jit(solution)/shard_map/ppermute | solution.py:554
  369.9 13.8 %collective-permute-start.73 = (bf16[2,48,1024]{2,1,0:T(8,128)(2,1)}, bf16[2,48,1024]{2,1,0:T(8,128)(2,1)}, u32[]{:S(2)}, u32[]{:S(2)}) collective-permute-start(bf16[2,48,1024]{2,1,0:T(8,128)(2,1)} %pad_maximum_fusion.29), channel_id=1, source_target_pairs={{0,12},{4,8},{8,4},{12,0},{1,13},{5,9},{9,5},{13,1},{2,14},{6,10},... | collective-permute-start | bytes 589832 | tf_op jit(solution)/shard_map/ppermute | solution.py:554
  384.9 26.0 %collective-permute-start.78 = (bf16[8,48,1024]{2,1,0:T(8,128)(2,1)S(1)}, bf16[8,48,1024]{2,1,0:T(8,128)(2,1)S(1)}, u32[]{:S(2)}, u32[]{:S(2)}) collective-permute-start(bf16[8,48,1024]{2,1,0:T(8,128)(2,1)S(1)} %bitcast.193), channel_id=1, source_target_pairs={{0,1},{1,2},{2,3},{4,5},{5,6},{6,7},{8,9},{9,10},{10,11},{12,13},{... | collective-permute-start | bytes 2359304 | tf_op jit(solution)/shard_map/ppermute | solution.py:615
  386.8 27.7 %collective-permute-start.80 = (bf16[8,48,1024]{2,1,0:T(8,128)(2,1)S(1)}, bf16[8,48,1024]{2,1,0:T(8,128)(2,1)S(1)}, u32[]{:S(2)}, u32[]{:S(2)}) collective-permute-start(bf16[8,48,1024]{2,1,0:T(8,128)(2,1)S(1)} %bitcast.194), channel_id=1, source_target_pairs={{1,0},{2,1},{3,2},{5,4},{6,5},{7,6},{9,8},{10,9},{11,10},{13,12},{... | collective-permute-start | bytes 2359304 | tf_op jit(solution)/shard_map/ppermute | solution.py:615
  390.8 96.9 %all-gather.10.cloned.1.call-start = ((), (), s32[]{:S(2)}) async-start(), calls=%async_computation.10 | async-start | bytes 1966080 | tf_op jit(solution)/shard_map/all_gather | solution.py:935
  391.8 29.6 %collective-permute-start.75 = (bf16[256,1536]{1,0:T(8,128)(2,1)}, bf16[256,1536]{1,0:T(8,128)(2,1)}, u32[]{:S(2)}, u32[]{:S(2)}) collective-permute-start(bf16[256,1536]{1,0:T(8,128)(2,1)} %get-tuple-element.461), channel_id=1, source_target_pairs={{0,4},{4,0},{8,12},{12,8},{1,5},{5,1},{9,13},{13,9},{2,6},{6,2},{1... | collective-permute-start | bytes 2359304 | tf_op jit(solution)/shard_map/ppermute | solution.py:554
  392.7 35.4 %collective-permute-start.76 = (bf16[256,1536]{1,0:T(8,128)(2,1)}, bf16[256,1536]{1,0:T(8,128)(2,1)}, u32[]{:S(2)}, u32[]{:S(2)}) collective-permute-start(bf16[256,1536]{1,0:T(8,128)(2,1)} %get-tuple-element.462), channel_id=1, source_target_pairs={{0,8},{4,12},{8,0},{12,4},{1,9},{5,13},{9,1},{13,5},{2,10},{6,14},... | collective-permute-start | bytes 2359304 | tf_op jit(solution)/shard_map/ppermute | solution.py:554
  393.9 34.2 %collective-permute-start.77 = (bf16[256,1536]{1,0:T(8,128)(2,1)}, bf16[256,1536]{1,0:T(8,128)(2,1)}, u32[]{:S(2)}, u32[]{:S(2)}) collective-permute-start(bf16[256,1536]{1,0:T(8,128)(2,1)} %get-tuple-element.463), channel_id=1, source_target_pairs={{0,12},{4,8},{8,4},{12,0},{1,13},{5,9},{9,5},{13,1},{2,14},{6,10},... | collective-permute-start | bytes 2359304 | tf_op jit(solution)/shard_map/ppermute | solution.py:554
  410.9 28.9 %collective-permute-start.79 = (bf16[8,48,1024]{2,1,0:T(8,128)(2,1)S(1)}, bf16[8,48,1024]{2,1,0:T(8,128)(2,1)}, u32[]{:S(2)}, u32[]{:S(2)}) collective-permute-start(bf16[8,48,1024]{2,1,0:T(8,128)(2,1)S(1)} %collective-permute-done.78.refs_2_), channel_id=1, source_target_pairs={{0,1},{1,2},{2,3},{4,5},{5,6},{6,7},{8,9},{9,10},{10,11},{12,13},{... | collective-permute-start | bytes 2359304 | tf_op jit(solution)/shard_map/ppermute | solution.py:615
  414.5 27.0 %collective-permute-start.81 = (bf16[8,48,1024]{2,1,0:T(8,128)(2,1)S(1)}, bf16[8,48,1024]{2,1,0:T(8,128)(2,1)}, u32[]{:S(2)}, u32[]{:S(2)}) collective-permute-start(bf16[8,48,1024]{2,1,0:T(8,128)(2,1)S(1)} %collective-permute-done.80.refs_4_), channel_id=1, source_target_pairs={{1,0},{2,1},{3,2},{5,4},{6,5},{7,6},{9,8},{10,9},{11,10},{13,12},{... | collective-permute-start | bytes 2359304 | tf_op jit(solution)/shard_map/ppermute | solution.py:615
  421.3 134.9 %all-gather.8.cloned.1.call-start = ((), (), s32[]{:S(2)}) async-start(), calls=%async_computation.9 | async-start | bytes 2211840 | tf_op jit(solution)/shard_map/all_gather | solution.py:950
  441.5 49.7 %collective-permute-start.82 = (bf16[8,48,1024]{2,1,0:T(8,128)(2,1)}, bf16[8,48,1024]{2,1,0:T(8,128)(2,1)}, u32[]{:S(2)}, u32[]{:S(2)}) collective-permute-start(bf16[8,48,1024]{2,1,0:T(8,128)(2,1)} %collective-permute-done.79.refs_1_), channel_id=1, source_target_pairs={{0,1},{1,2},{2,3},{4,5},{5,6},{6,7},{8,9},{9,10},{10,11},{12,13},{... | collective-permute-start | bytes 2359304 | tf_op jit(solution)/shard_map/ppermute | solution.py:615
  444.4 46.9 %collective-permute-start.83 = (bf16[8,48,1024]{2,1,0:T(8,128)(2,1)}, bf16[8,48,1024]{2,1,0:T(8,128)(2,1)}, u32[]{:S(2)}, u32[]{:S(2)}) collective-permute-start(bf16[8,48,1024]{2,1,0:T(8,128)(2,1)} %collective-permute-done.81.refs_5_), channel_id=1, source_target_pairs={{1,0},{2,1},{3,2},{5,4},{6,5},{7,6},{9,8},{10,9},{11,10},{13,12},{... | collective-permute-start | bytes 2359304 | tf_op jit(solution)/shard_map/ppermute | solution.py:615
  491.3 17.1 %collective-permute-start.84 = (bf16[128,1536]{1,0:T(8,128)(2,1)S(1)}, bf16[128,1536]{1,0:T(8,128)(2,1)S(1)}, u32[]{:S(2)}, u32[]{:S(2)}) collective-permute-start(bf16[128,1536]{1,0:T(8,128)(2,1)S(1)} %get-tuple-element.562), channel_id=1, source_target_pairs={{2,0},{0,1},{18,2},{16,3},{3,16},{1,17},{19,18},{17,19},{6,4},{4,5... | collective-permute-start | bytes 1179656 | tf_op jit(solution)/shard_map/ppermute | solution.py:671
  491.4 49.5 %collective-permute-start.85 = (bf16[128,1536]{1,0:T(8,128)(2,1)S(1)}, bf16[128,1536]{1,0:T(8,128)(2,1)S(1)}, u32[]{:S(2)}, u32[]{:S(2)}) collective-permute-start(bf16[128,1536]{1,0:T(8,128)(2,1)S(1)} %get-tuple-element.563), channel_id=1, source_target_pairs={{0,0},{2,1},{16,2},{18,3},{1,16},{3,17},{17,18},{19,19},{4,4},{6,5... | collective-permute-start | bytes 1179656 | tf_op jit(solution)/shard_map/ppermute | solution.py:671
  494.6 47.2 %collective-permute-start.86 = (bf16[128,1536]{1,0:T(8,128)(2,1)S(1)}, bf16[128,1536]{1,0:T(8,128)(2,1)S(1)}, u32[]{:S(2)}, u32[]{:S(2)}) collective-permute-start(bf16[128,1536]{1,0:T(8,128)(2,1)S(1)} %get-tuple-element.558), channel_id=1, source_target_pairs={{2,0},{0,1},{18,2},{16,3},{3,16},{1,17},{19,18},{17,19},{6,4},{4,5... | collective-permute-start | bytes 1179656 | tf_op jit(solution)/shard_map/ppermute | solution.py:671
  495.0 60.2 %collective-permute-start.87 = (bf16[128,1536]{1,0:T(8,128)(2,1)S(1)}, bf16[128,1536]{1,0:T(8,128)(2,1)S(1)}, u32[]{:S(2)}, u32[]{:S(2)}) collective-permute-start(bf16[128,1536]{1,0:T(8,128)(2,1)S(1)} %get-tuple-element.559), channel_id=1, source_target_pairs={{0,0},{2,1},{16,2},{18,3},{1,16},{3,17},{17,18},{19,19},{4,4},{6,5... | collective-permute-start | bytes 1179656 | tf_op jit(solution)/shard_map/ppermute | solution.py:671
  (124 other events, 1264.8 us)
Sparse Core Ops, SparseCore 0:
  108.3 60.3 all-gather.5
  270.6 57.7 reduce-scatter.4
  332.0 33.4 reduce-scatter.6
  368.2 29.9 reduce-scatter.8
  400.8 31.0 reduce-scatter.10
  433.3 54.3 all-gather.9
  489.9 58.0 all-gather.7

commit v6 on v5

--- a/solution.py
+++ b/solution.py
@@ -222,13 +222,11 @@
 
 def pack_qkv_kernel(ids, q_ref, k_ref, v_ref, small_ref, out_ref):
     rows = q_ref.shape[0]
-    zero = jnp.zeros((rows, HP - HD), BF)
     for dev in range(KVH):
         slot = ids[0] ^ dev
-        heads = [(q_ref, 2 * dev), (q_ref, 2 * dev + 1), (k_ref, dev), (v_ref, dev)]
-        for i, (ref, head) in enumerate(heads):
-            piece = ref[:, head * HD : (head + 1) * HD]
-            out_ref[slot, :rows, i * HP : (i + 1) * HP] = jnp.concatenate([piece, zero], 1)
+        pieces = [q_ref[:, 2 * dev * HD : 2 * (dev + 1) * HD]]
+        pieces += [ref[:, dev * HD : (dev + 1) * HD] for ref in (k_ref, v_ref)]
+        out_ref[slot, :rows, :] = jnp.concatenate(pieces, 1)
         out_ref[slot, rows:, :] = small_ref[...]
 
 
@@ -244,10 +242,12 @@
     got, x_refs = refs[:n_blk], refs[n_blk : n_blk + 2]
     w_ref, seg_ref, gain_ref, x_ref, c_ref, n_ref, small_sc = refs[n_blk + 2 :]
     n_rows = w_ref.shape[0] // (2 * n_blk)
+    zero = jnp.zeros((n_rows, HP - HD), BF)
     for k, ref in enumerate(got):
         for core in range(2):
             at = pl.multiple_of((ids[0] ^ (core * n_blk + k)) * n_rows, 16)
-            w_ref[pl.ds(at, n_rows), :] = ref[core, :n_rows, :]
+            heads = [ref[core, :n_rows, i * HD : (i + 1) * HD] for i in range(4)]
+            w_ref[pl.ds(at, n_rows), :] = jnp.concatenate([v for head in heads for v in (head, zero)], 1)
             small_sc[core * n_blk + k] = ref[core, n_rows:, :]
     gains = [[], []]
     for dev in range(2 * n_blk):
@@ -677,20 +677,19 @@
     n_rows = D // n_plane
     part = n_rows // n_head
     ff_here = FF // n_plane
-    width = 4 * HP
-    assert span % width == 0
-    seg_rows = span // width
-    small_rows = -(-(2 + 2 * seg_rows) // 16) * 16
-    gain_row = lambda v: jnp.pad(v, (0, width - n_rows))[None]
-    small = [gain_row(norm_gain_one), gain_row(norm_gain_two), segments[:, 0].astype(BF).reshape(2 * seg_rows, width)]
-    small.append(jnp.zeros((small_rows - 2 - 2 * seg_rows, width), BF))
+    width = 4 * HD
+    seg_rows = -(-2 * span // width)
+    small_rows = -(-(2 + seg_rows) // 16) * 16
+    gain_row = lambda v: jnp.pad(v, (0, width - n_rows))
+    small = [gain_row(norm_gain_one), gain_row(norm_gain_two), segments[:, 0].reshape(-1).astype(BF)]
     small = jnp.concatenate(small)
+    small = jnp.pad(small, (0, small_rows * width - small.shape[0])).reshape(small_rows, width)
     fence = Stages()
     join = jnp.concatenate
     share = n_rows // 4
 
     def pack_qkv(*values):
-        shape = jax.ShapeDtypeStruct((n_plane, n_rows + small_rows, 4 * HP), BF)
+        shape = jax.ShapeDtypeStruct((n_plane, n_rows + small_rows, width), BF)
         packed = place_call(pack_qkv_kernel, shape, ids, *values, name="pack_qkv")
         return packed.reshape((2, n_blk) + packed.shape[1:])
 
@@ -714,7 +713,7 @@
     qkv_w, seg_all, gains, x_low, cot, input_one = place_call(
         functools.partial(head_kernel, n_blk),
         (
-            jax.ShapeDtypeStruct((D, width), BF),
+            jax.ShapeDtypeStruct((D, 4 * HP), BF),
             jax.ShapeDtypeStruct((n_plane, small_rows, width), BF),
             jax.ShapeDtypeStruct((2, 1, D), F32),
             jax.ShapeDtypeStruct((own, D), BF),
@@ -728,7 +727,7 @@
         scratch=[pltpu.VMEM((n_plane, small_rows, width), BF)],
     )
     gain_one, gain_two = gains[0, 0], gains[1, 0]
-    seg_all = seg_all[:, 2 : 2 + 2 * seg_rows].reshape(2, n_blk, 2, span)
+    seg_all = seg_all[:, 2 : 2 + seg_rows].reshape(n_plane, -1)[:, : 2 * span].reshape(2, n_blk, 2, span)
     seg_seq = lax.dynamic_index_in_dim(seg_all, my_seq & 1, 0, keepdims=False)
     seg_seq = lax.dynamic_index_in_dim(seg_seq, my_seq >> 1, 1, keepdims=False)
     chunks = seg_seq.astype(jnp.int32).reshape(n_blk * n_head, tok)

time: 577 us -> 577 us (level)
    unnamed x198 -> x201, local copies, waits for them, and re-layouts: 21.4 us -> 21.5 us
  transfers between devices with their start and end apart: 99 -> 99, of which waited for: 42 -> 42; matrix products, arithmetic and copies ran while one was open for 12% -> 11% of each run, Pallas kernels for 22% -> 22%
where the time goes in v6:
time: 577 us; the launch traced here: 569 us
  waiting for transfers between devices  234 us (41%)
  Pallas kernels  137 us (24%)
  starting transfers between devices  94 us (16%)
  other arithmetic  45.5 us (8%)
  local copies, waits for them, and re-layouts  41.9 us (7%)
  between operations  16.5 us (3%)
    ppermute x80, waiting for transfers between devices, swap(): lax.ppermute(value, axis, [(i, i ^ mask) for i in range(lax.axis_size(axi...  124 us
    ppermute x80, starting transfers between devices, swap(): lax.ppermute(value, axis, [(i, i ^ mask) for i in range(lax.axis_size(axi...  62.9 us
    ppermute x4, waiting for transfers between devices, from_plane(): lax.ppermute(value[k * tok:(k + 1) * tok], ('dp', 'head'), back)  45.8 us
    pallas_call x5, Pallas kernels, simple_call(): pl.pallas_call(kernel, out_shape=out_shape, in_specs=whole(len(values)),...  37.7 us
    ppermute x3, waiting for transfers between devices, line_step(): lax.ppermute(left, 'head', up)  23.5 us
    all_gather x1, waiting for transfers between devices, per_device(): late_down = lax.all_gather(down_mine, 'head', axis=0)  22 us
    pallas_call x4, Pallas kernels, ff_call(): pl.pallas_call(ff_kernel, out_shape=(jax.ShapeDtypeStruct((2, rows, width...  21.7 us
    unnamed x201, local copies, waits for them, and re-layouts  21.5 us
  transfers between devices with their start and end apart: 99, of which 42 were waited for; matrix products, arithmetic and copies ran while one was open for 11% of the time, Pallas kernels for 22%

profile of v6, /device:TPU:8, one launch (start us, length us, event | category | flops | bytes accessed | tf_op | source)
XLA Modules:
  0.0 569.4 jit_solution(11507065648183363041)
XLA Ops:
  17.0 2.0 collective-permute-done
  19.2 3.4 collective-permute-done.1.refs_5_.refs_1_
  24.6 3.5 collective-permute-start.6
  38.6 4.0 collective-permute-done.3.refs_1_
  42.6 5.8 %collective-permute-done.4.refs_2_ = bf16[2,208,384]{2,1,0:T(8,128)(2,1)S(1)} collective-permute-done((bf16[2,208,384]{2,1,0:T(8,128)(2,1)S(1)}, bf16[2,208,384]{2,1,0:T(8,128)(2,1)S(1)}, u32[]{:S(2)}, u32[]{:S(2)}) %collective-permute-start.4) | collective-permute-done | bytes 319520 | tf_op jit(solution)/shard_map/ppermute | solution.py:554
  50.0 12.6 %collective-permute-done.6.refs_4_ = bf16[256,1536]{1,0:T(8,128)(2,1)S(1)} collective-permute-done((bf16[256,1536]{1,0:T(8,128)(2,1)S(1)}, bf16[256,1536]{1,0:T(8,128)(2,1)S(1)}, u32[]{:S(2)}, u32[]{:S(2)}) %collective-permute-start.6) | collective-permute-done | bytes 786464 | tf_op jit(solution)/shard_map/ppermute | solution.py:664
  68.6 17.4 %collective-permute-done.9.refs_1_ = bf16[256,1536]{1,0:T(8,128)(2,1)S(1)} collective-permute-done((bf16[256,1536]{1,0:T(8,128)(2,1)S(1)}, bf16[256,1536]{1,0:T(8,128)(2,1)S(1)}, u32[]{:S(2)}, u32[]{:S(2)}) %collective-permute-start.9) | collective-permute-done | bytes 786464 | tf_op jit(solution)/shard_map/ppermute | solution.py:554
  90.7 2.4 collective-permute-start.16
  93.2 11.2 %collective-permute-done.14 = bf16[2,48,1024]{2,1,0:T(8,128)(2,1)S(1)} collective-permute-done((bf16[2,48,1024]{2,1,0:T(8,128)(2,1)}, bf16[2,48,1024]{2,1,0:T(8,128)(2,1)S(1)}, u32[]{:S(2)}, u32[]{:S(2)}) %collective-permute-start.14) | collective-permute-done | bytes 196640 | tf_op jit(solution)/shard_map/ppermute | solution.py:554
  104.3 2.3 collective-permute-done.16
  117.9 7.6 %project_qkv.1.q_ref.kv_ref = bf16[2048,512]{1,0:T(8,128)(2,1)} custom-call(bf16[256,1536]{1,0:T(8,128)(2,1)S(1)} %copy-done.26, bf16[256,1536]{1,0:T(8,128)(2,1)S(1)} %collective-permute-done.9.refs_1_, bf16[256,1536]{1,0:T(8,128)(2,1)} %copy-done.11, bf16[256,1536]{1,0:T(8,128)(2,1)} %copy-done.15, bf16[256,1536]{1,0:T(8,128)(2,1)} %collective-permute-done.11.refs_4_, ...), custom_call_target="tpu_custom_call" | custom-call | flops 50331648 | bytes 155648 | tf_op jit(solution)/shard_map/project_qkv/pallas_call | solution.py:436
  127.1 14.9 %attn_fwd.1 = (bf16[2048,256]{1,0:T(8,128)(2,1)S(1)}, f32[8,2,256]{2,1,0:T(2,128)S(1)}) custom-call(s32[8,8]{1,0:T(8,128)S(1)} %and_convert_fusion.need, bf16[2048,512]{1,0:T(8,128)(2,1)S(1)} %copy-done, bf16[2048,512]{1,0:T(8,128)(2,1)S(1)} %copy-done, f32[8,1,256]{2,1,0:T(1,128)S(1)} %bitcast.199, f32[8,1,256]{2,1,0:T(1,128)S(1)} %bitcast.203, ...), custom_call_target="tpu_custom_call" | custom-call | flops 67108864 | bytes 131072 | tf_op jit(solution)/shard_map/attn_fwd/pallas_call | solution.py:176
  143.4 2.3 collective-permute-done.24
  150.2 1.8 slice.385
  152.0 3.1 collective-permute-done.25.refs_1_
  155.1 5.9 %collective-permute-done.26.refs_2_ = bf16[2,256,256]{2,1,0:T(8,128)(2,1)S(1)} collective-permute-done((bf16[2,256,256]{2,1,0:T(8,128)(2,1)S(1)}, bf16[2,256,256]{2,1,0:T(8,128)(2,1)S(1)}, u32[]{:S(2)}, u32[]{:S(2)}) %collective-permute-start.26) | collective-permute-done | bytes 262176 | tf_op jit(solution)/shard_map/ppermute | solution.py:554
  161.6 5.8 %out_project.1 = (f32[256,1536]{1,0:T(8,128)}, bf16[256,1536]{1,0:T(8,128)(2,1)}) custom-call(bf16[2,256,256]{2,1,0:T(8,128)(2,1)S(1)} %pad_maximum_fusion.14.refs_0_, bf16[2,256,256]{2,1,0:T(8,128)(2,1)S(1)} %collective-permute-done.25.refs_1_, bf16[2,256,256]{2,1,0:T(8,128)(2,1)S(1)} %collective-permute-done.26.refs_2_, ...), custom_call_target="tpu_custom_call" | custom-call | flops 18874368 | bytes 139360 | tf_op jit(solution)/shard_map/out_project/pallas_call | solution.py:436
  171.6 1.9 copy-done.39
  175.1 4.7 ff.4
  179.8 9.8 %collective-permute-done.35.n0.refs_1_ = bf16[256,1536]{1,0:T(8,128)(2,1)} collective-permute-done((bf16[256,1536]{1,0:T(8,128)(2,1)}, bf16[256,1536]{1,0:T(8,128)(2,1)}, u32[]{:S(2)}, u32[]{:S(2)}) %collective-permute-start.35) | collective-permute-done | bytes 786464 | tf_op jit(solution)/shard_map/ppermute | solution.py:554
  197.4 5.8 %ff.5 = (bf16[2,256,512]{2,1,0:T(8,128)(2,1)S(1)}, bf16[2,256,1024]{2,1,0:T(8,128)(2,1)S(1)}, f32[256,1536]{1,0:T(8,128)S(1)}, bf16[256,1536]{1,0:T(8,128)(2,1)S(1)}) custom-call(bf16[256,1536]{1,0:T(8,128)(2,1)} %collective-permute-done.35.n0.refs_1_, bf16[256,1536]{1,0:T(8,128)(2,1)S(1)} %collective-permute-done.42.n1.refs_5_, ...), custom_call_target="tpu_custom_call" | custom-call | flops 62914560 | bytes 196608 | tf_op jit(solution)/shard_map/ff/pallas_call | solution.py:366
  205.1 6.5 %ff.6 = (bf16[2,256,512]{2,1,0:T(8,128)(2,1)S(1)}, bf16[2,256,1024]{2,1,0:T(8,128)(2,1)S(1)}, f32[256,1536]{1,0:T(8,128)S(1)}, bf16[256,1536]{1,0:T(8,128)(2,1)S(1)}) custom-call(bf16[256,1536]{1,0:T(8,128)(2,1)} %collective-permute-done.36.n0.refs_2_, bf16[256,1536]{1,0:T(8,128)(2,1)S(1)} %collective-permute-done.43.n1.refs_6_, ...), custom_call_target="tpu_custom_call" | custom-call | flops 62914560 | bytes 196608 | tf_op jit(solution)/shard_map/ff/pallas_call | solution.py:366
  216.9 4.7 ff.7
  228.1 16.8 %ff_weight.1 = (bf16[4,8,48,1024]{3,2,1,0:T(8,128)(2,1)}, bf16[512,1536]{1,0:T(8,128)(2,1)}) custom-call(bf16[256,1536]{1,0:T(8,128)(2,1)} %get-tuple-element.339.n0.refs_0_, bf16[256,1536]{1,0:T(8,128)(2,1)} %collective-permute-done.35.n0.refs_1_, bf16[256,1536]{1,0:T(8,128)(2,1)} %collective-permute-done.36.n0.refs_2_, bf16[256,1536]{1,0:T(8,128)(2,1)} %copy-done.17, ...), custom_call_target="tpu_custom_call" | custom-call | flops 150994944 | bytes 393216 | tf_op jit(solution)/shard_map/ff_weight/pallas_call | solution.py:413
  245.0 17.3 %collective-permute-done.51.refs_10_ = bf16[256,1536]{1,0:T(8,128)(2,1)} collective-permute-done((bf16[256,1536]{1,0:T(8,128)(2,1)S(1)}, bf16[256,1536]{1,0:T(8,128)(2,1)}, u32[]{:S(2)}, u32[]{:S(2)}) %collective-permute-start.51) | collective-permute-done | bytes 786464 | tf_op jit(solution)/shard_map/ppermute | solution.py:554
  262.3 7.4 %branch.1 = (f32[256,1536]{1,0:T(8,128)}, bf16[256,1536]{1,0:T(8,128)(2,1)}, bf16[2,4,256,256]{3,2,1,0:T(8,128)(2,1)}) custom-call(bf16[192,1536]{1,0:T(8,128)(2,1)} %refs_0_.1, bf16[192,1536]{1,0:T(8,128)(2,1)S(1)} %copy-done.21, bf16[192,1536]{1,0:T(8,128)(2,1)S(1)} %copy-done.24, bf16[192,1536]{1,0:T(8,128)(2,1)} %copy-done.63, ...), custom_call_target="tpu_custom_call" | custom-call | flops 18874368 | bytes 225376 | tf_op jit(solution)/shard_map/branch/pallas_call | solution.py:436
  273.5 8.3 %back_project.2 = (f32[4,256,1536]{2,1,0:T(8,128)}, bf16[4,256,1536]{2,1,0:T(8,128)(2,1)}) custom-call(bf16[2,256,512]{2,1,0:T(8,128)(2,1)S(1)} %copy-done.43, bf16[2,256,512]{2,1,0:T(8,128)(2,1)S(1)} %copy-done.45, bf16[2,256,512]{2,1,0:T(8,128)(2,1)S(1)} %copy-done.47, bf16[2,256,512]{2,1,0:T(8,128)(2,1)} %copy-done.48, bf16[512,1536]{1,0:T(8,128)(2,1)} %refs_4_.3), custom_call_target="tpu_custom_call" | custom-call | flops 50331648 | bytes 204800 | tf_op jit(solution)/shard_map/back_project/pallas_call | solution.py:436
  284.0 1.8 collective-permute-start.56
  285.9 5.7 collective-permute-done.54
  291.6 4.9 collective-permute-done.55
  298.7 19.9 %attn_bwd.1.refs_8_.refs_0_ = bf16[2048,512]{1,0:T(8,128)(2,1)S(1)} custom-call(s32[8,8]{1,0:T(8,128)S(1)} %and_convert_fusion.need, bf16[2048,512]{1,0:T(8,128)(2,1)} %project_qkv.1.q_ref.kv_ref, bf16[2048,512]{1,0:T(8,128)(2,1)} %project_qkv.1.q_ref.kv_ref, f32[8,1,256]{2,1,0:T(1,128)S(1)} %bitcast.201, f32[8,1,256]{2,1,0:T(1,128)S(1)} %bitcast.205, ...), custom_call_target="tpu_custom_call" | custom-call | flops 167772160 | bytes 131072 | tf_op jit(solution)/shard_map/attn_bwd/pallas_call | solution.py:193
  318.7 2.1 slice.402
  322.3 1.8 slice.403
  324.6 4.6 add_convert_fusion.4
  332.4 7.6 %qkv_weight.1 = bf16[4,8,48,384]{3,2,1,0:T(8,128)(2,1)} custom-call(bf16[256,1536]{1,0:T(8,128)(2,1)S(1)} %copy-done.27, bf16[256,1536]{1,0:T(8,128)(2,1)S(1)} %copy-done.10, bf16[256,1536]{1,0:T(8,128)(2,1)S(1)} %copy-done.12, bf16[256,1536]{1,0:T(8,128)(2,1)S(1)} %copy-done.16, bf16[256,1536]{1,0:T(8,128)(2,1)} %collective-permute-done.11.refs_4_, ...), custom_call_target="tpu_custom_call" | custom-call | flops 100663296 | bytes 196608 | tf_op jit(solution)/shard_map/qkv_weight/pallas_call | solution.py:534
  348.4 8.6 %back_project.3 = (f32[4,256,1536]{2,1,0:T(8,128)}, bf16[4,256,1536]{2,1,0:T(8,128)(2,1)}) custom-call(bf16[2048,512]{1,0:T(8,128)(2,1)} %copy-done.2, bf16[1536,512]{1,0:T(8,128)(2,1)S(1)} %copy-done.8), custom_call_target="tpu_custom_call" | custom-call | flops 50331648 | bytes 204800 | tf_op jit(solution)/shard_map/back_project/pallas_call | solution.py:436
  359.1 7.0 %collective-permute-done.69 = bf16[256,1536]{1,0:T(8,128)(2,1)S(1)} collective-permute-done((bf16[256,1536]{1,0:T(8,128)(2,1)S(1)}, bf16[256,1536]{1,0:T(8,128)(2,1)S(1)}, u32[]{:S(2)}, u32[]{:S(2)}) %collective-permute-start.69) | collective-permute-done | bytes 786464 | tf_op jit(solution)/shard_map/ppermute | solution.py:554
  371.8 6.0 %out_weight.1 = bf16[192,1536]{1,0:T(8,128)(2,1)} custom-call(bf16[2048,256]{1,0:T(8,128)(2,1)} %copy-done.5, bf16[256,1536]{1,0:T(8,128)(2,1)S(1)} %copy-done.59, bf16[256,1536]{1,0:T(8,128)(2,1)} %collective-permute-done.58.refs_2_, bf16[256,1536]{1,0:T(8,128)(2,1)} %collective-permute-done.59.refs_3_, ...), custom_call_target="tpu_custom_call" | custom-call | flops 50331648 | bytes 147456 | tf_op jit(solution)/shard_map/out_weight/pallas_call | solution.py:913
  377.8 6.3 %fusion.10 = (bf16[256,1536]{1,0:T(8,128)(2,1)}, bf16[256,1536]{1,0:T(8,128)(2,1)}, bf16[256,1536]{1,0:T(8,128)(2,1)}, f32[256,1536]{1,0:T(8,128)}) fusion(f32[4,256,1536]{2,1,0:T(8,128)} %get-tuple-element.458, bf16[4,256,1536]{2,1,0:T(8,128)(2,1)} %collective-permute-done.74), kind=kLoop, calls=%fused_computation.29 | loop fusion | flops 4325376 | bytes 13369344 | tf_op jit(solution)/shard_map/convert_element_type | solution.py:930
  385.3 1.9 collective-permute-start.78
  387.2 4.0 collective-permute-start.80
  395.7 15.6 %collective-permute-done.78.refs_2_ = bf16[8,48,1024]{2,1,0:T(8,128)(2,1)S(1)} collective-permute-done((bf16[8,48,1024]{2,1,0:T(8,128)(2,1)S(1)}, bf16[8,48,1024]{2,1,0:T(8,128)(2,1)S(1)}, u32[]{:S(2)}, u32[]{:S(2)}) %collective-permute-start.78) | collective-permute-done | bytes 786464 | tf_op jit(solution)/shard_map/ppermute | solution.py:615
  411.3 3.6 collective-permute-start.79
  415.0 3.1 collective-permute-start.81
  418.1 3.7 add_convert_fusion
  421.8 6.7 %collective-permute-done.76 = bf16[256,1536]{1,0:T(8,128)(2,1)} collective-permute-done((bf16[256,1536]{1,0:T(8,128)(2,1)}, bf16[256,1536]{1,0:T(8,128)(2,1)}, u32[]{:S(2)}, u32[]{:S(2)}) %collective-permute-start.76) | collective-permute-done | bytes 786464 | tf_op jit(solution)/shard_map/ppermute | solution.py:554
  428.5 3.9 reduce-scatter.11.cloned.1.call-done
  432.4 7.9 %collective-permute-done.79.refs_1_ = bf16[8,48,1024]{2,1,0:T(8,128)(2,1)} collective-permute-done((bf16[8,48,1024]{2,1,0:T(8,128)(2,1)S(1)}, bf16[8,48,1024]{2,1,0:T(8,128)(2,1)}, u32[]{:S(2)}, u32[]{:S(2)}) %collective-permute-start.79) | collective-permute-done | bytes 786464 | tf_op jit(solution)/shard_map/ppermute | solution.py:615
  440.3 1.7 collective-permute-done.81.refs_5_
  442.1 2.8 collective-permute-start.82
  444.9 3.9 collective-permute-start.83
  450.4 3.0 fusion.2
  453.5 3.3 fusion.6
  457.8 2.4 collective-permute-start.91
  461.5 1.9 collective-permute-done.91
  466.2 22.0 %all-gather.10.cloned.1.call-done = bf16[512,1536]{1,0:T(8,128)(2,1)} async-done(((bf16[128,1536]{1,0:T(8,128)(2,1)}), bf16[512,1536]{1,0:T(8,128)(2,1)}) %all-gather.10.cloned.1.call-update) | async-done | bytes 1572880 | tf_op jit(solution)/shard_map/all_gather | solution.py:934
  488.2 3.5 convert_element_type.227
  491.8 3.2 collective-permute-start.85
  495.5 3.8 collective-permute-start.87
  499.3 5.0 place_columns.1
  504.4 2.5 multiply_reduce_fusion.1
  508.9 32.4 %collective-permute-done.85 = bf16[128,1536]{1,0:T(8,128)(2,1)S(1)} collective-permute-done((bf16[128,1536]{1,0:T(8,128)(2,1)S(1)}, bf16[128,1536]{1,0:T(8,128)(2,1)S(1)}, u32[]{:S(2)}, u32[]{:S(2)}) %collective-permute-start.85) | collective-permute-done | bytes 393248 | tf_op jit(solution)/shard_map/ppermute | solution.py:671
  542.4 13.3 %collective-permute-done.87 = bf16[128,1536]{1,0:T(8,128)(2,1)S(1)} collective-permute-done((bf16[128,1536]{1,0:T(8,128)(2,1)S(1)}, bf16[128,1536]{1,0:T(8,128)(2,1)S(1)}, u32[]{:S(2)}, u32[]{:S(2)}) %collective-permute-start.87) | collective-permute-done | bytes 393248 | tf_op jit(solution)/shard_map/ppermute | solution.py:671
  558.2 3.9 last.1
  (498 shorter events, 128.4 us)
Async XLA Ops:
  7.2 164.4 %all-gather.6.cloned.1.call-start = ((), (), s32[]{:S(2)}) async-start(), calls=%async_computation.4 | async-start | bytes 3932160 | tf_op jit(solution)/shard_map/all_gather | solution.py:786
  7.2 15.3 %collective-permute-start.1 = (bf16[192,1536]{1,0:T(8,128)(2,1)}, bf16[192,1536]{1,0:T(8,128)(2,1)S(1)}, u32[]{:S(2)}, u32[]{:S(2)}) collective-permute-start(bf16[192,1536]{1,0:T(8,128)(2,1)} %refs_0_.1), channel_id=1, source_target_pairs={{0,4},{4,0},{8,12},{12,8},{1,5},{5,1},{9,13},{13,9},{2,6},{6,2},{1... | collective-permute-start | bytes 1769480 | tf_op jit(solution)/shard_map/ppermute | solution.py:554
  8.8 15.0 %collective-permute-start.2 = (bf16[192,1536]{1,0:T(8,128)(2,1)}, bf16[192,1536]{1,0:T(8,128)(2,1)S(1)}, u32[]{:S(2)}, u32[]{:S(2)}) collective-permute-start(bf16[192,1536]{1,0:T(8,128)(2,1)} %refs_0_.1), channel_id=1, source_target_pairs={{0,8},{4,12},{8,0},{12,4},{1,9},{5,13},{9,1},{13,5},{2,10},{6,14},... | collective-permute-start | bytes 1769480 | tf_op jit(solution)/shard_map/ppermute | solution.py:554
  24.6 37.9 %collective-permute-start.6 = (bf16[256,1536]{1,0:T(8,128)(2,1)S(1)}, bf16[256,1536]{1,0:T(8,128)(2,1)S(1)}, u32[]{:S(2)}, u32[]{:S(2)}) collective-permute-start(bf16[256,1536]{1,0:T(8,128)(2,1)S(1)} %pad_maximum_fusion.1), channel_id=1, source_target_pairs={{0,0},{1,2},{2,16},{3,18},{16,1},{17,3},{18,17},{19,19},{4,4},{5,6... | collective-permute-start | bytes 2359304 | tf_op jit(solution)/shard_map/ppermute | solution.py:664
  32.1 30.5 %collective-permute-start.7 = (bf16[256,1536]{1,0:T(8,128)(2,1)S(1)}, bf16[256,1536]{1,0:T(8,128)(2,1)S(1)}, u32[]{:S(2)}, u32[]{:S(2)}) collective-permute-start(bf16[256,1536]{1,0:T(8,128)(2,1)S(1)} %pad_maximum_fusion.2), channel_id=1, source_target_pairs={{0,2},{1,0},{2,18},{3,16},{16,3},{17,1},{18,19},{19,17},{4,6},{5,4... | collective-permute-start | bytes 2359304 | tf_op jit(solution)/shard_map/ppermute | solution.py:664
  32.8 15.6 %collective-permute-start.4 = (bf16[2,208,384]{2,1,0:T(8,128)(2,1)S(1)}, bf16[2,208,384]{2,1,0:T(8,128)(2,1)S(1)}, u32[]{:S(2)}, u32[]{:S(2)}) collective-permute-start(bf16[2,208,384]{2,1,0:T(8,128)(2,1)S(1)} %get-tuple-element.260), channel_id=1, source_target_pairs={{0,8},{4,12},{8,0},{12,4},{1,9},{5,13},{9,1},{13,5},{2,10},{6,14},... | collective-permute-start | bytes 958472 | tf_op jit(solution)/shard_map/ppermute | solution.py:554
  34.3 15.7 %collective-permute-start.5 = (bf16[2,208,384]{2,1,0:T(8,128)(2,1)S(1)}, bf16[2,208,384]{2,1,0:T(8,128)(2,1)S(1)}, u32[]{:S(2)}, u32[]{:S(2)}) collective-permute-start(bf16[2,208,384]{2,1,0:T(8,128)(2,1)S(1)} %get-tuple-element.261), channel_id=1, source_target_pairs={{0,12},{4,8},{8,4},{12,0},{1,13},{5,9},{9,5},{13,1},{2,14},{6,10},... | collective-permute-start | bytes 958472 | tf_op jit(solution)/shard_map/ppermute | solution.py:554
  66.2 19.9 %collective-permute-start.9 = (bf16[256,1536]{1,0:T(8,128)(2,1)S(1)}, bf16[256,1536]{1,0:T(8,128)(2,1)S(1)}, u32[]{:S(2)}, u32[]{:S(2)}) collective-permute-start(bf16[256,1536]{1,0:T(8,128)(2,1)S(1)} %get-tuple-element.295.refs_0_), channel_id=1, source_target_pairs={{0,4},{4,0},{8,12},{12,8},{1,5},{5,1},{9,13},{13,9},{2,6},{6,2},{1... | collective-permute-start | bytes 2359304 | tf_op jit(solution)/shard_map/ppermute | solution.py:554
  66.7 19.6 %collective-permute-start.10 = (bf16[256,1536]{1,0:T(8,128)(2,1)S(1)}, bf16[256,1536]{1,0:T(8,128)(2,1)S(1)}, u32[]{:S(2)}, u32[]{:S(2)}) collective-permute-start(bf16[256,1536]{1,0:T(8,128)(2,1)S(1)} %get-tuple-element.295.refs_0_), channel_id=1, source_target_pairs={{0,8},{4,12},{8,0},{12,4},{1,9},{5,13},{9,1},{13,5},{2,10},{6,14},... | collective-permute-start | bytes 2359304 | tf_op jit(solution)/shard_map/ppermute | solution.py:554
  68.2 18.1 %collective-permute-start.11 = (bf16[256,1536]{1,0:T(8,128)(2,1)S(1)}, bf16[256,1536]{1,0:T(8,128)(2,1)}, u32[]{:S(2)}, u32[]{:S(2)}) collective-permute-start(bf16[256,1536]{1,0:T(8,128)(2,1)S(1)} %get-tuple-element.295.refs_0_), channel_id=1, source_target_pairs={{0,16},{16,0},{1,17},{17,1},{2,18},{18,2},{3,19},{19,3},{4,20},{20... | collective-permute-start | bytes 2359304 | tf_op jit(solution)/shard_map/ppermute | solution.py:554
  86.4 20.2 %collective-permute-start.12 = (bf16[128,1536]{1,0:T(8,128)(2,1)S(1)}, bf16[128,1536]{1,0:T(8,128)(2,1)S(1)}, u32[]{:S(2)}, u32[]{:S(2)}) collective-permute-start(bf16[128,1536]{1,0:T(8,128)(2,1)S(1)} %slice.365), channel_id=1, source_target_pairs={{0,8},{4,12},{8,0},{12,4},{1,9},{5,13},{9,1},{13,5},{2,10},{6,14},... | collective-permute-start | bytes 1179656 | tf_op jit(solution)/shard_map/ppermute | solution.py:554
  88.0 18.6 %collective-permute-start.13 = (bf16[128,1536]{1,0:T(8,128)(2,1)S(1)}, bf16[128,1536]{1,0:T(8,128)(2,1)S(1)}, u32[]{:S(2)}, u32[]{:S(2)}) collective-permute-start(bf16[128,1536]{1,0:T(8,128)(2,1)S(1)} %slice.366), channel_id=1, source_target_pairs={{0,4},{4,0},{8,12},{12,8},{1,5},{5,1},{9,13},{13,9},{2,6},{6,2},{1... | collective-permute-start | bytes 1179656 | tf_op jit(solution)/shard_map/ppermute | solution.py:554
  89.6 14.7 %collective-permute-start.14 = (bf16[2,48,1024]{2,1,0:T(8,128)(2,1)}, bf16[2,48,1024]{2,1,0:T(8,128)(2,1)S(1)}, u32[]{:S(2)}, u32[]{:S(2)}) collective-permute-start(bf16[2,48,1024]{2,1,0:T(8,128)(2,1)} %pad_maximum_fusion.23), channel_id=1, source_target_pairs={{0,4},{4,0},{8,12},{12,8},{1,5},{5,1},{9,13},{13,9},{2,6},{6,2},{1... | collective-permute-start | bytes 589832 | tf_op jit(solution)/shard_map/ppermute | solution.py:554
  90.2 14.1 %collective-permute-start.15 = (bf16[2,48,1024]{2,1,0:T(8,128)(2,1)}, bf16[2,48,1024]{2,1,0:T(8,128)(2,1)S(1)}, u32[]{:S(2)}, u32[]{:S(2)}) collective-permute-start(bf16[2,48,1024]{2,1,0:T(8,128)(2,1)} %pad_maximum_fusion.24), channel_id=1, source_target_pairs={{0,8},{4,12},{8,0},{12,4},{1,9},{5,13},{9,1},{13,5},{2,10},{6,14},... | collective-permute-start | bytes 589832 | tf_op jit(solution)/shard_map/ppermute | solution.py:554
  90.7 15.9 %collective-permute-start.16 = (bf16[2,48,1024]{2,1,0:T(8,128)(2,1)}, bf16[2,48,1024]{2,1,0:T(8,128)(2,1)S(1)}, u32[]{:S(2)}, u32[]{:S(2)}) collective-permute-start(bf16[2,48,1024]{2,1,0:T(8,128)(2,1)} %pad_maximum_fusion.25), channel_id=1, source_target_pairs={{0,12},{4,8},{8,4},{12,0},{1,13},{5,9},{9,5},{13,1},{2,14},{6,10},... | collective-permute-start | bytes 589832 | tf_op jit(solution)/shard_map/ppermute | solution.py:554
  104.3 43.1 %collective-permute-start.28 = (bf16[192,1536]{1,0:T(8,128)(2,1)}, bf16[192,1536]{1,0:T(8,128)(2,1)}, u32[]{:S(2)}, u32[]{:S(2)}) collective-permute-start(bf16[192,1536]{1,0:T(8,128)(2,1)} %refs_0_.1), channel_id=1, source_target_pairs={{0,16},{16,0},{1,17},{17,1},{2,18},{18,2},{3,19},{19,3},{4,20},{20... | collective-permute-start | bytes 1769480 | tf_op jit(solution)/shard_map/ppermute | solution.py:554
  108.5 233.4 %reduce-scatter.5.cloned.1.call-start = ((), (), s32[]{:S(2)}) async-start(), calls=%async_computation.5 | async-start | bytes 3932160 | tf_op jit(solution)/shard_map/reduce_scatter | solution.py:842
  111.4 31.3 %collective-permute-start.20 = (bf16[256,1536]{1,0:T(8,128)(2,1)S(1)}, bf16[256,1536]{1,0:T(8,128)(2,1)S(1)}, u32[]{:S(2)}, u32[]{:S(2)}) collective-permute-start(bf16[256,1536]{1,0:T(8,128)(2,1)S(1)} %get-tuple-element.310.c0.refs_8_.refs_13_), channel_id=1, source_target_pairs={{0,4},{4,0},{8,12},{12,8},{1,5},{5,1},{9,13},{13,9},{2,6},{6,2},{1... | collective-permute-start | bytes 2359304 | tf_op jit(solution)/shard_map/ppermute | solution.py:554
  112.8 29.8 %collective-permute-start.21 = (bf16[256,1536]{1,0:T(8,128)(2,1)S(1)}, bf16[256,1536]{1,0:T(8,128)(2,1)}, u32[]{:S(2)}, u32[]{:S(2)}) collective-permute-start(bf16[256,1536]{1,0:T(8,128)(2,1)S(1)} %get-tuple-element.310.c0.refs_8_.refs_13_), channel_id=1, source_target_pairs={{0,8},{4,12},{8,0},{12,4},{1,9},{5,13},{9,1},{13,5},{2,10},{6,14},... | collective-permute-start | bytes 2359304 | tf_op jit(solution)/shard_map/ppermute | solution.py:554
  115.4 26.6 %collective-permute-start.22 = (bf16[96,1536]{1,0:T(8,128)(2,1)S(1)}, bf16[96,1536]{1,0:T(8,128)(2,1)S(1)}, u32[]{:S(2)}, u32[]{:S(2)}) collective-permute-start(bf16[96,1536]{1,0:T(8,128)(2,1)S(1)} %slice.369), channel_id=1, source_target_pairs={{0,8},{4,12},{8,0},{12,4},{1,9},{5,13},{9,1},{13,5},{2,10},{6,14},... | collective-permute-start | bytes 884744 | tf_op jit(solution)/shard_map/ppermute | solution.py:554
  117.0 25.2 %collective-permute-start.23 = (bf16[96,1536]{1,0:T(8,128)(2,1)S(1)}, bf16[96,1536]{1,0:T(8,128)(2,1)S(1)}, u32[]{:S(2)}, u32[]{:S(2)}) collective-permute-start(bf16[96,1536]{1,0:T(8,128)(2,1)S(1)} %slice.370), channel_id=1, source_target_pairs={{0,4},{4,0},{8,12},{12,8},{1,5},{5,1},{9,13},{13,9},{2,6},{6,2},{1... | collective-permute-start | bytes 884744 | tf_op jit(solution)/shard_map/ppermute | solution.py:554
  152.0 15.4 %collective-permute-start.32 = (bf16[256,1536]{1,0:T(8,128)(2,1)S(1)}, bf16[256,1536]{1,0:T(8,128)(2,1)S(1)}, u32[]{:S(2)}, u32[]{:S(2)}) collective-permute-start(bf16[256,1536]{1,0:T(8,128)(2,1)S(1)} %get-tuple-element.310.c0.refs_8_.refs_13_), channel_id=1, source_target_pairs={{0,16},{16,0},{1,17},{17,1},{2,18},{18,2},{3,19},{19,3},{4,20},{20... | collective-permute-start | bytes 2359304 | tf_op jit(solution)/shard_map/ppermute | solution.py:554
  169.4 20.2 %collective-permute-start.35 = (bf16[256,1536]{1,0:T(8,128)(2,1)}, bf16[256,1536]{1,0:T(8,128)(2,1)}, u32[]{:S(2)}, u32[]{:S(2)}) collective-permute-start(bf16[256,1536]{1,0:T(8,128)(2,1)} %get-tuple-element.339.n0.refs_0_), channel_id=1, source_target_pairs={{0,4},{4,0},{8,12},{12,8},{1,5},{5,1},{9,13},{13,9},{2,6},{6,2},{1... | collective-permute-start | bytes 2359304 | tf_op jit(solution)/shard_map/ppermute | solution.py:554
  170.6 20.0 %collective-permute-start.36 = (bf16[256,1536]{1,0:T(8,128)(2,1)}, bf16[256,1536]{1,0:T(8,128)(2,1)}, u32[]{:S(2)}, u32[]{:S(2)}) collective-permute-start(bf16[256,1536]{1,0:T(8,128)(2,1)} %get-tuple-element.339.n0.refs_0_), channel_id=1, source_target_pairs={{0,8},{4,12},{8,0},{12,4},{1,9},{5,13},{9,1},{13,5},{2,10},{6,14},... | collective-permute-start | bytes 2359304 | tf_op jit(solution)/shard_map/ppermute | solution.py:554
  190.6 14.4 %collective-permute-start.43 = (bf16[256,1536]{1,0:T(8,128)(2,1)}, bf16[256,1536]{1,0:T(8,128)(2,1)S(1)}, u32[]{:S(2)}, u32[]{:S(2)}) collective-permute-start(bf16[256,1536]{1,0:T(8,128)(2,1)} %collective-permute-done.36.n0.refs_2_), channel_id=1, source_target_pairs={{0,16},{16,0},{1,17},{17,1},{2,18},{18,2},{3,19},{19,3},{4,20},{20... | collective-permute-start | bytes 2359304 | tf_op jit(solution)/shard_map/ppermute | solution.py:554
  193.2 19.4 %collective-permute-start.38 = (bf16[128,1536]{1,0:T(8,128)(2,1)S(1)}, bf16[128,1536]{1,0:T(8,128)(2,1)S(1)}, u32[]{:S(2)}, u32[]{:S(2)}) collective-permute-start(bf16[128,1536]{1,0:T(8,128)(2,1)S(1)} %slice.387), channel_id=1, source_target_pairs={{0,8},{4,12},{8,0},{12,4},{1,9},{5,13},{9,1},{13,5},{2,10},{6,14},... | collective-permute-start | bytes 1179656 | tf_op jit(solution)/shard_map/ppermute | solution.py:554
  194.1 18.5 %collective-permute-start.39 = (bf16[128,1536]{1,0:T(8,128)(2,1)S(1)}, bf16[128,1536]{1,0:T(8,128)(2,1)S(1)}, u32[]{:S(2)}, u32[]{:S(2)}) collective-permute-start(bf16[128,1536]{1,0:T(8,128)(2,1)S(1)} %slice.388), channel_id=1, source_target_pairs={{0,4},{4,0},{8,12},{12,8},{1,5},{5,1},{9,13},{13,9},{2,6},{6,2},{1... | collective-permute-start | bytes 1179656 | tf_op jit(solution)/shard_map/ppermute | solution.py:554
  195.6 17.1 %collective-permute-start.40 = (bf16[128,1536]{1,0:T(8,128)(2,1)S(1)}, bf16[128,1536]{1,0:T(8,128)(2,1)S(1)}, u32[]{:S(2)}, u32[]{:S(2)}) collective-permute-start(bf16[128,1536]{1,0:T(8,128)(2,1)S(1)} %copy-done.84), channel_id=1, source_target_pairs={{0,8},{4,12},{8,0},{12,4},{1,9},{5,13},{9,1},{13,5},{2,10},{6,14},... | collective-permute-start | bytes 1179656 | tf_op jit(solution)/shard_map/ppermute | solution.py:554
  196.1 17.2 %collective-permute-start.41 = (bf16[128,1536]{1,0:T(8,128)(2,1)S(1)}, bf16[128,1536]{1,0:T(8,128)(2,1)S(1)}, u32[]{:S(2)}, u32[]{:S(2)}) collective-permute-start(bf16[128,1536]{1,0:T(8,128)(2,1)S(1)} %copy-done.83), channel_id=1, source_target_pairs={{0,4},{4,0},{8,12},{12,8},{1,5},{5,1},{9,13},{13,9},{2,6},{6,2},{1... | collective-permute-start | bytes 1179656 | tf_op jit(solution)/shard_map/ppermute | solution.py:554
  224.5 20.4 %collective-permute-start.50 = (bf16[256,1536]{1,0:T(8,128)(2,1)S(1)}, bf16[256,1536]{1,0:T(8,128)(2,1)S(1)}, u32[]{:S(2)}, u32[]{:S(2)}) collective-permute-start(bf16[256,1536]{1,0:T(8,128)(2,1)S(1)} %add_convert_fusion.7), channel_id=1, source_target_pairs={{0,4},{4,0},{8,12},{12,8},{1,5},{5,1},{9,13},{13,9},{2,6},{6,2},{1... | collective-permute-start | bytes 2359304 | tf_op jit(solution)/shard_map/ppermute | solution.py:554
  226.0 36.3 %collective-permute-start.51 = (bf16[256,1536]{1,0:T(8,128)(2,1)S(1)}, bf16[256,1536]{1,0:T(8,128)(2,1)}, u32[]{:S(2)}, u32[]{:S(2)}) collective-permute-start(bf16[256,1536]{1,0:T(8,128)(2,1)S(1)} %add_convert_fusion.6), channel_id=1, source_target_pairs={{0,8},{4,12},{8,0},{12,4},{1,9},{5,13},{9,1},{13,5},{2,10},{6,14},... | collective-permute-start | bytes 2359304 | tf_op jit(solution)/shard_map/ppermute | solution.py:554
  226.5 35.8 %collective-permute-start.52 = (bf16[256,1536]{1,0:T(8,128)(2,1)S(1)}, bf16[256,1536]{1,0:T(8,128)(2,1)}, u32[]{:S(2)}, u32[]{:S(2)}) collective-permute-start(bf16[256,1536]{1,0:T(8,128)(2,1)S(1)} %add_convert_fusion.5), channel_id=1, source_target_pairs={{0,12},{4,8},{8,4},{12,0},{1,13},{5,9},{9,5},{13,1},{2,14},{6,10},... | collective-permute-start | bytes 2359304 | tf_op jit(solution)/shard_map/ppermute | solution.py:554
  270.9 113.2 %reduce-scatter.7.cloned.1.call-start = ((), (), s32[]{:S(2)}) async-start(), calls=%async_computation.6 | async-start | bytes 1966080 | tf_op jit(solution)/shard_map/reduce_scatter | solution.py:842
  281.8 14.7 %collective-permute-start.57 = (bf16[4,256,1536]{2,1,0:T(8,128)(2,1)}, bf16[4,256,1536]{2,1,0:T(8,128)(2,1)S(1)}, u32[]{:S(2)}, u32[]{:S(2)}) collective-permute-start(bf16[4,256,1536]{2,1,0:T(8,128)(2,1)} %get-tuple-element.423), channel_id=1, source_target_pairs={{0,16},{16,0},{1,17},{17,1},{2,18},{18,2},{3,19},{19,3},{4,20},{20... | collective-permute-start | bytes 9437192 | tf_op jit(solution)/shard_map/ppermute | solution.py:554
  296.5 22.2 %collective-permute-start.58 = (bf16[256,1536]{1,0:T(8,128)(2,1)S(1)}, bf16[256,1536]{1,0:T(8,128)(2,1)}, u32[]{:S(2)}, u32[]{:S(2)}) collective-permute-start(bf16[256,1536]{1,0:T(8,128)(2,1)S(1)} %copy-done.58), channel_id=1, source_target_pairs={{0,4},{4,0},{8,12},{12,8},{1,5},{5,1},{9,13},{13,9},{2,6},{6,2},{1... | collective-permute-start | bytes 2359304 | tf_op jit(solution)/shard_map/ppermute | solution.py:554
  298.0 20.6 %collective-permute-start.59 = (bf16[256,1536]{1,0:T(8,128)(2,1)S(1)}, bf16[256,1536]{1,0:T(8,128)(2,1)}, u32[]{:S(2)}, u32[]{:S(2)}) collective-permute-start(bf16[256,1536]{1,0:T(8,128)(2,1)S(1)} %copy-done.58), channel_id=1, source_target_pairs={{0,8},{4,12},{8,0},{12,4},{1,9},{5,13},{9,1},{13,5},{2,10},{6,14},... | collective-permute-start | bytes 2359304 | tf_op jit(solution)/shard_map/ppermute | solution.py:554
  320.7 19.2 %collective-permute-start.60 = (bf16[128,1536]{1,0:T(8,128)(2,1)}, bf16[128,1536]{1,0:T(8,128)(2,1)S(1)}, u32[]{:S(2)}, u32[]{:S(2)}) collective-permute-start(bf16[128,1536]{1,0:T(8,128)(2,1)} %slice.402), channel_id=1, source_target_pairs={{0,8},{4,12},{8,0},{12,4},{1,9},{5,13},{9,1},{13,5},{2,10},{6,14},... | collective-permute-start | bytes 1179656 | tf_op jit(solution)/shard_map/ppermute | solution.py:554
  324.0 16.5 %collective-permute-start.61 = (bf16[128,1536]{1,0:T(8,128)(2,1)}, bf16[128,1536]{1,0:T(8,128)(2,1)}, u32[]{:S(2)}, u32[]{:S(2)}) collective-permute-start(bf16[128,1536]{1,0:T(8,128)(2,1)} %slice.403), channel_id=1, source_target_pairs={{0,4},{4,0},{8,12},{12,8},{1,5},{5,1},{9,13},{13,9},{2,6},{6,2},{1... | collective-permute-start | bytes 1179656 | tf_op jit(solution)/shard_map/ppermute | solution.py:554
  332.2 89.6 %reduce-scatter.9.cloned.1.call-start = ((), (), s32[]{:S(2)}) async-start(), calls=%async_computation.7 | async-start | bytes 1474560 | tf_op jit(solution)/shard_map/reduce_scatter | solution.py:842
  332.2 14.1 %collective-permute-start.64 = (bf16[256,1536]{1,0:T(8,128)(2,1)}, bf16[256,1536]{1,0:T(8,128)(2,1)}, u32[]{:S(2)}, u32[]{:S(2)}) collective-permute-start(bf16[256,1536]{1,0:T(8,128)(2,1)} %get-tuple-element.429.refs_1_), channel_id=1, source_target_pairs={{0,16},{16,0},{1,17},{17,1},{2,18},{18,2},{3,19},{19,3},{4,20},{20... | collective-permute-start | bytes 2359304 | tf_op jit(solution)/shard_map/ppermute | solution.py:554
  340.0 19.1 %collective-permute-start.65 = (bf16[256,1536]{1,0:T(8,128)(2,1)}, bf16[256,1536]{1,0:T(8,128)(2,1)S(1)}, u32[]{:S(2)}, u32[]{:S(2)}) collective-permute-start(bf16[256,1536]{1,0:T(8,128)(2,1)} %collective-permute-done.58.refs_2_), channel_id=1, source_target_pairs={{0,16},{16,0},{1,17},{17,1},{2,18},{18,2},{3,19},{19,3},{4,20},{20... | collective-permute-start | bytes 2359304 | tf_op jit(solution)/shard_map/ppermute | solution.py:554
  340.6 18.6 %collective-permute-start.66 = (bf16[256,1536]{1,0:T(8,128)(2,1)}, bf16[256,1536]{1,0:T(8,128)(2,1)S(1)}, u32[]{:S(2)}, u32[]{:S(2)}) collective-permute-start(bf16[256,1536]{1,0:T(8,128)(2,1)} %collective-permute-done.59.refs_3_), channel_id=1, source_target_pairs={{0,16},{16,0},{1,17},{17,1},{2,18},{18,2},{3,19},{19,3},{4,20},{20... | collective-permute-start | bytes 2359304 | tf_op jit(solution)/shard_map/ppermute | solution.py:554
  343.1 16.0 %collective-permute-start.67 = (bf16[256,1536]{1,0:T(8,128)(2,1)S(1)}, bf16[256,1536]{1,0:T(8,128)(2,1)S(1)}, u32[]{:S(2)}, u32[]{:S(2)}) collective-permute-start(bf16[256,1536]{1,0:T(8,128)(2,1)S(1)} %constant_dynamic-update-slice_fusion.10.refs_4_), channel_id=1, source_target_pairs={{0,16},{16,0},{1,17},{17,1},{2,18},{18,2},{3,19},{19,3},{4,20},{20... | collective-permute-start | bytes 2359304 | tf_op jit(solution)/shard_map/ppermute | solution.py:554
  346.4 19.8 %collective-permute-start.69 = (bf16[256,1536]{1,0:T(8,128)(2,1)S(1)}, bf16[256,1536]{1,0:T(8,128)(2,1)S(1)}, u32[]{:S(2)}, u32[]{:S(2)}) collective-permute-start(bf16[256,1536]{1,0:T(8,128)(2,1)S(1)} %pad_maximum_fusion.4), channel_id=1, source_target_pairs={{0,4},{4,0},{8,12},{12,8},{1,5},{5,1},{9,13},{13,9},{2,6},{6,2},{1... | collective-permute-start | bytes 2359304 | tf_op jit(solution)/shard_map/ppermute | solution.py:554
  347.0 19.4 %collective-permute-start.70 = (bf16[256,1536]{1,0:T(8,128)(2,1)S(1)}, bf16[256,1536]{1,0:T(8,128)(2,1)S(1)}, u32[]{:S(2)}, u32[]{:S(2)}) collective-permute-start(bf16[256,1536]{1,0:T(8,128)(2,1)S(1)} %pad_maximum_fusion.5), channel_id=1, source_target_pairs={{0,8},{4,12},{8,0},{12,4},{1,9},{5,13},{9,1},{13,5},{2,10},{6,14},... | collective-permute-start | bytes 2359304 | tf_op jit(solution)/shard_map/ppermute | solution.py:554
  367.9 64.5 %reduce-scatter.11.cloned.1.call-start = ((), (), s32[]{:S(2)}) async-start(), calls=%async_computation.8 | async-start | bytes 737280 | tf_op jit(solution)/shard_map/reduce_scatter | solution.py:842
  368.2 15.9 %collective-permute-start.71 = (bf16[2,48,1024]{2,1,0:T(8,128)(2,1)}, bf16[2,48,1024]{2,1,0:T(8,128)(2,1)S(1)}, u32[]{:S(2)}, u32[]{:S(2)}) collective-permute-start(bf16[2,48,1024]{2,1,0:T(8,128)(2,1)} %pad_maximum_fusion.27), channel_id=1, source_target_pairs={{0,4},{4,0},{8,12},{12,8},{1,5},{5,1},{9,13},{13,9},{2,6},{6,2},{1... | collective-permute-start | bytes 589832 | tf_op jit(solution)/shard_map/ppermute | solution.py:554
  369.2 15.0 %collective-permute-start.72 = (bf16[2,48,1024]{2,1,0:T(8,128)(2,1)}, bf16[2,48,1024]{2,1,0:T(8,128)(2,1)}, u32[]{:S(2)}, u32[]{:S(2)}) collective-permute-start(bf16[2,48,1024]{2,1,0:T(8,128)(2,1)} %pad_maximum_fusion.28), channel_id=1, source_target_pairs={{0,8},{4,12},{8,0},{12,4},{1,9},{5,13},{9,1},{13,5},{2,10},{6,14},... | collective-permute-start | bytes 589832 | tf_op jit(solution)/shard_map/ppermute | solution.py:554
  370.2 13.9 %collective-permute-start.73 = (bf16[2,48,1024]{2,1,0:T(8,128)(2,1)}, bf16[2,48,1024]{2,1,0:T(8,128)(2,1)}, u32[]{:S(2)}, u32[]{:S(2)}) collective-permute-start(bf16[2,48,1024]{2,1,0:T(8,128)(2,1)} %pad_maximum_fusion.29), channel_id=1, source_target_pairs={{0,12},{4,8},{8,4},{12,0},{1,13},{5,9},{9,5},{13,1},{2,14},{6,10},... | collective-permute-start | bytes 589832 | tf_op jit(solution)/shard_map/ppermute | solution.py:554
  385.3 26.0 %collective-permute-start.78 = (bf16[8,48,1024]{2,1,0:T(8,128)(2,1)S(1)}, bf16[8,48,1024]{2,1,0:T(8,128)(2,1)S(1)}, u32[]{:S(2)}, u32[]{:S(2)}) collective-permute-start(bf16[8,48,1024]{2,1,0:T(8,128)(2,1)S(1)} %bitcast.195), channel_id=1, source_target_pairs={{0,1},{1,2},{2,3},{4,5},{5,6},{6,7},{8,9},{9,10},{10,11},{12,13},{... | collective-permute-start | bytes 2359304 | tf_op jit(solution)/shard_map/ppermute | solution.py:615
  387.2 27.7 %collective-permute-start.80 = (bf16[8,48,1024]{2,1,0:T(8,128)(2,1)S(1)}, bf16[8,48,1024]{2,1,0:T(8,128)(2,1)S(1)}, u32[]{:S(2)}, u32[]{:S(2)}) collective-permute-start(bf16[8,48,1024]{2,1,0:T(8,128)(2,1)S(1)} %bitcast.196), channel_id=1, source_target_pairs={{1,0},{2,1},{3,2},{5,4},{6,5},{7,6},{9,8},{10,9},{11,10},{13,12},{... | collective-permute-start | bytes 2359304 | tf_op jit(solution)/shard_map/ppermute | solution.py:615
  391.2 97.0 %all-gather.10.cloned.1.call-start = ((), (), s32[]{:S(2)}) async-start(), calls=%async_computation.10 | async-start | bytes 1966080 | tf_op jit(solution)/shard_map/all_gather | solution.py:934
  392.2 29.6 %collective-permute-start.75 = (bf16[256,1536]{1,0:T(8,128)(2,1)}, bf16[256,1536]{1,0:T(8,128)(2,1)}, u32[]{:S(2)}, u32[]{:S(2)}) collective-permute-start(bf16[256,1536]{1,0:T(8,128)(2,1)} %get-tuple-element.461), channel_id=1, source_target_pairs={{0,4},{4,0},{8,12},{12,8},{1,5},{5,1},{9,13},{13,9},{2,6},{6,2},{1... | collective-permute-start | bytes 2359304 | tf_op jit(solution)/shard_map/ppermute | solution.py:554
  393.1 35.4 %collective-permute-start.76 = (bf16[256,1536]{1,0:T(8,128)(2,1)}, bf16[256,1536]{1,0:T(8,128)(2,1)}, u32[]{:S(2)}, u32[]{:S(2)}) collective-permute-start(bf16[256,1536]{1,0:T(8,128)(2,1)} %get-tuple-element.462), channel_id=1, source_target_pairs={{0,8},{4,12},{8,0},{12,4},{1,9},{5,13},{9,1},{13,5},{2,10},{6,14},... | collective-permute-start | bytes 2359304 | tf_op jit(solution)/shard_map/ppermute | solution.py:554
  394.2 34.4 %collective-permute-start.77 = (bf16[256,1536]{1,0:T(8,128)(2,1)}, bf16[256,1536]{1,0:T(8,128)(2,1)}, u32[]{:S(2)}, u32[]{:S(2)}) collective-permute-start(bf16[256,1536]{1,0:T(8,128)(2,1)} %get-tuple-element.463), channel_id=1, source_target_pairs={{0,12},{4,8},{8,4},{12,0},{1,13},{5,9},{9,5},{13,1},{2,14},{6,10},... | collective-permute-start | bytes 2359304 | tf_op jit(solution)/shard_map/ppermute | solution.py:554
  411.3 29.0 %collective-permute-start.79 = (bf16[8,48,1024]{2,1,0:T(8,128)(2,1)S(1)}, bf16[8,48,1024]{2,1,0:T(8,128)(2,1)}, u32[]{:S(2)}, u32[]{:S(2)}) collective-permute-start(bf16[8,48,1024]{2,1,0:T(8,128)(2,1)S(1)} %collective-permute-done.78.refs_2_), channel_id=1, source_target_pairs={{0,1},{1,2},{2,3},{4,5},{5,6},{6,7},{8,9},{9,10},{10,11},{12,13},{... | collective-permute-start | bytes 2359304 | tf_op jit(solution)/shard_map/ppermute | solution.py:615
  415.0 27.1 %collective-permute-start.81 = (bf16[8,48,1024]{2,1,0:T(8,128)(2,1)S(1)}, bf16[8,48,1024]{2,1,0:T(8,128)(2,1)}, u32[]{:S(2)}, u32[]{:S(2)}) collective-permute-start(bf16[8,48,1024]{2,1,0:T(8,128)(2,1)S(1)} %collective-permute-done.80.refs_4_), channel_id=1, source_target_pairs={{1,0},{2,1},{3,2},{5,4},{6,5},{7,6},{9,8},{10,9},{11,10},{13,12},{... | collective-permute-start | bytes 2359304 | tf_op jit(solution)/shard_map/ppermute | solution.py:615
  421.8 135.0 %all-gather.8.cloned.1.call-start = ((), (), s32[]{:S(2)}) async-start(), calls=%async_computation.9 | async-start | bytes 2211840 | tf_op jit(solution)/shard_map/all_gather | solution.py:949
  442.1 49.6 %collective-permute-start.82 = (bf16[8,48,1024]{2,1,0:T(8,128)(2,1)}, bf16[8,48,1024]{2,1,0:T(8,128)(2,1)}, u32[]{:S(2)}, u32[]{:S(2)}) collective-permute-start(bf16[8,48,1024]{2,1,0:T(8,128)(2,1)} %collective-permute-done.79.refs_1_), channel_id=1, source_target_pairs={{0,1},{1,2},{2,3},{4,5},{5,6},{6,7},{8,9},{9,10},{10,11},{12,13},{... | collective-permute-start | bytes 2359304 | tf_op jit(solution)/shard_map/ppermute | solution.py:615
  444.9 46.8 %collective-permute-start.83 = (bf16[8,48,1024]{2,1,0:T(8,128)(2,1)}, bf16[8,48,1024]{2,1,0:T(8,128)(2,1)}, u32[]{:S(2)}, u32[]{:S(2)}) collective-permute-start(bf16[8,48,1024]{2,1,0:T(8,128)(2,1)} %collective-permute-done.81.refs_5_), channel_id=1, source_target_pairs={{1,0},{2,1},{3,2},{5,4},{6,5},{7,6},{9,8},{10,9},{11,10},{13,12},{... | collective-permute-start | bytes 2359304 | tf_op jit(solution)/shard_map/ppermute | solution.py:615
  491.8 17.1 %collective-permute-start.84 = (bf16[128,1536]{1,0:T(8,128)(2,1)S(1)}, bf16[128,1536]{1,0:T(8,128)(2,1)S(1)}, u32[]{:S(2)}, u32[]{:S(2)}) collective-permute-start(bf16[128,1536]{1,0:T(8,128)(2,1)S(1)} %get-tuple-element.558), channel_id=1, source_target_pairs={{2,0},{0,1},{18,2},{16,3},{3,16},{1,17},{19,18},{17,19},{6,4},{4,5... | collective-permute-start | bytes 1179656 | tf_op jit(solution)/shard_map/ppermute | solution.py:671
  491.8 49.5 %collective-permute-start.85 = (bf16[128,1536]{1,0:T(8,128)(2,1)S(1)}, bf16[128,1536]{1,0:T(8,128)(2,1)S(1)}, u32[]{:S(2)}, u32[]{:S(2)}) collective-permute-start(bf16[128,1536]{1,0:T(8,128)(2,1)S(1)} %get-tuple-element.559), channel_id=1, source_target_pairs={{0,0},{2,1},{16,2},{18,3},{1,16},{3,17},{17,18},{19,19},{4,4},{6,5... | collective-permute-start | bytes 1179656 | tf_op jit(solution)/shard_map/ppermute | solution.py:671
  495.1 47.2 %collective-permute-start.86 = (bf16[128,1536]{1,0:T(8,128)(2,1)S(1)}, bf16[128,1536]{1,0:T(8,128)(2,1)S(1)}, u32[]{:S(2)}, u32[]{:S(2)}) collective-permute-start(bf16[128,1536]{1,0:T(8,128)(2,1)S(1)} %get-tuple-element.554), channel_id=1, source_target_pairs={{2,0},{0,1},{18,2},{16,3},{3,16},{1,17},{19,18},{17,19},{6,4},{4,5... | collective-permute-start | bytes 1179656 | tf_op jit(solution)/shard_map/ppermute | solution.py:671
  495.5 60.2 %collective-permute-start.87 = (bf16[128,1536]{1,0:T(8,128)(2,1)S(1)}, bf16[128,1536]{1,0:T(8,128)(2,1)S(1)}, u32[]{:S(2)}, u32[]{:S(2)}) collective-permute-start(bf16[128,1536]{1,0:T(8,128)(2,1)S(1)} %get-tuple-element.555), channel_id=1, source_target_pairs={{0,0},{2,1},{16,2},{18,3},{1,16},{3,17},{17,18},{19,19},{4,4},{6,5... | collective-permute-start | bytes 1179656 | tf_op jit(solution)/shard_map/ppermute | solution.py:671
  (124 other events, 1267.3 us)
Sparse Core Ops, SparseCore 0:
  108.6 60.3 all-gather.5
  271.0 57.7 reduce-scatter.4
  332.3 33.4 reduce-scatter.6
  368.6 29.9 reduce-scatter.8
  401.3 31.0 reduce-scatter.10
  433.8 54.3 all-gather.9
  490.3 58.0 all-gather.7
